TPU v7x, 32 devices: a whole 2x2x4 slice. The times are simulated.
32 devices in a mesh: dp: 16 (over z, y, x), tensor: 2 (over core).
Axes of the slice: x: 2, y: 2, z: 4, core: 2. Of those that a mesh axis runs over, the one named last changes fastest.
Arguments:
- normed: bfloat16 [3072, 8192], P('dp', 'tensor'), may hold values from -6 to 6
- stored_queries: bfloat16 [3072, 4096], P('dp', 'tensor'), may hold values from -170 to 170
- stored_keys: bfloat16 [3072, 1024], P('dp', 'tensor'), may hold values from -7 to 7
- stored_values: bfloat16 [3072, 1024], P('dp', 'tensor'), may hold values from -6 to 6
- head_output_grad: bfloat16 [3072, 4096], P('dp', 'tensor'), may hold values from -6 to 6
- document_index: int32 [16, 192], P('dp'), may hold values from 0 to 7, never falling along the last dimension, each value on 1 to 72 neighbouring positions
- query_projection_weight: bfloat16 [8192, 4096], P('dp', 'tensor'), may hold values from -0.0625 to 0.0625
- key_projection_weight: bfloat16 [8192, 1024], P('dp', 'tensor'), may hold values from -0.0625 to 0.0625
- value_projection_weight: bfloat16 [8192, 1024], P('dp', 'tensor'), may hold values from -0.0625 to 0.0625
- adapter_down_maps: bfloat16 [8192, 192], P('tensor'), may hold values from -0.0625 to 0.0625
- query_up_map: bfloat16 [64, 4096], P(None, 'tensor'), may hold values from -0.75 to 0.75
- key_value_up_maps: bfloat16 [2, 64, 1024], P(None, None, 'tensor'), may hold values from -0.75 to 0.75
Outputs:
- normed_input_grad: bfloat16 [3072, 8192], P('dp', 'tensor')
- down_grad: float32 [8192, 192], P('tensor')
- query_up_grad: float32 [64, 4096], P(None, 'tensor')
- key_value_up_grad: float32 [2, 64, 1024], P(None, None, 'tensor')
All inputs are finite; a program needn't handle non-finite values.
Results may differ from a plain program's by a relative error of at most 0.0095.
Values may be sent and summed in bfloat16 or wider, within the bound.
No kernel may reach another device: no remote copies, remote signals or barrier semaphores. Data moves between devices by JAX's collectives and lax.ppermute only.
A program may use at most 192 MiB of HBM per device.

v0:
```python
import math

import jax
import jax.numpy as jnp
from jax import lax
from jax.sharding import PartitionSpec as P

QUERY_HEADS = 32
KEY_HEADS = 8
HEAD_SIZE = 128
ADAPTER_RANK = 64


adapter_scale = 0.5


def attention_backward(queries, keyrows, value_row_block, output_gradient, ids):
    token_count = queries.shape[0]
    key_value_heads = keyrows.shape[1] // HEAD_SIZE
    query_group = QUERY_HEADS // KEY_HEADS
    scale = 1.0 / math.sqrt(HEAD_SIZE)
    qmat = queries.reshape(token_count, key_value_heads, query_group, HEAD_SIZE)
    kmat = keyrows.reshape(token_count, key_value_heads, HEAD_SIZE)
    value_matrix = value_row_block.reshape(token_count, key_value_heads, HEAD_SIZE)
    output_matrix = output_gradient.reshape(token_count, key_value_heads, query_group, HEAD_SIZE)
    same = ids[:, None] == ids[None, :]
    scores = jnp.einsum("bmav,wmv->mabw", qmat, kmat, preferred_element_type=jnp.float32) * scale
    scores = jnp.where(same[None, None], scores, -1e30)
    probs = jax.nn.softmax(scores, axis=-1)
    probs_half = probs.astype(jnp.bfloat16)
    value_gradient = jnp.einsum(
        "kgtu,tkgd->ukd", probs_half, output_matrix, preferred_element_type=jnp.float32
    ).astype(jnp.bfloat16)
    probability_grad = jnp.einsum(
        "bmav,wmv->mabw", output_matrix, value_matrix, preferred_element_type=jnp.float32
    )
    row_dots = jnp.sum(probs * probability_grad, axis=-1, keepdims=True)
    score_grad = (probs * (probability_grad - row_dots) * scale).astype(jnp.bfloat16)
    query_gradient = jnp.einsum(
        "kgtu,ukd->tkgd", score_grad, kmat, preferred_element_type=jnp.float32
    ).astype(jnp.bfloat16)
    key_gradient = jnp.einsum(
        "kgtu,tkgd->ukd", score_grad, qmat, preferred_element_type=jnp.float32
    ).astype(jnp.bfloat16)
    return (
        query_gradient.reshape(token_count, -1),
        key_gradient.reshape(token_count, -1),
        value_gradient.reshape(token_count, -1),
    )


def rows_product(left, piece):
    return lax.dot_general(
        left, piece, (((1,), (1,)), ((), ())), preferred_element_type=jnp.float32
    )


def adapter_total(
    normed, adapter_middle, middle_gradient, query_gradient, key_gradient, value_gradient
):
    down_local = lax.dot_general(
        normed, middle_gradient, (((0,), (0,)), ((), ())), preferred_element_type=jnp.float32
    )
    local_query = adapter_scale * lax.dot_general(
        adapter_middle[:, 0:ADAPTER_RANK],
        query_gradient,
        (((0,), (0,)), ((), ())),
        preferred_element_type=jnp.float32,
    )
    local_key = adapter_scale * lax.dot_general(
        adapter_middle[:, ADAPTER_RANK : 2 * ADAPTER_RANK],
        key_gradient,
        (((0,), (0,)), ((), ())),
        preferred_element_type=jnp.float32,
    )
    local_value = adapter_scale * lax.dot_general(
        adapter_middle[:, 2 * ADAPTER_RANK : 3 * ADAPTER_RANK],
        value_gradient,
        (((0,), (0,)), ((), ())),
        preferred_element_type=jnp.float32,
    )
    down_total, query_total, key_value_total = lax.psum(
        (down_local, local_query, jnp.stack([local_key, local_value])), "dp"
    )
    return (down_total, query_total, key_value_total)


def shards(
    normed,
    stored_queries,
    stored_keys,
    stored_values,
    head_output_grad,
    document_index,
    query_projection_weight,
    key_projection_weight,
    value_projection_weight,
    adapter_down_maps,
    query_up_map,
    key_value_up_maps,
):
    query_gradient, key_gradient, value_gradient = attention_backward(
        stored_queries, stored_keys, stored_values, head_output_grad, document_index[0]
    )
    local_middle = jnp.dot(normed, adapter_down_maps, preferred_element_type=jnp.float32)
    grad_local = jnp.concatenate(
        [
            adapter_scale * rows_product(query_gradient, query_up_map),
            adapter_scale * rows_product(key_gradient, key_value_up_maps[0]),
            adapter_scale * rows_product(value_gradient, key_value_up_maps[1]),
        ],
        axis=1,
    )
    middle_total, grad_sum = (
        lax.psum(local_middle.astype(jnp.bfloat16), "tensor").astype(jnp.float32),
        lax.psum(grad_local.astype(jnp.bfloat16), "tensor").astype(jnp.float32),
    )
    adapter_middle = middle_total.astype(jnp.bfloat16)
    middle_gradient = grad_sum.astype(jnp.bfloat16)
    base_term = rows_product(
        query_gradient, lax.all_gather(query_projection_weight, "dp", axis=0, tiled=True)
    )
    base_term = base_term + rows_product(
        key_gradient, lax.all_gather(key_projection_weight, "dp", axis=0, tiled=True)
    )
    base_term = base_term + rows_product(
        value_gradient, lax.all_gather(value_projection_weight, "dp", axis=0, tiled=True)
    )
    base_offset = lax.psum_scatter(
        base_term.astype(jnp.bfloat16), "tensor", scatter_dimension=1, tiled=True
    ).astype(jnp.float32)
    normed_input_grad = (
        base_offset
        + lax.dot_general(
            middle_gradient,
            adapter_down_maps,
            (((1,), (1,)), ((), ())),
            preferred_element_type=jnp.float32,
        )
    ).astype(jnp.bfloat16)
    down_total, query_total, key_value_total = adapter_total(
        normed, adapter_middle, middle_gradient, query_gradient, key_gradient, value_gradient
    )
    return (normed_input_grad, down_total, query_total, key_value_total)


def solution(mesh):
    in_specs = (
        P("dp", "tensor"),
        P("dp", "tensor"),
        P("dp", "tensor"),
        P("dp", "tensor"),
        P("dp", "tensor"),
        P("dp", None),
        P("dp", "tensor"),
        P("dp", "tensor"),
        P("dp", "tensor"),
        P("tensor", None),
        P(None, "tensor"),
        P(None, None, "tensor"),
    )
    out_specs = (P("dp", "tensor"), P("tensor", None), P(None, "tensor"), P(None, None, "tensor"))
    return jax.shard_map(shards, mesh=mesh, in_specs=in_specs, out_specs=out_specs, check_vma=False)
```

profile of v0, /device:TPU:1, one launch (start us, length us, event | category | flops | bytes accessed | tf_op | source)
XLA Modules:
  0.0 784.4 jit_solution(11246477289122399510)
XLA Ops:
  10.9 2.6 reshape.63
  13.6 1.2 reshape.64
  15.5 2.2 fusion.34
  17.7 2.6 fusion.67
  20.3 7.6 fusion.15
  29.2 6.3 fusion.24
  35.5 2.7 fusion.25
  39.6 1.2 convolution_convert_fusion.1
  41.1 323.1 %all-gather.4.cloned.1.call-done = bf16[8192,2048]{1,0:T(8,128)(2,1)} async-done(((bf16[512,2048]{1,0:T(8,128)(2,1)}), bf16[8192,2048]{1,0:T(8,128)(2,1)}) %all-gather.4.cloned.1.call-update) | async-done | bytes 33554448 | tf_op jit(solution)/shard_map/all_gather | solution.py:121
  364.2 18.5 %fusion.68 = f32[192,8192]{1,0:T(8,128)} fusion(bf16[192,2048]{1,0:T(8,128)(2,1)S(1)} %reshape.66, bf16[8192,2048]{1,0:T(8,128)(2,1)} %all-gather.4.cloned.1.call-done), kind=kOutput, calls=%fused_computation.82 | convolution fusion | flops 6442450944 | bytes 40632320 | tf_op jit(solution)/shard_map/dot_general | solution.py:53
  382.7 94.9 %all-gather.6.cloned.1.call-done = bf16[8192,512]{1,0:T(8,128)(2,1)} async-done(((bf16[512,512]{1,0:T(8,128)(2,1)}), bf16[8192,512]{1,0:T(8,128)(2,1)}) %all-gather.6.cloned.1.call-update) | async-done | bytes 8388624 | tf_op jit(solution)/shard_map/all_gather | solution.py:124
  477.7 10.6 %convolution_add_fusion.1 = f32[192,8192]{1,0:T(8,128)} fusion(f32[192,8192]{1,0:T(8,128)} %fusion.68, bf16[8192,512]{1,0:T(8,128)(2,1)} %all-gather.6.cloned.1.call-done, bf16[4,24,8,128]{3,2,1,0:T(8,128)(2,1)S(1)} %fusion.24), kind=kOutput, calls=%fused_computation.3 | convolution fusion | flops 1612185600 | bytes 21168128 | tf_op jit(solution)/shard_map/dot_general | solution.py:53
  488.3 103.2 %all-gather.8.cloned.1.call-done = bf16[8192,512]{1,0:T(8,128)(2,1)} async-done(((bf16[512,512]{1,0:T(8,128)(2,1)}), bf16[8192,512]{1,0:T(8,128)(2,1)}) %all-gather.8.cloned.1.call-update) | async-done | bytes 8388624 | tf_op jit(solution)/shard_map/all_gather | solution.py:127
  591.5 9.7 %fusion.2 = bf16[192,8192]{1,0:T(8,128)(2,1)} fusion(f32[192,8192]{1,0:T(8,128)} %convolution_add_fusion.1, bf16[8192,512]{1,0:T(8,128)(2,1)} %all-gather.8.cloned.1.call-done, bf16[4,24,8,128]{3,2,1,0:T(8,128)(2,1)S(1)} %fusion.25), kind=kOutput, calls=%fused_computation.4 | convolution fusion | flops 1613758464 | bytes 18022400 | tf_op jit(solution)/shard_map/dot_general | solution.py:53
  601.3 1.0 fusion.28
  602.3 1.1 fusion.29
  603.4 0.7 pad_maximum_fusion
  604.1 1.9 convolution_multiply_fusion
  606.0 3.2 convolution_bitcast_fusion
  609.2 2.3 reduce-scatter.2.cloned.1.call-done
  611.5 3.1 fusion.3
  614.6 157.2 %all-reduce.5.cloned.1.call-done = (f32[4096,192]{0,1:T(8,128)}, f32[64,2048]{1,0:T(8,128)}, f32[2,64,512]{2,1,0:T(8,128)}) async-done(((f32[4096,192]{0,1:T(8,128)}, f32[64,2048]{1,0:T(8,128)}, f32[2,64,512]{2,1,0:T(8,128)}), (f32[4096,192]{0,1:T(8,128)}, f32[64,2048]{1,0:T(8,128)}, f32[2,64,512]{2,1,0:T(8,128)})) %all-reduce.5.cloned.1.call-update) | async-done | bytes 3932176 | tf_op jit(solution)/shard_map/psum | solution.py:82
  771.8 3.9 copy.92
  775.7 0.8 copy.93
  (52 shorter events, 7.3 us)
Async XLA Ops:
  8.0 31.6 %copy-start = (bf16[192,4096]{1,0:T(8,128)(2,1)S(1)}, bf16[192,4096]{1,0:T(8,128)(2,1)}, u32[]{:S(2)}) copy-start(bf16[192,4096]{1,0:T(8,128)(2,1)} %param.12) | copy-start | bytes 4718596
  8.0 2.3 copy-start.6
  8.0 5.5 copy-start.11
  8.0 6.7 copy-start.12
  8.0 356.2 %all-gather.4.cloned.1.call-start = ((), (), s32[]{:S(2)}) async-start(), calls=%async_computation.1 | async-start | bytes 35651584 | tf_op jit(solution)/shard_map/all_gather | solution.py:121
  8.8 468.9 %all-gather.6.cloned.1.call-start = ((), (), s32[]{:S(2)}) async-start(), calls=%async_computation.2 | async-start | bytes 8912896 | tf_op jit(solution)/shard_map/all_gather | solution.py:124
  9.5 582.0 %all-gather.8.cloned.1.call-start = ((), (), s32[]{:S(2)}) async-start(), calls=%async_computation.3 | async-start | bytes 8912896 | tf_op jit(solution)/shard_map/all_gather | solution.py:127
  10.3 591.1 %all-reduce.7.cloned.1.call-start = ((), (), s32[]{:S(2)}) async-start(), calls=%async_computation.6 | async-start | bytes 393216 | tf_op jit(solution)/shard_map/psum | solution.py:116
  10.9 4.6 copy-start.1
  13.5 4.2 copy-start.3
  29.2 6.3 copy-start.2
  35.5 2.7 copy-start.13
  35.5 3.1 copy-start.10
  35.5 4.1 copy-start.4
  40.9 570.6 %reduce-scatter.2.cloned.1.call-start = ((), (), s32[]{:S(2)}) async-start(), calls=%async_computation.4 | async-start | bytes 4718592 | tf_op jit(solution)/shard_map/reduce_scatter | solution.py:129
  601.2 170.6 %all-reduce.5.cloned.1.call-start = ((), (), s32[]{:S(2)}) async-start(), calls=%async_computation.5 | async-start | bytes 7864320 | tf_op jit(solution)/shard_map/psum | solution.py:82
  609.2 2.3 copy-start.5
  609.2 2.3 copy-start.8
  771.8 3.9 copy-start.7
  771.8 4.7 copy-start.9
Sparse Core Ops, SparseCore 0:
  11.7 352.5 all-gather.3
  367.0 110.6 all-gather.5
  480.5 111.0 all-gather.7
  609.5 162.2 all-reduce.4
Sparse Core Ops, SparseCore 1:
  41.0 20.4 all-reduce.6
  601.3 10.1 reduce-scatter.1
where the time goes:
time: 785 us; the launch traced here: 784 us
  waiting for transfers between devices  683 us (87%)
  matrix products  70.4 us (9%)
  between operations  15.4 us (2%)
  local copies, waits for them, and re-layouts  11.1 us (1%)
    all_gather x1, waiting for transfers between devices, shards(): lax.all_gather(query_projection_weight, 'dp', axis=0, tiled=True)  323 us
    psum x1, waiting for transfers between devices, adapter_total(): lax.psum((down_local, local_query, jnp.stack([local_key, local_value])),...  157 us
    all_gather x1, waiting for transfers between devices, shards(): lax.all_gather(value_projection_weight, 'dp', axis=0, tiled=True)  103 us
    all_gather x1, waiting for transfers between devices, shards(): lax.all_gather(key_projection_weight, 'dp', axis=0, tiled=True)  94.9 us
    dot_general x6, matrix products, rows_product(): lax.dot_general(left, piece, (((1,), (1,)), ((), ())), preferred_element_...  39.6 us
  transfers between devices with their start and end apart: 6, of which 5 were waited for; matrix products, arithmetic and copies ran while one was open for 10% of the time, Pallas kernels for 0%

commit v1 on v0

v1 whole, which is shorter than its diff:
```python
import math

import jax
import jax.numpy as jnp
from jax import lax
from jax.sharding import Mesh
from jax.sharding import PartitionSpec as P

QUERY_HEADS = 32
KEY_HEADS = 8
HEAD_SIZE = 128
ADAPTER_RANK = 64


adapter_scale = 0.5


def attention_backward(queries, keyrows, value_row_block, output_gradient, ids):
    token_count = queries.shape[0]
    key_value_heads = keyrows.shape[1] // HEAD_SIZE
    query_group = QUERY_HEADS // KEY_HEADS
    scale = 1.0 / math.sqrt(HEAD_SIZE)
    qmat = queries.reshape(token_count, key_value_heads, query_group, HEAD_SIZE)
    kmat = keyrows.reshape(token_count, key_value_heads, HEAD_SIZE)
    value_matrix = value_row_block.reshape(token_count, key_value_heads, HEAD_SIZE)
    output_matrix = output_gradient.reshape(token_count, key_value_heads, query_group, HEAD_SIZE)
    same = ids[:, None] == ids[None, :]
    scores = jnp.einsum("bmav,wmv->mabw", qmat, kmat, preferred_element_type=jnp.float32) * scale
    scores = jnp.where(same[None, None], scores, -1e30)
    probs = jax.nn.softmax(scores, axis=-1)
    probs_half = probs.astype(jnp.bfloat16)
    value_gradient = jnp.einsum(
        "kgtu,tkgd->ukd", probs_half, output_matrix, preferred_element_type=jnp.float32
    ).astype(jnp.bfloat16)
    probability_grad = jnp.einsum(
        "bmav,wmv->mabw", output_matrix, value_matrix, preferred_element_type=jnp.float32
    )
    row_dots = jnp.sum(probs * probability_grad, axis=-1, keepdims=True)
    score_grad = (probs * (probability_grad - row_dots) * scale).astype(jnp.bfloat16)
    query_gradient = jnp.einsum(
        "kgtu,ukd->tkgd", score_grad, kmat, preferred_element_type=jnp.float32
    ).astype(jnp.bfloat16)
    key_gradient = jnp.einsum(
        "kgtu,tkgd->ukd", score_grad, qmat, preferred_element_type=jnp.float32
    ).astype(jnp.bfloat16)
    return (
        query_gradient.reshape(token_count, -1),
        key_gradient.reshape(token_count, -1),
        value_gradient.reshape(token_count, -1),
    )


def rows_product(left, piece):
    return lax.dot_general(
        left, piece, (((1,), (1,)), ((), ())), preferred_element_type=jnp.float32
    )


def up_gradients(adapter_middle, query_gradient, key_gradient, value_gradient):
    rank = ADAPTER_RANK
    parts = []
    for place, gradient in enumerate((query_gradient, key_gradient, value_gradient)):
        parts.append(
            adapter_scale
            * lax.dot_general(
                adapter_middle[:, place * rank : (place + 1) * rank],
                gradient,
                (((0,), (0,)), ((), ())),
                preferred_element_type=jnp.float32,
            )
        )
    return parts


def make_shards(outer, inner, tensor):
    every = ("hi", "lo")

    def shards(
        normed,
        stored_queries,
        stored_keys,
        stored_values,
        head_output_grad,
        document_index,
        query_projection_weight,
        key_projection_weight,
        value_projection_weight,
        adapter_down_maps,
        query_up_map,
        key_value_up_maps,
    ):
        weights = lax.all_gather(
            jnp.concatenate(
                [query_projection_weight, key_projection_weight, value_projection_weight], axis=1
            ),
            "lo",
            axis=0,
            tiled=True,
        )
        query_gradient, key_gradient, value_gradient = attention_backward(
            stored_queries, stored_keys, stored_values, head_output_grad, document_index[0]
        )
        own = jnp.concatenate([query_gradient, key_gradient, value_gradient], axis=1)
        gathered = lax.all_gather(own, "hi", axis=0, tiled=True)
        local_middle = jnp.dot(normed, adapter_down_maps, preferred_element_type=jnp.float32)
        grad_local = jnp.concatenate(
            [
                adapter_scale * rows_product(query_gradient, query_up_map),
                adapter_scale * rows_product(key_gradient, key_value_up_maps[0]),
                adapter_scale * rows_product(value_gradient, key_value_up_maps[1]),
            ],
            axis=1,
        )
        middle_total, grad_sum = (
            lax.psum(local_middle.astype(jnp.bfloat16), "tensor").astype(jnp.float32),
            lax.psum(grad_local.astype(jnp.bfloat16), "tensor").astype(jnp.float32),
        )
        adapter_middle = middle_total.astype(jnp.bfloat16)
        middle_gradient = grad_sum.astype(jnp.bfloat16)

        down_local = lax.dot_general(
            normed, middle_gradient, (((0,), (0,)), ((), ())), preferred_element_type=jnp.float32
        )
        ups = up_gradients(adapter_middle, query_gradient, key_gradient, value_gradient)
        up_local = jnp.concatenate(ups, axis=1)
        down_piece = lax.psum_scatter(down_local, every, scatter_dimension=0, tiled=True)
        up_piece = lax.psum_scatter(up_local, every, scatter_dimension=1, tiled=True)
        down_total = lax.all_gather(down_piece, every, axis=0, tiled=True)
        up_total = lax.all_gather(up_piece, every, axis=1, tiled=True)
        q_width = query_gradient.shape[1]
        k_width = key_gradient.shape[1]
        query_total = up_total[:, :q_width]
        key_value_total = jnp.stack(
            [up_total[:, q_width : q_width + k_width], up_total[:, q_width + k_width :]]
        )

        term = rows_product(gathered, weights).astype(jnp.bfloat16)
        tokens = own.shape[0]
        block = weights.shape[0]
        summed = lax.psum_scatter(term, "tensor", scatter_dimension=1, tiled=True)
        piece = block // tensor
        moved = lax.all_to_all(
            summed.reshape(outer, tokens, piece), "hi", split_axis=0, concat_axis=0, tiled=True
        )
        moved = moved.reshape(tensor, outer // tensor, tokens, piece)
        moved = lax.all_to_all(moved, "tensor", split_axis=0, concat_axis=0, tiled=True)
        base = moved.transpose(2, 1, 0, 3).reshape(tokens, -1).astype(jnp.float32)
        normed_input_grad = (base + rows_product(middle_gradient, adapter_down_maps)).astype(
            jnp.bfloat16
        )
        return (normed_input_grad, down_total, query_total, key_value_total)

    return shards


def solution(mesh):
    ranks = mesh.shape["dp"]
    tensor = mesh.shape["tensor"]
    inner = math.gcd(ranks, 4)
    outer = ranks // inner
    split = Mesh(mesh.devices.reshape(outer, inner, tensor), ("hi", "lo", "tensor"))
    rows = ("hi", "lo")
    in_specs = (
        P(rows, "tensor"),
        P(rows, "tensor"),
        P(rows, "tensor"),
        P(rows, "tensor"),
        P(rows, "tensor"),
        P(rows, None),
        P(rows, "tensor"),
        P(rows, "tensor"),
        P(rows, "tensor"),
        P("tensor", None),
        P(None, "tensor"),
        P(None, None, "tensor"),
    )
    out_specs = (P(rows, "tensor"), P("tensor", None), P(None, "tensor"), P(None, None, "tensor"))
    return jax.shard_map(
        make_shards(outer, inner, tensor),
        mesh=split,
        in_specs=in_specs,
        out_specs=out_specs,
        check_vma=False,
    )
```

time: 785 us -> 620 us (0.79)
  waiting for transfers between devices: 683 us -> 465 us
  blocking collectives: 0 us -> 47.9 us
  matrix products: 70.4 us -> 47.4 us
  local copies, waits for them, and re-layouts: 11.1 us -> 26.9 us
    all_gather x3, waiting for transfers between devices: 521 us -> 229 us  [the longest x1 124 us: shards(): lax.all_gather(jnp.concatenate([query_projection_weight, key_projection_w...]
    psum x1 -> x0, waiting for transfers between devices: 157 us -> none  [adapter_total(): lax.psum((down_local, local_query, jnp.stack([local_key, local_value])),...]
    unnamed x6 -> x8, waiting for transfers between devices: 2.11 us -> 138 us
    reduce_scatter x1 -> x2, waiting for transfers between devices: 2.31 us -> 81.8 us  [the longest x1 66.8 us: shards(): lax.psum_scatter(down_local, every, scatter_dimension=0, tiled=True)]
    all_gather x0 -> x1, blocking collectives: none -> 42.1 us  [shards(): up_total = lax.all_gather(up_piece, every, axis=1, tiled=True)]
    dot_general x6 -> x5, matrix products: 39.6 us -> 22.6 us  [rows_product(): lax.dot_general(left, piece, (((1,), (1,)), ((), ())), preferred_element_...]
    psum x1, waiting for transfers between devices: 0.03 us -> 16.2 us  [shards(): lax.psum(grad_local.astype(jnp.bfloat16), 'tensor').astype(jnp.float32)]
    convert_element_type x0 -> x2, local copies, waits for them, and re-layouts: none -> 10.2 us  [shards(): base = moved.transpose(2, 1, 0, 3).reshape(tokens, -1).astype(jnp.float32)]
  transfers between devices with their start and end apart: 6 -> 8, of which waited for: 5 -> 7; matrix products, arithmetic and copies ran while one was open for 10% -> 5% of each run, Pallas kernels for 0% -> 0%
where the time goes in v1:
time: 620 us; the launch traced here: 619 us
  waiting for transfers between devices  465 us (75%)
  blocking collectives  47.9 us (8%)
  matrix products  47.4 us (8%)
  local copies, waits for them, and re-layouts  26.9 us (4%)
  between operations  15.4 us (2%)
  other arithmetic  10.9 us (2%)
    unnamed x8, waiting for transfers between devices  138 us
    all_gather x1, waiting for transfers between devices, shards(): lax.all_gather(jnp.concatenate([query_projection_weight, key_projection_w...  124 us
    all_gather x1, waiting for transfers between devices, shards(): gathered = lax.all_gather(own, 'hi', axis=0, tiled=True)  72.7 us
    reduce_scatter x1, waiting for transfers between devices, shards(): lax.psum_scatter(down_local, every, scatter_dimension=0, tiled=True)  66.8 us
    all_gather x1, blocking collectives, shards(): up_total = lax.all_gather(up_piece, every, axis=1, tiled=True)  42.1 us
    all_gather x1, waiting for transfers between devices, shards(): down_total = lax.all_gather(down_piece, every, axis=0, tiled=True)  32.4 us
    dot_general x5, matrix products, rows_product(): lax.dot_general(left, piece, (((1,), (1,)), ((), ())), preferred_element_...  22.6 us
    psum x1, waiting for transfers between devices, shards(): lax.psum(grad_local.astype(jnp.bfloat16), 'tensor').astype(jnp.float32)  16.2 us
  transfers between devices with their start and end apart: 8, of which 7 were waited for; matrix products, arithmetic and copies ran while one was open for 5% of the time, Pallas kernels for 0%

profile of v1, /device:TPU:1, one launch (start us, length us, event | category | flops | bytes accessed | tf_op | source)
XLA Modules:
  0.0 618.7 jit_solution(5851322405791780330)
XLA Ops:
  8.1 2.4 reshape.72
  12.9 2.3 reshape.74
  17.0 2.6 fusion.52
  19.6 2.2 fusion.31
  21.8 6.9 %fusion.14 = bf16[192,4,4,128]{3,0,2,1:T(8,128)(2,1)} fusion(f32[4,192,192,4]{2,1,3,0:T(8,128)} %fusion.31, bf16[192,4,128,1]{2,1,0,3:T(4,128)(2,1)S(1)} %bitcast.122, f32[4,4,192,192]{2,3,1,0:T(8,128)} %get-tuple-element.9, f32[4,4,192]{2,1,0:T(4,128)S(1)} %get-tuple-element.8), kind=kOutput, calls=%fused_computation.26 | convolution fusion | flops 155520192 | bytes 5713920 | tf_op jit(solution)/shard_map/kgtu,ukd->tkgd/dot_general | solution.py:40
  28.7 6.0 fusion.23
  34.7 2.6 fusion.24
  42.0 2.6 convolution_convert_fusion.2
  46.6 3.1 pad_maximum_fusion
  49.8 16.2 %all-reduce.3.cloned.1.call-done = (bf16[192,192]{0,1:T(8,128)(2,1)}, bf16[192,192]{1,0:T(8,128)(2,1)}) async-done(((bf16[192,192]{0,1:T(8,128)(2,1)}, bf16[192,192]{1,0:T(8,128)(2,1)}), (bf16[192,192]{0,1:T(8,128)(2,1)}, bf16[192,192]{1,0:T(8,128)(2,1)})) %all-reduce.3.cloned.1.call-update) | async-done | bytes 147472 | tf_op jit(solution)/shard_map/psum | solution.py:116
  66.0 3.1 convolution_bitcast_fusion
  69.4 72.7 %all-gather.5.cloned.1.call-done = bf16[768,3072]{1,0:T(8,128)(2,1)} async-done(((bf16[192,3072]{1,0:T(8,128)(2,1)}), bf16[768,3072]{1,0:T(8,128)(2,1)}) %all-gather.5.cloned.1.call-update) | async-done | bytes 4718608 | tf_op jit(solution)/shard_map/all_gather | solution.py:104
  142.1 123.9 %all-gather.7.cloned.1.call-done = bf16[2048,3072]{1,0:T(8,128)(2,1)} async-done(((bf16[512,3072]{1,0:T(8,128)(2,1)}), bf16[2048,3072]{1,0:T(8,128)(2,1)}) %all-gather.7.cloned.1.call-update) | async-done | bytes 12582928 | tf_op jit(solution)/shard_map/all_gather | solution.py:92
  266.1 15.4 %convolution_convert_fusion = bf16[768,2048]{1,0:T(8,128)(2,1)} fusion(bf16[768,3072]{1,0:T(8,128)(2,1)} %all-gather.5.cloned.1.call-done, bf16[2048,3072]{1,0:T(8,128)(2,1)} %all-gather.7.cloned.1.call-done), kind=kOutput, calls=%fused_computation.5 | convolution fusion | flops 9665249280 | bytes 20447232 | tf_op jit(solution)/shard_map/dot_general | solution.py:54
  284.9 66.8 %reduce-scatter.8.cloned.1.call-done = f32[256,192]{0,1:T(8,128)} async-done(((f32[4096,192]{0,1:T(8,128)}), f32[256,192]{0,1:T(8,128)}) %reduce-scatter.8.cloned.1.call-update) | async-done | bytes 196624 | tf_op jit(solution)/shard_map/reduce_scatter | solution.py:126
  351.8 14.9 %reduce-scatter.6.cloned.1.call-done = bf16[768,1024]{1,0:T(8,128)(2,1)} async-done(((bf16[768,2048]{1,0:T(8,128)(2,1)}), bf16[768,1024]{1,0:T(8,128)(2,1)}) %reduce-scatter.6.cloned.1.call-update) | async-done | bytes 1572880 | tf_op jit(solution)/shard_map/reduce_scatter | solution.py:140
  366.7 4.7 all-to-all-start
  371.4 138.0 %reduce-scatter.10.cloned.1.call-done = f32[192,64]{1,0:T(8,128)} async-done(((f32[3072,64]{1,0:T(8,128)}), f32[192,64]{1,0:T(8,128)}) %reduce-scatter.10.cloned.1.call-update) | async-done | bytes 49168
  510.3 42.1 %all-gather = f32[16,192,64]{1,2,0:T(8,128)S(1)} all-gather(f32[1,192,64]{1,2,0:T(8,128)S(1)} %bitcast.124), channel_id=1, replica_groups=mesh['hi'=4,'lo'=4,'tensor'=2] {'hi','lo'}, dimensions={0}, use_global_device_ids=true | all-gather | bytes 835584 | tf_op jit(solution)/shard_map/all_gather | solution.py:129
  555.0 32.4 %all-gather.9.cloned.1.call-done = f32[4096,192]{0,1:T(8,128)} async-done(((f32[256,192]{0,1:T(8,128)}), f32[4096,192]{0,1:T(8,128)}) %all-gather.9.cloned.1.call-update) | async-done | bytes 3145744 | tf_op jit(solution)/shard_map/all_gather | solution.py:128
  589.0 5.8 all_to_all.10
  595.9 4.5 copy.63
  600.4 5.8 reshape.80
  606.2 3.8 fusion.2
  (59 shorter events, 22.4 us)
Async XLA Ops:
  8.0 34.0 %copy-start = (bf16[192,4096]{1,0:T(8,128)(2,1)S(1)}, bf16[192,4096]{1,0:T(8,128)(2,1)}, u32[]{:S(2)}) copy-start(bf16[192,4096]{1,0:T(8,128)(2,1)} %param.12) | copy-start | bytes 4718596
  8.0 58.0 %all-reduce.3.cloned.1.call-start = ((), (), s32[]{:S(2)}) async-start(), calls=%async_computation.11 | async-start | bytes 393216 | tf_op jit(solution)/shard_map/psum | solution.py:116
  16.2 0.8 copy-start.8
  34.7 2.6 copy-start.4
  44.6 2.0 copy-start.5
  45.3 96.8 %all-gather.5.cloned.1.call-start = ((), (), s32[]{:S(2)}) async-start(), calls=%async_computation.5 | async-start | bytes 5898240 | tf_op jit(solution)/shard_map/all_gather | solution.py:104
  46.6 219.5 %all-gather.7.cloned.1.call-start = ((), (), s32[]{:S(2)}) async-start(), calls=%async_computation.6 | async-start | bytes 15728640 | tf_op jit(solution)/shard_map/all_gather | solution.py:92
  49.8 301.9 %reduce-scatter.8.cloned.1.call-start = ((), (), s32[]{:S(2)}) async-start(), calls=%async_computation.8 | async-start | bytes 3342336 | tf_op jit(solution)/shard_map/reduce_scatter | solution.py:126
  69.2 297.5 %reduce-scatter.6.cloned.1.call-start = ((), (), s32[]{:S(2)}) async-start(), calls=%async_computation.7 | async-start | bytes 4718592 | tf_op jit(solution)/shard_map/reduce_scatter | solution.py:140
  281.5 0.9 copy-start.7
  281.5 227.9 %reduce-scatter.10.cloned.1.call-start = ((), (), s32[]{:S(2)}) async-start(), calls=%async_computation.10 | async-start | bytes 1671168
  284.8 302.6 %all-gather.9.cloned.1.call-start = ((), (), s32[]{:S(2)}) async-start(), calls=%async_computation.9 | async-start | bytes 3342336 | tf_op jit(solution)/shard_map/all_gather | solution.py:128
  366.7 220.7 %all-to-all-start = ((bf16[4,192,1024]{2,1,0:T(8,128)(2,1)}), bf16[4,192,1024]{2,1,0:T(8,128)(2,1)S(1)}, u32[]{:S(2)}, u32[]{:S(2)}) async-start(bf16[4,192,1024]{2,1,0:T(8,128)(2,1)} %bitcast.120), calls=%async_computation.1 | async-start | bytes 3145728 | tf_op jit(solution)/shard_map/all_to_all | solution.py:142
  600.4 5.8 copy-start.3
  600.4 5.8 copy-start.6
  606.2 3.8 copy-start.2
  606.2 5.5 copy-start.1
Sparse Core Ops, SparseCore 0:
  45.4 20.5 all-reduce.2
  71.0 280.6 reduce-scatter.7
  354.5 12.0 reduce-scatter.5
  372.6 136.6 reduce-scatter.9
  512.3 75.0 all-gather.8
Sparse Core Ops, SparseCore 1:
  47.9 94.2 all-gather.4
  144.4 121.6 all-gather.6

commit v2 on v1

--- a/solution.py
+++ b/solution.py
@@ -3,6 +3,8 @@
 import jax
 import jax.numpy as jnp
 from jax import lax
+from jax.experimental import pallas as pl
+from jax.experimental.pallas import tpu as pltpu
 from jax.sharding import Mesh
 from jax.sharding import PartitionSpec as P
 
@@ -72,7 +74,7 @@
     return parts
 
 
-def make_shards(outer, inner, tensor):
+def general_shards(outer, inner, tensor):
     every = ("hi", "lo")
 
     def shards(
@@ -153,12 +155,277 @@
     return shards
 
 
+SIZES = (4, 4, 2)
+AXES = ("hi", "lo", "tensor")
+
+
+def send(value, target):
+    pairs = []
+    for rank in range(32):
+        hi, lo, core = rank // 8, rank // 2 % 4, rank % 2
+        there = target(hi, lo, core)
+        if there is not None:
+            pairs.append((rank, there[0] * 8 + there[1] * 2 + there[2]))
+    return lax.ppermute(value, AXES, pairs)
+
+
+def swap_lo(value, bit):
+    return send(value, lambda hi, lo, core: (hi, lo ^ bit, core))
+
+
+def swap_core(value):
+    return send(value, lambda hi, lo, core: (hi, lo, 1 - core))
+
+
+def turn_hi(value, step):
+    return send(value, lambda hi, lo, core: ((hi + step) % 4, lo, core))
+
+
+def move_hi(value, step, first, last):
+    return send(
+        value,
+        lambda hi, lo, core: (hi + step, lo, core) if first <= hi <= last else None,
+    )
+
+
+def pick(value, index, axis):
+    return lax.dynamic_index_in_dim(value, index, axis, keepdims=False)
+
+
+def term_kernel(turn_ref, a0, a1, a2, a3, right_ref, out_ref, left, arrived):
+    del turn_ref
+    tokens = a0.shape[0]
+
+    @pl.when(pl.program_id(0) == 0)
+    def _():
+        copies = [
+            pltpu.make_async_copy(a, left.at[pl.ds(n * tokens, tokens), :], arrived.at[n])
+            for n, a in enumerate((a0, a1, a2, a3))
+        ]
+        for copy in copies:
+            copy.start()
+        for copy in copies:
+            copy.wait()
+
+    out_ref[...] = lax.dot_general(
+        left[...],
+        right_ref[...],
+        (((1,), (1,)), ((), ())),
+        preferred_element_type=jnp.float32,
+    ).astype(jnp.bfloat16)[None]
+
+
+def term_halves(slots, weights, core):
+    tokens, depth = slots[0].shape
+    rows = weights.shape[0] // 2
+    return pl.pallas_call(
+        term_kernel,
+        out_shape=jax.ShapeDtypeStruct((2, 4 * tokens, rows), jnp.bfloat16),
+        grid_spec=pltpu.PrefetchScalarGridSpec(
+            num_scalar_prefetch=1,
+            grid=(2,),
+            in_specs=[pl.BlockSpec(memory_space=pl.ANY)] * 4
+            + [pl.BlockSpec((rows, depth), lambda i, turn: (lax.rem(turn[0] + 1 - i, 2), 0))],
+            out_specs=pl.BlockSpec((1, 4 * tokens, rows), lambda i, turn: (1 - i, 0, 0)),
+            scratch_shapes=[
+                pltpu.VMEM((4 * tokens, depth), jnp.bfloat16),
+                pltpu.SemaphoreType.DMA((4,)),
+            ],
+        ),
+        compiler_params=pltpu.CompilerParams(vmem_limit_bytes=40 << 20),
+        cost_estimate=pl.CostEstimate(
+            flops=16 * tokens * depth * rows,
+            bytes_accessed=8 * tokens * depth + 4 * rows * depth + 16 * tokens * rows,
+            transcendentals=0,
+        ),
+        name="term",
+    )(core[None], *slots, weights)
+
+
+def finish_kernel(order_ref, piece_ref, middle_ref, down_ref, out_ref):
+    del order_ref
+    added = lax.dot_general(
+        middle_ref[...],
+        down_ref[...],
+        (((1,), (1,)), ((), ())),
+        preferred_element_type=jnp.float32,
+    )
+    out_ref[...] = (piece_ref[0].astype(jnp.float32) + added).astype(jnp.bfloat16)
+
+
+def finish(pieces, order, middle_gradient, down_maps, width):
+    tokens = pieces.shape[1]
+    columns = down_maps.shape[0]
+    rank = middle_gradient.shape[1]
+    each = pieces.shape[2] // width
+    return pl.pallas_call(
+        finish_kernel,
+        out_shape=jax.ShapeDtypeStruct((tokens, columns), jnp.bfloat16),
+        grid_spec=pltpu.PrefetchScalarGridSpec(
+            num_scalar_prefetch=1,
+            grid=(columns // width,),
+            in_specs=[
+                pl.BlockSpec(
+                    (1, tokens, width),
+                    lambda c, order: (lax.div(order[c], each), 0, lax.rem(order[c], each)),
+                ),
+                pl.BlockSpec((tokens, rank), lambda c, order: (0, 0)),
+                pl.BlockSpec((width, rank), lambda c, order: (c, 0)),
+            ],
+            out_specs=pl.BlockSpec((tokens, width), lambda c, order: (0, c)),
+        ),
+        cost_estimate=pl.CostEstimate(
+            flops=2 * tokens * columns * rank,
+            bytes_accessed=4 * tokens * columns + 2 * columns * rank,
+            transcendentals=0,
+        ),
+        name="finish",
+    )(order, pieces, middle_gradient, down_maps)
+
+
+def plane_scatter(value, bits):
+    lo = lax.axis_index("lo")
+    for bit in bits:
+        mine = (lo // bit) % 2
+        axis = 2 if bit == 1 and value.ndim == 5 else 1
+        sent = pick(value, 1 - mine, axis).astype(jnp.bfloat16)
+        value = pick(value, mine, axis) + swap_lo(sent, bit).astype(jnp.float32)
+    return value
+
+
+def dp_pieces(down_local, up_local):
+    rows, rank = down_local.shape
+    return jnp.concatenate(
+        [
+            down_local.reshape(16, rows // 16, rank),
+            up_local.reshape(-1, 16, rank).transpose(1, 0, 2),
+        ],
+        axis=1,
+    )
+
+
+def dp_scatter(pieces):
+    hi = lax.axis_index("hi")
+    pieces = pieces.reshape(4, 2, 2, *pieces.shape[1:])
+    column = jnp.concatenate(
+        [plane_scatter(pieces[:2], (1, 2)), plane_scatter(pieces[2:], (2, 1))], axis=0
+    )
+    total = pick(column, hi, 0)
+    for step in range(1, 4):
+        sent = pick(column, (hi + step) % 4, 0).astype(jnp.bfloat16)
+        total = total + turn_hi(sent, step).astype(jnp.float32)
+    return total.astype(jnp.bfloat16)
+
+
+def gather_hi(own):
+    hi = lax.axis_index("hi")
+    right, left = [own], [own]
+    for step in range(1, 4):
+        right.append(move_hi(right[-1], 1, step - 1, 2))
+        left.append(move_hi(left[-1], -1, 1, 4 - step))
+    slots = [
+        own,
+        jnp.where(hi == 3, right[1], left[1]),
+        jnp.where(hi < 2, left[2], right[2]),
+        jnp.where(hi == 0, left[3], jnp.where(hi == 3, right[3], right[1])),
+    ]
+    table = jnp.array([[0, 1, 2, 3], [3, 0, 1, 2], [2, 3, 0, 1], [3, 2, 1, 0]], jnp.int32)
+    return slots, pick(table, hi, 0)
+
+
+def fast_shards():
+    def shards(
+        normed,
+        stored_queries,
+        stored_keys,
+        stored_values,
+        head_output_grad,
+        document_index,
+        query_projection_weight,
+        key_projection_weight,
+        value_projection_weight,
+        adapter_down_maps,
+        query_up_map,
+        key_value_up_maps,
+    ):
+        hi, lo, core = (lax.axis_index(name) for name in AXES)
+        own_weights = jnp.concatenate(
+            [query_projection_weight, key_projection_weight, value_projection_weight], axis=1
+        )
+        cut = own_weights.shape[0] // 2
+        weights = []
+        for part in range(2):
+            rows = own_weights[part * cut : (part + 1) * cut]
+            weights.append(lax.all_gather(rows, "lo", axis=0, tiled=True))
+
+        query_gradient, key_gradient, value_gradient = attention_backward(
+            stored_queries, stored_keys, stored_values, head_output_grad, document_index[0]
+        )
+        own = jnp.concatenate([query_gradient, key_gradient, value_gradient], axis=1)
+        slots, slot_of = gather_hi(own)
+
+        middle_local = jnp.concatenate(
+            [
+                jnp.dot(normed, adapter_down_maps, preferred_element_type=jnp.float32),
+                adapter_scale * rows_product(query_gradient, query_up_map),
+                adapter_scale * rows_product(key_gradient, key_value_up_maps[0]),
+                adapter_scale * rows_product(value_gradient, key_value_up_maps[1]),
+            ],
+            axis=1,
+        )
+        middle = (middle_local + swap_core(middle_local)).astype(jnp.bfloat16)
+        rank = adapter_down_maps.shape[1]
+        adapter_middle, middle_gradient = middle[:, :rank], middle[:, rank:]
+        down_local = lax.dot_general(
+            normed, middle_gradient, (((0,), (0,)), ((), ())), preferred_element_type=jnp.float32
+        )
+        ups = up_gradients(adapter_middle, query_gradient, key_gradient, value_gradient)
+        piece = dp_scatter(dp_pieces(down_local, jnp.concatenate(ups, axis=1)))
+        piece = lax.optimization_barrier((piece, weights[1]))[0]
+        every = lax.all_gather(piece, ("hi", "lo"), axis=0)
+        down_rows = down_local.shape[0]
+        down_total = every[:, : down_rows // 16].reshape(down_rows, rank).astype(jnp.float32)
+        up_total = every[:, down_rows // 16 :].transpose(1, 0, 2).reshape(ADAPTER_RANK, -1)
+        up_total = up_total.astype(jnp.float32)
+        q_width = query_gradient.shape[1]
+        k_width = key_gradient.shape[1]
+        query_total = up_total[:, :q_width]
+        key_value_total = jnp.stack(
+            [up_total[:, q_width : q_width + k_width], up_total[:, q_width + k_width :]]
+        )
+
+        tokens = own.shape[0]
+        source = (hi % 2) * 2 + core
+
+        def owner(step):
+            return lambda hi, lo, core: (((hi % 2) * 2 + core + step) % 4, lo, hi // 2)
+
+        received = []
+        for part in range(2):
+            halves = term_halves(slots, weights[part], core)
+            other = swap_core(halves[1])
+            summed = halves[0].astype(jnp.float32) + other.astype(jnp.float32)
+            summed = summed.astype(jnp.bfloat16).reshape(4, tokens, -1)
+            for step in range(4):
+                there = pick(slot_of, (source + step) % 4, 0)
+                received.append(send(pick(summed, there, 0), owner(step)))
+        pieces = jnp.stack(received)
+        spot = jnp.arange(16, dtype=jnp.int32)
+        from_hi, from_lo, part = spot // 8, spot // 2 % 4, spot % 2
+        step = (hi - (from_hi * 2 + from_lo // 2)) % 4
+        order = ((part * 4 + step) * 2 + from_lo % 2).astype(jnp.int32)
+        normed_input_grad = finish(pieces, order, middle_gradient, adapter_down_maps, cut)
+        return (normed_input_grad, down_total, query_total, key_value_total)
+
+    return shards
+
+
 def solution(mesh):
     ranks = mesh.shape["dp"]
     tensor = mesh.shape["tensor"]
     inner = math.gcd(ranks, 4)
     outer = ranks // inner
-    split = Mesh(mesh.devices.reshape(outer, inner, tensor), ("hi", "lo", "tensor"))
+    split = Mesh(mesh.devices.reshape(outer, inner, tensor), AXES)
     rows = ("hi", "lo")
     in_specs = (
         P(rows, "tensor"),
@@ -176,7 +443,7 @@
     )
     out_specs = (P(rows, "tensor"), P("tensor", None), P(None, "tensor"), P(None, None, "tensor"))
     return jax.shard_map(
-        make_shards(outer, inner, tensor),
+        fast_shards() if (outer, inner, tensor) == SIZES else general_shards(outer, inner, tensor),
         mesh=split,
         in_specs=in_specs,
         out_specs=out_specs,

time: 620 us -> 286 us (0.46)
  waiting for transfers between devices: 465 us -> 97.6 us
  blocking collectives: 47.9 us -> 0 us
  starting transfers between devices: 5.17 us -> 50.3 us
  Pallas kernels: 0 us -> 24.5 us
  matrix products: 47.4 us -> 24.1 us
  local copies, waits for them, and re-layouts: 26.9 us -> 44.7 us
  other arithmetic: 10.9 us -> 21.4 us
  between operations: 15.4 us -> 22.1 us
    all_gather x3, waiting for transfers between devices: 229 us -> 9.25 us  [the longest x2 9.24 us: shards(): weights.append(lax.all_gather(rows, 'lo', axis=0, tiled=True))]
    unnamed x8 -> x3, waiting for transfers between devices: 138 us -> 0.72 us
    ppermute x0 -> x24, waiting for transfers between devices: none -> 87.7 us  [send(): return lax.ppermute(value, AXES, pairs)]
    reduce_scatter x2 -> x0, waiting for transfers between devices: 81.8 us -> none  [the longest x1 66.8 us: shards(): lax.psum_scatter(down_local, every, scatter_dimension=0, tiled=True)]
    ppermute x0 -> x24, starting transfers between devices: none -> 50.2 us  [send(): return lax.ppermute(value, AXES, pairs)]
    all_gather x1 -> x0, blocking collectives: 42.1 us -> none  [shards(): up_total = lax.all_gather(up_piece, every, axis=1, tiled=True)]
    pallas_call x0 -> x3, Pallas kernels: none -> 24.5 us  [the longest x2 12.6 us: term_halves(): pl.pallas_call(term_kernel, out_shape=jax.ShapeDtypeStruct((2, 4 * tokens...]
    unnamed x22 -> x93, local copies, waits for them, and re-layouts: 5.69 us -> 28.4 us
  transfers between devices with their start and end apart: 8 -> 27, of which waited for: 7 -> 9; matrix products, arithmetic and copies ran while one was open for 5% -> 21% of each run, Pallas kernels for 0% -> 9%
where the time goes in v2:
time: 286 us; the launch traced here: 285 us
  waiting for transfers between devices  97.6 us (34%)
  starting transfers between devices  50.3 us (18%)
  local copies, waits for them, and re-layouts  44.7 us (16%)
  Pallas kernels  24.5 us (9%)
  matrix products  24.1 us (8%)
  between operations  22.1 us (8%)
  other arithmetic  21.4 us (7%)
    ppermute x24, waiting for transfers between devices, send(): return lax.ppermute(value, AXES, pairs)  87.7 us
    ppermute x24, starting transfers between devices, send(): return lax.ppermute(value, AXES, pairs)  50.2 us
    unnamed x93, local copies, waits for them, and re-layouts  28.4 us
    pallas_call x2, Pallas kernels, term_halves(): pl.pallas_call(term_kernel, out_shape=jax.ShapeDtypeStruct((2, 4 * tokens...  12.6 us
    pallas_call x1, Pallas kernels, finish(): pl.pallas_call(finish_kernel, out_shape=jax.ShapeDtypeStruct((tokens, col...  11.9 us
    all_gather x2, waiting for transfers between devices, shards(): weights.append(lax.all_gather(rows, 'lo', axis=0, tiled=True))  9.24 us
    dot_general x1, matrix products, attention_backward(): jnp.einsum('kgtu,ukd->tkgd', score_grad, kmat, preferred_element_type=jnp...  6.61 us
    dot_general x1, matrix products, attention_backward(): jnp.einsum('kgtu,tkgd->ukd', score_grad, qmat, preferred_element_type=jnp...  6.3 us
  transfers between devices with their start and end apart: 27, of which 9 were waited for; matrix products, arithmetic and copies ran while one was open for 21% of the time, Pallas kernels for 9%

profile of v2, /device:TPU:1, one launch (start us, length us, event | category | flops | bytes accessed | tf_op | source)
XLA Modules:
  0.0 284.7 jit_solution(1296473009405031385)
XLA Ops:
  22.3 6.6 %fusion.16 = bf16[192,4,4,128]{3,0,2,1:T(8,128)(2,1)S(1)} fusion(f32[4,192,192,4]{2,1,3,0:T(8,128)} %fusion.30, bf16[192,4,128,1]{2,1,0,3:T(4,128)(2,1)S(1)} %bitcast.214, f32[4,4,192,192]{2,3,1,0:T(8,128)} %get-tuple-element.30, f32[4,4,192]{2,1,0:T(4,128)S(1)} %get-tuple-element.29), kind=kOutput, calls=%fused_computation.38 | convolution fusion | flops 155520192 | bytes 5713920 | tf_op jit(solution)/shard_map/kgtu,ukd->tkgd/dot_general | solution.py:42
  30.1 6.3 %fusion.25 = bf16[4,24,8,128]{3,2,1,0:T(8,128)(2,1)S(1)} fusion(f32[4,192,192,4]{2,1,3,0:T(8,128)} %fusion.30, bf16[192,4,4,128]{3,2,1,0:T(4,128)(2,1)} %copy-done.19, f32[4,4,192,192]{2,3,1,0:T(8,128)} %get-tuple-element.30, f32[4,4,192]{2,1,0:T(4,128)S(1)} %get-tuple-element.29), kind=kOutput, calls=%fused_computation.50 | convolution fusion | flops 155225280 | bytes 5713920 | tf_op jit(solution)/shard_map/kgtu,tkgd->ukd/dot_general | solution.py:45
  36.5 2.6 fusion.26
  43.9 6.1 %collective-permute-start = (bf16[192,3072]{1,0:T(8,128)(2,1)S(1)}, bf16[192,3072]{1,0:T(8,128)(2,1)}, u32[]{:S(2)}, u32[]{:S(2)}) collective-permute-start(bf16[192,3072]{1,0:T(8,128)(2,1)S(1)} %bitcast_dynamic-update-slice_fusion.a0), channel_id=1, source_target_pairs={{0,8},{1,9},{2,10},{3,11},{4,12},{5,13},{6,14},{7,15},{8,16},{9,17... | collective-permute-start | bytes 3538952 | tf_op jit(solution)/shard_map/ppermute | solution.py:169
  66.1 7.3 %collective-permute-done.1 = bf16[192,3072]{1,0:T(8,128)(2,1)} collective-permute-done((bf16[192,3072]{1,0:T(8,128)(2,1)S(1)}, bf16[192,3072]{1,0:T(8,128)(2,1)}, u32[]{:S(2)}, u32[]{:S(2)}) %collective-permute-start.1) | collective-permute-done | bytes 1179680 | tf_op jit(solution)/shard_map/ppermute | solution.py:169
  76.4 13.5 %collective-permute-done.17 = bf16[2,2,320,192]{2,3,1,0:T(8,128)(2,1)S(1)} collective-permute-done((bf16[2,2,320,192]{2,3,1,0:T(8,128)(2,1)S(1)}, bf16[2,2,320,192]{2,3,1,0:T(8,128)(2,1)S(1)}, u32[]{:S(2)}, u32[]{:S(2)}) %collective-permute-start.17) | collective-permute-done | bytes 491552 | tf_op jit(solution)/shard_map/ppermute | solution.py:169
  95.2 6.9 %collective-permute-done.18 = bf16[2,320,192]{1,2,0:T(8,128)(2,1)S(1)} collective-permute-done((bf16[2,320,192]{1,2,0:T(8,128)(2,1)S(1)}, bf16[2,320,192]{1,2,0:T(8,128)(2,1)S(1)}, u32[]{:S(2)}, u32[]{:S(2)}) %collective-permute-start.18) | collective-permute-done | bytes 245792 | tf_op jit(solution)/shard_map/ppermute | solution.py:169
  105.7 3.8 %collective-permute-start.23 = (bf16[320,192]{0,1:T(8,128)(2,1)S(1)}, bf16[320,192]{0,1:T(8,128)(2,1)S(1)}, u32[]{:S(2)}, u32[]{:S(2)}) collective-permute-start(bf16[320,192]{0,1:T(8,128)(2,1)S(1)} %get-tuple-element.14), channel_id=1, source_target_pairs={{0,24},{1,25},{2,26},{3,27},{4,28},{5,29},{6,30},{7,31},{8,0},{9,1... | collective-permute-start | bytes 368648 | tf_op jit(solution)/shard_map/ppermute | solution.py:169
  112.9 27.3 %collective-permute-done.23 = bf16[320,192]{0,1:T(8,128)(2,1)S(1)} collective-permute-done((bf16[320,192]{0,1:T(8,128)(2,1)S(1)}, bf16[320,192]{0,1:T(8,128)(2,1)S(1)}, u32[]{:S(2)}, u32[]{:S(2)}) %collective-permute-start.23) | collective-permute-done | bytes 122912 | tf_op jit(solution)/shard_map/ppermute | solution.py:169
  142.4 4.0 %select_select_fusion = (bf16[192,3072]{1,0:T(8,128)(2,1)}, bf16[192,3072]{1,0:T(8,128)(2,1)}) fusion(bf16[192,3072]{1,0:T(8,128)(2,1)} %collective-permute-done.4, bf16[192,3072]{1,0:T(8,128)(2,1)} %collective-permute-done.5, bf16[192,3072]{1,0:T(8,128)(2,1)} %collective-permute-done, pred[]{:T(512)S(6)} %eq.53, pred[]{:T(512)S(6)} %eq.52, ...), kind=kLoop, calls=%fused_computation.45 | loop fusion | flops 1769472 | bytes 7077890 | tf_op jit(solution)/shard_map/jit(_where)/select_n | solution.py:330
  150.2 2.8 copy-done.12
  153.0 6.3 %term.2 = bf16[2,768,512]{2,1,0:T(8,128)(2,1)S(1)} custom-call(s32[1]{0:T(128)} %bitcast.turn_ref, bf16[192,3072]{1,0:T(8,128)(2,1)S(1)} %copy-done.9, bf16[192,3072]{1,0:T(8,128)(2,1)S(1)} %copy-done.6, bf16[192,3072]{1,0:T(8,128)(2,1)S(1)} %broadcast_select_fusion.a2, bf16[192,3072]{1,0:T(8,128)(2,1)S(1)} %copy-done.4, bf16[1024,3072]{1,0:T(8,128)(2,1)S(1)} %copy-done.12), custom_call_target="tpu_custom_call" | custom-call | flops 4831838208 | bytes 12582912 | tf_op jit(solution)/shard_map/term/pallas_call | solution.py:221
  162.6 9.2 %all-gather.8.cloned.1.call-done.right_ref = bf16[1024,3072]{1,0:T(8,128)(2,1)} async-done(((bf16[256,3072]{1,0:T(8,128)(2,1)}), bf16[1024,3072]{1,0:T(8,128)(2,1)}) %all-gather.8.cloned.1.call-update) | async-done | bytes 6291472 | tf_op jit(solution)/shard_map/all_gather | solution.py:359
  176.9 2.8 copy-done.11
  179.7 6.3 %term.3 = bf16[2,768,512]{2,1,0:T(8,128)(2,1)S(1)} custom-call(s32[1]{0:T(128)} %bitcast.turn_ref, bf16[192,3072]{1,0:T(8,128)(2,1)S(1)} %copy-done.10, bf16[192,3072]{1,0:T(8,128)(2,1)S(1)} %copy-done.7, bf16[192,3072]{1,0:T(8,128)(2,1)S(1)} %copy-done.3, bf16[192,3072]{1,0:T(8,128)(2,1)S(1)} %copy-done.5, bf16[1024,3072]{1,0:T(8,128)(2,1)S(1)} %copy-done.11), custom_call_target="tpu_custom_call" | custom-call | flops 4831838208 | bytes 12582912 | tf_op jit(solution)/shard_map/term/pallas_call | solution.py:221
  193.3 3.9 %copy.120.down_ref = bf16[4096,192]{1,0:T(8,128)(2,1)} copy(bf16[4096,192]{0,1:T(8,128)(2,1)} %param.22) | data formatting | bytes 3145728 | tf_op args[9]
  202.4 3.1 %collective-permute-start.7 = (bf16[192,512]{1,0:T(8,128)(2,1)S(1)}, bf16[192,512]{1,0:T(8,128)(2,1)S(1)}, u32[]{:S(2)}, u32[]{:S(2)}) collective-permute-start(bf16[192,512]{1,0:T(8,128)(2,1)S(1)} %get-tuple-element.24), channel_id=1, source_target_pairs={{0,0},{1,8},{2,2},{3,10},{4,4},{5,12},{6,6},{7,14},{8,16},{9,24},{... | collective-permute-start | bytes 589832 | tf_op jit(solution)/shard_map/ppermute | solution.py:169
  205.5 3.4 %collective-permute-start.8 = (bf16[192,512]{1,0:T(8,128)(2,1)S(1)}, bf16[192,512]{1,0:T(8,128)(2,1)S(1)}, u32[]{:S(2)}, u32[]{:S(2)}) collective-permute-start(bf16[192,512]{1,0:T(8,128)(2,1)S(1)} %get-tuple-element.23), channel_id=1, source_target_pairs={{0,8},{1,16},{2,10},{3,18},{4,12},{5,20},{6,14},{7,22},{8,24},{9,0... | collective-permute-start | bytes 589832 | tf_op jit(solution)/shard_map/ppermute | solution.py:169
  209.9 3.5 %collective-permute-start.10 = (bf16[192,512]{1,0:T(8,128)(2,1)S(1)}, bf16[192,512]{1,0:T(8,128)(2,1)S(1)}, u32[]{:S(2)}, u32[]{:S(2)}) collective-permute-start(bf16[192,512]{1,0:T(8,128)(2,1)S(1)} %get-tuple-element.21), channel_id=1, source_target_pairs={{0,24},{1,0},{2,26},{3,2},{4,28},{5,4},{6,30},{7,6},{8,8},{9,16},{... | collective-permute-start | bytes 589832 | tf_op jit(solution)/shard_map/ppermute | solution.py:169
  216.7 7.8 %collective-permute-done.7 = bf16[192,512]{1,0:T(8,128)(2,1)S(1)} collective-permute-done((bf16[192,512]{1,0:T(8,128)(2,1)S(1)}, bf16[192,512]{1,0:T(8,128)(2,1)S(1)}, u32[]{:S(2)}, u32[]{:S(2)}) %collective-permute-start.7) | collective-permute-done | bytes 196640 | tf_op jit(solution)/shard_map/ppermute | solution.py:169
  226.5 4.5 %collective-permute-start.14 = (bf16[192,512]{1,0:T(8,128)(2,1)S(1)}, bf16[192,512]{1,0:T(8,128)(2,1)S(1)}, u32[]{:S(2)}, u32[]{:S(2)}) collective-permute-start(bf16[192,512]{1,0:T(8,128)(2,1)S(1)} %get-tuple-element.18), channel_id=1, source_target_pairs={{0,16},{1,24},{2,18},{3,26},{4,20},{5,28},{6,22},{7,30},{8,0},{9,8... | collective-permute-start | bytes 589832 | tf_op jit(solution)/shard_map/ppermute | solution.py:169
  233.0 18.3 %collective-permute-done.12 = bf16[192,512]{1,0:T(8,128)(2,1)S(1)} collective-permute-done((bf16[192,512]{1,0:T(8,128)(2,1)S(1)}, bf16[192,512]{1,0:T(8,128)(2,1)S(1)}, u32[]{:S(2)}, u32[]{:S(2)}) %collective-permute-start.12) | collective-permute-done | bytes 196640 | tf_op jit(solution)/shard_map/ppermute | solution.py:169
  251.4 6.3 %collective-permute-done.15 = bf16[192,512]{1,0:T(8,128)(2,1)S(1)} collective-permute-done((bf16[192,512]{1,0:T(8,128)(2,1)S(1)}, bf16[192,512]{1,0:T(8,128)(2,1)S(1)}, u32[]{:S(2)}, u32[]{:S(2)}) %collective-permute-start.15) | collective-permute-done | bytes 196640 | tf_op jit(solution)/shard_map/ppermute | solution.py:169
  258.9 11.9 %finish.1 = bf16[192,4096]{1,0:T(8,128)(2,1)} custom-call(s32[16]{0:T(128)} %fusion.73.order_ref, bf16[8,192,512]{2,1,0:T(8,128)(2,1)} %copy-done.21, bf16[192,192]{1,0:T(8,128)(2,1)} %slice.94.middle_ref, bf16[4096,192]{1,0:T(8,128)(2,1)} %copy.120.down_ref), custom_call_target="tpu_custom_call" | custom-call | flops 301989888 | bytes 4718592 | tf_op jit(solution)/shard_map/finish/pallas_call | solution.py:261
  (187 shorter events, 88.1 us)
Async XLA Ops:
  7.2 139.2 %all-gather.6.cloned.1.call-start = ((), (), s32[]{:S(2)}) async-start(), calls=%async_computation | async-start | bytes 7864320 | tf_op jit(solution)/shard_map/all_gather | solution.py:359
  11.2 160.6 %all-gather.8.cloned.1.call-start = ((), (), s32[]{:S(2)}) async-start(), calls=%async_computation.1 | async-start | bytes 7864320 | tf_op jit(solution)/shard_map/all_gather | solution.py:359
  12.0 258.8 %all-gather.10.cloned.1.call-start = ((), (), s32[]{:S(2)}) async-start(), calls=%async_computation.2 | async-start | bytes 2506752 | tf_op jit(solution)/shard_map/all_gather | solution.py:385
  42.6 30.8 %collective-permute-start.1 = (bf16[192,3072]{1,0:T(8,128)(2,1)S(1)}, bf16[192,3072]{1,0:T(8,128)(2,1)}, u32[]{:S(2)}, u32[]{:S(2)}) collective-permute-start(bf16[192,3072]{1,0:T(8,128)(2,1)S(1)} %bitcast_dynamic-update-slice_fusion.a0), channel_id=1, source_target_pairs={{8,0},{9,1},{10,2},{11,3},{12,4},{13,5},{14,6},{15,7},{16,8},{17,9... | collective-permute-start | bytes 3538952 | tf_op jit(solution)/shard_map/ppermute | solution.py:169
  43.9 30.8 %collective-permute-start = (bf16[192,3072]{1,0:T(8,128)(2,1)S(1)}, bf16[192,3072]{1,0:T(8,128)(2,1)}, u32[]{:S(2)}, u32[]{:S(2)}) collective-permute-start(bf16[192,3072]{1,0:T(8,128)(2,1)S(1)} %bitcast_dynamic-update-slice_fusion.a0), channel_id=1, source_target_pairs={{0,8},{1,9},{2,10},{3,11},{4,12},{5,13},{6,14},{7,15},{8,16},{9,17... | collective-permute-start | bytes 3538952 | tf_op jit(solution)/shard_map/ppermute | solution.py:169
  62.0 27.9 %collective-permute-start.17 = (bf16[2,2,320,192]{2,3,1,0:T(8,128)(2,1)S(1)}, bf16[2,2,320,192]{2,3,1,0:T(8,128)(2,1)S(1)}, u32[]{:S(2)}, u32[]{:S(2)}) collective-permute-start(bf16[2,2,320,192]{2,3,1,0:T(8,128)(2,1)S(1)} %fusion.35), channel_id=1, source_target_pairs={{0,2},{1,3},{2,0},{3,1},{4,6},{5,7},{6,4},{7,5},{8,10},{9,11},{10,... | collective-permute-start | bytes 1474568 | tf_op jit(solution)/shard_map/ppermute | solution.py:169
  64.8 27.9 %collective-permute-start.19 = (bf16[2,2,320,192]{2,3,0,1:T(8,128)(2,1)S(1)}, bf16[2,2,320,192]{2,3,0,1:T(8,128)(2,1)}, u32[]{:S(2)}, u32[]{:S(2)}) collective-permute-start(bf16[2,2,320,192]{2,3,0,1:T(8,128)(2,1)S(1)} %fusion.36), channel_id=1, source_target_pairs={{0,4},{1,5},{2,6},{3,7},{4,0},{5,1},{6,2},{7,3},{8,12},{9,13},{10,... | collective-permute-start | bytes 1474568 | tf_op jit(solution)/shard_map/ppermute | solution.py:169
  73.4 29.1 %collective-permute-start.2 = (bf16[192,3072]{1,0:T(8,128)(2,1)}, bf16[192,3072]{1,0:T(8,128)(2,1)}, u32[]{:S(2)}, u32[]{:S(2)}) collective-permute-start(bf16[192,3072]{1,0:T(8,128)(2,1)} %collective-permute-done.1), channel_id=1, source_target_pairs={{8,0},{9,1},{10,2},{11,3},{12,4},{13,5},{14,6},{15,7},{16,8},{17,9... | collective-permute-start | bytes 3538952 | tf_op jit(solution)/shard_map/ppermute | solution.py:169
  74.7 29.1 %collective-permute-start.3 = (bf16[192,3072]{1,0:T(8,128)(2,1)}, bf16[192,3072]{1,0:T(8,128)(2,1)}, u32[]{:S(2)}, u32[]{:S(2)}) collective-permute-start(bf16[192,3072]{1,0:T(8,128)(2,1)} %collective-permute-done), channel_id=1, source_target_pairs={{8,16},{9,17},{10,18},{11,19},{12,20},{13,21},{14,22},{15,23},{16,... | collective-permute-start | bytes 3538952 | tf_op jit(solution)/shard_map/ppermute | solution.py:169
  102.5 39.8 %collective-permute-start.4 = (bf16[192,3072]{1,0:T(8,128)(2,1)}, bf16[192,3072]{1,0:T(8,128)(2,1)}, u32[]{:S(2)}, u32[]{:S(2)}) collective-permute-start(bf16[192,3072]{1,0:T(8,128)(2,1)} %collective-permute-done.2), channel_id=1, source_target_pairs={{8,0},{9,1},{10,2},{11,3},{12,4},{13,5},{14,6},{15,7}} | collective-permute-start | bytes 3538952 | tf_op jit(solution)/shard_map/ppermute | solution.py:169
  103.8 38.6 %collective-permute-start.5 = (bf16[192,3072]{1,0:T(8,128)(2,1)}, bf16[192,3072]{1,0:T(8,128)(2,1)}, u32[]{:S(2)}, u32[]{:S(2)}) collective-permute-start(bf16[192,3072]{1,0:T(8,128)(2,1)} %collective-permute-done.3), channel_id=1, source_target_pairs={{16,24},{17,25},{18,26},{19,27},{20,28},{21,29},{22,30},{23,31}} | collective-permute-start | bytes 3538952 | tf_op jit(solution)/shard_map/ppermute | solution.py:169
  105.7 34.5 %collective-permute-start.23 = (bf16[320,192]{0,1:T(8,128)(2,1)S(1)}, bf16[320,192]{0,1:T(8,128)(2,1)S(1)}, u32[]{:S(2)}, u32[]{:S(2)}) collective-permute-start(bf16[320,192]{0,1:T(8,128)(2,1)S(1)} %get-tuple-element.14), channel_id=1, source_target_pairs={{0,24},{1,25},{2,26},{3,27},{4,28},{5,29},{6,30},{7,31},{8,0},{9,1... | collective-permute-start | bytes 368648 | tf_op jit(solution)/shard_map/ppermute | solution.py:169
  109.5 30.7 %collective-permute-start.22 = (bf16[320,192]{0,1:T(8,128)(2,1)S(1)}, bf16[320,192]{0,1:T(8,128)(2,1)S(1)}, u32[]{:S(2)}, u32[]{:S(2)}) collective-permute-start(bf16[320,192]{0,1:T(8,128)(2,1)S(1)} %get-tuple-element.13), channel_id=1, source_target_pairs={{0,16},{1,17},{2,18},{3,19},{4,20},{5,21},{6,22},{7,23},{8,24},{9,... | collective-permute-start | bytes 368648 | tf_op jit(solution)/shard_map/ppermute | solution.py:169
  111.5 28.7 %collective-permute-start.21 = (bf16[320,192]{0,1:T(8,128)(2,1)S(1)}, bf16[320,192]{0,1:T(8,128)(2,1)S(1)}, u32[]{:S(2)}, u32[]{:S(2)}) collective-permute-start(bf16[320,192]{0,1:T(8,128)(2,1)S(1)} %get-tuple-element.12), channel_id=1, source_target_pairs={{0,8},{1,9},{2,10},{3,11},{4,12},{5,13},{6,14},{7,15},{8,16},{9,17... | collective-permute-start | bytes 368648 | tf_op jit(solution)/shard_map/ppermute | solution.py:169
  160.3 40.7 %collective-permute-start.6 = (bf16[768,512]{1,0:T(8,128)(2,1)}, bf16[768,512]{1,0:T(8,128)(2,1)}, u32[]{:S(2)}, u32[]{:S(2)}) collective-permute-start(bf16[768,512]{1,0:T(8,128)(2,1)} %slice_bitcast_fusion.2), channel_id=1, source_target_pairs={{0,1},{1,0},{2,3},{3,2},{4,5},{5,4},{6,7},{7,6},{8,9},{9,8},{10,11... | collective-permute-start | bytes 2359304 | tf_op jit(solution)/shard_map/ppermute | solution.py:169
  186.9 26.5 %collective-permute-start.11 = (bf16[768,512]{1,0:T(8,128)(2,1)}, bf16[768,512]{1,0:T(8,128)(2,1)}, u32[]{:S(2)}, u32[]{:S(2)}) collective-permute-start(bf16[768,512]{1,0:T(8,128)(2,1)} %slice_bitcast_fusion), channel_id=1, source_target_pairs={{0,1},{1,0},{2,3},{3,2},{4,5},{5,4},{6,7},{7,6},{8,9},{9,8},{10,11... | collective-permute-start | bytes 2359304 | tf_op jit(solution)/shard_map/ppermute | solution.py:169
  202.4 22.1 %collective-permute-start.7 = (bf16[192,512]{1,0:T(8,128)(2,1)S(1)}, bf16[192,512]{1,0:T(8,128)(2,1)S(1)}, u32[]{:S(2)}, u32[]{:S(2)}) collective-permute-start(bf16[192,512]{1,0:T(8,128)(2,1)S(1)} %get-tuple-element.24), channel_id=1, source_target_pairs={{0,0},{1,8},{2,2},{3,10},{4,4},{5,12},{6,6},{7,14},{8,16},{9,24},{... | collective-permute-start | bytes 589832 | tf_op jit(solution)/shard_map/ppermute | solution.py:169
  205.5 20.9 %collective-permute-start.8 = (bf16[192,512]{1,0:T(8,128)(2,1)S(1)}, bf16[192,512]{1,0:T(8,128)(2,1)S(1)}, u32[]{:S(2)}, u32[]{:S(2)}) collective-permute-start(bf16[192,512]{1,0:T(8,128)(2,1)S(1)} %get-tuple-element.23), channel_id=1, source_target_pairs={{0,8},{1,16},{2,10},{3,18},{4,12},{5,20},{6,14},{7,22},{8,24},{9,0... | collective-permute-start | bytes 589832 | tf_op jit(solution)/shard_map/ppermute | solution.py:169
  208.9 22.1 %collective-permute-start.9 = (bf16[192,512]{1,0:T(8,128)(2,1)S(1)}, bf16[192,512]{1,0:T(8,128)(2,1)S(1)}, u32[]{:S(2)}, u32[]{:S(2)}) collective-permute-start(bf16[192,512]{1,0:T(8,128)(2,1)S(1)} %get-tuple-element.22), channel_id=1, source_target_pairs={{0,16},{1,24},{2,18},{3,26},{4,20},{5,28},{6,22},{7,30},{8,0},{9,8... | collective-permute-start | bytes 589832 | tf_op jit(solution)/shard_map/ppermute | solution.py:169
  209.9 23.1 %collective-permute-start.10 = (bf16[192,512]{1,0:T(8,128)(2,1)S(1)}, bf16[192,512]{1,0:T(8,128)(2,1)S(1)}, u32[]{:S(2)}, u32[]{:S(2)}) collective-permute-start(bf16[192,512]{1,0:T(8,128)(2,1)S(1)} %get-tuple-element.21), channel_id=1, source_target_pairs={{0,24},{1,0},{2,26},{3,2},{4,28},{5,4},{6,30},{7,6},{8,8},{9,16},{... | collective-permute-start | bytes 589832 | tf_op jit(solution)/shard_map/ppermute | solution.py:169
  214.8 36.5 %collective-permute-start.12 = (bf16[192,512]{1,0:T(8,128)(2,1)S(1)}, bf16[192,512]{1,0:T(8,128)(2,1)S(1)}, u32[]{:S(2)}, u32[]{:S(2)}) collective-permute-start(bf16[192,512]{1,0:T(8,128)(2,1)S(1)} %get-tuple-element.20), channel_id=1, source_target_pairs={{0,0},{1,8},{2,2},{3,10},{4,4},{5,12},{6,6},{7,14},{8,16},{9,24},{... | collective-permute-start | bytes 589832 | tf_op jit(solution)/shard_map/ppermute | solution.py:169
  224.5 26.8 %collective-permute-start.13 = (bf16[192,512]{1,0:T(8,128)(2,1)S(1)}, bf16[192,512]{1,0:T(8,128)(2,1)S(1)}, u32[]{:S(2)}, u32[]{:S(2)}) collective-permute-start(bf16[192,512]{1,0:T(8,128)(2,1)S(1)} %get-tuple-element.19), channel_id=1, source_target_pairs={{0,8},{1,16},{2,10},{3,18},{4,12},{5,20},{6,14},{7,22},{8,24},{9,0... | collective-permute-start | bytes 589832 | tf_op jit(solution)/shard_map/ppermute | solution.py:169
  226.5 24.9 %collective-permute-start.14 = (bf16[192,512]{1,0:T(8,128)(2,1)S(1)}, bf16[192,512]{1,0:T(8,128)(2,1)S(1)}, u32[]{:S(2)}, u32[]{:S(2)}) collective-permute-start(bf16[192,512]{1,0:T(8,128)(2,1)S(1)} %get-tuple-element.18), channel_id=1, source_target_pairs={{0,16},{1,24},{2,18},{3,26},{4,20},{5,28},{6,22},{7,30},{8,0},{9,8... | collective-permute-start | bytes 589832 | tf_op jit(solution)/shard_map/ppermute | solution.py:169
  231.0 26.6 %collective-permute-start.15 = (bf16[192,512]{1,0:T(8,128)(2,1)S(1)}, bf16[192,512]{1,0:T(8,128)(2,1)S(1)}, u32[]{:S(2)}, u32[]{:S(2)}) collective-permute-start(bf16[192,512]{1,0:T(8,128)(2,1)S(1)} %get-tuple-element.17), channel_id=1, source_target_pairs={{0,24},{1,0},{2,26},{3,2},{4,28},{5,4},{6,30},{7,6},{8,8},{9,16},{... | collective-permute-start | bytes 589832 | tf_op jit(solution)/shard_map/ppermute | solution.py:169
  (42 other events, 182.2 us)
Sparse Core Ops, SparseCore 0:
  11.4 86.2 all-gather.5
  100.1 71.6 all-gather.7
  175.2 81.7 all-gather.9

commit v3 on v2

--- a/solution.py
+++ b/solution.py
@@ -169,6 +169,10 @@
     return lax.ppermute(value, AXES, pairs)
 
 
+def after(value, first):
+    return lax.optimization_barrier((value, first))[0]
+
+
 def swap_lo(value, bit):
     return send(value, lambda hi, lo, core: (hi, lo ^ bit, core))
 
@@ -192,41 +196,148 @@
     return lax.dynamic_index_in_dim(value, index, axis, keepdims=False)
 
 
-def term_kernel(turn_ref, a0, a1, a2, a3, right_ref, out_ref, left, arrived):
+def attention_kernel(
+    query_ref, key_ref, value_ref, grad_ref, row_ids, column_ids, up_ref, key_up_ref, own_ref, middle_ref
+):
+    head = pl.program_id(0)
+    group = query_ref.shape[1] // HEAD_SIZE
+    scale = 1.0 / math.sqrt(HEAD_SIZE)
+    tokens = query_ref.shape[0]
+
+    def stacked(ref):
+        return jnp.concatenate(
+            [ref[:, j * HEAD_SIZE : (j + 1) * HEAD_SIZE] for j in range(group)], axis=0
+        )
+
+    def product(left, right, dims):
+        return lax.dot_general(
+            left, right, ((dims[:1], dims[1:]), ((), ())), preferred_element_type=jnp.float32
+        )
+
+    queries, gradients = stacked(query_ref), stacked(grad_ref)
+    keys, values = key_ref[...], value_ref[...]
+    same = jnp.concatenate([row_ids[...] == column_ids[...]] * group, axis=0)
+    scores = jnp.where(same, product(queries, keys, (1, 1)) * scale, -1e30)
+    raised = jnp.exp(scores - jnp.max(scores, axis=-1, keepdims=True))
+    probs = raised / jnp.sum(raised, axis=-1, keepdims=True)
+    value_gradient = product(probs.astype(jnp.bfloat16), gradients, (0, 0)).astype(jnp.bfloat16)
+    prob_grad = product(gradients, values, (1, 1))
+    dots = jnp.sum(probs * prob_grad, axis=-1, keepdims=True)
+    score_grad = (probs * (prob_grad - dots) * scale).astype(jnp.bfloat16)
+    stacked_gradient = product(score_grad, keys, (1, 0)).astype(jnp.bfloat16)
+    key_gradient = product(score_grad, queries, (0, 0)).astype(jnp.bfloat16)
+    query_gradient = jnp.concatenate(
+        [stacked_gradient[j * tokens : (j + 1) * tokens] for j in range(group)], axis=1
+    )
+
+    count = own_ref.shape[1] // ((group + 2) * HEAD_SIZE)
+
+    def columns(start, width):
+        return pl.ds(pl.multiple_of(start, HEAD_SIZE), width)
+
+    own_ref[:, columns(head * group * HEAD_SIZE, group * HEAD_SIZE)] = query_gradient
+    own_ref[:, columns((count * group + head) * HEAD_SIZE, HEAD_SIZE)] = key_gradient
+    own_ref[:, columns((count * (group + 1) + head) * HEAD_SIZE, HEAD_SIZE)] = value_gradient
+
+    @pl.when(head == 0)
+    def _():
+        middle_ref[...] = jnp.zeros_like(middle_ref)
+
+    middle_ref[...] += adapter_scale * jnp.concatenate(
+        [
+            product(query_gradient, up_ref[...], (1, 1)),
+            product(key_gradient, key_up_ref[0], (1, 1)),
+            product(value_gradient, key_up_ref[1], (1, 1)),
+        ],
+        axis=1,
+    )
+
+
+def attention(queries, keys, values, gradients, ids, query_up_map, key_value_up_maps):
+    tokens, key_width = keys.shape
+    heads = key_width // HEAD_SIZE
+    wide = queries.shape[1] // heads
+    rank = query_up_map.shape[0]
+    return pl.pallas_call(
+        attention_kernel,
+        out_shape=(
+            jax.ShapeDtypeStruct((tokens, queries.shape[1] + 2 * key_width), jnp.bfloat16),
+            jax.ShapeDtypeStruct((tokens, 3 * rank), jnp.float32),
+        ),
+        grid=(heads,),
+        in_specs=[
+            pl.BlockSpec((tokens, wide), lambda h: (0, h)),
+            pl.BlockSpec((tokens, HEAD_SIZE), lambda h: (0, h)),
+            pl.BlockSpec((tokens, HEAD_SIZE), lambda h: (0, h)),
+            pl.BlockSpec((tokens, wide), lambda h: (0, h)),
+            pl.BlockSpec((tokens, 1), lambda h: (0, 0)),
+            pl.BlockSpec((1, tokens), lambda h: (0, 0)),
+            pl.BlockSpec((rank, wide), lambda h: (0, h)),
+            pl.BlockSpec((2, rank, HEAD_SIZE), lambda h: (0, 0, h)),
+        ],
+        out_specs=(
+            pl.BlockSpec((tokens, queries.shape[1] + 2 * key_width), lambda h: (0, 0)),
+            pl.BlockSpec((tokens, 3 * rank), lambda h: (0, 0)),
+        ),
+        compiler_params=pltpu.CompilerParams(vmem_limit_bytes=32 << 20),
+        cost_estimate=pl.CostEstimate(
+            flops=10 * tokens * tokens * queries.shape[1],
+            bytes_accessed=6 * tokens * queries.shape[1],
+            transcendentals=tokens * tokens * queries.shape[1] // HEAD_SIZE,
+        ),
+        name="attention",
+    )(
+        queries,
+        keys,
+        values,
+        gradients,
+        ids.reshape(tokens, 1),
+        ids.reshape(1, tokens),
+        query_up_map,
+        key_value_up_maps,
+    )
+
+
+def term_kernel(turn_ref, *refs):
     del turn_ref
-    tokens = a0.shape[0]
+    slots, rights, (out_ref, left, arrived) = refs[:4], refs[4:-3], refs[-3:]
+    tokens = slots[0].shape[0]
 
     @pl.when(pl.program_id(0) == 0)
     def _():
         copies = [
             pltpu.make_async_copy(a, left.at[pl.ds(n * tokens, tokens), :], arrived.at[n])
-            for n, a in enumerate((a0, a1, a2, a3))
+            for n, a in enumerate(slots)
         ]
         for copy in copies:
             copy.start()
         for copy in copies:
             copy.wait()
 
-    out_ref[...] = lax.dot_general(
-        left[...],
-        right_ref[...],
-        (((1,), (1,)), ((), ())),
-        preferred_element_type=jnp.float32,
-    ).astype(jnp.bfloat16)[None]
+    width = rights[0].shape[0]
+    for n, right in enumerate(rights):
+        out_ref[0, :, n * width : (n + 1) * width] = lax.dot_general(
+            left[...],
+            right[...],
+            (((1,), (1,)), ((), ())),
+            preferred_element_type=jnp.float32,
+        ).astype(jnp.bfloat16)
 
 
 def term_halves(slots, weights, core):
     tokens, depth = slots[0].shape
-    rows = weights.shape[0] // 2
+    rows = weights[0].shape[0] // 2
+    count = len(weights)
     return pl.pallas_call(
         term_kernel,
-        out_shape=jax.ShapeDtypeStruct((2, 4 * tokens, rows), jnp.bfloat16),
+        out_shape=jax.ShapeDtypeStruct((2, 4 * tokens, count * rows), jnp.bfloat16),
         grid_spec=pltpu.PrefetchScalarGridSpec(
             num_scalar_prefetch=1,
             grid=(2,),
             in_specs=[pl.BlockSpec(memory_space=pl.ANY)] * 4
-            + [pl.BlockSpec((rows, depth), lambda i, turn: (lax.rem(turn[0] + 1 - i, 2), 0))],
-            out_specs=pl.BlockSpec((1, 4 * tokens, rows), lambda i, turn: (1 - i, 0, 0)),
+            + [pl.BlockSpec((rows, depth), lambda i, turn: (lax.rem(turn[0] + 1 - i, 2), 0))]
+            * count,
+            out_specs=pl.BlockSpec((1, 4 * tokens, count * rows), lambda i, turn: (1 - i, 0, 0)),
             scratch_shapes=[
                 pltpu.VMEM((4 * tokens, depth), jnp.bfloat16),
                 pltpu.SemaphoreType.DMA((4,)),
@@ -234,53 +345,40 @@
         ),
         compiler_params=pltpu.CompilerParams(vmem_limit_bytes=40 << 20),
         cost_estimate=pl.CostEstimate(
-            flops=16 * tokens * depth * rows,
-            bytes_accessed=8 * tokens * depth + 4 * rows * depth + 16 * tokens * rows,
+            flops=16 * tokens * depth * rows * count,
+            bytes_accessed=8 * tokens * depth + (4 * rows * depth + 16 * tokens * rows) * count,
             transcendentals=0,
         ),
         name="term",
-    )(core[None], *slots, weights)
-
-
-def finish_kernel(order_ref, piece_ref, middle_ref, down_ref, out_ref):
-    del order_ref
-    added = lax.dot_general(
-        middle_ref[...],
-        down_ref[...],
-        (((1,), (1,)), ((), ())),
-        preferred_element_type=jnp.float32,
-    )
-    out_ref[...] = (piece_ref[0].astype(jnp.float32) + added).astype(jnp.bfloat16)
-
-
-def finish(pieces, order, middle_gradient, down_maps, width):
-    tokens = pieces.shape[1]
-    columns = down_maps.shape[0]
-    rank = middle_gradient.shape[1]
-    each = pieces.shape[2] // width
+    )(core[None], *slots, *weights)
+
+
+def finish_kernel(spot_ref, added_ref, *refs):
+    pieces, out_ref = refs[:-1], refs[-1]
+    width = pieces[-1].shape[1]
+    place = 0
+    for piece in pieces:
+        for start in range(0, piece.shape[1], width):
+            there = pl.ds(pl.multiple_of(spot_ref[place] * width, width), width)
+            out_ref[:, there] = (
+                piece[:, start : start + width].astype(jnp.float32) + added_ref[:, there]
+            ).astype(jnp.bfloat16)
+            place += 1
+
+
+def finish(pieces, spots, added):
     return pl.pallas_call(
         finish_kernel,
-        out_shape=jax.ShapeDtypeStruct((tokens, columns), jnp.bfloat16),
-        grid_spec=pltpu.PrefetchScalarGridSpec(
-            num_scalar_prefetch=1,
-            grid=(columns // width,),
-            in_specs=[
-                pl.BlockSpec(
-                    (1, tokens, width),
-                    lambda c, order: (lax.div(order[c], each), 0, lax.rem(order[c], each)),
-                ),
-                pl.BlockSpec((tokens, rank), lambda c, order: (0, 0)),
-                pl.BlockSpec((width, rank), lambda c, order: (c, 0)),
-            ],
-            out_specs=pl.BlockSpec((tokens, width), lambda c, order: (0, c)),
-        ),
+        out_shape=jax.ShapeDtypeStruct(added.shape, jnp.bfloat16),
+        in_specs=[pl.BlockSpec(memory_space=pltpu.SMEM)]
+        + [pl.BlockSpec(memory_space=pltpu.VMEM)] * (1 + len(pieces)),
+        out_specs=pl.BlockSpec(memory_space=pltpu.VMEM),
+        compiler_params=pltpu.CompilerParams(vmem_limit_bytes=24 << 20),
         cost_estimate=pl.CostEstimate(
-            flops=2 * tokens * columns * rank,
-            bytes_accessed=4 * tokens * columns + 2 * columns * rank,
-            transcendentals=0,
+            flops=added.size, bytes_accessed=8 * added.size, transcendentals=0
         ),
         name="finish",
-    )(order, pieces, middle_gradient, down_maps)
+    )(spots, added, *pieces)
 
 
 def plane_scatter(value, bits):
@@ -317,12 +415,30 @@
     return total.astype(jnp.bfloat16)
 
 
+def dp_gather(piece):
+    hi, lo = lax.axis_index("hi"), lax.axis_index("lo")
+    turned = jnp.stack([piece] + [turn_hi(piece, step) for step in range(1, 4)])
+    column = jnp.stack([pick(turned, (hi - z) % 4, 0) for z in range(4)])
+    planes = []
+    for value, bits in ((column[:2], (1, 2)), (column[2:], (2, 1))):
+        for bit in bits:
+            other = swap_lo(value, bit)
+            first = (lo // bit) % 2 == 0
+            axis = 1 if bit == 2 or value.ndim == 3 else 2
+            value = jnp.stack(
+                [jnp.where(first, value, other), jnp.where(first, other, value)], axis=axis
+            )
+        planes.append(value)
+    return jnp.concatenate(planes, axis=0).reshape(16, *piece.shape)
+
+
 def gather_hi(own):
     hi = lax.axis_index("hi")
     right, left = [own], [own]
     for step in range(1, 4):
         right.append(move_hi(right[-1], 1, step - 1, 2))
         left.append(move_hi(left[-1], -1, 1, 4 - step))
+    passed = (right[2], left[2])
     slots = [
         own,
         jnp.where(hi == 3, right[1], left[1]),
@@ -330,7 +446,7 @@
         jnp.where(hi == 0, left[3], jnp.where(hi == 3, right[3], right[1])),
     ]
     table = jnp.array([[0, 1, 2, 3], [3, 0, 1, 2], [2, 3, 0, 1], [3, 2, 1, 0]], jnp.int32)
-    return slots, pick(table, hi, 0)
+    return slots, pick(table, hi, 0), passed
 
 
 def fast_shards():
@@ -353,42 +469,49 @@
             [query_projection_weight, key_projection_weight, value_projection_weight], axis=1
         )
         cut = own_weights.shape[0] // 2
-        weights = []
-        for part in range(2):
-            rows = own_weights[part * cut : (part + 1) * cut]
-            weights.append(lax.all_gather(rows, "lo", axis=0, tiled=True))
-
-        query_gradient, key_gradient, value_gradient = attention_backward(
-            stored_queries, stored_keys, stored_values, head_output_grad, document_index[0]
-        )
-        own = jnp.concatenate([query_gradient, key_gradient, value_gradient], axis=1)
-        slots, slot_of = gather_hi(own)
+        by_x, by_y = swap_lo(own_weights, 1), swap_lo(own_weights, 2)
+        stored_queries = after(stored_queries, own_weights)
+
+        own, middle_part = attention(
+            stored_queries,
+            stored_keys,
+            stored_values,
+            head_output_grad,
+            document_index[0],
+            query_up_map,
+            key_value_up_maps,
+        )
+        q_width = stored_queries.shape[1]
+        k_width = stored_keys.shape[1]
+        query_gradient = own[:, :q_width]
+        key_gradient = own[:, q_width : q_width + k_width]
+        value_gradient = own[:, q_width + k_width :]
+        slots, slot_of, passed = gather_hi(own)
+
+        by_x, by_y = after((by_x, by_y), passed)
+        across = (swap_lo(by_x[:cut], 2), swap_lo(by_y[cut:], 1))
 
         middle_local = jnp.concatenate(
             [
                 jnp.dot(normed, adapter_down_maps, preferred_element_type=jnp.float32),
-                adapter_scale * rows_product(query_gradient, query_up_map),
-                adapter_scale * rows_product(key_gradient, key_value_up_maps[0]),
-                adapter_scale * rows_product(value_gradient, key_value_up_maps[1]),
+                middle_part,
             ],
             axis=1,
         )
         middle = (middle_local + swap_core(middle_local)).astype(jnp.bfloat16)
         rank = adapter_down_maps.shape[1]
         adapter_middle, middle_gradient = middle[:, :rank], middle[:, rank:]
+        adapter_middle, late_gradient = after((adapter_middle, middle_gradient), (by_x, by_y))
         down_local = lax.dot_general(
-            normed, middle_gradient, (((0,), (0,)), ((), ())), preferred_element_type=jnp.float32
+            normed, late_gradient, (((0,), (0,)), ((), ())), preferred_element_type=jnp.float32
         )
         ups = up_gradients(adapter_middle, query_gradient, key_gradient, value_gradient)
         piece = dp_scatter(dp_pieces(down_local, jnp.concatenate(ups, axis=1)))
-        piece = lax.optimization_barrier((piece, weights[1]))[0]
-        every = lax.all_gather(piece, ("hi", "lo"), axis=0)
+        every = dp_gather(piece)
         down_rows = down_local.shape[0]
         down_total = every[:, : down_rows // 16].reshape(down_rows, rank).astype(jnp.float32)
         up_total = every[:, down_rows // 16 :].transpose(1, 0, 2).reshape(ADAPTER_RANK, -1)
         up_total = up_total.astype(jnp.float32)
-        q_width = query_gradient.shape[1]
-        k_width = key_gradient.shape[1]
         query_total = up_total[:, :q_width]
         key_value_total = jnp.stack(
             [up_total[:, q_width : q_width + k_width], up_total[:, q_width + k_width :]]
@@ -400,21 +523,27 @@
         def owner(step):
             return lambda hi, lo, core: (((hi % 2) * 2 + core + step) % 4, lo, hi // 2)
 
+        added = rows_product(middle_gradient, adapter_down_maps)
         received = []
         for part in range(2):
-            halves = term_halves(slots, weights[part], core)
+            if part:
+                blocks = (jnp.concatenate(after(across, summed), axis=0),)
+            else:
+                blocks = (own_weights, by_x, by_y)
+            halves = term_halves(slots, blocks, core)
             other = swap_core(halves[1])
             summed = halves[0].astype(jnp.float32) + other.astype(jnp.float32)
             summed = summed.astype(jnp.bfloat16).reshape(4, tokens, -1)
             for step in range(4):
                 there = pick(slot_of, (source + step) % 4, 0)
                 received.append(send(pick(summed, there, 0), owner(step)))
-        pieces = jnp.stack(received)
-        spot = jnp.arange(16, dtype=jnp.int32)
-        from_hi, from_lo, part = spot // 8, spot // 2 % 4, spot % 2
-        step = (hi - (from_hi * 2 + from_lo // 2)) % 4
-        order = ((part * 4 + step) * 2 + from_lo % 2).astype(jnp.int32)
-        normed_input_grad = finish(pieces, order, middle_gradient, adapter_down_maps, cut)
+        spots = [
+            (((hi - step) % 4) // 2) * 8 + (lo ^ block) * 2 + (hi - step) % 2
+            for blocks in ((0, 1, 2), (3,))
+            for step in range(4)
+            for block in blocks
+        ]
+        normed_input_grad = finish(received, jnp.stack(spots).astype(jnp.int32), added)
         return (normed_input_grad, down_total, query_total, key_value_total)
 
     return shards

time: 286 us -> 240 us (0.84)
  matrix products: 24.1 us -> 4.15 us
  starting transfers between devices: 50.3 us -> 68 us
  between operations: 22.1 us -> 8.83 us
  local copies, waits for them, and re-layouts: 44.7 us -> 32.2 us
  waiting for transfers between devices: 97.6 us -> 86.9 us
  other arithmetic: 21.4 us -> 14.5 us
    dot_general x6 -> x1, matrix products: 19.9 us -> 0.6 us  [shards(): lax.dot_general(normed, late_gradient, (((0,), (0,)), ((), ())), preferre...]
    ppermute x24 -> x35, starting transfers between devices: 50.2 us -> 68 us  [send(): return lax.ppermute(value, AXES, pairs)]
    unnamed x93 -> x47, local copies, waits for them, and re-layouts: 28.4 us -> 15.7 us
    all_gather x3 -> x0, waiting for transfers between devices: 9.25 us -> none  [the longest x2 9.24 us: shards(): weights.append(lax.all_gather(rows, 'lo', axis=0, tiled=True))]
    reshape x5 -> x0, local copies, waits for them, and re-layouts: 4.71 us -> none  [the longest x1 2.29 us: attention_backward(): qmat = queries.reshape(token_count, key_value_heads, query_group, HEAD_SIZE)]
    slice x1 -> x2, local copies, waits for them, and re-layouts: 1.88 us -> 5.41 us  [shards(): across = (swap_lo(by_x[:cut], 2), swap_lo(by_y[cut:], 1))]
    pallas_call x1 -> x2, Pallas kernels: 11.9 us -> 8.98 us  [the longest x1 6.97 us: attention(): pl.pallas_call(attention_kernel, out_shape=(jax.ShapeDtypeStruct((tokens,...]
    ppermute x24 -> x35, waiting for transfers between devices: 87.7 us -> 86.9 us  [send(): return lax.ppermute(value, AXES, pairs)]
  transfers between devices with their start and end apart: 27 -> 35, of which waited for: 9 -> 11; matrix products, arithmetic and copies ran while one was open for 21% -> 15% of each run, Pallas kernels for 9% -> 9%
where the time goes in v3:
time: 240 us; the launch traced here: 239 us
  waiting for transfers between devices  86.9 us (36%)
  starting transfers between devices  68 us (28%)
  local copies, waits for them, and re-layouts  32.2 us (13%)
  Pallas kernels  24.1 us (10%)
  other arithmetic  14.5 us (6%)
  between operations  8.83 us (4%)
  matrix products  4.15 us (2%)
    ppermute x35, waiting for transfers between devices, send(): return lax.ppermute(value, AXES, pairs)  86.9 us
    ppermute x35, starting transfers between devices, send(): return lax.ppermute(value, AXES, pairs)  68 us
    unnamed x47, local copies, waits for them, and re-layouts  15.7 us
    pallas_call x2, Pallas kernels, term_halves(): pl.pallas_call(term_kernel, out_shape=jax.ShapeDtypeStruct((2, 4 * tokens...  15.1 us
    pallas_call x1, Pallas kernels, attention(): pl.pallas_call(attention_kernel, out_shape=(jax.ShapeDtypeStruct((tokens,...  6.97 us
    slice x2, local copies, waits for them, and re-layouts, shards(): across = (swap_lo(by_x[:cut], 2), swap_lo(by_y[cut:], 1))  5.41 us
  transfers between devices with their start and end apart: 35, of which 11 were waited for; matrix products, arithmetic and copies ran while one was open for 15% of the time, Pallas kernels for 9%

profile of v3, /device:TPU:1, one launch (start us, length us, event | category | flops | bytes accessed | tf_op | source)
XLA Modules:
  0.0 238.6 jit_solution(9717762786193457920)
XLA Ops:
  0.7 3.3 %constant_dynamic-update-slice_fusion.2 = bf16[512,3072]{1,0:T(8,128)(2,1)} fusion(bf16[512,2048]{1,0:T(8,128)(2,1)} %param.19), kind=kLoop, calls=%fused_computation.91 | loop fusion | bytes 4194304
  13.2 7.0 %attention.1 = (bf16[192,3072]{1,0:T(8,128)(2,1)S(1)}, f32[192,192]{1,0:T(8,128)S(1)}) custom-call(bf16[192,2048]{1,0:T(8,128)(2,1)S(1)} %copy-done.7, bf16[192,512]{1,0:T(8,128)(2,1)S(1)} %copy-done.10, bf16[192,512]{1,0:T(8,128)(2,1)S(1)} %copy-done.11, bf16[192,2048]{1,0:T(8,128)(2,1)S(1)} %copy-done.8, s32[192,1]{1,0:T(8,128)S(1)} %copy.32.row_ids, ...), custom_call_target="tpu_custom_call" | custom-call | flops 754974720 | bytes 2359296 | tf_op jit(solution)/shard_map/attention/pallas_call | solution.py:261
  21.5 5.0 %collective-permute-start.1 = (bf16[192,3072]{1,0:T(8,128)(2,1)S(1)}, bf16[192,3072]{1,0:T(8,128)(2,1)}, u32[]{:S(2)}, u32[]{:S(2)}) collective-permute-start(bf16[192,3072]{1,0:T(8,128)(2,1)S(1)} %get-tuple-element.15.refs_0_), channel_id=1, source_target_pairs={{0,8},{1,9},{2,10},{3,11},{4,12},{5,13},{6,14},{7,15},{8,16},{9,17... | collective-permute-start | bytes 3538952 | tf_op jit(solution)/shard_map/ppermute | solution.py:169
  26.5 21.9 %collective-permute-done.2 = bf16[192,3072]{1,0:T(8,128)(2,1)} collective-permute-done((bf16[192,3072]{1,0:T(8,128)(2,1)S(1)}, bf16[192,3072]{1,0:T(8,128)(2,1)}, u32[]{:S(2)}, u32[]{:S(2)}) %collective-permute-start.2) | collective-permute-done | bytes 1179680 | tf_op jit(solution)/shard_map/ppermute | solution.py:169
  65.2 10.7 %collective-permute-done.3 = bf16[192,3072]{1,0:T(8,128)(2,1)} collective-permute-done((bf16[192,3072]{1,0:T(8,128)(2,1)}, bf16[192,3072]{1,0:T(8,128)(2,1)}, u32[]{:S(2)}, u32[]{:S(2)}) %collective-permute-start.3) | collective-permute-done | bytes 1179680 | tf_op jit(solution)/shard_map/ppermute | solution.py:169
  78.9 2.5 %broadcast_select_fusion.refs_2_ = bf16[192,3072]{1,0:T(8,128)(2,1)} fusion(bf16[192,3072]{1,0:T(8,128)(2,1)} %collective-permute-done.3, bf16[192,3072]{1,0:T(8,128)(2,1)} %collective-permute-done.4, pred[]{:T(512)S(6)} %lt.231), kind=kLoop, calls=%fused_computation.26 | loop fusion | flops 589824 | bytes 3538945 | tf_op jit(solution)/shard_map/jit(_where)/select_n | solution.py:445
  82.1 2.8 %slice.76 = bf16[256,3072]{1,0:T(8,128)(2,1)} slice(bf16[512,3072]{1,0:T(8,128)(2,1)} %collective-permute-done.7.refs_5_), slice={[0:256], [0:3072]} | slice | bytes 3145728 | tf_op jit(solution)/shard_map/slice | solution.py:492
  84.9 2.7 %slice.77 = bf16[256,3072]{1,0:T(8,128)(2,1)} slice(bf16[512,3072]{1,0:T(8,128)(2,1)} %collective-permute-done.8.refs_6_), slice={[256:512], [0:3072]} | slice | bytes 3145728 | tf_op jit(solution)/shard_map/slice | solution.py:492
  88.5 2.8 %copy.41 = f32[64,3072]{0,1:T(8,128)} copy(f32[64,3072]{1,0:T(8,128)} %pad_maximum_fusion.2) | data formatting | bytes 1572864 | tf_op jit(solution)/shard_map/reshape | solution.py:399
  95.7 6.8 %collective-permute-done.5 = bf16[192,3072]{1,0:T(8,128)(2,1)} collective-permute-done((bf16[192,3072]{1,0:T(8,128)(2,1)}, bf16[192,3072]{1,0:T(8,128)(2,1)}, u32[]{:S(2)}, u32[]{:S(2)}) %collective-permute-start.5) | collective-permute-done | bytes 1179680 | tf_op jit(solution)/shard_map/ppermute | solution.py:169
  105.0 32.0 %collective-permute-done.23 = bf16[2,2,320,192]{2,3,1,0:T(8,128)(2,1)S(1)} collective-permute-done((bf16[2,2,320,192]{2,3,1,0:T(8,128)(2,1)S(1)}, bf16[2,2,320,192]{2,3,1,0:T(8,128)(2,1)S(1)}, u32[]{:S(2)}, u32[]{:S(2)}) %collective-permute-start.23) | collective-permute-done | bytes 491552 | tf_op jit(solution)/shard_map/ppermute | solution.py:169
  138.8 4.6 %collective-permute-done.24 = bf16[2,320,192]{1,2,0:T(8,128)(2,1)S(1)} collective-permute-done((bf16[2,320,192]{1,2,0:T(8,128)(2,1)S(1)}, bf16[2,320,192]{1,2,0:T(8,128)(2,1)S(1)}, u32[]{:S(2)}, u32[]{:S(2)}) %collective-permute-start.24) | collective-permute-done | bytes 245792 | tf_op jit(solution)/shard_map/ppermute | solution.py:169
  144.4 2.9 %collective-permute-start.25 = (bf16[320,192]{0,1:T(8,128)(2,1)S(1)}, bf16[320,192]{0,1:T(8,128)(2,1)S(1)}, u32[]{:S(2)}, u32[]{:S(2)}) collective-permute-start(bf16[320,192]{0,1:T(8,128)(2,1)S(1)} %get-tuple-element.30), channel_id=1, source_target_pairs={{0,8},{1,9},{2,10},{3,11},{4,12},{5,13},{6,14},{7,15},{8,16},{9,17... | collective-permute-start | bytes 368648 | tf_op jit(solution)/shard_map/ppermute | solution.py:169
  147.3 2.8 %collective-permute-start.26 = (bf16[320,192]{0,1:T(8,128)(2,1)S(1)}, bf16[320,192]{0,1:T(8,128)(2,1)S(1)}, u32[]{:S(2)}, u32[]{:S(2)}) collective-permute-start(bf16[320,192]{0,1:T(8,128)(2,1)S(1)} %get-tuple-element.31), channel_id=1, source_target_pairs={{0,16},{1,17},{2,18},{3,19},{4,20},{5,21},{6,22},{7,23},{8,24},{9,... | collective-permute-start | bytes 368648 | tf_op jit(solution)/shard_map/ppermute | solution.py:169
  152.4 11.2 %term.2 = bf16[2,768,768]{2,1,0:T(8,128)(2,1)S(1)} custom-call(s32[1]{0:T(128)} %bitcast.17.turn_ref, bf16[192,3072]{1,0:T(8,128)(2,1)S(1)} %get-tuple-element.15.refs_0_, bf16[192,3072]{1,0:T(8,128)(2,1)S(1)} %get-tuple-element.38.refs_1_, bf16[192,3072]{1,0:T(8,128)(2,1)S(1)} %copy-done.3, bf16[192,3072]{1,0:T(8,128)(2,1)S(1)} %get-tuple-element.37.refs_3_, ...), custom_call_target="tpu_custom_call" | custom-call | flops 7247757312 | bytes 16515072 | tf_op jit(solution)/shard_map/term/pallas_call | solution.py:331
  165.3 3.6 %collective-permute-done.30 = bf16[320,192]{0,1:T(8,128)(2,1)S(1)} collective-permute-done((bf16[320,192]{0,1:T(8,128)(2,1)S(1)}, bf16[320,192]{0,1:T(8,128)(2,1)S(1)}, u32[]{:S(2)}, u32[]{:S(2)}) %collective-permute-start.30) | collective-permute-done | bytes 122912 | tf_op jit(solution)/shard_map/ppermute | solution.py:169
  168.9 9.5 %collective-permute-start.9 = (bf16[768,768]{1,0:T(8,128)(2,1)S(1)}, bf16[768,768]{1,0:T(8,128)(2,1)S(1)}, u32[]{:S(2)}, u32[]{:S(2)}) collective-permute-start(bf16[768,768]{1,0:T(8,128)(2,1)S(1)} %slice_bitcast_fusion), channel_id=1, source_target_pairs={{0,1},{1,0},{2,3},{3,2},{4,5},{5,4},{6,7},{7,6},{8,9},{9,8},{10,11... | collective-permute-start | bytes 3538952 | tf_op jit(solution)/shard_map/ppermute | solution.py:169
  188.2 6.1 %collective-permute-start.13 = (bf16[192,768]{1,0:T(8,128)(2,1)}, bf16[192,768]{1,0:T(8,128)(2,1)S(1)}, u32[]{:S(2)}, u32[]{:S(2)}) collective-permute-start(bf16[192,768]{1,0:T(8,128)(2,1)} %get-tuple-element.33), channel_id=1, source_target_pairs={{0,24},{1,0},{2,26},{3,2},{4,28},{5,4},{6,30},{7,6},{8,8},{9,16},{... | collective-permute-start | bytes 884744 | tf_op jit(solution)/shard_map/ppermute | solution.py:169
  194.3 2.7 %collective-permute-start.12 = (bf16[192,768]{1,0:T(8,128)(2,1)}, bf16[192,768]{1,0:T(8,128)(2,1)S(1)}, u32[]{:S(2)}, u32[]{:S(2)}) collective-permute-start(bf16[192,768]{1,0:T(8,128)(2,1)} %get-tuple-element.34), channel_id=1, source_target_pairs={{0,16},{1,24},{2,18},{3,26},{4,20},{5,28},{6,22},{7,30},{8,0},{9,8... | collective-permute-start | bytes 884744 | tf_op jit(solution)/shard_map/ppermute | solution.py:169
  197.0 3.6 %collective-permute-start.11 = (bf16[192,768]{1,0:T(8,128)(2,1)}, bf16[192,768]{1,0:T(8,128)(2,1)S(1)}, u32[]{:S(2)}, u32[]{:S(2)}) collective-permute-start(bf16[192,768]{1,0:T(8,128)(2,1)} %get-tuple-element.35), channel_id=1, source_target_pairs={{0,8},{1,16},{2,10},{3,18},{4,12},{5,20},{6,14},{7,22},{8,24},{9,0... | collective-permute-start | bytes 884744 | tf_op jit(solution)/shard_map/ppermute | solution.py:169
  200.8 3.9 %term.3 = bf16[2,768,256]{2,1,0:T(8,128)(2,1)S(1)} custom-call(s32[1]{0:T(128)} %bitcast.17.turn_ref, bf16[192,3072]{1,0:T(8,128)(2,1)S(1)} %get-tuple-element.15.refs_0_, bf16[192,3072]{1,0:T(8,128)(2,1)S(1)} %get-tuple-element.38.refs_1_, bf16[192,3072]{1,0:T(8,128)(2,1)S(1)} %copy-done.3, bf16[192,3072]{1,0:T(8,128)(2,1)S(1)} %get-tuple-element.37.refs_3_, ...), custom_call_target="tpu_custom_call" | custom-call | flops 2415919104 | bytes 8650752 | tf_op jit(solution)/shard_map/term/pallas_call | solution.py:331
  219.2 2.3 collective-permute-start.20
  221.6 4.6 %collective-permute-start.19 = (bf16[192,256]{1,0:T(8,128)(2,1)S(1)}, bf16[192,256]{1,0:T(8,128)(2,1)S(1)}, u32[]{:S(2)}, u32[]{:S(2)}) collective-permute-start(bf16[192,256]{1,0:T(8,128)(2,1)S(1)} %get-tuple-element.48), channel_id=1, source_target_pairs={{0,16},{1,24},{2,18},{3,26},{4,20},{5,28},{6,22},{7,30},{8,0},{9,8... | collective-permute-start | bytes 294920 | tf_op jit(solution)/shard_map/ppermute | solution.py:169
  228.8 2.5 %collective-permute-start.17 = (bf16[192,256]{1,0:T(8,128)(2,1)S(1)}, bf16[192,256]{1,0:T(8,128)(2,1)S(1)}, u32[]{:S(2)}, u32[]{:S(2)}) collective-permute-start(bf16[192,256]{1,0:T(8,128)(2,1)S(1)} %get-tuple-element.50), channel_id=1, source_target_pairs={{0,0},{1,8},{2,2},{3,10},{4,4},{5,12},{6,6},{7,14},{8,16},{9,24},{... | collective-permute-start | bytes 294920 | tf_op jit(solution)/shard_map/ppermute | solution.py:169
  (152 shorter events, 72.3 us)
Async XLA Ops:
  5.7 75.7 %collective-permute-start.8 = (bf16[512,3072]{1,0:T(8,128)(2,1)}, bf16[512,3072]{1,0:T(8,128)(2,1)}, u32[]{:S(2)}, u32[]{:S(2)}) collective-permute-start(bf16[512,3072]{1,0:T(8,128)(2,1)} %constant_dynamic-update-slice_fusion.refs_4_), channel_id=1, source_target_pairs={{0,4},{1,5},{2,6},{3,7},{4,0},{5,1},{6,2},{7,3},{8,12},{9,13},{10,... | collective-permute-start | bytes 9437192 | tf_op jit(solution)/shard_map/ppermute | solution.py:169
  7.7 73.7 %collective-permute-start.7 = (bf16[512,3072]{1,0:T(8,128)(2,1)}, bf16[512,3072]{1,0:T(8,128)(2,1)}, u32[]{:S(2)}, u32[]{:S(2)}) collective-permute-start(bf16[512,3072]{1,0:T(8,128)(2,1)} %constant_dynamic-update-slice_fusion.refs_4_), channel_id=1, source_target_pairs={{0,2},{1,3},{2,0},{3,1},{4,6},{5,7},{6,4},{7,5},{8,10},{9,11},{10,... | collective-permute-start | bytes 9437192 | tf_op jit(solution)/shard_map/ppermute | solution.py:169
  20.2 28.2 %collective-permute-start.2 = (bf16[192,3072]{1,0:T(8,128)(2,1)S(1)}, bf16[192,3072]{1,0:T(8,128)(2,1)}, u32[]{:S(2)}, u32[]{:S(2)}) collective-permute-start(bf16[192,3072]{1,0:T(8,128)(2,1)S(1)} %get-tuple-element.15.refs_0_), channel_id=1, source_target_pairs={{8,0},{9,1},{10,2},{11,3},{12,4},{13,5},{14,6},{15,7},{16,8},{17,9... | collective-permute-start | bytes 3538952 | tf_op jit(solution)/shard_map/ppermute | solution.py:169
  21.5 28.2 %collective-permute-start.1 = (bf16[192,3072]{1,0:T(8,128)(2,1)S(1)}, bf16[192,3072]{1,0:T(8,128)(2,1)}, u32[]{:S(2)}, u32[]{:S(2)}) collective-permute-start(bf16[192,3072]{1,0:T(8,128)(2,1)S(1)} %get-tuple-element.15.refs_0_), channel_id=1, source_target_pairs={{0,8},{1,9},{2,10},{3,11},{4,12},{5,13},{6,14},{7,15},{8,16},{9,17... | collective-permute-start | bytes 3538952 | tf_op jit(solution)/shard_map/ppermute | solution.py:169
  48.4 27.5 %collective-permute-start.3 = (bf16[192,3072]{1,0:T(8,128)(2,1)}, bf16[192,3072]{1,0:T(8,128)(2,1)}, u32[]{:S(2)}, u32[]{:S(2)}) collective-permute-start(bf16[192,3072]{1,0:T(8,128)(2,1)} %collective-permute-done.2), channel_id=1, source_target_pairs={{8,0},{9,1},{10,2},{11,3},{12,4},{13,5},{14,6},{15,7},{16,8},{17,9... | collective-permute-start | bytes 3538952 | tf_op jit(solution)/shard_map/ppermute | solution.py:169
  49.7 27.5 %collective-permute-start.4 = (bf16[192,3072]{1,0:T(8,128)(2,1)}, bf16[192,3072]{1,0:T(8,128)(2,1)}, u32[]{:S(2)}, u32[]{:S(2)}) collective-permute-start(bf16[192,3072]{1,0:T(8,128)(2,1)} %collective-permute-done.1), channel_id=1, source_target_pairs={{8,16},{9,17},{10,18},{11,19},{12,20},{13,21},{14,22},{15,23},{16,... | collective-permute-start | bytes 3538952 | tf_op jit(solution)/shard_map/ppermute | solution.py:169
  75.9 26.6 %collective-permute-start.5 = (bf16[192,3072]{1,0:T(8,128)(2,1)}, bf16[192,3072]{1,0:T(8,128)(2,1)}, u32[]{:S(2)}, u32[]{:S(2)}) collective-permute-start(bf16[192,3072]{1,0:T(8,128)(2,1)} %collective-permute-done.3), channel_id=1, source_target_pairs={{8,0},{9,1},{10,2},{11,3},{12,4},{13,5},{14,6},{15,7}} | collective-permute-start | bytes 3538952 | tf_op jit(solution)/shard_map/ppermute | solution.py:169
  77.2 25.5 %collective-permute-start.6 = (bf16[192,3072]{1,0:T(8,128)(2,1)}, bf16[192,3072]{1,0:T(8,128)(2,1)}, u32[]{:S(2)}, u32[]{:S(2)}) collective-permute-start(bf16[192,3072]{1,0:T(8,128)(2,1)} %collective-permute-done.4), channel_id=1, source_target_pairs={{16,24},{17,25},{18,26},{19,27},{20,28},{21,29},{22,30},{23,31}} | collective-permute-start | bytes 3538952 | tf_op jit(solution)/shard_map/ppermute | solution.py:169
  91.3 103.0 %collective-permute-start.15 = (bf16[256,3072]{1,0:T(8,128)(2,1)}, bf16[256,3072]{1,0:T(8,128)(2,1)S(1)}, u32[]{:S(2)}, u32[]{:S(2)}) collective-permute-start(bf16[256,3072]{1,0:T(8,128)(2,1)} %slice.77), channel_id=1, source_target_pairs={{0,2},{1,3},{2,0},{3,1},{4,6},{5,7},{6,4},{7,5},{8,10},{9,11},{10,... | collective-permute-start | bytes 4718600 | tf_op jit(solution)/shard_map/ppermute | solution.py:169
  91.6 105.4 %collective-permute-start.14 = (bf16[256,3072]{1,0:T(8,128)(2,1)}, bf16[256,3072]{1,0:T(8,128)(2,1)S(1)}, u32[]{:S(2)}, u32[]{:S(2)}) collective-permute-start(bf16[256,3072]{1,0:T(8,128)(2,1)} %slice.76), channel_id=1, source_target_pairs={{0,4},{1,5},{2,6},{3,7},{4,0},{5,1},{6,2},{7,3},{8,12},{9,13},{10,... | collective-permute-start | bytes 4718600 | tf_op jit(solution)/shard_map/ppermute | solution.py:169
  94.6 42.3 %collective-permute-start.23 = (bf16[2,2,320,192]{2,3,1,0:T(8,128)(2,1)S(1)}, bf16[2,2,320,192]{2,3,1,0:T(8,128)(2,1)S(1)}, u32[]{:S(2)}, u32[]{:S(2)}) collective-permute-start(bf16[2,2,320,192]{2,3,1,0:T(8,128)(2,1)S(1)} %fusion.5), channel_id=1, source_target_pairs={{0,4},{1,5},{2,6},{3,7},{4,0},{5,1},{6,2},{7,3},{8,12},{9,13},{10,... | collective-permute-start | bytes 1474568 | tf_op jit(solution)/shard_map/ppermute | solution.py:169
  102.5 35.9 %collective-permute-start.21 = (bf16[2,2,320,192]{2,3,1,0:T(8,128)(2,1)S(1)}, bf16[2,2,320,192]{2,3,1,0:T(8,128)(2,1)S(1)}, u32[]{:S(2)}, u32[]{:S(2)}) collective-permute-start(bf16[2,2,320,192]{2,3,1,0:T(8,128)(2,1)S(1)} %fusion.4), channel_id=1, source_target_pairs={{0,2},{1,3},{2,0},{3,1},{4,6},{5,7},{6,4},{7,5},{8,10},{9,11},{10,... | collective-permute-start | bytes 1474568 | tf_op jit(solution)/shard_map/ppermute | solution.py:169
  144.4 19.2 %collective-permute-start.25 = (bf16[320,192]{0,1:T(8,128)(2,1)S(1)}, bf16[320,192]{0,1:T(8,128)(2,1)S(1)}, u32[]{:S(2)}, u32[]{:S(2)}) collective-permute-start(bf16[320,192]{0,1:T(8,128)(2,1)S(1)} %get-tuple-element.30), channel_id=1, source_target_pairs={{0,8},{1,9},{2,10},{3,11},{4,12},{5,13},{6,14},{7,15},{8,16},{9,17... | collective-permute-start | bytes 368648 | tf_op jit(solution)/shard_map/ppermute | solution.py:169
  147.3 16.3 %collective-permute-start.26 = (bf16[320,192]{0,1:T(8,128)(2,1)S(1)}, bf16[320,192]{0,1:T(8,128)(2,1)S(1)}, u32[]{:S(2)}, u32[]{:S(2)}) collective-permute-start(bf16[320,192]{0,1:T(8,128)(2,1)S(1)} %get-tuple-element.31), channel_id=1, source_target_pairs={{0,16},{1,17},{2,18},{3,19},{4,20},{5,21},{6,22},{7,23},{8,24},{9,... | collective-permute-start | bytes 368648 | tf_op jit(solution)/shard_map/ppermute | solution.py:169
  150.1 13.5 %collective-permute-start.27 = (bf16[320,192]{0,1:T(8,128)(2,1)S(1)}, bf16[320,192]{0,1:T(8,128)(2,1)S(1)}, u32[]{:S(2)}, u32[]{:S(2)}) collective-permute-start(bf16[320,192]{0,1:T(8,128)(2,1)S(1)} %get-tuple-element.32), channel_id=1, source_target_pairs={{0,24},{1,25},{2,26},{3,27},{4,28},{5,29},{6,30},{7,31},{8,0},{9,1... | collective-permute-start | bytes 368648 | tf_op jit(solution)/shard_map/ppermute | solution.py:169
  163.8 14.6 %collective-permute-start.29 = (bf16[320,192]{0,1:T(8,128)(2,1)S(1)}, bf16[320,192]{0,1:T(8,128)(2,1)S(1)}, u32[]{:S(2)}, u32[]{:S(2)}) collective-permute-start(bf16[320,192]{0,1:T(8,128)(2,1)S(1)} %fusion.15), channel_id=1, source_target_pairs={{0,16},{1,17},{2,18},{3,19},{4,20},{5,21},{6,22},{7,23},{8,24},{9,... | collective-permute-start | bytes 368648 | tf_op jit(solution)/shard_map/ppermute | solution.py:169
  164.2 14.3 %collective-permute-start.28 = (bf16[320,192]{0,1:T(8,128)(2,1)S(1)}, bf16[320,192]{0,1:T(8,128)(2,1)S(1)}, u32[]{:S(2)}, u32[]{:S(2)}) collective-permute-start(bf16[320,192]{0,1:T(8,128)(2,1)S(1)} %fusion.15), channel_id=1, source_target_pairs={{0,8},{1,9},{2,10},{3,11},{4,12},{5,13},{6,14},{7,15},{8,16},{9,17... | collective-permute-start | bytes 368648 | tf_op jit(solution)/shard_map/ppermute | solution.py:169
  168.9 17.9 %collective-permute-start.9 = (bf16[768,768]{1,0:T(8,128)(2,1)S(1)}, bf16[768,768]{1,0:T(8,128)(2,1)S(1)}, u32[]{:S(2)}, u32[]{:S(2)}) collective-permute-start(bf16[768,768]{1,0:T(8,128)(2,1)S(1)} %slice_bitcast_fusion), channel_id=1, source_target_pairs={{0,1},{1,0},{2,3},{3,2},{4,5},{5,4},{6,7},{7,6},{8,9},{9,8},{10,11... | collective-permute-start | bytes 3538952 | tf_op jit(solution)/shard_map/ppermute | solution.py:169
  185.3 20.1 %collective-permute-start.32 = (bf16[2,2,320,192]{2,3,0,1:T(8,128)(2,1)S(1)}, bf16[2,2,320,192]{2,3,0,1:T(8,128)(2,1)S(1)}, u32[]{:S(2)}, u32[]{:S(2)}) collective-permute-start(bf16[2,2,320,192]{2,3,0,1:T(8,128)(2,1)S(1)} %pad_maximum_fusion.4), channel_id=1, source_target_pairs={{0,4},{1,5},{2,6},{3,7},{4,0},{5,1},{6,2},{7,3},{8,12},{9,13},{10,... | collective-permute-start | bytes 1474568 | tf_op jit(solution)/shard_map/ppermute | solution.py:169
  186.8 21.1 %collective-permute-start.34 = (bf16[2,2,320,192]{2,3,0,1:T(8,128)(2,1)S(1)}, bf16[2,2,320,192]{2,3,0,1:T(8,128)(2,1)S(1)}, u32[]{:S(2)}, u32[]{:S(2)}) collective-permute-start(bf16[2,2,320,192]{2,3,0,1:T(8,128)(2,1)S(1)} %pad_maximum_fusion.5), channel_id=1, source_target_pairs={{0,2},{1,3},{2,0},{3,1},{4,6},{5,7},{6,4},{7,5},{8,10},{9,11},{10,... | collective-permute-start | bytes 1474568 | tf_op jit(solution)/shard_map/ppermute | solution.py:169
  188.2 33.4 %collective-permute-start.13 = (bf16[192,768]{1,0:T(8,128)(2,1)}, bf16[192,768]{1,0:T(8,128)(2,1)S(1)}, u32[]{:S(2)}, u32[]{:S(2)}) collective-permute-start(bf16[192,768]{1,0:T(8,128)(2,1)} %get-tuple-element.33), channel_id=1, source_target_pairs={{0,24},{1,0},{2,26},{3,2},{4,28},{5,4},{6,30},{7,6},{8,8},{9,16},{... | collective-permute-start | bytes 884744 | tf_op jit(solution)/shard_map/ppermute | solution.py:169
  194.3 31.9 %collective-permute-start.12 = (bf16[192,768]{1,0:T(8,128)(2,1)}, bf16[192,768]{1,0:T(8,128)(2,1)S(1)}, u32[]{:S(2)}, u32[]{:S(2)}) collective-permute-start(bf16[192,768]{1,0:T(8,128)(2,1)} %get-tuple-element.34), channel_id=1, source_target_pairs={{0,16},{1,24},{2,18},{3,26},{4,20},{5,28},{6,22},{7,30},{8,0},{9,8... | collective-permute-start | bytes 884744 | tf_op jit(solution)/shard_map/ppermute | solution.py:169
  197.0 31.1 %collective-permute-start.11 = (bf16[192,768]{1,0:T(8,128)(2,1)}, bf16[192,768]{1,0:T(8,128)(2,1)S(1)}, u32[]{:S(2)}, u32[]{:S(2)}) collective-permute-start(bf16[192,768]{1,0:T(8,128)(2,1)} %get-tuple-element.35), channel_id=1, source_target_pairs={{0,8},{1,16},{2,10},{3,18},{4,12},{5,20},{6,14},{7,22},{8,24},{9,0... | collective-permute-start | bytes 884744 | tf_op jit(solution)/shard_map/ppermute | solution.py:169
  205.4 26.6 %collective-permute-start.10 = (bf16[192,768]{1,0:T(8,128)(2,1)}, bf16[192,768]{1,0:T(8,128)(2,1)S(1)}, u32[]{:S(2)}, u32[]{:S(2)}) collective-permute-start(bf16[192,768]{1,0:T(8,128)(2,1)} %get-tuple-element.36), channel_id=1, source_target_pairs={{0,0},{1,8},{2,2},{3,10},{4,4},{5,12},{6,6},{7,14},{8,16},{9,24},{... | collective-permute-start | bytes 884744 | tf_op jit(solution)/shard_map/ppermute | solution.py:169
  (32 other events, 278.0 us)

commit v4 on v3

--- a/solution.py
+++ b/solution.py
@@ -298,51 +298,66 @@
     )
 
 
-def term_kernel(turn_ref, *refs):
-    del turn_ref
-    slots, rights, (out_ref, left, arrived) = refs[:4], refs[4:-3], refs[-3:]
-    tokens = slots[0].shape[0]
-
-    @pl.when(pl.program_id(0) == 0)
-    def _():
-        copies = [
-            pltpu.make_async_copy(a, left.at[pl.ds(n * tokens, tokens), :], arrived.at[n])
-            for n, a in enumerate(slots)
-        ]
-        for copy in copies:
-            copy.start()
-        for copy in copies:
-            copy.wait()
-
-    width = rights[0].shape[0]
-    for n, right in enumerate(rights):
-        out_ref[0, :, n * width : (n + 1) * width] = lax.dot_general(
-            left[...],
-            right[...],
-            (((1,), (1,)), ((), ())),
-            preferred_element_type=jnp.float32,
-        ).astype(jnp.bfloat16)
-
-
-def term_halves(slots, weights, core):
-    tokens, depth = slots[0].shape
-    rows = weights[0].shape[0] // 2
+def term_kernel(place_ref, *refs):
+    blocks, weights = refs[:7], refs[7:-6]
+    kept_ref, sent_ref, left, right, arrived, landed = refs[-6:]
+    tokens = blocks[0].shape[0]
+    core, hi = place_ref[0], place_ref[1]
+    count = len(weights) // 2
+    width = weights[0].shape[0]
+
+    for n in range(4):
+        there = left.at[pl.ds(n * tokens, tokens), :]
+        for step, block in zip((0, 1, 2, 3, -1, -2, -3), blocks):
+
+            @pl.when(hi == n + step)
+            def _(block=block, there=there, n=n):
+                pltpu.make_async_copy(block, there, arrived.at[n]).start()
+
+    for turn in range(2):
+        for n in range(count):
+            slot = turn * count + n
+            for half in range(2):
+
+                @pl.when(core == (half + 1 - turn) % 2)
+                def _(n=n, half=half, slot=slot):
+                    pltpu.make_async_copy(
+                        weights[2 * n + half], right.at[slot], landed.at[slot]
+                    ).start()
+
+    for n in range(4):
+        there = left.at[pl.ds(n * tokens, tokens), :]
+        pltpu.make_async_copy(blocks[0], there, arrived.at[n]).wait()
+    for turn, out_ref in enumerate((sent_ref, kept_ref)):
+        for n in range(count):
+            slot = turn * count + n
+            pltpu.make_async_copy(weights[2 * n], right.at[slot], landed.at[slot]).wait()
+            out_ref[:, n * width : (n + 1) * width] = lax.dot_general(
+                left[...],
+                right[slot],
+                (((1,), (1,)), ((), ())),
+                preferred_element_type=jnp.float32,
+            ).astype(jnp.bfloat16)
+
+
+def term_halves(blocks, weights, core, hi):
+    tokens, depth = blocks[0].shape
+    rows = weights[0][0].shape[0]
     count = len(weights)
+    flat = [w for pair in weights for w in pair]
+    out = jax.ShapeDtypeStruct((4 * tokens, count * rows), jnp.bfloat16)
     return pl.pallas_call(
         term_kernel,
-        out_shape=jax.ShapeDtypeStruct((2, 4 * tokens, count * rows), jnp.bfloat16),
-        grid_spec=pltpu.PrefetchScalarGridSpec(
-            num_scalar_prefetch=1,
-            grid=(2,),
-            in_specs=[pl.BlockSpec(memory_space=pl.ANY)] * 4
-            + [pl.BlockSpec((rows, depth), lambda i, turn: (lax.rem(turn[0] + 1 - i, 2), 0))]
-            * count,
-            out_specs=pl.BlockSpec((1, 4 * tokens, count * rows), lambda i, turn: (1 - i, 0, 0)),
-            scratch_shapes=[
-                pltpu.VMEM((4 * tokens, depth), jnp.bfloat16),
-                pltpu.SemaphoreType.DMA((4,)),
-            ],
-        ),
+        out_shape=(out, out),
+        in_specs=[pl.BlockSpec(memory_space=pltpu.SMEM)]
+        + [pl.BlockSpec(memory_space=pl.ANY)] * (7 + len(flat)),
+        out_specs=(pl.BlockSpec(memory_space=pltpu.VMEM),) * 2,
+        scratch_shapes=[
+            pltpu.VMEM((4 * tokens, depth), jnp.bfloat16),
+            pltpu.VMEM((2 * count, rows, depth), jnp.bfloat16),
+            pltpu.SemaphoreType.DMA((4,)),
+            pltpu.SemaphoreType.DMA((2 * count,)),
+        ],
         compiler_params=pltpu.CompilerParams(vmem_limit_bytes=40 << 20),
         cost_estimate=pl.CostEstimate(
             flops=16 * tokens * depth * rows * count,
@@ -350,7 +365,7 @@
             transcendentals=0,
         ),
         name="term",
-    )(core[None], *slots, *weights)
+    )(jnp.stack([core, hi]), *blocks, *flat)
 
 
 def finish_kernel(spot_ref, added_ref, *refs):
@@ -381,72 +396,49 @@
     )(spots, added, *pieces)
 
 
-def plane_scatter(value, bits):
-    lo = lax.axis_index("lo")
-    for bit in bits:
-        mine = (lo // bit) % 2
-        axis = 2 if bit == 1 and value.ndim == 5 else 1
-        sent = pick(value, 1 - mine, axis).astype(jnp.bfloat16)
-        value = pick(value, mine, axis) + swap_lo(sent, bit).astype(jnp.float32)
-    return value
-
-
-def dp_pieces(down_local, up_local):
-    rows, rank = down_local.shape
+def dp_pieces(down_turned, up_local):
+    rank, rows = down_turned.shape
+    width = rows // 16
     return jnp.concatenate(
         [
-            down_local.reshape(16, rows // 16, rank),
-            up_local.reshape(-1, 16, rank).transpose(1, 0, 2),
+            down_turned.reshape(rank, 4, 4, width).transpose(2, 1, 0, 3),
+            up_local.reshape(4, 16, -1, width).transpose(2, 0, 1, 3).reshape(4, 4, -1, width),
         ],
-        axis=1,
-    )
-
-
-def dp_scatter(pieces):
+        axis=2,
+    ).astype(jnp.bfloat16)
+
+
+def dp_results(every, rank, up_shape):
+    rows, width = every.shape[2:]
+    down = every[:, :, :rank].transpose(1, 0, 3, 2).reshape(16 * width, rank)
+    up = every[:, :, rank:].reshape(-1, 4, 16, width).transpose(1, 2, 0, 3).reshape(up_shape)
+    return down.astype(jnp.float32), up.astype(jnp.float32)
+
+
+def scatter_sum(value, axis):
+    return jnp.sum(
+        lax.all_to_all(value, axis, 0, 0), axis=0, dtype=jnp.float32
+    ).astype(jnp.bfloat16)
+
+
+def gather_line(piece):
     hi = lax.axis_index("hi")
-    pieces = pieces.reshape(4, 2, 2, *pieces.shape[1:])
-    column = jnp.concatenate(
-        [plane_scatter(pieces[:2], (1, 2)), plane_scatter(pieces[2:], (2, 1))], axis=0
-    )
-    total = pick(column, hi, 0)
-    for step in range(1, 4):
-        sent = pick(column, (hi + step) % 4, 0).astype(jnp.bfloat16)
-        total = total + turn_hi(sent, step).astype(jnp.float32)
-    return total.astype(jnp.bfloat16)
-
-
-def dp_gather(piece):
-    hi, lo = lax.axis_index("hi"), lax.axis_index("lo")
     turned = jnp.stack([piece] + [turn_hi(piece, step) for step in range(1, 4)])
-    column = jnp.stack([pick(turned, (hi - z) % 4, 0) for z in range(4)])
-    planes = []
-    for value, bits in ((column[:2], (1, 2)), (column[2:], (2, 1))):
-        for bit in bits:
-            other = swap_lo(value, bit)
-            first = (lo // bit) % 2 == 0
-            axis = 1 if bit == 2 or value.ndim == 3 else 2
-            value = jnp.stack(
-                [jnp.where(first, value, other), jnp.where(first, other, value)], axis=axis
-            )
-        planes.append(value)
-    return jnp.concatenate(planes, axis=0).reshape(16, *piece.shape)
-
-
-def gather_hi(own):
-    hi = lax.axis_index("hi")
+    return jnp.stack([pick(turned, (hi - z) % 4, 0) for z in range(4)])
+
+
+def gather(value, axis):
+    return lax.all_to_all(jnp.broadcast_to(value[None], (4, *value.shape)), axis, 0, 0)
+
+
+def chain_hi(own, first):
     right, left = [own], [own]
     for step in range(1, 4):
         right.append(move_hi(right[-1], 1, step - 1, 2))
         left.append(move_hi(left[-1], -1, 1, 4 - step))
-    passed = (right[2], left[2])
-    slots = [
-        own,
-        jnp.where(hi == 3, right[1], left[1]),
-        jnp.where(hi < 2, left[2], right[2]),
-        jnp.where(hi == 0, left[3], jnp.where(hi == 3, right[3], right[1])),
-    ]
-    table = jnp.array([[0, 1, 2, 3], [3, 0, 1, 2], [2, 3, 0, 1], [3, 2, 1, 0]], jnp.int32)
-    return slots, pick(table, hi, 0), passed
+        if step < 3:
+            right[step], left[step] = after((right[step], left[step]), first[step - 1])
+    return right[1:], left[1:]
 
 
 def fast_shards():
@@ -465,12 +457,14 @@
         key_value_up_maps,
     ):
         hi, lo, core = (lax.axis_index(name) for name in AXES)
-        own_weights = jnp.concatenate(
-            [query_projection_weight, key_projection_weight, value_projection_weight], axis=1
-        )
-        cut = own_weights.shape[0] // 2
-        by_x, by_y = swap_lo(own_weights, 1), swap_lo(own_weights, 2)
-        stored_queries = after(stored_queries, own_weights)
+        parts = (query_projection_weight, key_projection_weight, value_projection_weight)
+        cut = query_projection_weight.shape[0] // 2
+        own_a = jnp.concatenate([w[:cut] for w in parts], axis=1)
+        own_b = jnp.concatenate([w[cut:] for w in parts], axis=1)
+        x_a, y_a = swap_lo(own_a, 1), swap_lo(own_a, 2)
+        next_b = after(own_b, (x_a, y_a))
+        x_b, y_b = swap_lo(next_b, 1), swap_lo(next_b, 2)
+        stored_queries = after(stored_queries, own_a)
 
         own, middle_part = attention(
             stored_queries,
@@ -486,10 +480,13 @@
         query_gradient = own[:, :q_width]
         key_gradient = own[:, q_width : q_width + k_width]
         value_gradient = own[:, q_width + k_width :]
-        slots, slot_of, passed = gather_hi(own)
-
-        by_x, by_y = after((by_x, by_y), passed)
-        across = (swap_lo(by_x[:cut], 2), swap_lo(by_y[cut:], 1))
+        right, left = chain_hi(own, ((x_a, y_a), (x_b, y_b)))
+        blocks = (own, *right, *left)
+        across_a, across_b = after((x_a, y_b), (right[1], left[1]))
+        quarter = cut // 2
+        across = [(swap_lo(across_a[:quarter], 2), swap_lo(across_b[:quarter], 1))]
+        rest_a, rest_b = after((across_a[quarter:], across_b[quarter:]), across[0])
+        across.append((swap_lo(rest_a, 2), swap_lo(rest_b, 1)))
 
         middle_local = jnp.concatenate(
             [
@@ -501,22 +498,13 @@
         middle = (middle_local + swap_core(middle_local)).astype(jnp.bfloat16)
         rank = adapter_down_maps.shape[1]
         adapter_middle, middle_gradient = middle[:, :rank], middle[:, rank:]
-        adapter_middle, late_gradient = after((adapter_middle, middle_gradient), (by_x, by_y))
-        down_local = lax.dot_general(
-            normed, late_gradient, (((0,), (0,)), ((), ())), preferred_element_type=jnp.float32
+        down_turned = lax.dot_general(
+            middle_gradient, normed, (((0,), (0,)), ((), ())), preferred_element_type=jnp.float32
         )
         ups = up_gradients(adapter_middle, query_gradient, key_gradient, value_gradient)
-        piece = dp_scatter(dp_pieces(down_local, jnp.concatenate(ups, axis=1)))
-        every = dp_gather(piece)
-        down_rows = down_local.shape[0]
-        down_total = every[:, : down_rows // 16].reshape(down_rows, rank).astype(jnp.float32)
-        up_total = every[:, down_rows // 16 :].transpose(1, 0, 2).reshape(ADAPTER_RANK, -1)
-        up_total = up_total.astype(jnp.float32)
-        query_total = up_total[:, :q_width]
-        key_value_total = jnp.stack(
-            [up_total[:, q_width : q_width + k_width], up_total[:, q_width + k_width :]]
-        )
-
+        up_local = jnp.concatenate(ups, axis=1)
+        column = scatter_sum(dp_pieces(down_turned, up_local), "lo")
+        piece = scatter_sum(column, "hi")
         tokens = own.shape[0]
         source = (hi % 2) * 2 + core
 
@@ -527,16 +515,23 @@
         received = []
         for part in range(2):
             if part:
-                blocks = (jnp.concatenate(after(across, summed), axis=0),)
+                weights = after(across, summed)
             else:
-                blocks = (own_weights, by_x, by_y)
-            halves = term_halves(slots, blocks, core)
-            other = swap_core(halves[1])
-            summed = halves[0].astype(jnp.float32) + other.astype(jnp.float32)
+                weights = ((own_a, own_b), (x_a, x_b), (y_a, y_b))
+            kept, sent = term_halves(after(blocks, (piece, across[0])), weights, core, hi)
+            summed = kept.astype(jnp.float32) + swap_core(sent).astype(jnp.float32)
             summed = summed.astype(jnp.bfloat16).reshape(4, tokens, -1)
+            if not part:
+                first_line = after(piece, summed)
             for step in range(4):
-                there = pick(slot_of, (source + step) % 4, 0)
-                received.append(send(pick(summed, there, 0), owner(step)))
+                received.append(send(pick(summed, (source + step) % 4, 0), owner(step)))
+        every = gather(gather_line(first_line), "lo")
+        down_total, up_total = dp_results(every, rank, up_local.shape)
+        query_total = up_total[:, :q_width]
+        key_value_total = jnp.stack(
+            [up_total[:, q_width : q_width + k_width], up_total[:, q_width + k_width :]]
+        )
+
         spots = [
             (((hi - step) % 4) // 2) * 8 + (lo ^ block) * 2 + (hi - step) % 2
             for blocks in ((0, 1, 2), (3,))

time: 240 us -> 242 us (level)
  Pallas kernels: 24.1 us -> 43 us
  waiting for transfers between devices: 86.9 us -> 76.5 us
  between operations: 8.83 us -> 1.16 us
    ppermute x35 -> x28, waiting for transfers between devices: 86.9 us -> 57.3 us  [send(): return lax.ppermute(value, AXES, pairs)]
    all_to_all x0 -> x3, waiting for transfers between devices: none -> 19.1 us  [the longest x2 19.1 us: scatter_sum(): lax.all_to_all(value, axis, 0, 0)]
    pallas_call x2, Pallas kernels: 15.1 us -> 34.1 us  [term_halves(): pl.pallas_call(term_kernel, out_shape=(out, out), in_specs=[pl.BlockSpec(...]
    ppermute x35 -> x28, starting transfers between devices: 68 us -> 53.4 us  [send(): return lax.ppermute(value, AXES, pairs)]
    all_to_all x0 -> x3, starting transfers between devices: none -> 13.2 us  [the longest x2 8.78 us: scatter_sum(): lax.all_to_all(value, axis, 0, 0)]
    unnamed x47 -> x37, local copies, waits for them, and re-layouts: 15.7 us -> 3.7 us
    convert_element_type x5 -> x3, local copies, waits for them, and re-layouts: 2.23 us -> 9.45 us  [dp_results(): return (down.astype(jnp.float32), up.astype(jnp.float32))]
    select_n x2 -> x0, other arithmetic: 4.67 us -> none  [the longest x1 2.45 us: gather_hi(): jnp.where(hi < 2, left[2], right[2])]
  transfers between devices with their start and end apart: 35 -> 31, of which waited for: 11 -> 13; matrix products, arithmetic and copies ran while one was open for 15% -> 13% of each run, Pallas kernels for 9% -> 9%
where the time goes in v4:
time: 242 us; the launch traced here: 241 us
  waiting for transfers between devices  76.5 us (32%)
  starting transfers between devices  66.6 us (28%)
  Pallas kernels  43 us (18%)
  local copies, waits for them, and re-layouts  33.9 us (14%)
  other arithmetic  15.8 us (7%)
  matrix products  3.73 us (2%)
    ppermute x28, waiting for transfers between devices, send(): return lax.ppermute(value, AXES, pairs)  57.3 us
    ppermute x28, starting transfers between devices, send(): return lax.ppermute(value, AXES, pairs)  53.4 us
    pallas_call x2, Pallas kernels, term_halves(): pl.pallas_call(term_kernel, out_shape=(out, out), in_specs=[pl.BlockSpec(...  34.1 us
    all_to_all x2, waiting for transfers between devices, scatter_sum(): lax.all_to_all(value, axis, 0, 0)  19.1 us
    convert_element_type x3, local copies, waits for them, and re-layouts, dp_results(): return (down.astype(jnp.float32), up.astype(jnp.float32))  9.45 us
    all_to_all x2, starting transfers between devices, scatter_sum(): lax.all_to_all(value, axis, 0, 0)  8.78 us
    pallas_call x1, Pallas kernels, attention(): pl.pallas_call(attention_kernel, out_shape=(jax.ShapeDtypeStruct((tokens,...  6.96 us
    slice x2, local copies, waits for them, and re-layouts, shards(): rest_a, rest_b = after((across_a[quarter:], across_b[quarter:]), across[0])  5.24 us
  transfers between devices with their start and end apart: 31, of which 13 were waited for; matrix products, arithmetic and copies ran while one was open for 13% of the time, Pallas kernels for 9%

profile of v4, /device:TPU:1, one launch (start us, length us, event | category | flops | bytes accessed | tf_op | source)
XLA Modules:
  0.0 240.8 jit_solution(1810738843900302582)
XLA Ops:
  0.7 2.9 %fusion.12 = (bf16[256,2048]{1,0:T(8,128)(2,1)}, bf16[256,2048]{1,0:T(8,128)(2,1)S(1)}) fusion(bf16[512,2048]{1,0:T(8,128)(2,1)} %param.18), kind=kLoop, calls=%fused_computation.45 | loop fusion | bytes 4194304 | tf_op jit(solution)/shard_map/slice | solution.py:463
  12.3 7.0 %attention.1 = (bf16[192,3072]{1,0:T(8,128)(2,1)S(1)}, f32[192,192]{1,0:T(8,128)S(1)}) custom-call(bf16[192,2048]{1,0:T(8,128)(2,1)S(1)} %copy-done.3, bf16[192,512]{1,0:T(8,128)(2,1)S(1)} %copy-done.6, bf16[192,512]{1,0:T(8,128)(2,1)S(1)} %copy-done.7, bf16[192,2048]{1,0:T(8,128)(2,1)S(1)} %copy-done.4, s32[192,1]{1,0:T(8,128)S(1)} %copy.35.row_ids, ...), custom_call_target="tpu_custom_call" | custom-call | flops 754974720 | bytes 2359296 | tf_op jit(solution)/shard_map/attention/pallas_call | solution.py:261
  20.7 5.0 %collective-permute-start.1 = (bf16[192,3072]{1,0:T(8,128)(2,1)S(1)}, bf16[192,3072]{1,0:T(8,128)(2,1)}, u32[]{:S(2)}, u32[]{:S(2)}) collective-permute-start(bf16[192,3072]{1,0:T(8,128)(2,1)S(1)} %get-tuple-element.42.refs_0_), channel_id=1, source_target_pairs={{0,8},{1,9},{2,10},{3,11},{4,12},{5,13},{6,14},{7,15},{8,16},{9,17... | collective-permute-start | bytes 3538952 | tf_op jit(solution)/shard_map/ppermute | solution.py:169
  29.7 12.5 %collective-permute-done.4.refs_11_ = bf16[256,3072]{1,0:T(8,128)(2,1)} collective-permute-done((bf16[256,3072]{1,0:T(8,128)(2,1)}, bf16[256,3072]{1,0:T(8,128)(2,1)}, u32[]{:S(2)}, u32[]{:S(2)}) %collective-permute-start.4) | collective-permute-done | bytes 1572896 | tf_op jit(solution)/shard_map/ppermute | solution.py:169
  44.9 2.8 %collective-permute-done.2.refs_4_ = bf16[192,3072]{1,0:T(8,128)(2,1)} collective-permute-done((bf16[192,3072]{1,0:T(8,128)(2,1)S(1)}, bf16[192,3072]{1,0:T(8,128)(2,1)}, u32[]{:S(2)}, u32[]{:S(2)}) %collective-permute-start.2) | collective-permute-done | bytes 1179680 | tf_op jit(solution)/shard_map/ppermute | solution.py:169
  56.2 2.9 %reshape.36 = bf16[192,4,4,256]{3,2,1,0:T(4,128)(2,1)S(1)} reshape(bf16[192,4096]{1,0:T(8,128)(2,1)} %convolution_convert_fusion) | data formatting | bytes 3145728 | tf_op jit(solution)/shard_map/reshape | solution.py:404
  62.2 4.4 %all-to-all-start = ((bf16[4,4,240,256]{3,1,2,0:T(4,128)(2,1)}), bf16[4,4,240,256]{3,1,2,0:T(4,128)(2,1)}, u32[]{:S(2)}, u32[]{:S(2)}) async-start(bf16[4,4,240,256]{3,1,2,0:T(4,128)(2,1)} %pad_maximum_fusion), calls=%async_computation | async-start | bytes 3932160 | tf_op jit(solution)/shard_map/all_to_all | solution.py:420
  66.7 14.1 %collective-permute-done.6.refs_5_ = bf16[192,3072]{1,0:T(8,128)(2,1)} collective-permute-done((bf16[192,3072]{1,0:T(8,128)(2,1)}, bf16[192,3072]{1,0:T(8,128)(2,1)}, u32[]{:S(2)}, u32[]{:S(2)}) %collective-permute-start.6) | collective-permute-done | bytes 1179680 | tf_op jit(solution)/shard_map/ppermute | solution.py:169
  88.5 10.3 %all-to-all-done = bf16[4,4,240,256]{3,1,2,0:T(4,128)(2,1)} async-done(((bf16[4,4,240,256]{3,1,2,0:T(4,128)(2,1)}), bf16[4,4,240,256]{3,1,2,0:T(4,128)(2,1)}, u32[]{:S(2)}, u32[]{:S(2)}) %all-to-all-start) | async-done | bytes 1966112 | tf_op jit(solution)/shard_map/all_to_all | solution.py:420
  98.8 3.5 %reduce_sum.24 = bf16[4,240,256]{2,0,1:T(4,128)(2,1)} reduce(bf16[4,4,240,256]{3,1,2,0:T(4,128)(2,1)} %all-to-all-done, bf16[]{:T(256)} %constant.241.clone.1), dimensions={0}, to_apply=%region_0.0 | reduce | flops 737280 | bytes 2457602 | tf_op jit(solution)/shard_map/reduce_sum | solution.py:419
  104.2 4.4 %all-to-all-start.1 = ((bf16[4,240,256]{2,1,0:T(8,128)(2,1)}), bf16[4,240,256]{2,1,0:T(8,128)(2,1)}, u32[]{:S(2)}, u32[]{:S(2)}) async-start(bf16[4,240,256]{2,1,0:T(8,128)(2,1)} %copy.40), calls=%async_computation.1 | async-start | bytes 983040 | tf_op jit(solution)/shard_map/all_to_all | solution.py:420
  108.6 8.8 %all-to-all-done.1 = bf16[4,240,256]{2,1,0:T(8,128)(2,1)} async-done(((bf16[4,240,256]{2,1,0:T(8,128)(2,1)}), bf16[4,240,256]{2,1,0:T(8,128)(2,1)}, u32[]{:S(2)}, u32[]{:S(2)}) %all-to-all-start.1) | async-done | bytes 491552 | tf_op jit(solution)/shard_map/all_to_all | solution.py:420
  118.6 20.9 %term.2 = (bf16[768,768]{1,0:T(8,128)(2,1)S(1)}, bf16[768,768]{1,0:T(8,128)(2,1)S(1)}) custom-call(s32[2]{0:T(128)S(1)} %pad_add_fusion.place_ref, bf16[192,3072]{1,0:T(8,128)(2,1)S(1)} %get-tuple-element.42.refs_0_, bf16[192,3072]{1,0:T(8,128)(2,1)} %collective-permute-done.1.refs_1_, bf16[192,3072]{1,0:T(8,128)(2,1)} %collective-permute-done.5.refs_2_, ...), custom_call_target="tpu_custom_call" | custom-call | flops 7247757312 | bytes 16515072 | tf_op jit(solution)/shard_map/term/pallas_call | solution.py:349
  139.5 7.5 %collective-permute-start.13 = (bf16[768,768]{1,0:T(8,128)(2,1)S(1)}, bf16[768,768]{1,0:T(8,128)(2,1)S(1)}, u32[]{:S(2)}, u32[]{:S(2)}) collective-permute-start(bf16[768,768]{1,0:T(8,128)(2,1)S(1)} %get-tuple-element.50), channel_id=1, source_target_pairs={{0,1},{1,0},{2,3},{3,2},{4,5},{5,4},{6,7},{7,6},{8,9},{9,8},{10,11... | collective-permute-start | bytes 3538952 | tf_op jit(solution)/shard_map/ppermute | solution.py:169
  152.2 3.6 %collective-permute-done.27 = bf16[240,256]{1,0:T(8,128)(2,1)S(1)} collective-permute-done((bf16[240,256]{1,0:T(8,128)(2,1)S(1)}, bf16[240,256]{1,0:T(8,128)(2,1)S(1)}, u32[]{:S(2)}, u32[]{:S(2)}) %collective-permute-start.27) | collective-permute-done | bytes 122912 | tf_op jit(solution)/shard_map/ppermute | solution.py:169
  155.9 6.4 %collective-permute-done.26 = bf16[240,256]{1,0:T(8,128)(2,1)S(1)} collective-permute-done((bf16[240,256]{1,0:T(8,128)(2,1)S(1)}, bf16[240,256]{1,0:T(8,128)(2,1)S(1)}, u32[]{:S(2)}, u32[]{:S(2)}) %collective-permute-start.26) | collective-permute-done | bytes 122912 | tf_op jit(solution)/shard_map/ppermute | solution.py:169
  164.7 4.4 %all-to-all-start.2 = ((bf16[4,4,240,256]{3,2,1,0:T(8,128)(2,1)}), bf16[4,4,240,256]{3,2,1,0:T(8,128)(2,1)}, u32[]{:S(2)}, u32[]{:S(2)}) async-start(bf16[4,4,240,256]{3,2,1,0:T(8,128)(2,1)} %broadcast_in_dim.2), calls=%async_computation.2 | async-start | bytes 3932160 | tf_op jit(solution)/shard_map/all_to_all | solution.py:431
  169.2 13.2 %term.3 = (bf16[768,256]{1,0:T(8,128)(2,1)S(1)}, bf16[768,256]{1,0:T(8,128)(2,1)}) custom-call(s32[2]{0:T(128)S(1)} %pad_add_fusion.place_ref, bf16[192,3072]{1,0:T(8,128)(2,1)S(1)} %get-tuple-element.42.refs_0_, bf16[192,3072]{1,0:T(8,128)(2,1)} %collective-permute-done.1.refs_1_, bf16[192,3072]{1,0:T(8,128)(2,1)} %collective-permute-done.5.refs_2_, ...), custom_call_target="tpu_custom_call" | custom-call | flops 2415919104 | bytes 8650752 | tf_op jit(solution)/shard_map/term/pallas_call | solution.py:349
  192.1 3.5 %collective-permute-start.14 = (bf16[192,768]{1,0:T(8,128)(2,1)S(1)}, bf16[192,768]{1,0:T(8,128)(2,1)S(1)}, u32[]{:S(2)}, u32[]{:S(2)}) collective-permute-start(bf16[192,768]{1,0:T(8,128)(2,1)S(1)} %get-tuple-element.69), channel_id=1, source_target_pairs={{0,0},{1,8},{2,2},{3,10},{4,4},{5,12},{6,6},{7,14},{8,16},{9,24},{... | collective-permute-start | bytes 884744 | tf_op jit(solution)/shard_map/ppermute | solution.py:169
  197.7 8.1 %collective-permute-done.17.refs_3_ = bf16[192,768]{1,0:T(8,128)(2,1)S(1)} collective-permute-done((bf16[192,768]{1,0:T(8,128)(2,1)S(1)}, bf16[192,768]{1,0:T(8,128)(2,1)S(1)}, u32[]{:S(2)}, u32[]{:S(2)}) %collective-permute-start.17) | collective-permute-done | bytes 294944 | tf_op jit(solution)/shard_map/ppermute | solution.py:169
  205.9 7.8 %collective-permute-start.22 = (bf16[192,256]{1,0:T(8,128)(2,1)S(1)}, bf16[192,256]{1,0:T(8,128)(2,1)S(1)}, u32[]{:S(2)}, u32[]{:S(2)}) collective-permute-start(bf16[192,256]{1,0:T(8,128)(2,1)S(1)} %get-tuple-element.82), channel_id=1, source_target_pairs={{0,8},{1,16},{2,10},{3,18},{4,12},{5,20},{6,14},{7,22},{8,24},{9,0... | collective-permute-start | bytes 294920 | tf_op jit(solution)/shard_map/ppermute | solution.py:169
  216.3 5.5 %collective-permute-done.14.refs_0_ = bf16[192,768]{1,0:T(8,128)(2,1)S(1)} collective-permute-done((bf16[192,768]{1,0:T(8,128)(2,1)S(1)}, bf16[192,768]{1,0:T(8,128)(2,1)S(1)}, u32[]{:S(2)}, u32[]{:S(2)}) %collective-permute-start.14) | collective-permute-done | bytes 294944 | tf_op jit(solution)/shard_map/ppermute | solution.py:169
  231.0 3.6 %copy.41 = f32[4,4,256,192]{2,1,0,3:T(4,128)} copy(f32[4,4,256,192]{2,3,0,1:T(8,128)S(1)} %convert_bitcast_fusion) | data formatting | bytes 6291456 | tf_op jit(solution)/shard_map/convert_element_type | solution.py:415
  234.7 5.3 %reshape.41 = f32[4096,192]{0,1:T(8,128)} reshape(f32[4,4,256,192]{2,1,0,3:T(4,128)} %copy.41) | data formatting | bytes 6291456 | tf_op jit(solution)/shard_map/convert_element_type | solution.py:415
  (123 shorter events, 71.1 us)
Async XLA Ops:
  5.7 36.5 %collective-permute-start.4 = (bf16[256,3072]{1,0:T(8,128)(2,1)}, bf16[256,3072]{1,0:T(8,128)(2,1)}, u32[]{:S(2)}, u32[]{:S(2)}) collective-permute-start(bf16[256,3072]{1,0:T(8,128)(2,1)} %pad_maximum_fusion.1.refs_7_), channel_id=1, source_target_pairs={{0,4},{1,5},{2,6},{3,7},{4,0},{5,1},{6,2},{7,3},{8,12},{9,13},{10,... | collective-permute-start | bytes 4718600 | tf_op jit(solution)/shard_map/ppermute | solution.py:169
  7.8 35.3 %collective-permute-start.3 = (bf16[256,3072]{1,0:T(8,128)(2,1)}, bf16[256,3072]{1,0:T(8,128)(2,1)}, u32[]{:S(2)}, u32[]{:S(2)}) collective-permute-start(bf16[256,3072]{1,0:T(8,128)(2,1)} %pad_maximum_fusion.1.refs_7_), channel_id=1, source_target_pairs={{0,2},{1,3},{2,0},{3,1},{4,6},{5,7},{6,4},{7,5},{8,10},{9,11},{10,... | collective-permute-start | bytes 4718600 | tf_op jit(solution)/shard_map/ppermute | solution.py:169
  19.3 28.4 %collective-permute-start.2 = (bf16[192,3072]{1,0:T(8,128)(2,1)S(1)}, bf16[192,3072]{1,0:T(8,128)(2,1)}, u32[]{:S(2)}, u32[]{:S(2)}) collective-permute-start(bf16[192,3072]{1,0:T(8,128)(2,1)S(1)} %get-tuple-element.42.refs_0_), channel_id=1, source_target_pairs={{8,0},{9,1},{10,2},{11,3},{12,4},{13,5},{14,6},{15,7},{16,8},{17,9... | collective-permute-start | bytes 3538952 | tf_op jit(solution)/shard_map/ppermute | solution.py:169
  20.7 27.7 %collective-permute-start.1 = (bf16[192,3072]{1,0:T(8,128)(2,1)S(1)}, bf16[192,3072]{1,0:T(8,128)(2,1)}, u32[]{:S(2)}, u32[]{:S(2)}) collective-permute-start(bf16[192,3072]{1,0:T(8,128)(2,1)S(1)} %get-tuple-element.42.refs_0_), channel_id=1, source_target_pairs={{0,8},{1,9},{2,10},{3,11},{4,12},{5,13},{6,14},{7,15},{8,16},{9,17... | collective-permute-start | bytes 3538952 | tf_op jit(solution)/shard_map/ppermute | solution.py:169
  26.5 18.1 %collective-permute-start = (f32[192,384]{1,0:T(8,128)S(1)}, f32[192,384]{1,0:T(8,128)S(1)}, u32[]{:S(2)}, u32[]{:S(2)}) collective-permute-start(f32[192,384]{1,0:T(8,128)S(1)} %pad_maximum_fusion.6), channel_id=1, source_target_pairs={{0,1},{1,0},{2,3},{3,2},{4,5},{5,4},{6,7},{7,6},{8,9},{9,8},{10,11... | collective-permute-start | bytes 884744 | tf_op jit(solution)/shard_map/ppermute | solution.py:169
  43.0 37.8 %collective-permute-start.8 = (bf16[256,3072]{1,0:T(8,128)(2,1)}, bf16[256,3072]{1,0:T(8,128)(2,1)}, u32[]{:S(2)}, u32[]{:S(2)}) collective-permute-start(bf16[256,3072]{1,0:T(8,128)(2,1)} %pad_maximum_fusion.2.refs_8_), channel_id=1, source_target_pairs={{0,4},{1,5},{2,6},{3,7},{4,0},{5,1},{6,2},{7,3},{8,12},{9,13},{10,... | collective-permute-start | bytes 4718600 | tf_op jit(solution)/shard_map/ppermute | solution.py:169
  43.3 37.4 %collective-permute-start.7 = (bf16[256,3072]{1,0:T(8,128)(2,1)}, bf16[256,3072]{1,0:T(8,128)(2,1)}, u32[]{:S(2)}, u32[]{:S(2)}) collective-permute-start(bf16[256,3072]{1,0:T(8,128)(2,1)} %pad_maximum_fusion.2.refs_8_), channel_id=1, source_target_pairs={{0,2},{1,3},{2,0},{3,1},{4,6},{5,7},{6,4},{7,5},{8,10},{9,11},{10,... | collective-permute-start | bytes 4718600 | tf_op jit(solution)/shard_map/ppermute | solution.py:169
  48.5 18.2 %collective-permute-start.5 = (bf16[192,3072]{1,0:T(8,128)(2,1)}, bf16[192,3072]{1,0:T(8,128)(2,1)}, u32[]{:S(2)}, u32[]{:S(2)}) collective-permute-start(bf16[192,3072]{1,0:T(8,128)(2,1)} %collective-permute-done.1.refs_1_), channel_id=1, source_target_pairs={{8,16},{9,17},{10,18},{11,19},{12,20},{13,21},{14,22},{15,23},{16,... | collective-permute-start | bytes 3538952 | tf_op jit(solution)/shard_map/ppermute | solution.py:169
  50.1 30.6 %collective-permute-start.6 = (bf16[192,3072]{1,0:T(8,128)(2,1)}, bf16[192,3072]{1,0:T(8,128)(2,1)}, u32[]{:S(2)}, u32[]{:S(2)}) collective-permute-start(bf16[192,3072]{1,0:T(8,128)(2,1)} %collective-permute-done.2.refs_4_), channel_id=1, source_target_pairs={{8,0},{9,1},{10,2},{11,3},{12,4},{13,5},{14,6},{15,7},{16,8},{17,9... | collective-permute-start | bytes 3538952 | tf_op jit(solution)/shard_map/ppermute | solution.py:169
  62.2 36.6 %all-to-all-start = ((bf16[4,4,240,256]{3,1,2,0:T(4,128)(2,1)}), bf16[4,4,240,256]{3,1,2,0:T(4,128)(2,1)}, u32[]{:S(2)}, u32[]{:S(2)}) async-start(bf16[4,4,240,256]{3,1,2,0:T(4,128)(2,1)} %pad_maximum_fusion), calls=%async_computation | async-start | bytes 3932160 | tf_op jit(solution)/shard_map/all_to_all | solution.py:420
  80.8 37.8 %collective-permute-start.9 = (bf16[192,3072]{1,0:T(8,128)(2,1)}, bf16[192,3072]{1,0:T(8,128)(2,1)S(1)}, u32[]{:S(2)}, u32[]{:S(2)}) collective-permute-start(bf16[192,3072]{1,0:T(8,128)(2,1)} %collective-permute-done.5.refs_2_), channel_id=1, source_target_pairs={{16,24},{17,25},{18,26},{19,27},{20,28},{21,29},{22,30},{23,31}} | collective-permute-start | bytes 3538952 | tf_op jit(solution)/shard_map/ppermute | solution.py:169
  81.5 37.1 %collective-permute-start.10 = (bf16[192,3072]{1,0:T(8,128)(2,1)}, bf16[192,3072]{1,0:T(8,128)(2,1)}, u32[]{:S(2)}, u32[]{:S(2)}) collective-permute-start(bf16[192,3072]{1,0:T(8,128)(2,1)} %collective-permute-done.6.refs_5_), channel_id=1, source_target_pairs={{8,0},{9,1},{10,2},{11,3},{12,4},{13,5},{14,6},{15,7}} | collective-permute-start | bytes 3538952 | tf_op jit(solution)/shard_map/ppermute | solution.py:169
  85.4 33.1 %collective-permute-start.11 = (bf16[128,3072]{1,0:T(8,128)(2,1)}, bf16[128,3072]{1,0:T(8,128)(2,1)S(1)}, u32[]{:S(2)}, u32[]{:S(2)}) collective-permute-start(bf16[128,3072]{1,0:T(8,128)(2,1)} %get-tuple-element.65), channel_id=1, source_target_pairs={{0,4},{1,5},{2,6},{3,7},{4,0},{5,1},{6,2},{7,3},{8,12},{9,13},{10,... | collective-permute-start | bytes 2359304 | tf_op jit(solution)/shard_map/ppermute | solution.py:169
  88.3 30.3 %collective-permute-start.12 = (bf16[128,3072]{1,0:T(8,128)(2,1)}, bf16[128,3072]{1,0:T(8,128)(2,1)}, u32[]{:S(2)}, u32[]{:S(2)}) collective-permute-start(bf16[128,3072]{1,0:T(8,128)(2,1)} %get-tuple-element.63), channel_id=1, source_target_pairs={{0,2},{1,3},{2,0},{3,1},{4,6},{5,7},{6,4},{7,5},{8,10},{9,11},{10,... | collective-permute-start | bytes 2359304 | tf_op jit(solution)/shard_map/ppermute | solution.py:169
  147.0 22.2 %collective-permute-start.18 = (bf16[128,3072]{1,0:T(8,128)(2,1)}, bf16[128,3072]{1,0:T(8,128)(2,1)}, u32[]{:S(2)}, u32[]{:S(2)}) collective-permute-start(bf16[128,3072]{1,0:T(8,128)(2,1)} %get-tuple-element.51), channel_id=1, source_target_pairs={{0,4},{1,5},{2,6},{3,7},{4,0},{5,1},{6,2},{7,3},{8,12},{9,13},{10,... | collective-permute-start | bytes 2359304 | tf_op jit(solution)/shard_map/ppermute | solution.py:169
  148.2 20.9 %collective-permute-start.19 = (bf16[128,3072]{1,0:T(8,128)(2,1)}, bf16[128,3072]{1,0:T(8,128)(2,1)}, u32[]{:S(2)}, u32[]{:S(2)}) collective-permute-start(bf16[128,3072]{1,0:T(8,128)(2,1)} %get-tuple-element.52), channel_id=1, source_target_pairs={{0,2},{1,3},{2,0},{3,1},{4,6},{5,7},{6,4},{7,5},{8,10},{9,11},{10,... | collective-permute-start | bytes 2359304 | tf_op jit(solution)/shard_map/ppermute | solution.py:169
  164.7 61.6 %all-to-all-start.2 = ((bf16[4,4,240,256]{3,2,1,0:T(8,128)(2,1)}), bf16[4,4,240,256]{3,2,1,0:T(8,128)(2,1)}, u32[]{:S(2)}, u32[]{:S(2)}) async-start(bf16[4,4,240,256]{3,2,1,0:T(8,128)(2,1)} %broadcast_in_dim.2), calls=%async_computation.2 | async-start | bytes 3932160 | tf_op jit(solution)/shard_map/all_to_all | solution.py:431
  185.3 20.5 %collective-permute-start.17 = (bf16[192,768]{1,0:T(8,128)(2,1)S(1)}, bf16[192,768]{1,0:T(8,128)(2,1)S(1)}, u32[]{:S(2)}, u32[]{:S(2)}) collective-permute-start(bf16[192,768]{1,0:T(8,128)(2,1)S(1)} %get-tuple-element.66), channel_id=1, source_target_pairs={{0,24},{1,0},{2,26},{3,2},{4,28},{5,4},{6,30},{7,6},{8,8},{9,16},{... | collective-permute-start | bytes 884744 | tf_op jit(solution)/shard_map/ppermute | solution.py:169
  187.7 18.2 %collective-permute-start.16 = (bf16[192,768]{1,0:T(8,128)(2,1)S(1)}, bf16[192,768]{1,0:T(8,128)(2,1)S(1)}, u32[]{:S(2)}, u32[]{:S(2)}) collective-permute-start(bf16[192,768]{1,0:T(8,128)(2,1)S(1)} %get-tuple-element.67), channel_id=1, source_target_pairs={{0,16},{1,24},{2,18},{3,26},{4,20},{5,28},{6,22},{7,30},{8,0},{9,8... | collective-permute-start | bytes 884744 | tf_op jit(solution)/shard_map/ppermute | solution.py:169
  189.5 24.2 %collective-permute-start.15 = (bf16[192,768]{1,0:T(8,128)(2,1)S(1)}, bf16[192,768]{1,0:T(8,128)(2,1)S(1)}, u32[]{:S(2)}, u32[]{:S(2)}) collective-permute-start(bf16[192,768]{1,0:T(8,128)(2,1)S(1)} %get-tuple-element.68), channel_id=1, source_target_pairs={{0,8},{1,16},{2,10},{3,18},{4,12},{5,20},{6,14},{7,22},{8,24},{9,0... | collective-permute-start | bytes 884744 | tf_op jit(solution)/shard_map/ppermute | solution.py:169
  192.1 29.7 %collective-permute-start.14 = (bf16[192,768]{1,0:T(8,128)(2,1)S(1)}, bf16[192,768]{1,0:T(8,128)(2,1)S(1)}, u32[]{:S(2)}, u32[]{:S(2)}) collective-permute-start(bf16[192,768]{1,0:T(8,128)(2,1)S(1)} %get-tuple-element.69), channel_id=1, source_target_pairs={{0,0},{1,8},{2,2},{3,10},{4,4},{5,12},{6,6},{7,14},{8,16},{9,24},{... | collective-permute-start | bytes 884744 | tf_op jit(solution)/shard_map/ppermute | solution.py:169
  195.8 26.0 %collective-permute-start.24 = (bf16[192,256]{1,0:T(8,128)(2,1)S(1)}, bf16[192,256]{1,0:T(8,128)(2,1)S(1)}, u32[]{:S(2)}, u32[]{:S(2)}) collective-permute-start(bf16[192,256]{1,0:T(8,128)(2,1)S(1)} %get-tuple-element.80), channel_id=1, source_target_pairs={{0,24},{1,0},{2,26},{3,2},{4,28},{5,4},{6,30},{7,6},{8,8},{9,16},{... | collective-permute-start | bytes 294920 | tf_op jit(solution)/shard_map/ppermute | solution.py:169
  205.9 15.9 %collective-permute-start.23 = (bf16[192,256]{1,0:T(8,128)(2,1)S(1)}, bf16[192,256]{1,0:T(8,128)(2,1)S(1)}, u32[]{:S(2)}, u32[]{:S(2)}) collective-permute-start(bf16[192,256]{1,0:T(8,128)(2,1)S(1)} %get-tuple-element.81), channel_id=1, source_target_pairs={{0,16},{1,24},{2,18},{3,26},{4,20},{5,28},{6,22},{7,30},{8,0},{9,8... | collective-permute-start | bytes 294920 | tf_op jit(solution)/shard_map/ppermute | solution.py:169
  205.9 15.9 %collective-permute-start.22 = (bf16[192,256]{1,0:T(8,128)(2,1)S(1)}, bf16[192,256]{1,0:T(8,128)(2,1)S(1)}, u32[]{:S(2)}, u32[]{:S(2)}) collective-permute-start(bf16[192,256]{1,0:T(8,128)(2,1)S(1)} %get-tuple-element.82), channel_id=1, source_target_pairs={{0,8},{1,16},{2,10},{3,18},{4,12},{5,20},{6,14},{7,22},{8,24},{9,0... | collective-permute-start | bytes 294920 | tf_op jit(solution)/shard_map/ppermute | solution.py:169
  (25 other events, 244.6 us)

commit v5 on v4

--- a/solution.py
+++ b/solution.py
@@ -179,10 +179,6 @@
 
 def swap_core(value):
     return send(value, lambda hi, lo, core: (hi, lo, 1 - core))
-
-
-def turn_hi(value, step):
-    return send(value, lambda hi, lo, core: ((hi + step) % 4, lo, core))
 
 
 def move_hi(value, step, first, last):
@@ -299,65 +295,56 @@
 
 
 def term_kernel(place_ref, *refs):
-    blocks, weights = refs[:7], refs[7:-6]
-    kept_ref, sent_ref, left, right, arrived, landed = refs[-6:]
+    blocks, weights, (sent_ref, kept_ref, left, arrived) = refs[:7], refs[7:-4], refs[-4:]
     tokens = blocks[0].shape[0]
-    core, hi = place_ref[0], place_ref[1]
-    count = len(weights) // 2
-    width = weights[0].shape[0]
-
-    for n in range(4):
-        there = left.at[pl.ds(n * tokens, tokens), :]
-        for step, block in zip((0, 1, 2, 3, -1, -2, -3), blocks):
-
-            @pl.when(hi == n + step)
-            def _(block=block, there=there, n=n):
-                pltpu.make_async_copy(block, there, arrived.at[n]).start()
-
-    for turn in range(2):
-        for n in range(count):
-            slot = turn * count + n
-            for half in range(2):
-
-                @pl.when(core == (half + 1 - turn) % 2)
-                def _(n=n, half=half, slot=slot):
-                    pltpu.make_async_copy(
-                        weights[2 * n + half], right.at[slot], landed.at[slot]
-                    ).start()
-
-    for n in range(4):
-        there = left.at[pl.ds(n * tokens, tokens), :]
-        pltpu.make_async_copy(blocks[0], there, arrived.at[n]).wait()
+    hi = place_ref[1]
+
+    @pl.when(pl.program_id(0) == 0)
+    def _():
+        for n in range(4):
+            there = left.at[pl.ds(n * tokens, tokens), :]
+            for step, block in zip((0, 1, 2, 3, -1, -2, -3), blocks):
+
+                @pl.when(hi == n + step)
+                def _(block=block, there=there, n=n):
+                    pltpu.make_async_copy(block, there, arrived.at[n]).start()
+
+        for n in range(4):
+            there = left.at[pl.ds(n * tokens, tokens), :]
+            pltpu.make_async_copy(blocks[0], there, arrived.at[n]).wait()
+
     for turn, out_ref in enumerate((sent_ref, kept_ref)):
-        for n in range(count):
-            slot = turn * count + n
-            pltpu.make_async_copy(weights[2 * n], right.at[slot], landed.at[slot]).wait()
-            out_ref[:, n * width : (n + 1) * width] = lax.dot_general(
-                left[...],
-                right[slot],
-                (((1,), (1,)), ((), ())),
-                preferred_element_type=jnp.float32,
-            ).astype(jnp.bfloat16)
+
+        @pl.when(pl.program_id(0) == turn)
+        def _(out_ref=out_ref):
+            width = 2 * weights[0].shape[0]
+            for n in range(len(weights) // 2):
+                right = jnp.concatenate([weights[2 * n][...], weights[2 * n + 1][...]], axis=0)
+                out_ref[:, n * width : (n + 1) * width] = lax.dot_general(
+                    left[...], right, (((1,), (1,)), ((), ())), preferred_element_type=jnp.float32
+                ).astype(jnp.bfloat16)
 
 
 def term_halves(blocks, weights, core, hi):
     tokens, depth = blocks[0].shape
-    rows = weights[0][0].shape[0]
+    rows = weights[0].shape[0] // 2
     count = len(weights)
-    flat = [w for pair in weights for w in pair]
     out = jax.ShapeDtypeStruct((4 * tokens, count * rows), jnp.bfloat16)
     return pl.pallas_call(
         term_kernel,
         out_shape=(out, out),
-        in_specs=[pl.BlockSpec(memory_space=pltpu.SMEM)]
-        + [pl.BlockSpec(memory_space=pl.ANY)] * (7 + len(flat)),
-        out_specs=(pl.BlockSpec(memory_space=pltpu.VMEM),) * 2,
-        scratch_shapes=[
-            pltpu.VMEM((4 * tokens, depth), jnp.bfloat16),
-            pltpu.VMEM((2 * count, rows, depth), jnp.bfloat16),
-            pltpu.SemaphoreType.DMA((4,)),
-            pltpu.SemaphoreType.DMA((2 * count,)),
-        ],
+        grid_spec=pltpu.PrefetchScalarGridSpec(
+            num_scalar_prefetch=1,
+            grid=(2,),
+            in_specs=[pl.BlockSpec(memory_space=pl.ANY)] * 7
+            + [pl.BlockSpec((rows, depth), lambda i, place: (lax.rem(place[0] + 1 - i, 2), 0))]
+            * count,
+            out_specs=(pl.BlockSpec(out.shape, lambda i, place: (0, 0)),) * 2,
+            scratch_shapes=[
+                pltpu.VMEM((4 * tokens, depth), jnp.bfloat16),
+                pltpu.SemaphoreType.DMA((4,)),
+            ],
+        ),
         compiler_params=pltpu.CompilerParams(vmem_limit_bytes=40 << 20),
         cost_estimate=pl.CostEstimate(
             flops=16 * tokens * depth * rows * count,
@@ -365,12 +352,12 @@
             transcendentals=0,
         ),
         name="term",
-    )(jnp.stack([core, hi]), *blocks, *flat)
+    )(jnp.stack([core, hi]), *blocks, *weights)
 
 
 def finish_kernel(spot_ref, added_ref, *refs):
     pieces, out_ref = refs[:-1], refs[-1]
-    width = pieces[-1].shape[1]
+    width = sum(piece.shape[1] for piece in pieces) // spot_ref.shape[0]
     place = 0
     for piece in pieces:
         for start in range(0, piece.shape[1], width):
@@ -421,12 +408,6 @@
     ).astype(jnp.bfloat16)
 
 
-def gather_line(piece):
-    hi = lax.axis_index("hi")
-    turned = jnp.stack([piece] + [turn_hi(piece, step) for step in range(1, 4)])
-    return jnp.stack([pick(turned, (hi - z) % 4, 0) for z in range(4)])
-
-
 def gather(value, axis):
     return lax.all_to_all(jnp.broadcast_to(value[None], (4, *value.shape)), axis, 0, 0)
 
@@ -436,8 +417,8 @@
     for step in range(1, 4):
         right.append(move_hi(right[-1], 1, step - 1, 2))
         left.append(move_hi(left[-1], -1, 1, 4 - step))
-        if step < 3:
-            right[step], left[step] = after((right[step], left[step]), first[step - 1])
+        if step == 1:
+            right[1], left[1] = after((right[1], left[1]), first)
     return right[1:], left[1:]
 
 
@@ -480,13 +461,10 @@
         query_gradient = own[:, :q_width]
         key_gradient = own[:, q_width : q_width + k_width]
         value_gradient = own[:, q_width + k_width :]
-        right, left = chain_hi(own, ((x_a, y_a), (x_b, y_b)))
+        right, left = chain_hi(own, (x_a, y_a))
         blocks = (own, *right, *left)
-        across_a, across_b = after((x_a, y_b), (right[1], left[1]))
-        quarter = cut // 2
-        across = [(swap_lo(across_a[:quarter], 2), swap_lo(across_b[:quarter], 1))]
-        rest_a, rest_b = after((across_a[quarter:], across_b[quarter:]), across[0])
-        across.append((swap_lo(rest_a, 2), swap_lo(rest_b, 1)))
+        from_a, from_b = after((x_a, y_b), (x_b, right[1], left[1]))
+        weights = (own_a, own_b, x_a, x_b, y_a, y_b, swap_lo(from_a, 2), swap_lo(from_b, 1))
 
         middle_local = jnp.concatenate(
             [
@@ -496,6 +474,7 @@
             axis=1,
         )
         middle = (middle_local + swap_core(middle_local)).astype(jnp.bfloat16)
+        middle = after(middle, (x_a, y_a))
         rank = adapter_down_maps.shape[1]
         adapter_middle, middle_gradient = middle[:, :rank], middle[:, rank:]
         down_turned = lax.dot_general(
@@ -504,7 +483,7 @@
         ups = up_gradients(adapter_middle, query_gradient, key_gradient, value_gradient)
         up_local = jnp.concatenate(ups, axis=1)
         column = scatter_sum(dp_pieces(down_turned, up_local), "lo")
-        piece = scatter_sum(column, "hi")
+        piece = scatter_sum(after(column, (right[1], left[1])), "hi")
         tokens = own.shape[0]
         source = (hi % 2) * 2 + core
 
@@ -512,20 +491,14 @@
             return lambda hi, lo, core: (((hi % 2) * 2 + core + step) % 4, lo, hi // 2)
 
         added = rows_product(middle_gradient, adapter_down_maps)
-        received = []
-        for part in range(2):
-            if part:
-                weights = after(across, summed)
-            else:
-                weights = ((own_a, own_b), (x_a, x_b), (y_a, y_b))
-            kept, sent = term_halves(after(blocks, (piece, across[0])), weights, core, hi)
-            summed = kept.astype(jnp.float32) + swap_core(sent).astype(jnp.float32)
-            summed = summed.astype(jnp.bfloat16).reshape(4, tokens, -1)
-            if not part:
-                first_line = after(piece, summed)
-            for step in range(4):
-                received.append(send(pick(summed, (source + step) % 4, 0), owner(step)))
-        every = gather(gather_line(first_line), "lo")
+        sent, kept = term_halves(blocks, weights, core, hi)
+        line = after(gather(after(piece, (right[2], left[2])), "hi"), weights[-2:])
+        summed = kept.astype(jnp.float32) + swap_core(sent).astype(jnp.float32)
+        summed = summed.astype(jnp.bfloat16).reshape(4, tokens, -1)
+        received = [
+            send(pick(summed, (source + step) % 4, 0), owner(step)) for step in range(4)
+        ]
+        every = after(gather(line, "lo"), received[0])
         down_total, up_total = dp_results(every, rank, up_local.shape)
         query_total = up_total[:, :q_width]
         key_value_total = jnp.stack(
@@ -533,10 +506,10 @@
         )
 
         spots = [
-            (((hi - step) % 4) // 2) * 8 + (lo ^ block) * 2 + (hi - step) % 2
-            for blocks in ((0, 1, 2), (3,))
+            (((hi - step) % 4) // 2) * 16 + (lo ^ block) * 4 + part * 2 + (hi - step) % 2
             for step in range(4)
-            for block in blocks
+            for block in range(4)
+            for part in range(2)
         ]
         normed_input_grad = finish(received, jnp.stack(spots).astype(jnp.int32), added)
         return (normed_input_grad, down_total, query_total, key_value_total)

time: 242 us -> 247 us (1.021)
  the two profiles are of different devices: /device:TPU:1 before, /device:TPU:26 now
where the time goes in v5:
time: 247 us; the launch traced here: 245 us
  waiting for transfers between devices  101 us (41%)
  starting transfers between devices  42.7 us (17%)
  local copies, waits for them, and re-layouts  38.3 us (16%)
  Pallas kernels  26.4 us (11%)
  blocking collectives  17 us (7%)
  other arithmetic  12.9 us (5%)
  matrix products  5.42 us (2%)
    ppermute x18, waiting for transfers between devices, send(): return lax.ppermute(value, AXES, pairs)  48.6 us
    all_to_all x2, waiting for transfers between devices, scatter_sum(): lax.all_to_all(value, axis, 0, 0)  43.2 us
    ppermute x18, starting transfers between devices, send(): return lax.ppermute(value, AXES, pairs)  25.2 us
    pallas_call x1, Pallas kernels, term_halves(): pl.pallas_call(term_kernel, out_shape=(out, out), grid_spec=pltpu.Prefetc...  17.1 us
    all_to_all x1, blocking collectives, gather(): lax.all_to_all(jnp.broadcast_to(value[None], (4, *value.shape)), axis, 0, 0)  17 us
    all_to_all x2, starting transfers between devices, scatter_sum(): lax.all_to_all(value, axis, 0, 0)  12.5 us
    unnamed x45, local copies, waits for them, and re-layouts  11 us
    all_to_all x1, waiting for transfers between devices, gather(): lax.all_to_all(jnp.broadcast_to(value[None], (4, *value.shape)), axis, 0, 0)  9.47 us
  transfers between devices with their start and end apart: 21, of which 8 were waited for; matrix products, arithmetic and copies ran while one was open for 17% of the time, Pallas kernels for 10%

profile of v5, /device:TPU:26, one launch (start us, length us, event | category | flops | bytes accessed | tf_op | source)
XLA Modules:
  0.0 245.2 jit_solution(3733495842725772404)
XLA Ops:
  0.7 2.9 %fusion.12 = (bf16[256,2048]{1,0:T(8,128)(2,1)}, bf16[256,2048]{1,0:T(8,128)(2,1)S(1)}) fusion(bf16[512,2048]{1,0:T(8,128)(2,1)} %param.18), kind=kLoop, calls=%fused_computation.34 | loop fusion | bytes 4194304 | tf_op jit(solution)/shard_map/slice | solution.py:444
  11.8 7.0 %attention.1 = (bf16[192,3072]{1,0:T(8,128)(2,1)S(1)}, f32[192,192]{1,0:T(8,128)S(1)}) custom-call(bf16[192,2048]{1,0:T(8,128)(2,1)S(1)} %copy-done.8, bf16[192,512]{1,0:T(8,128)(2,1)S(1)} %copy-done.11, bf16[192,512]{1,0:T(8,128)(2,1)S(1)} %copy-done.12, bf16[192,2048]{1,0:T(8,128)(2,1)S(1)} %copy-done.9, s32[192,1]{1,0:T(8,128)S(1)} %copy.32.row_ids, ...), custom_call_target="tpu_custom_call" | custom-call | flops 754974720 | bytes 2359296 | tf_op jit(solution)/shard_map/attention/pallas_call | solution.py:257
  18.8 3.7 %collective-permute-start.4 = (bf16[192,3072]{1,0:T(8,128)(2,1)S(1)}, bf16[192,3072]{1,0:T(8,128)(2,1)}, u32[]{:S(2)}, u32[]{:S(2)}) collective-permute-start(bf16[192,3072]{1,0:T(8,128)(2,1)S(1)} %get-tuple-element.22.refs_0_), channel_id=1, source_target_pairs={{8,0},{9,1},{10,2},{11,3},{12,4},{13,5},{14,6},{15,7},{16,8},{17,9... | collective-permute-start | bytes 3538952 | tf_op jit(solution)/shard_map/ppermute | solution.py:169
  25.9 14.9 %collective-permute-done.2.refs_11_ = bf16[256,3072]{1,0:T(8,128)(2,1)} collective-permute-done((bf16[256,3072]{1,0:T(8,128)(2,1)S(1)}, bf16[256,3072]{1,0:T(8,128)(2,1)}, u32[]{:S(2)}, u32[]{:S(2)}) %collective-permute-start.2) | collective-permute-done | bytes 1572896 | tf_op jit(solution)/shard_map/ppermute | solution.py:169
  43.2 2.9 %collective-permute-done.4.refs_4_ = bf16[192,3072]{1,0:T(8,128)(2,1)} collective-permute-done((bf16[192,3072]{1,0:T(8,128)(2,1)S(1)}, bf16[192,3072]{1,0:T(8,128)(2,1)}, u32[]{:S(2)}, u32[]{:S(2)}) %collective-permute-start.4) | collective-permute-done | bytes 1179680 | tf_op jit(solution)/shard_map/ppermute | solution.py:169
  46.1 5.3 %collective-permute-done.3.refs_1_ = bf16[192,3072]{1,0:T(8,128)(2,1)} collective-permute-done((bf16[192,3072]{1,0:T(8,128)(2,1)S(1)}, bf16[192,3072]{1,0:T(8,128)(2,1)}, u32[]{:S(2)}, u32[]{:S(2)}) %collective-permute-start.3) | collective-permute-done | bytes 1179680 | tf_op jit(solution)/shard_map/ppermute | solution.py:169
  61.9 2.9 %reshape.35 = bf16[192,4,4,256]{3,2,1,0:T(4,128)(2,1)S(1)} reshape(bf16[192,4096]{1,0:T(8,128)(2,1)} %convolution_convert_fusion) | data formatting | bytes 3145728 | tf_op jit(solution)/shard_map/reshape | solution.py:391
  65.4 14.1 %collective-permute-done.5.refs_2_ = bf16[192,3072]{1,0:T(8,128)(2,1)} collective-permute-done((bf16[192,3072]{1,0:T(8,128)(2,1)}, bf16[192,3072]{1,0:T(8,128)(2,1)}, u32[]{:S(2)}, u32[]{:S(2)}) %collective-permute-start.5) | collective-permute-done | bytes 1179680 | tf_op jit(solution)/shard_map/ppermute | solution.py:169
  81.6 2.5 %pad_maximum_fusion = bf16[4,4,240,256]{3,1,2,0:T(4,128)(2,1)} fusion(bf16[4,4,48,256]{3,1,2,0:T(4,128)(2,1)S(1)} %copy-done.17, bf16[4,4,192,256]{3,1,2,0:T(4,128)(2,1)S(1)} %bitcast.69), kind=kLoop, calls=%fused_computation.5 | loop fusion | flops 983040 | bytes 3932160 | tf_op jit(solution)/shard_map/concatenate | solution.py:389
  84.2 5.2 %all-to-all-start = ((bf16[4,4,240,256]{3,1,2,0:T(4,128)(2,1)}), bf16[4,4,240,256]{3,1,2,0:T(4,128)(2,1)}, u32[]{:S(2)}, u32[]{:S(2)}) async-start(bf16[4,4,240,256]{3,1,2,0:T(4,128)(2,1)} %pad_maximum_fusion), calls=%async_computation | async-start | bytes 3932160 | tf_op jit(solution)/shard_map/all_to_all | solution.py:407
  92.4 43.2 %all-to-all-done = bf16[4,4,240,256]{3,1,2,0:T(4,128)(2,1)} async-done(((bf16[4,4,240,256]{3,1,2,0:T(4,128)(2,1)}), bf16[4,4,240,256]{3,1,2,0:T(4,128)(2,1)}, u32[]{:S(2)}, u32[]{:S(2)}) %all-to-all-start) | async-done | bytes 1966112 | tf_op jit(solution)/shard_map/all_to_all | solution.py:407
  135.6 3.5 %reduce_sum.24 = bf16[4,240,256]{2,0,1:T(4,128)(2,1)} reduce(bf16[4,4,240,256]{3,1,2,0:T(4,128)(2,1)} %all-to-all-done, bf16[]{:T(256)} %constant.301.clone.1), dimensions={0}, to_apply=%region_0.0 | reduce | flops 737280 | bytes 2457602 | tf_op jit(solution)/shard_map/reduce_sum | solution.py:406
  141.0 7.3 %all-to-all-start.1 = ((bf16[4,240,256]{2,1,0:T(8,128)(2,1)}), bf16[4,240,256]{2,1,0:T(8,128)(2,1)}, u32[]{:S(2)}, u32[]{:S(2)}) async-start(bf16[4,240,256]{2,1,0:T(8,128)(2,1)} %copy.37), calls=%async_computation.1 | async-start | bytes 983040 | tf_op jit(solution)/shard_map/all_to_all | solution.py:407
  151.9 17.1 %term.1 = (bf16[768,1024]{1,0:T(8,128)(2,1)}, bf16[768,1024]{1,0:T(8,128)(2,1)S(1)}) custom-call(s32[2]{0:T(128)S(1)} %pad_add_fusion.place_ref, bf16[192,3072]{1,0:T(8,128)(2,1)S(1)} %copy-done.4, bf16[192,3072]{1,0:T(8,128)(2,1)} %collective-permute-done.3.refs_1_, bf16[192,3072]{1,0:T(8,128)(2,1)} %collective-permute-done.5.refs_2_, ...), custom_call_target="tpu_custom_call" | custom-call | flops 9663676416 | bytes 20447232 | tf_op jit(solution)/shard_map/term/pallas_call | solution.py:333
  170.2 17.0 %all_to_all.20 = bf16[4,240,256]{2,1,0:T(8,128)(2,1)S(1)} all-to-all(bf16[4,240,256]{2,1,0:T(8,128)(2,1)S(1)} %broadcast_in_dim.4), channel_id=1, replica_groups=mesh['hi'=4,'lo'=4,'tensor'=2] {'hi'}, dimensions={0} | all-to-all | bytes 983040 | tf_op jit(solution)/shard_map/all_to_all | solution.py:412
  188.6 5.0 %all-to-all-start.3 = ((bf16[4,4,240,256]{3,2,1,0:T(8,128)(2,1)}), bf16[4,4,240,256]{3,2,1,0:T(8,128)(2,1)}, u32[]{:S(2)}, u32[]{:S(2)}) async-start(bf16[4,4,240,256]{3,2,1,0:T(8,128)(2,1)} %broadcast_in_dim.5), calls=%async_computation.3 | async-start | bytes 3932160 | tf_op jit(solution)/shard_map/all_to_all | solution.py:412
  197.7 2.3 fusion.7.added_ref
  200.0 4.5 %collective-permute-start.17 = (bf16[192,1024]{1,0:T(8,128)(2,1)}, bf16[192,1024]{1,0:T(8,128)(2,1)S(1)}, u32[]{:S(2)}, u32[]{:S(2)}) collective-permute-start(bf16[192,1024]{1,0:T(8,128)(2,1)} %get-tuple-element.36), channel_id=1, source_target_pairs={{0,24},{1,0},{2,26},{3,2},{4,28},{5,4},{6,30},{7,6},{8,8},{9,16},{... | collective-permute-start | bytes 1179656 | tf_op jit(solution)/shard_map/ppermute | solution.py:169
  204.6 2.4 collective-permute-start.15
  207.0 9.5 %all-to-all-done.3 = bf16[4,4,240,256]{3,2,1,0:T(8,128)(2,1)} async-done(((bf16[4,4,240,256]{3,2,1,0:T(8,128)(2,1)}), bf16[4,4,240,256]{3,2,1,0:T(8,128)(2,1)}, u32[]{:S(2)}, u32[]{:S(2)}) %all-to-all-start.3) | async-done | bytes 1966112 | tf_op jit(solution)/shard_map/all_to_all | solution.py:412
  216.5 10.2 %collective-permute-done.14.refs_0_ = bf16[192,1024]{1,0:T(8,128)(2,1)S(1)} collective-permute-done((bf16[192,1024]{1,0:T(8,128)(2,1)}, bf16[192,1024]{1,0:T(8,128)(2,1)S(1)}, u32[]{:S(2)}, u32[]{:S(2)}) %collective-permute-start.14) | collective-permute-done | bytes 393248 | tf_op jit(solution)/shard_map/ppermute | solution.py:169
  231.3 3.7 %copy.38 = f32[4,4,256,192]{2,1,0,3:T(4,128)} copy(f32[4,4,256,192]{2,3,0,1:T(8,128)S(1)} %convert_bitcast_fusion) | data formatting | bytes 6291456 | tf_op jit(solution)/shard_map/convert_element_type | solution.py:402
  235.0 5.2 %reshape.38 = f32[4096,192]{0,1:T(8,128)} reshape(f32[4,4,256,192]{2,1,0,3:T(4,128)} %copy.38) | data formatting | bytes 6291456 | tf_op jit(solution)/shard_map/convert_element_type | solution.py:402
  242.9 2.3 finish.1
  (105 shorter events, 49.5 us)
Async XLA Ops:
  0.6 23.2 %copy-start = (bf16[192,4096]{1,0:T(8,128)(2,1)S(1)}, bf16[192,4096]{1,0:T(8,128)(2,1)}, u32[]{:S(2)}) copy-start(bf16[192,4096]{1,0:T(8,128)(2,1)} %param.12) | copy-start | bytes 4718596
  4.5 36.3 %collective-permute-start.2 = (bf16[256,3072]{1,0:T(8,128)(2,1)S(1)}, bf16[256,3072]{1,0:T(8,128)(2,1)}, u32[]{:S(2)}, u32[]{:S(2)}) collective-permute-start(bf16[256,3072]{1,0:T(8,128)(2,1)S(1)} %pad_maximum_fusion.1.refs_7_), channel_id=1, source_target_pairs={{0,4},{1,5},{2,6},{3,7},{4,0},{5,1},{6,2},{7,3},{8,12},{9,13},{10,... | collective-permute-start | bytes 4718600 | tf_op jit(solution)/shard_map/ppermute | solution.py:169
  6.1 36.0 %collective-permute-start.1 = (bf16[256,3072]{1,0:T(8,128)(2,1)S(1)}, bf16[256,3072]{1,0:T(8,128)(2,1)}, u32[]{:S(2)}, u32[]{:S(2)}) collective-permute-start(bf16[256,3072]{1,0:T(8,128)(2,1)S(1)} %pad_maximum_fusion.1.refs_7_), channel_id=1, source_target_pairs={{0,2},{1,3},{2,0},{3,1},{4,6},{5,7},{6,4},{7,5},{8,10},{9,11},{10,... | collective-permute-start | bytes 4718600 | tf_op jit(solution)/shard_map/ppermute | solution.py:169
  18.8 36.0 %copy-start.3 = (bf16[192,3072]{1,0:T(8,128)(2,1)}, bf16[192,3072]{1,0:T(8,128)(2,1)S(1)}, u32[]{:S(2)}) copy-start(bf16[192,3072]{1,0:T(8,128)(2,1)S(1)} %get-tuple-element.22.refs_0_) | copy-start | bytes 3538948
  18.8 27.3 %collective-permute-start.4 = (bf16[192,3072]{1,0:T(8,128)(2,1)S(1)}, bf16[192,3072]{1,0:T(8,128)(2,1)}, u32[]{:S(2)}, u32[]{:S(2)}) collective-permute-start(bf16[192,3072]{1,0:T(8,128)(2,1)S(1)} %get-tuple-element.22.refs_0_), channel_id=1, source_target_pairs={{8,0},{9,1},{10,2},{11,3},{12,4},{13,5},{14,6},{15,7},{16,8},{17,9... | collective-permute-start | bytes 3538952 | tf_op jit(solution)/shard_map/ppermute | solution.py:169
  22.5 28.9 %collective-permute-start.3 = (bf16[192,3072]{1,0:T(8,128)(2,1)S(1)}, bf16[192,3072]{1,0:T(8,128)(2,1)}, u32[]{:S(2)}, u32[]{:S(2)}) collective-permute-start(bf16[192,3072]{1,0:T(8,128)(2,1)S(1)} %get-tuple-element.22.refs_0_), channel_id=1, source_target_pairs={{0,8},{1,9},{2,10},{3,11},{4,12},{5,13},{6,14},{7,15},{8,16},{9,17... | collective-permute-start | bytes 3538952 | tf_op jit(solution)/shard_map/ppermute | solution.py:169
  24.5 18.6 %collective-permute-start = (f32[192,384]{1,0:T(8,128)S(1)}, f32[192,384]{1,0:T(8,128)S(1)}, u32[]{:S(2)}, u32[]{:S(2)}) collective-permute-start(f32[192,384]{1,0:T(8,128)S(1)} %pad_maximum_fusion.4), channel_id=1, source_target_pairs={{0,1},{1,0},{2,3},{3,2},{4,5},{5,4},{6,7},{7,6},{8,9},{9,8},{10,11... | collective-permute-start | bytes 884744 | tf_op jit(solution)/shard_map/ppermute | solution.py:169
  42.1 37.5 %collective-permute-start.10 = (bf16[256,3072]{1,0:T(8,128)(2,1)}, bf16[256,3072]{1,0:T(8,128)(2,1)}, u32[]{:S(2)}, u32[]{:S(2)}) collective-permute-start(bf16[256,3072]{1,0:T(8,128)(2,1)} %pad_maximum_fusion.2.refs_8_), channel_id=1, source_target_pairs={{0,4},{1,5},{2,6},{3,7},{4,0},{5,1},{6,2},{7,3},{8,12},{9,13},{10,... | collective-permute-start | bytes 4718600 | tf_op jit(solution)/shard_map/ppermute | solution.py:169
  42.6 37.0 %collective-permute-start.9 = (bf16[256,3072]{1,0:T(8,128)(2,1)}, bf16[256,3072]{1,0:T(8,128)(2,1)}, u32[]{:S(2)}, u32[]{:S(2)}) collective-permute-start(bf16[256,3072]{1,0:T(8,128)(2,1)} %pad_maximum_fusion.2.refs_8_), channel_id=1, source_target_pairs={{0,2},{1,3},{2,0},{3,1},{4,6},{5,7},{6,4},{7,5},{8,10},{9,11},{10,... | collective-permute-start | bytes 4718600 | tf_op jit(solution)/shard_map/ppermute | solution.py:169
  51.4 28.2 %collective-permute-start.5 = (bf16[192,3072]{1,0:T(8,128)(2,1)}, bf16[192,3072]{1,0:T(8,128)(2,1)}, u32[]{:S(2)}, u32[]{:S(2)}) collective-permute-start(bf16[192,3072]{1,0:T(8,128)(2,1)} %collective-permute-done.3.refs_1_), channel_id=1, source_target_pairs={{8,16},{9,17},{10,18},{11,19},{12,20},{13,21},{14,22},{15,23},{16,... | collective-permute-start | bytes 3538952 | tf_op jit(solution)/shard_map/ppermute | solution.py:169
  52.7 26.9 %collective-permute-start.7 = (bf16[192,3072]{1,0:T(8,128)(2,1)}, bf16[192,3072]{1,0:T(8,128)(2,1)}, u32[]{:S(2)}, u32[]{:S(2)}) collective-permute-start(bf16[192,3072]{1,0:T(8,128)(2,1)} %collective-permute-done.4.refs_4_), channel_id=1, source_target_pairs={{8,0},{9,1},{10,2},{11,3},{12,4},{13,5},{14,6},{15,7},{16,8},{17,9... | collective-permute-start | bytes 3538952 | tf_op jit(solution)/shard_map/ppermute | solution.py:169
  64.8 16.9 %copy-start.17 = (bf16[4,4,48,256]{3,1,2,0:T(4,128)(2,1)S(1)}, bf16[4,4,48,256]{3,1,2,0:T(4,128)(2,1)}, u32[]{:S(2)}) copy-start(bf16[4,4,48,256]{3,1,2,0:T(4,128)(2,1)} %copy.35) | copy-start | bytes 1179652
  79.5 69.8 %collective-permute-start.11 = (bf16[256,3072]{1,0:T(8,128)(2,1)}, bf16[256,3072]{1,0:T(8,128)(2,1)}, u32[]{:S(2)}, u32[]{:S(2)}) collective-permute-start(bf16[256,3072]{1,0:T(8,128)(2,1)} %collective-permute-done.1.refs_9_), channel_id=1, source_target_pairs={{0,4},{1,5},{2,6},{3,7},{4,0},{5,1},{6,2},{7,3},{8,12},{9,13},{10,... | collective-permute-start | bytes 4718600 | tf_op jit(solution)/shard_map/ppermute | solution.py:169
  80.4 69.0 %collective-permute-start.12 = (bf16[256,3072]{1,0:T(8,128)(2,1)}, bf16[256,3072]{1,0:T(8,128)(2,1)}, u32[]{:S(2)}, u32[]{:S(2)}) collective-permute-start(bf16[256,3072]{1,0:T(8,128)(2,1)} %collective-permute-done.10.refs_12_), channel_id=1, source_target_pairs={{0,2},{1,3},{2,0},{3,1},{4,6},{5,7},{6,4},{7,5},{8,10},{9,11},{10,... | collective-permute-start | bytes 4718600 | tf_op jit(solution)/shard_map/ppermute | solution.py:169
  84.2 51.5 %all-to-all-start = ((bf16[4,4,240,256]{3,1,2,0:T(4,128)(2,1)}), bf16[4,4,240,256]{3,1,2,0:T(4,128)(2,1)}, u32[]{:S(2)}, u32[]{:S(2)}) async-start(bf16[4,4,240,256]{3,1,2,0:T(4,128)(2,1)} %pad_maximum_fusion), calls=%async_computation | async-start | bytes 3932160 | tf_op jit(solution)/shard_map/all_to_all | solution.py:407
  89.3 59.0 %collective-permute-start.6 = (bf16[192,3072]{1,0:T(8,128)(2,1)}, bf16[192,3072]{1,0:T(8,128)(2,1)S(1)}, u32[]{:S(2)}, u32[]{:S(2)}) collective-permute-start(bf16[192,3072]{1,0:T(8,128)(2,1)} %collective-permute-done.5.refs_2_), channel_id=1, source_target_pairs={{16,24},{17,25},{18,26},{19,27},{20,28},{21,29},{22,30},{23,31}} | collective-permute-start | bytes 3538952 | tf_op jit(solution)/shard_map/ppermute | solution.py:169
  90.6 58.7 %collective-permute-start.8 = (bf16[192,3072]{1,0:T(8,128)(2,1)}, bf16[192,3072]{1,0:T(8,128)(2,1)}, u32[]{:S(2)}, u32[]{:S(2)}) collective-permute-start(bf16[192,3072]{1,0:T(8,128)(2,1)} %collective-permute-done.7.refs_5_), channel_id=1, source_target_pairs={{8,0},{9,1},{10,2},{11,3},{12,4},{13,5},{14,6},{15,7}} | collective-permute-start | bytes 3538952 | tf_op jit(solution)/shard_map/ppermute | solution.py:169
  141.0 28.1 %all-to-all-start.1 = ((bf16[4,240,256]{2,1,0:T(8,128)(2,1)}), bf16[4,240,256]{2,1,0:T(8,128)(2,1)}, u32[]{:S(2)}, u32[]{:S(2)}) async-start(bf16[4,240,256]{2,1,0:T(8,128)(2,1)} %copy.37), calls=%async_computation.1 | async-start | bytes 983040 | tf_op jit(solution)/shard_map/all_to_all | solution.py:407
  169.0 24.6 %collective-permute-start.13 = (bf16[768,1024]{1,0:T(8,128)(2,1)}, bf16[768,1024]{1,0:T(8,128)(2,1)S(1)}, u32[]{:S(2)}, u32[]{:S(2)}) collective-permute-start(bf16[768,1024]{1,0:T(8,128)(2,1)} %get-tuple-element.29), channel_id=1, source_target_pairs={{0,1},{1,0},{2,3},{3,2},{4,5},{5,4},{6,7},{7,6},{8,9},{9,8},{10,11... | collective-permute-start | bytes 4718600 | tf_op jit(solution)/shard_map/ppermute | solution.py:169
  188.6 27.9 %all-to-all-start.3 = ((bf16[4,4,240,256]{3,2,1,0:T(8,128)(2,1)}), bf16[4,4,240,256]{3,2,1,0:T(8,128)(2,1)}, u32[]{:S(2)}, u32[]{:S(2)}) async-start(bf16[4,4,240,256]{3,2,1,0:T(8,128)(2,1)} %broadcast_in_dim.5), calls=%async_computation.3 | async-start | bytes 3932160 | tf_op jit(solution)/shard_map/all_to_all | solution.py:412
  195.4 31.2 %collective-permute-start.14 = (bf16[192,1024]{1,0:T(8,128)(2,1)}, bf16[192,1024]{1,0:T(8,128)(2,1)S(1)}, u32[]{:S(2)}, u32[]{:S(2)}) collective-permute-start(bf16[192,1024]{1,0:T(8,128)(2,1)} %get-tuple-element.39), channel_id=1, source_target_pairs={{0,0},{1,8},{2,2},{3,10},{4,4},{5,12},{6,6},{7,14},{8,16},{9,24},{... | collective-permute-start | bytes 1179656 | tf_op jit(solution)/shard_map/ppermute | solution.py:169
  200.0 41.0 %collective-permute-start.17 = (bf16[192,1024]{1,0:T(8,128)(2,1)}, bf16[192,1024]{1,0:T(8,128)(2,1)S(1)}, u32[]{:S(2)}, u32[]{:S(2)}) collective-permute-start(bf16[192,1024]{1,0:T(8,128)(2,1)} %get-tuple-element.36), channel_id=1, source_target_pairs={{0,24},{1,0},{2,26},{3,2},{4,28},{5,4},{6,30},{7,6},{8,8},{9,16},{... | collective-permute-start | bytes 1179656 | tf_op jit(solution)/shard_map/ppermute | solution.py:169
  204.5 36.5 %collective-permute-start.16 = (bf16[192,1024]{1,0:T(8,128)(2,1)}, bf16[192,1024]{1,0:T(8,128)(2,1)S(1)}, u32[]{:S(2)}, u32[]{:S(2)}) collective-permute-start(bf16[192,1024]{1,0:T(8,128)(2,1)} %get-tuple-element.37), channel_id=1, source_target_pairs={{0,16},{1,24},{2,18},{3,26},{4,20},{5,28},{6,22},{7,30},{8,0},{9,8... | collective-permute-start | bytes 1179656 | tf_op jit(solution)/shard_map/ppermute | solution.py:169
  204.6 36.4 %collective-permute-start.15 = (bf16[192,1024]{1,0:T(8,128)(2,1)}, bf16[192,1024]{1,0:T(8,128)(2,1)S(1)}, u32[]{:S(2)}, u32[]{:S(2)}) collective-permute-start(bf16[192,1024]{1,0:T(8,128)(2,1)} %get-tuple-element.38), channel_id=1, source_target_pairs={{0,8},{1,16},{2,10},{3,18},{4,12},{5,20},{6,14},{7,22},{8,24},{9,0... | collective-permute-start | bytes 1179656 | tf_op jit(solution)/shard_map/ppermute | solution.py:169
  (19 other events, 56.1 us)

commit v6 on v5

--- a/solution.py
+++ b/solution.py
@@ -1,3 +1,4 @@
+import functools
 import math
 
 import jax
@@ -294,7 +295,7 @@
     )
 
 
-def term_kernel(place_ref, *refs):
+def term_kernel(cuts, place_ref, *refs):
     blocks, weights, (sent_ref, kept_ref, left, arrived) = refs[:7], refs[7:-4], refs[-4:]
     tokens = blocks[0].shape[0]
     hi = place_ref[1]
@@ -313,32 +314,50 @@
             there = left.at[pl.ds(n * tokens, tokens), :]
             pltpu.make_async_copy(blocks[0], there, arrived.at[n]).wait()
 
+    pairs = len(weights) // (2 * len(cuts))
     for turn, out_ref in enumerate((sent_ref, kept_ref)):
 
         @pl.when(pl.program_id(0) == turn)
         def _(out_ref=out_ref):
             width = 2 * weights[0].shape[0]
-            for n in range(len(weights) // 2):
-                right = jnp.concatenate([weights[2 * n][...], weights[2 * n + 1][...]], axis=0)
-                out_ref[:, n * width : (n + 1) * width] = lax.dot_general(
-                    left[...], right, (((1,), (1,)), ((), ())), preferred_element_type=jnp.float32
-                ).astype(jnp.bfloat16)
+            for n in range(pairs):
+                total = None
+                for m, (start, stop) in enumerate(cuts):
+                    part = 2 * (n * len(cuts) + m)
+                    right = jnp.concatenate([weights[part][...], weights[part + 1][...]], axis=0)
+                    product = lax.dot_general(
+                        left[:, start:stop],
+                        right,
+                        (((1,), (1,)), ((), ())),
+                        preferred_element_type=jnp.float32,
+                    )
+                    total = product if total is None else total + product
+                out_ref[:, n * width : (n + 1) * width] = total.astype(jnp.bfloat16)
 
 
 def term_halves(blocks, weights, core, hi):
     tokens, depth = blocks[0].shape
-    rows = weights[0].shape[0] // 2
-    count = len(weights)
+    rows = weights[0][0].shape[0] // 2
+    count = len(weights[0])
+    cuts, start = [], 0
+    for piece in weights:
+        cuts.append((start, start + piece[0].shape[1]))
+        start += piece[0].shape[1]
+    flat = [w for n in range(0, count, 2) for piece in weights for w in piece[n : n + 2]]
     out = jax.ShapeDtypeStruct((4 * tokens, count * rows), jnp.bfloat16)
     return pl.pallas_call(
-        term_kernel,
+        functools.partial(term_kernel, tuple(cuts)),
         out_shape=(out, out),
         grid_spec=pltpu.PrefetchScalarGridSpec(
             num_scalar_prefetch=1,
             grid=(2,),
             in_specs=[pl.BlockSpec(memory_space=pl.ANY)] * 7
-            + [pl.BlockSpec((rows, depth), lambda i, place: (lax.rem(place[0] + 1 - i, 2), 0))]
-            * count,
+            + [
+                pl.BlockSpec(
+                    (rows, w.shape[1]), lambda i, place: (lax.rem(place[0] + 1 - i, 2), 0)
+                )
+                for w in flat
+            ],
             out_specs=(pl.BlockSpec(out.shape, lambda i, place: (0, 0)),) * 2,
             scratch_shapes=[
                 pltpu.VMEM((4 * tokens, depth), jnp.bfloat16),
@@ -352,20 +371,21 @@
             transcendentals=0,
         ),
         name="term",
-    )(jnp.stack([core, hi]), *blocks, *weights)
+    )(jnp.stack([core, hi]), *blocks, *flat)
 
 
 def finish_kernel(spot_ref, added_ref, *refs):
     pieces, out_ref = refs[:-1], refs[-1]
-    width = sum(piece.shape[1] for piece in pieces) // spot_ref.shape[0]
+    width = 128
     place = 0
     for piece in pieces:
-        for start in range(0, piece.shape[1], width):
-            there = pl.ds(pl.multiple_of(spot_ref[place] * width, width), width)
-            out_ref[:, there] = (
-                piece[:, start : start + width].astype(jnp.float32) + added_ref[:, there]
-            ).astype(jnp.bfloat16)
-            place += 1
+        for h in range(piece.shape[0]):
+            for start in range(0, piece.shape[2], width):
+                there = pl.ds(pl.multiple_of(spot_ref[place] * width, width), width)
+                out_ref[:, there] = (
+                    piece[h, :, start : start + width].astype(jnp.float32) + added_ref[:, there]
+                ).astype(jnp.bfloat16)
+                place += 1
 
 
 def finish(pieces, spots, added):
@@ -410,6 +430,12 @@
 
 def gather(value, axis):
     return lax.all_to_all(jnp.broadcast_to(value[None], (4, *value.shape)), axis, 0, 0)
+
+
+def gather_plane(value):
+    lo = lax.axis_index("lo")
+    others = jnp.stack([value] + [swap_lo(value, bit) for bit in range(1, 4)])
+    return jnp.stack([pick(others, lo ^ place, 0) for place in range(4)])
 
 
 def chain_hi(own, first):
@@ -464,7 +490,10 @@
         right, left = chain_hi(own, (x_a, y_a))
         blocks = (own, *right, *left)
         from_a, from_b = after((x_a, y_b), (x_b, right[1], left[1]))
-        weights = (own_a, own_b, x_a, x_b, y_a, y_b, swap_lo(from_a, 2), swap_lo(from_b, 1))
+        q_width = stored_queries.shape[1]
+        first = (swap_lo(from_a[:, :q_width], 2), swap_lo(from_b[:, :q_width], 1))
+        from_a, from_b = after((from_a, from_b), first)
+        second = (swap_lo(from_a[:, q_width:], 2), swap_lo(from_b[:, q_width:], 1))
 
         middle_local = jnp.concatenate(
             [
@@ -485,20 +514,20 @@
         column = scatter_sum(dp_pieces(down_turned, up_local), "lo")
         piece = scatter_sum(after(column, (right[1], left[1])), "hi")
         tokens = own.shape[0]
-        source = (hi % 2) * 2 + core
-
-        def owner(step):
-            return lambda hi, lo, core: (((hi % 2) * 2 + core + step) % 4, lo, hi // 2)
-
         added = rows_product(middle_gradient, adapter_down_maps)
-        sent, kept = term_halves(blocks, weights, core, hi)
-        line = after(gather(after(piece, (right[2], left[2])), "hi"), weights[-2:])
-        summed = kept.astype(jnp.float32) + swap_core(sent).astype(jnp.float32)
-        summed = summed.astype(jnp.bfloat16).reshape(4, tokens, -1)
-        received = [
-            send(pick(summed, (source + step) % 4, 0), owner(step)) for step in range(4)
-        ]
-        every = after(gather(line, "lo"), received[0])
+        pieces = []
+        for part in range(2):
+            if part:
+                weights = after((first, second), summed)
+            else:
+                weights = ((own_a, own_b, x_a, x_b, y_a, y_b),)
+            sent, kept = term_halves(after(blocks, (first, piece)), weights, core, hi)
+            summed = kept.astype(jnp.float32) + swap_core(sent).astype(jnp.float32)
+            summed = summed.astype(jnp.bfloat16).reshape(4, tokens, -1)
+            moved = lax.all_to_all(summed, "hi", 0, 0)
+            pieces.append(lax.dynamic_slice_in_dim(moved, 2 * core, 2, 0))
+            pieces.append(swap_core(lax.dynamic_slice_in_dim(moved, 2 - 2 * core, 2, 0)))
+        every = gather_plane(gather(piece, "hi"))
         down_total, up_total = dp_results(every, rank, up_local.shape)
         query_total = up_total[:, :q_width]
         key_value_total = jnp.stack(
@@ -506,12 +535,14 @@
         )
 
         spots = [
-            (((hi - step) % 4) // 2) * 16 + (lo ^ block) * 4 + part * 2 + (hi - step) % 2
-            for step in range(4)
-            for block in range(4)
+            h * 16 + (lo ^ block) * 4 + part * 2 + other
+            for blocks in ((0, 1, 2), (3,))
+            for other in (core, 1 - core)
+            for h in range(2)
+            for block in blocks
             for part in range(2)
         ]
-        normed_input_grad = finish(received, jnp.stack(spots).astype(jnp.int32), added)
+        normed_input_grad = finish(pieces, jnp.stack(spots).astype(jnp.int32), added)
         return (normed_input_grad, down_total, query_total, key_value_total)
 
     return shards

time: 247 us -> 241 us (0.976)
  the two profiles are of different devices: /device:TPU:26 before, /device:TPU:1 now
where the time goes in v6:
time: 241 us; the launch traced here: 239 us
  waiting for transfers between devices  72 us (30%)
  starting transfers between devices  66.9 us (28%)
  local copies, waits for them, and re-layouts  43.2 us (18%)
  Pallas kernels  30.7 us (13%)
  other arithmetic  18.6 us (8%)
  matrix products  6.78 us (3%)
    ppermute x22, starting transfers between devices, send(): return lax.ppermute(value, AXES, pairs)  45 us
    ppermute x22, waiting for transfers between devices, send(): return lax.ppermute(value, AXES, pairs)  42.4 us
    pallas_call x2, Pallas kernels, term_halves(): pl.pallas_call(functools.partial(term_kernel, tuple(cuts)), out_shape=(ou...  21.3 us
    all_to_all x2, waiting for transfers between devices, scatter_sum(): lax.all_to_all(value, axis, 0, 0)  18.6 us
    convert_element_type x3, local copies, waits for them, and re-layouts, dp_results(): return (down.astype(jnp.float32), up.astype(jnp.float32))  11.3 us
    all_to_all x1, waiting for transfers between devices, gather(): lax.all_to_all(jnp.broadcast_to(value[None], (4, *value.shape)), axis, 0, 0)  11 us
    all_to_all x2, starting transfers between devices, scatter_sum(): lax.all_to_all(value, axis, 0, 0)  9.01 us
    unnamed x41, local copies, waits for them, and re-layouts  8.74 us
  transfers between devices with their start and end apart: 27, of which 11 were waited for; matrix products, arithmetic and copies ran while one was open for 23% of the time, Pallas kernels for 6%

profile of v6, /device:TPU:1, one launch (start us, length us, event | category | flops | bytes accessed | tf_op | source)
XLA Modules:
  0.0 239.2 jit_solution(5041167414972358652)
XLA Ops:
  0.7 2.9 %fusion.12 = (bf16[256,2048]{1,0:T(8,128)(2,1)}, bf16[256,2048]{1,0:T(8,128)(2,1)S(1)}) fusion(bf16[512,2048]{1,0:T(8,128)(2,1)} %param.18), kind=kLoop, calls=%fused_computation.42 | loop fusion | bytes 4194304 | tf_op jit(solution)/shard_map/slice | solution.py:470
  12.4 7.0 %attention.1 = (bf16[192,3072]{1,0:T(8,128)(2,1)S(1)}, f32[192,192]{1,0:T(8,128)S(1)}) custom-call(bf16[192,2048]{1,0:T(8,128)(2,1)S(1)} %copy-done.7, bf16[192,512]{1,0:T(8,128)(2,1)S(1)} %copy-done.10, bf16[192,512]{1,0:T(8,128)(2,1)S(1)} %copy-done.11, bf16[192,2048]{1,0:T(8,128)(2,1)S(1)} %copy-done.8, s32[192,1]{1,0:T(8,128)S(1)} %copy.35.row_ids, ...), custom_call_target="tpu_custom_call" | custom-call | flops 754974720 | bytes 2359296 | tf_op jit(solution)/shard_map/attention/pallas_call | solution.py:258
  20.8 5.0 %collective-permute-start.3 = (bf16[192,3072]{1,0:T(8,128)(2,1)S(1)}, bf16[192,3072]{1,0:T(8,128)(2,1)}, u32[]{:S(2)}, u32[]{:S(2)}) collective-permute-start(bf16[192,3072]{1,0:T(8,128)(2,1)S(1)} %get-tuple-element.41.refs_0_), channel_id=1, source_target_pairs={{0,8},{1,9},{2,10},{3,11},{4,12},{5,13},{6,14},{7,15},{8,16},{9,17... | collective-permute-start | bytes 3538952 | tf_op jit(solution)/shard_map/ppermute | solution.py:170
  29.9 12.3 %collective-permute-done.2.refs_11_ = bf16[256,3072]{1,0:T(8,128)(2,1)} collective-permute-done((bf16[256,3072]{1,0:T(8,128)(2,1)}, bf16[256,3072]{1,0:T(8,128)(2,1)}, u32[]{:S(2)}, u32[]{:S(2)}) %collective-permute-start.2) | collective-permute-done | bytes 1572896 | tf_op jit(solution)/shard_map/ppermute | solution.py:170
  61.8 4.4 %all-to-all-start = ((bf16[4,4,240,256]{3,1,2,0:T(4,128)(2,1)}), bf16[4,4,240,256]{3,1,2,0:T(4,128)(2,1)}, u32[]{:S(2)}, u32[]{:S(2)}) async-start(bf16[4,4,240,256]{3,1,2,0:T(4,128)(2,1)} %pad_maximum_fusion), calls=%async_computation | async-start | bytes 3932160 | tf_op jit(solution)/shard_map/all_to_all | solution.py:427
  66.9 16.3 %collective-permute-done.7.refs_5_ = bf16[192,3072]{1,0:T(8,128)(2,1)} collective-permute-done((bf16[192,3072]{1,0:T(8,128)(2,1)}, bf16[192,3072]{1,0:T(8,128)(2,1)}, u32[]{:S(2)}, u32[]{:S(2)}) %collective-permute-start.7) | collective-permute-done | bytes 1179680 | tf_op jit(solution)/shard_map/ppermute | solution.py:170
  89.6 9.8 %all-to-all-done = bf16[4,4,240,256]{3,1,2,0:T(4,128)(2,1)} async-done(((bf16[4,4,240,256]{3,1,2,0:T(4,128)(2,1)}), bf16[4,4,240,256]{3,1,2,0:T(4,128)(2,1)}, u32[]{:S(2)}, u32[]{:S(2)}) %all-to-all-start) | async-done | bytes 1966112 | tf_op jit(solution)/shard_map/all_to_all | solution.py:427
  103.0 4.6 %all-to-all-start.1 = ((bf16[4,240,256]{2,1,0:T(8,128)(2,1)}), bf16[4,240,256]{2,1,0:T(8,128)(2,1)S(1)}, u32[]{:S(2)}, u32[]{:S(2)}) async-start(bf16[4,240,256]{2,1,0:T(8,128)(2,1)} %copy.40), calls=%async_computation.1 | async-start | bytes 983040 | tf_op jit(solution)/shard_map/all_to_all | solution.py:427
  107.7 8.8 %all-to-all-done.1 = bf16[4,240,256]{2,1,0:T(8,128)(2,1)S(1)} async-done(((bf16[4,240,256]{2,1,0:T(8,128)(2,1)}), bf16[4,240,256]{2,1,0:T(8,128)(2,1)S(1)}, u32[]{:S(2)}, u32[]{:S(2)}) %all-to-all-start.1) | async-done | bytes 491552 | tf_op jit(solution)/shard_map/all_to_all | solution.py:427
  117.6 3.4 %collective-permute-done.12.refs_8_ = bf16[256,2048]{1,0:T(8,128)(2,1)} collective-permute-done((bf16[256,2048]{1,0:T(8,128)(2,1)}, bf16[256,2048]{1,0:T(8,128)(2,1)}, u32[]{:S(2)}, u32[]{:S(2)}) %collective-permute-start.12) | collective-permute-done | bytes 1048608 | tf_op jit(solution)/shard_map/ppermute | solution.py:170
  123.2 14.4 %term.2 = (bf16[768,768]{1,0:T(8,128)(2,1)}, bf16[768,768]{1,0:T(8,128)(2,1)S(1)}) custom-call(s32[2]{0:T(128)S(1)} %pad_add_fusion.place_ref, bf16[192,3072]{1,0:T(8,128)(2,1)S(1)} %get-tuple-element.41.refs_0_, bf16[192,3072]{1,0:T(8,128)(2,1)} %collective-permute-done.3.refs_1_, bf16[192,3072]{1,0:T(8,128)(2,1)} %collective-permute-done.5.refs_2_, ...), custom_call_target="tpu_custom_call" | custom-call | flops 7247757312 | bytes 16515072 | tf_op jit(solution)/shard_map/term/pallas_call | solution.py:348
  137.6 3.1 %collective-permute-start.13 = (bf16[768,768]{1,0:T(8,128)(2,1)}, bf16[768,768]{1,0:T(8,128)(2,1)}, u32[]{:S(2)}, u32[]{:S(2)}) collective-permute-start(bf16[768,768]{1,0:T(8,128)(2,1)} %get-tuple-element.49), channel_id=1, source_target_pairs={{0,1},{1,0},{2,3},{3,2},{4,5},{5,4},{6,7},{7,6},{8,9},{9,8},{10,11... | collective-permute-start | bytes 3538952 | tf_op jit(solution)/shard_map/ppermute | solution.py:170
  141.5 4.3 %all-to-all-start.4 = ((bf16[4,240,256]{2,1,0:T(8,128)(2,1)}), bf16[4,240,256]{2,1,0:T(8,128)(2,1)S(1)}, u32[]{:S(2)}, u32[]{:S(2)}) async-start(bf16[4,240,256]{2,1,0:T(8,128)(2,1)} %broadcast_in_dim.2), calls=%async_computation.4 | async-start | bytes 983040 | tf_op jit(solution)/shard_map/all_to_all | solution.py:432
  148.4 11.0 %all-to-all-done.4 = bf16[4,240,256]{2,1,0:T(8,128)(2,1)S(1)} async-done(((bf16[4,240,256]{2,1,0:T(8,128)(2,1)}), bf16[4,240,256]{2,1,0:T(8,128)(2,1)S(1)}, u32[]{:S(2)}, u32[]{:S(2)}) %all-to-all-start.4) | async-done | bytes 491552 | tf_op jit(solution)/shard_map/all_to_all | solution.py:432
  159.4 4.3 %all-to-all-start.2 = ((bf16[4,192,768]{2,1,0:T(8,128)(2,1)}), bf16[4,192,768]{2,1,0:T(8,128)(2,1)}, u32[]{:S(2)}, u32[]{:S(2)}) async-start(bf16[4,192,768]{2,1,0:T(8,128)(2,1)} %bitcast.67), calls=%async_computation.2 | async-start | bytes 2359296 | tf_op jit(solution)/shard_map/all_to_all | solution.py:527
  170.8 3.7 %fusion.7.added_ref = f32[192,4096]{1,0:T(8,128)} fusion(bf16[4096,192]{0,1:T(8,128)(2,1)} %param.21, bf16[192,384]{1,0:T(8,128)(2,1)S(1)} %add_convert_fusion.2), kind=kOutput, calls=%fused_computation.28 | convolution fusion | flops 301989888 | bytes 4816896 | tf_op jit(solution)/shard_map/dot_general | solution.py:57
  174.5 5.5 %collective-permute-done.16.refs_10_ = bf16[256,1024]{1,0:T(8,128)(2,1)S(1)} collective-permute-done((bf16[256,1024]{1,0:T(8,128)(2,1)}, bf16[256,1024]{1,0:T(8,128)(2,1)S(1)}, u32[]{:S(2)}, u32[]{:S(2)}) %collective-permute-start.16) | collective-permute-done | bytes 524320 | tf_op jit(solution)/shard_map/ppermute | solution.py:170
  179.9 6.9 %term.3 = (bf16[768,256]{1,0:T(8,128)(2,1)S(1)}, bf16[768,256]{1,0:T(8,128)(2,1)S(1)}) custom-call(s32[2]{0:T(128)S(1)} %pad_add_fusion.place_ref, bf16[192,3072]{1,0:T(8,128)(2,1)S(1)} %get-tuple-element.41.refs_0_, bf16[192,3072]{1,0:T(8,128)(2,1)} %collective-permute-done.3.refs_1_, bf16[192,3072]{1,0:T(8,128)(2,1)} %collective-permute-done.5.refs_2_, ...), custom_call_target="tpu_custom_call" | custom-call | flops 2415919104 | bytes 8650752 | tf_op jit(solution)/shard_map/term/pallas_call | solution.py:348
  186.9 14.8 %collective-permute-start.17 = (bf16[768,256]{1,0:T(8,128)(2,1)S(1)}, bf16[768,256]{1,0:T(8,128)(2,1)S(1)}, u32[]{:S(2)}, u32[]{:S(2)}) collective-permute-start(bf16[768,256]{1,0:T(8,128)(2,1)S(1)} %get-tuple-element.57), channel_id=1, source_target_pairs={{0,1},{1,0},{2,3},{3,2},{4,5},{5,4},{6,7},{7,6},{8,9},{9,8},{10,11... | collective-permute-start | bytes 1179656 | tf_op jit(solution)/shard_map/ppermute | solution.py:170
  204.5 4.4 %all-to-all-start.3 = ((bf16[4,192,256]{2,1,0:T(8,128)(2,1)}), bf16[4,192,256]{2,1,0:T(8,128)(2,1)S(1)}, u32[]{:S(2)}, u32[]{:S(2)}) async-start(bf16[4,192,256]{2,1,0:T(8,128)(2,1)} %bitcast.39), calls=%async_computation.3 | async-start | bytes 786432 | tf_op jit(solution)/shard_map/all_to_all | solution.py:527
  208.9 3.4 %convert_bitcast_fusion = f32[4,4,256,192]{2,3,0,1:T(8,128)} fusion(bf16[4,4,240,256]{3,2,1,0:T(8,128)(2,1)} %pad_maximum_fusion.2), kind=kLoop, calls=%fused_computation.1 | loop fusion | flops 786432 | bytes 4718592 | tf_op jit(solution)/shard_map/convert_element_type | solution.py:422
  218.4 3.2 %collective-permute-start.18 = (bf16[2,192,256]{2,1,0:T(8,128)(2,1)S(1)}, bf16[2,192,256]{2,1,0:T(8,128)(2,1)S(1)}, u32[]{:S(2)}, u32[]{:S(2)}) collective-permute-start(bf16[2,192,256]{2,1,0:T(8,128)(2,1)S(1)} %get-tuple-element.72), channel_id=1, source_target_pairs={{0,1},{1,0},{2,3},{3,2},{4,5},{5,4},{6,7},{7,6},{8,9},{9,8},{10,11... | collective-permute-start | bytes 589832 | tf_op jit(solution)/shard_map/ppermute | solution.py:170
  223.5 5.6 %copy.41 = f32[4,4,256,192]{2,1,0,3:T(4,128)} copy(f32[4,4,256,192]{2,3,0,1:T(8,128)} %convert_bitcast_fusion) | data formatting | bytes 6291456 | tf_op jit(solution)/shard_map/convert_element_type | solution.py:422
  229.1 5.2 %reshape.41 = f32[4096,192]{0,1:T(8,128)} reshape(f32[4,4,256,192]{2,1,0,3:T(4,128)} %copy.41) | data formatting | bytes 6291456 | tf_op jit(solution)/shard_map/convert_element_type | solution.py:422
  (121 shorter events, 73.9 us)
Async XLA Ops:
  5.7 36.5 %collective-permute-start.2 = (bf16[256,3072]{1,0:T(8,128)(2,1)}, bf16[256,3072]{1,0:T(8,128)(2,1)}, u32[]{:S(2)}, u32[]{:S(2)}) collective-permute-start(bf16[256,3072]{1,0:T(8,128)(2,1)} %pad_maximum_fusion.3.refs_7_), channel_id=1, source_target_pairs={{0,4},{1,5},{2,6},{3,7},{4,0},{5,1},{6,2},{7,3},{8,12},{9,13},{10,... | collective-permute-start | bytes 4718600 | tf_op jit(solution)/shard_map/ppermute | solution.py:170
  7.8 35.3 %collective-permute-start.1 = (bf16[256,3072]{1,0:T(8,128)(2,1)}, bf16[256,3072]{1,0:T(8,128)(2,1)}, u32[]{:S(2)}, u32[]{:S(2)}) collective-permute-start(bf16[256,3072]{1,0:T(8,128)(2,1)} %pad_maximum_fusion.3.refs_7_), channel_id=1, source_target_pairs={{0,2},{1,3},{2,0},{3,1},{4,6},{5,7},{6,4},{7,5},{8,10},{9,11},{10,... | collective-permute-start | bytes 4718600 | tf_op jit(solution)/shard_map/ppermute | solution.py:170
  19.4 28.4 %collective-permute-start.4 = (bf16[192,3072]{1,0:T(8,128)(2,1)S(1)}, bf16[192,3072]{1,0:T(8,128)(2,1)}, u32[]{:S(2)}, u32[]{:S(2)}) collective-permute-start(bf16[192,3072]{1,0:T(8,128)(2,1)S(1)} %get-tuple-element.41.refs_0_), channel_id=1, source_target_pairs={{8,0},{9,1},{10,2},{11,3},{12,4},{13,5},{14,6},{15,7},{16,8},{17,9... | collective-permute-start | bytes 3538952 | tf_op jit(solution)/shard_map/ppermute | solution.py:170
  20.8 27.7 %collective-permute-start.3 = (bf16[192,3072]{1,0:T(8,128)(2,1)S(1)}, bf16[192,3072]{1,0:T(8,128)(2,1)}, u32[]{:S(2)}, u32[]{:S(2)}) collective-permute-start(bf16[192,3072]{1,0:T(8,128)(2,1)S(1)} %get-tuple-element.41.refs_0_), channel_id=1, source_target_pairs={{0,8},{1,9},{2,10},{3,11},{4,12},{5,13},{6,14},{7,15},{8,16},{9,17... | collective-permute-start | bytes 3538952 | tf_op jit(solution)/shard_map/ppermute | solution.py:170
  43.1 41.4 %collective-permute-start.10 = (bf16[256,3072]{1,0:T(8,128)(2,1)}, bf16[256,3072]{1,0:T(8,128)(2,1)}, u32[]{:S(2)}, u32[]{:S(2)}) collective-permute-start(bf16[256,3072]{1,0:T(8,128)(2,1)} %pad_maximum_fusion.4.refs_8_), channel_id=1, source_target_pairs={{0,2},{1,3},{2,0},{3,1},{4,6},{5,7},{6,4},{7,5},{8,10},{9,11},{10,... | collective-permute-start | bytes 4718600 | tf_op jit(solution)/shard_map/ppermute | solution.py:170
  44.3 40.2 %collective-permute-start.9 = (bf16[256,3072]{1,0:T(8,128)(2,1)}, bf16[256,3072]{1,0:T(8,128)(2,1)}, u32[]{:S(2)}, u32[]{:S(2)}) collective-permute-start(bf16[256,3072]{1,0:T(8,128)(2,1)} %pad_maximum_fusion.4.refs_8_), channel_id=1, source_target_pairs={{0,4},{1,5},{2,6},{3,7},{4,0},{5,1},{6,2},{7,3},{8,12},{9,13},{10,... | collective-permute-start | bytes 4718600 | tf_op jit(solution)/shard_map/ppermute | solution.py:170
  50.9 15.3 %collective-permute-start.5 = (bf16[192,3072]{1,0:T(8,128)(2,1)}, bf16[192,3072]{1,0:T(8,128)(2,1)}, u32[]{:S(2)}, u32[]{:S(2)}) collective-permute-start(bf16[192,3072]{1,0:T(8,128)(2,1)} %collective-permute-done.3.refs_1_), channel_id=1, source_target_pairs={{8,16},{9,17},{10,18},{11,19},{12,20},{13,21},{14,22},{15,23},{16,... | collective-permute-start | bytes 3538952 | tf_op jit(solution)/shard_map/ppermute | solution.py:170
  52.6 30.6 %collective-permute-start.7 = (bf16[192,3072]{1,0:T(8,128)(2,1)}, bf16[192,3072]{1,0:T(8,128)(2,1)}, u32[]{:S(2)}, u32[]{:S(2)}) collective-permute-start(bf16[192,3072]{1,0:T(8,128)(2,1)} %collective-permute-done.4.refs_4_), channel_id=1, source_target_pairs={{8,0},{9,1},{10,2},{11,3},{12,4},{13,5},{14,6},{15,7},{16,8},{17,9... | collective-permute-start | bytes 3538952 | tf_op jit(solution)/shard_map/ppermute | solution.py:170
  61.8 37.6 %all-to-all-start = ((bf16[4,4,240,256]{3,1,2,0:T(4,128)(2,1)}), bf16[4,4,240,256]{3,1,2,0:T(4,128)(2,1)}, u32[]{:S(2)}, u32[]{:S(2)}) async-start(bf16[4,4,240,256]{3,1,2,0:T(4,128)(2,1)} %pad_maximum_fusion), calls=%async_computation | async-start | bytes 3932160 | tf_op jit(solution)/shard_map/all_to_all | solution.py:427
  66.2 50.4 %collective-permute-start.6 = (bf16[192,3072]{1,0:T(8,128)(2,1)}, bf16[192,3072]{1,0:T(8,128)(2,1)S(1)}, u32[]{:S(2)}, u32[]{:S(2)}) collective-permute-start(bf16[192,3072]{1,0:T(8,128)(2,1)} %collective-permute-done.5.refs_2_), channel_id=1, source_target_pairs={{16,24},{17,25},{18,26},{19,27},{20,28},{21,29},{22,30},{23,31}} | collective-permute-start | bytes 3538952 | tf_op jit(solution)/shard_map/ppermute | solution.py:170
  83.2 34.4 %collective-permute-start.8 = (bf16[192,3072]{1,0:T(8,128)(2,1)}, bf16[192,3072]{1,0:T(8,128)(2,1)}, u32[]{:S(2)}, u32[]{:S(2)}) collective-permute-start(bf16[192,3072]{1,0:T(8,128)(2,1)} %collective-permute-done.7.refs_5_), channel_id=1, source_target_pairs={{8,0},{9,1},{10,2},{11,3},{12,4},{13,5},{14,6},{15,7}} | collective-permute-start | bytes 3538952 | tf_op jit(solution)/shard_map/ppermute | solution.py:170
  89.1 31.9 %collective-permute-start.12 = (bf16[256,2048]{1,0:T(8,128)(2,1)}, bf16[256,2048]{1,0:T(8,128)(2,1)}, u32[]{:S(2)}, u32[]{:S(2)}) collective-permute-start(bf16[256,2048]{1,0:T(8,128)(2,1)} %slice.78), channel_id=1, source_target_pairs={{0,2},{1,3},{2,0},{3,1},{4,6},{5,7},{6,4},{7,5},{8,10},{9,11},{10,... | collective-permute-start | bytes 3145736 | tf_op jit(solution)/shard_map/ppermute | solution.py:170
  89.5 32.4 %collective-permute-start.11 = (bf16[256,2048]{1,0:T(8,128)(2,1)}, bf16[256,2048]{1,0:T(8,128)(2,1)}, u32[]{:S(2)}, u32[]{:S(2)}) collective-permute-start(bf16[256,2048]{1,0:T(8,128)(2,1)} %slice.77), channel_id=1, source_target_pairs={{0,4},{1,5},{2,6},{3,7},{4,0},{5,1},{6,2},{7,3},{8,12},{9,13},{10,... | collective-permute-start | bytes 3145736 | tf_op jit(solution)/shard_map/ppermute | solution.py:170
  103.0 13.5 %all-to-all-start.1 = ((bf16[4,240,256]{2,1,0:T(8,128)(2,1)}), bf16[4,240,256]{2,1,0:T(8,128)(2,1)S(1)}, u32[]{:S(2)}, u32[]{:S(2)}) async-start(bf16[4,240,256]{2,1,0:T(8,128)(2,1)} %copy.40), calls=%async_computation.1 | async-start | bytes 983040 | tf_op jit(solution)/shard_map/all_to_all | solution.py:427
  141.5 17.9 %all-to-all-start.4 = ((bf16[4,240,256]{2,1,0:T(8,128)(2,1)}), bf16[4,240,256]{2,1,0:T(8,128)(2,1)S(1)}, u32[]{:S(2)}, u32[]{:S(2)}) async-start(bf16[4,240,256]{2,1,0:T(8,128)(2,1)} %broadcast_in_dim.2), calls=%async_computation.4 | async-start | bytes 983040 | tf_op jit(solution)/shard_map/all_to_all | solution.py:432
  159.4 45.1 %all-to-all-start.2 = ((bf16[4,192,768]{2,1,0:T(8,128)(2,1)}), bf16[4,192,768]{2,1,0:T(8,128)(2,1)}, u32[]{:S(2)}, u32[]{:S(2)}) async-start(bf16[4,192,768]{2,1,0:T(8,128)(2,1)} %bitcast.67), calls=%async_computation.2 | async-start | bytes 2359296 | tf_op jit(solution)/shard_map/all_to_all | solution.py:527
  167.4 12.5 %collective-permute-start.16 = (bf16[256,1024]{1,0:T(8,128)(2,1)}, bf16[256,1024]{1,0:T(8,128)(2,1)S(1)}, u32[]{:S(2)}, u32[]{:S(2)}) collective-permute-start(bf16[256,1024]{1,0:T(8,128)(2,1)} %slice.86), channel_id=1, source_target_pairs={{0,2},{1,3},{2,0},{3,1},{4,6},{5,7},{6,4},{7,5},{8,10},{9,11},{10,... | collective-permute-start | bytes 1572872 | tf_op jit(solution)/shard_map/ppermute | solution.py:170
  168.1 33.6 %collective-permute-start.21 = (bf16[4,240,256]{2,1,0:T(8,128)(2,1)S(1)}, bf16[4,240,256]{2,1,0:T(8,128)(2,1)S(1)}, u32[]{:S(2)}, u32[]{:S(2)}) collective-permute-start(bf16[4,240,256]{2,1,0:T(8,128)(2,1)S(1)} %all-to-all-done.4), channel_id=1, source_target_pairs={{0,6},{1,7},{2,4},{3,5},{4,2},{5,3},{6,0},{7,1},{8,14},{9,15},{10,... | collective-permute-start | bytes 1474568 | tf_op jit(solution)/shard_map/ppermute | solution.py:170
  170.3 31.4 %collective-permute-start.20 = (bf16[4,240,256]{2,1,0:T(8,128)(2,1)S(1)}, bf16[4,240,256]{2,1,0:T(8,128)(2,1)S(1)}, u32[]{:S(2)}, u32[]{:S(2)}) collective-permute-start(bf16[4,240,256]{2,1,0:T(8,128)(2,1)S(1)} %all-to-all-done.4), channel_id=1, source_target_pairs={{0,4},{1,5},{2,6},{3,7},{4,0},{5,1},{6,2},{7,3},{8,12},{9,13},{10,... | collective-permute-start | bytes 1474568 | tf_op jit(solution)/shard_map/ppermute | solution.py:170
  170.6 31.1 %collective-permute-start.19 = (bf16[4,240,256]{2,1,0:T(8,128)(2,1)S(1)}, bf16[4,240,256]{2,1,0:T(8,128)(2,1)S(1)}, u32[]{:S(2)}, u32[]{:S(2)}) collective-permute-start(bf16[4,240,256]{2,1,0:T(8,128)(2,1)S(1)} %all-to-all-done.4), channel_id=1, source_target_pairs={{0,2},{1,3},{2,0},{3,1},{4,6},{5,7},{6,4},{7,5},{8,10},{9,11},{10,... | collective-permute-start | bytes 1474568 | tf_op jit(solution)/shard_map/ppermute | solution.py:170
  186.9 16.8 %collective-permute-start.17 = (bf16[768,256]{1,0:T(8,128)(2,1)S(1)}, bf16[768,256]{1,0:T(8,128)(2,1)S(1)}, u32[]{:S(2)}, u32[]{:S(2)}) collective-permute-start(bf16[768,256]{1,0:T(8,128)(2,1)S(1)} %get-tuple-element.57), channel_id=1, source_target_pairs={{0,1},{1,0},{2,3},{3,2},{4,5},{5,4},{6,7},{7,6},{8,9},{9,8},{10,11... | collective-permute-start | bytes 1179656 | tf_op jit(solution)/shard_map/ppermute | solution.py:170
  204.5 13.9 %all-to-all-start.3 = ((bf16[4,192,256]{2,1,0:T(8,128)(2,1)}), bf16[4,192,256]{2,1,0:T(8,128)(2,1)S(1)}, u32[]{:S(2)}, u32[]{:S(2)}) async-start(bf16[4,192,256]{2,1,0:T(8,128)(2,1)} %bitcast.39), calls=%async_computation.3 | async-start | bytes 786432 | tf_op jit(solution)/shard_map/all_to_all | solution.py:527
  214.5 20.5 %collective-permute-start.14 = (bf16[2,192,768]{2,1,0:T(8,128)(2,1)}, bf16[2,192,768]{2,1,0:T(8,128)(2,1)S(1)}, u32[]{:S(2)}, u32[]{:S(2)}) collective-permute-start(bf16[2,192,768]{2,1,0:T(8,128)(2,1)} %get-tuple-element.64), channel_id=1, source_target_pairs={{0,1},{1,0},{2,3},{3,2},{4,5},{5,4},{6,7},{7,6},{8,9},{9,8},{10,11... | collective-permute-start | bytes 1769480 | tf_op jit(solution)/shard_map/ppermute | solution.py:170
  218.4 16.6 %collective-permute-start.18 = (bf16[2,192,256]{2,1,0:T(8,128)(2,1)S(1)}, bf16[2,192,256]{2,1,0:T(8,128)(2,1)S(1)}, u32[]{:S(2)}, u32[]{:S(2)}) collective-permute-start(bf16[2,192,256]{2,1,0:T(8,128)(2,1)S(1)} %get-tuple-element.72), channel_id=1, source_target_pairs={{0,1},{1,0},{2,3},{3,2},{4,5},{5,4},{6,7},{7,6},{8,9},{9,8},{10,11... | collective-permute-start | bytes 589832 | tf_op jit(solution)/shard_map/ppermute | solution.py:170
  (23 other events, 140.0 us)

commit v7 on v5

--- a/solution.py
+++ b/solution.py
@@ -491,8 +491,8 @@
             return lambda hi, lo, core: (((hi % 2) * 2 + core + step) % 4, lo, hi // 2)
 
         added = rows_product(middle_gradient, adapter_down_maps)
-        sent, kept = term_halves(blocks, weights, core, hi)
         line = after(gather(after(piece, (right[2], left[2])), "hi"), weights[-2:])
+        sent, kept = term_halves(after(blocks, line), weights, core, hi)
         summed = kept.astype(jnp.float32) + swap_core(sent).astype(jnp.float32)
         summed = summed.astype(jnp.bfloat16).reshape(4, tokens, -1)
         received = [

time: 247 us -> 220 us (0.89)
  the two profiles are of different devices: /device:TPU:26 before, /device:TPU:1 now
where the time goes in v7:
time: 220 us; the launch traced here: 219 us
  waiting for transfers between devices  63.5 us (29%)
  starting transfers between devices  45.8 us (21%)
  local copies, waits for them, and re-layouts  37.8 us (17%)
  Pallas kernels  27.8 us (13%)
  blocking collectives  20.9 us (10%)
  other arithmetic  12.9 us (6%)
  matrix products  8.38 us (4%)
    ppermute x18, waiting for transfers between devices, send(): return lax.ppermute(value, AXES, pairs)  38.6 us
    ppermute x18, starting transfers between devices, send(): return lax.ppermute(value, AXES, pairs)  33.3 us
    all_to_all x1, blocking collectives, scatter_sum(): lax.all_to_all(value, axis, 0, 0)  20.9 us
    all_to_all x2, waiting for transfers between devices, gather(): lax.all_to_all(jnp.broadcast_to(value[None], (4, *value.shape)), axis, 0, 0)  18.8 us
    pallas_call x1, Pallas kernels, term_halves(): pl.pallas_call(term_kernel, out_shape=(out, out), grid_spec=pltpu.Prefetc...  17.8 us
    unnamed x47, local copies, waits for them, and re-layouts  9.47 us
    convert_element_type x3, local copies, waits for them, and re-layouts, dp_results(): return (down.astype(jnp.float32), up.astype(jnp.float32))  9.38 us
    all_to_all x2, starting transfers between devices, gather(): lax.all_to_all(jnp.broadcast_to(value[None], (4, *value.shape)), axis, 0, 0)  8.07 us
  transfers between devices with their start and end apart: 21, of which 7 were waited for; matrix products, arithmetic and copies ran while one was open for 21% of the time, Pallas kernels for 4%

profile of v7, /device:TPU:1, one launch (start us, length us, event | category | flops | bytes accessed | tf_op | source)
XLA Modules:
  0.0 218.5 jit_solution(10699151307534361741)
XLA Ops:
  0.7 2.9 %fusion.12 = (bf16[256,2048]{1,0:T(8,128)(2,1)}, bf16[256,2048]{1,0:T(8,128)(2,1)S(1)}) fusion(bf16[512,2048]{1,0:T(8,128)(2,1)} %param.18), kind=kLoop, calls=%fused_computation.34 | loop fusion | bytes 4194304 | tf_op jit(solution)/shard_map/slice | solution.py:444
  13.0 7.7 %attention.1 = (bf16[192,3072]{1,0:T(8,128)(2,1)}, f32[192,192]{1,0:T(8,128)S(1)}) custom-call(bf16[192,2048]{1,0:T(8,128)(2,1)S(1)} %copy-done.6, bf16[192,512]{1,0:T(8,128)(2,1)S(1)} %copy-done.9, bf16[192,512]{1,0:T(8,128)(2,1)S(1)} %copy-done.10, bf16[192,2048]{1,0:T(8,128)(2,1)S(1)} %copy-done.7, s32[192,1]{1,0:T(8,128)S(1)} %copy.32.row_ids, ...), custom_call_target="tpu_custom_call" | custom-call | flops 754974720 | bytes 2359296 | tf_op jit(solution)/shard_map/attention/pallas_call | solution.py:257
  20.8 4.3 %collective-permute-start.3 = (bf16[192,3072]{1,0:T(8,128)(2,1)}, bf16[192,3072]{1,0:T(8,128)(2,1)}, u32[]{:S(2)}, u32[]{:S(2)}) collective-permute-start(bf16[192,3072]{1,0:T(8,128)(2,1)} %get-tuple-element.38.refs_0_), channel_id=1, source_target_pairs={{0,8},{1,9},{2,10},{3,11},{4,12},{5,13},{6,14},{7,15},{8,16},{9,17... | collective-permute-start | bytes 3538952 | tf_op jit(solution)/shard_map/ppermute | solution.py:169
  30.2 10.7 %collective-permute-done.1.refs_9_ = bf16[256,3072]{1,0:T(8,128)(2,1)} collective-permute-done((bf16[256,3072]{1,0:T(8,128)(2,1)S(1)}, bf16[256,3072]{1,0:T(8,128)(2,1)}, u32[]{:S(2)}, u32[]{:S(2)}) %collective-permute-start.1) | collective-permute-done | bytes 1572896 | tf_op jit(solution)/shard_map/ppermute | solution.py:169
  53.9 2.4 %reshape.34 = bf16[192,4,4,256]{3,2,1,0:T(4,128)(2,1)} reshape(bf16[192,4096]{1,0:T(8,128)(2,1)S(1)} %copy-done.12) | data formatting | bytes 3145728 | tf_op jit(solution)/shard_map/reshape | solution.py:391
  60.4 2.5 %pad_maximum_fusion = bf16[4,4,240,256]{3,1,2,0:T(4,128)(2,1)} fusion(bf16[4,4,48,256]{3,1,2,0:T(4,128)(2,1)S(1)} %copy-done.18, bf16[4,4,192,256]{3,1,2,0:T(4,128)(2,1)S(1)} %bitcast.69), kind=kLoop, calls=%fused_computation.5 | loop fusion | flops 983040 | bytes 3932160 | tf_op jit(solution)/shard_map/concatenate | solution.py:389
  62.9 4.4 %all-to-all-start = ((bf16[4,4,240,256]{3,1,2,0:T(4,128)(2,1)}), bf16[4,4,240,256]{3,1,2,0:T(4,128)(2,1)}, u32[]{:S(2)}, u32[]{:S(2)}) async-start(bf16[4,4,240,256]{3,1,2,0:T(4,128)(2,1)} %pad_maximum_fusion), calls=%async_computation | async-start | bytes 3932160 | tf_op jit(solution)/shard_map/all_to_all | solution.py:407
  69.1 19.7 %collective-permute-done.7.refs_5_ = bf16[192,3072]{1,0:T(8,128)(2,1)} collective-permute-done((bf16[192,3072]{1,0:T(8,128)(2,1)}, bf16[192,3072]{1,0:T(8,128)(2,1)}, u32[]{:S(2)}, u32[]{:S(2)}) %collective-permute-start.7) | collective-permute-done | bytes 1179680 | tf_op jit(solution)/shard_map/ppermute | solution.py:169
  91.4 6.1 %all-to-all-done = bf16[4,4,240,256]{3,1,2,0:T(4,128)(2,1)} async-done(((bf16[4,4,240,256]{3,1,2,0:T(4,128)(2,1)}), bf16[4,4,240,256]{3,1,2,0:T(4,128)(2,1)}, u32[]{:S(2)}, u32[]{:S(2)}) %all-to-all-start) | async-done | bytes 1966112 | tf_op jit(solution)/shard_map/all_to_all | solution.py:407
  97.5 3.5 %reduce_sum.24 = bf16[4,240,256]{2,0,1:T(4,128)(2,1)} reduce(bf16[4,4,240,256]{3,1,2,0:T(4,128)(2,1)} %all-to-all-done, bf16[]{:T(256)} %constant.301.clone.1), dimensions={0}, to_apply=%region_0.0 | reduce | flops 737280 | bytes 2457602 | tf_op jit(solution)/shard_map/reduce_sum | solution.py:406
  102.1 20.9 %all_to_all.20 = bf16[4,240,256]{2,1,0:T(8,128)(2,1)} all-to-all(bf16[4,240,256]{2,1,0:T(8,128)(2,1)S(1)} %copy.37), channel_id=1, replica_groups=mesh['hi'=4,'lo'=4,'tensor'=2] {'hi'}, dimensions={0} | all-to-all | bytes 983040 | tf_op jit(solution)/shard_map/all_to_all | solution.py:407
  125.0 3.6 %all-to-all-start.2 = ((bf16[4,240,256]{2,1,0:T(8,128)(2,1)}), bf16[4,240,256]{2,1,0:T(8,128)(2,1)S(1)}, u32[]{:S(2)}, u32[]{:S(2)}) async-start(bf16[4,240,256]{2,1,0:T(8,128)(2,1)} %broadcast_in_dim.4), calls=%async_computation.2 | async-start | bytes 983040 | tf_op jit(solution)/shard_map/all_to_all | solution.py:412
  128.7 8.7 %all-to-all-done.2 = bf16[4,240,256]{2,1,0:T(8,128)(2,1)S(1)} async-done(((bf16[4,240,256]{2,1,0:T(8,128)(2,1)}), bf16[4,240,256]{2,1,0:T(8,128)(2,1)S(1)}, u32[]{:S(2)}, u32[]{:S(2)}) %all-to-all-start.2) | async-done | bytes 491552 | tf_op jit(solution)/shard_map/all_to_all | solution.py:412
  139.5 17.8 %term.1 = (bf16[768,1024]{1,0:T(8,128)(2,1)}, bf16[768,1024]{1,0:T(8,128)(2,1)S(1)}) custom-call(s32[2]{0:T(128)S(1)} %pad_add_fusion.place_ref, bf16[192,3072]{1,0:T(8,128)(2,1)} %get-tuple-element.38.refs_0_, bf16[192,3072]{1,0:T(8,128)(2,1)} %collective-permute-done.3.refs_1_, bf16[192,3072]{1,0:T(8,128)(2,1)S(1)} %copy-done.5, ...), custom_call_target="tpu_custom_call" | custom-call | flops 9663676416 | bytes 20447232 | tf_op jit(solution)/shard_map/term/pallas_call | solution.py:333
  157.2 5.8 %collective-permute-start.13 = (bf16[768,1024]{1,0:T(8,128)(2,1)}, bf16[768,1024]{1,0:T(8,128)(2,1)S(1)}, u32[]{:S(2)}, u32[]{:S(2)}) collective-permute-start(bf16[768,1024]{1,0:T(8,128)(2,1)} %get-tuple-element.46), channel_id=1, source_target_pairs={{0,1},{1,0},{2,3},{3,2},{4,5},{5,4},{6,7},{7,6},{8,9},{9,8},{10,11... | collective-permute-start | bytes 4718600 | tf_op jit(solution)/shard_map/ppermute | solution.py:169
  164.5 4.4 %all-to-all-start.3 = ((bf16[4,4,240,256]{3,2,1,0:T(8,128)(2,1)}), bf16[4,4,240,256]{3,2,1,0:T(8,128)(2,1)}, u32[]{:S(2)}, u32[]{:S(2)}) async-start(bf16[4,4,240,256]{3,2,1,0:T(8,128)(2,1)} %broadcast_in_dim.5), calls=%async_computation.3 | async-start | bytes 3932160 | tf_op jit(solution)/shard_map/all_to_all | solution.py:412
  173.1 2.3 %fusion.7.added_ref = f32[192,4096]{1,0:T(8,128)} fusion(bf16[4096,192]{0,1:T(8,128)(2,1)S(1)} %copy-done.14, bf16[192,384]{1,0:T(8,128)(2,1)S(1)} %add_convert_fusion.1), kind=kOutput, calls=%fused_computation.28 | convolution fusion | flops 301989888 | bytes 4816896 | tf_op jit(solution)/shard_map/dot_general | solution.py:56
  175.4 4.5 %collective-permute-start.15 = (bf16[192,1024]{1,0:T(8,128)(2,1)}, bf16[192,1024]{1,0:T(8,128)(2,1)S(1)}, u32[]{:S(2)}, u32[]{:S(2)}) collective-permute-start(bf16[192,1024]{1,0:T(8,128)(2,1)} %get-tuple-element.52), channel_id=1, source_target_pairs={{0,8},{1,16},{2,10},{3,18},{4,12},{5,20},{6,14},{7,22},{8,24},{9,0... | collective-permute-start | bytes 1179656 | tf_op jit(solution)/shard_map/ppermute | solution.py:169
  179.9 2.5 %collective-permute-start.17 = (bf16[192,1024]{1,0:T(8,128)(2,1)}, bf16[192,1024]{1,0:T(8,128)(2,1)S(1)}, u32[]{:S(2)}, u32[]{:S(2)}) collective-permute-start(bf16[192,1024]{1,0:T(8,128)(2,1)} %get-tuple-element.50), channel_id=1, source_target_pairs={{0,24},{1,0},{2,26},{3,2},{4,28},{5,4},{6,30},{7,6},{8,8},{9,16},{... | collective-permute-start | bytes 1179656 | tf_op jit(solution)/shard_map/ppermute | solution.py:169
  182.5 10.1 %all-to-all-done.3 = bf16[4,4,240,256]{3,2,1,0:T(8,128)(2,1)} async-done(((bf16[4,4,240,256]{3,2,1,0:T(8,128)(2,1)}), bf16[4,4,240,256]{3,2,1,0:T(8,128)(2,1)}, u32[]{:S(2)}, u32[]{:S(2)}) %all-to-all-start.3) | async-done | bytes 1966112 | tf_op jit(solution)/shard_map/all_to_all | solution.py:412
  192.6 7.4 %collective-permute-done.14.refs_0_ = bf16[192,1024]{1,0:T(8,128)(2,1)S(1)} collective-permute-done((bf16[192,1024]{1,0:T(8,128)(2,1)}, bf16[192,1024]{1,0:T(8,128)(2,1)S(1)}, u32[]{:S(2)}, u32[]{:S(2)}) %collective-permute-start.14) | collective-permute-done | bytes 393248 | tf_op jit(solution)/shard_map/ppermute | solution.py:169
  203.8 3.7 %copy.38 = f32[4,4,256,192]{2,1,0,3:T(4,128)} copy(f32[4,4,256,192]{2,3,0,1:T(8,128)S(1)} %convert_bitcast_fusion) | data formatting | bytes 6291456 | tf_op jit(solution)/shard_map/convert_element_type | solution.py:402
  207.5 5.2 %reshape.38 = f32[4096,192]{0,1:T(8,128)} reshape(f32[4,4,256,192]{2,1,0,3:T(4,128)} %copy.38) | data formatting | bytes 6291456 | tf_op jit(solution)/shard_map/convert_element_type | solution.py:402
  216.2 2.3 %finish.1 = bf16[192,4096]{1,0:T(8,128)(2,1)} custom-call(s32[32]{0:T(128)S(1)} %stack.149.spot_ref, f32[192,4096]{1,0:T(8,128)S(1)} %copy-done.2, bf16[192,1024]{1,0:T(8,128)(2,1)S(1)} %collective-permute-done.14.refs_0_, bf16[192,1024]{1,0:T(8,128)(2,1)S(1)} %collective-permute-done.15.refs_1_, bf16[192,1024]{1,0:T(8,128)(2,1)S(1)} %collective-permute-done.16.refs_2_, ...), custom_call_target="tpu_custom_call" | custom-call | flops 786432 | bytes 6291456 | tf_op jit(solution)/shard_map/finish/pallas_call | solution.py:372
  (107 shorter events, 53.7 us)
Async XLA Ops:
  0.6 25.8 %copy-start = (bf16[192,4096]{1,0:T(8,128)(2,1)S(1)}, bf16[192,4096]{1,0:T(8,128)(2,1)}, u32[]{:S(2)}) copy-start(bf16[192,4096]{1,0:T(8,128)(2,1)} %param.12) | copy-start | bytes 4718596
  4.5 36.3 %collective-permute-start.1 = (bf16[256,3072]{1,0:T(8,128)(2,1)S(1)}, bf16[256,3072]{1,0:T(8,128)(2,1)}, u32[]{:S(2)}, u32[]{:S(2)}) collective-permute-start(bf16[256,3072]{1,0:T(8,128)(2,1)S(1)} %pad_maximum_fusion.1.refs_7_), channel_id=1, source_target_pairs={{0,2},{1,3},{2,0},{3,1},{4,6},{5,7},{6,4},{7,5},{8,10},{9,11},{10,... | collective-permute-start | bytes 4718600 | tf_op jit(solution)/shard_map/ppermute | solution.py:169
  6.6 35.0 %collective-permute-start.2 = (bf16[256,3072]{1,0:T(8,128)(2,1)S(1)}, bf16[256,3072]{1,0:T(8,128)(2,1)}, u32[]{:S(2)}, u32[]{:S(2)}) collective-permute-start(bf16[256,3072]{1,0:T(8,128)(2,1)S(1)} %pad_maximum_fusion.1.refs_7_), channel_id=1, source_target_pairs={{0,4},{1,5},{2,6},{3,7},{4,0},{5,1},{6,2},{7,3},{8,12},{9,13},{10,... | collective-permute-start | bytes 4718600 | tf_op jit(solution)/shard_map/ppermute | solution.py:169
  20.8 37.5 %collective-permute-start.3 = (bf16[192,3072]{1,0:T(8,128)(2,1)}, bf16[192,3072]{1,0:T(8,128)(2,1)}, u32[]{:S(2)}, u32[]{:S(2)}) collective-permute-start(bf16[192,3072]{1,0:T(8,128)(2,1)} %get-tuple-element.38.refs_0_), channel_id=1, source_target_pairs={{0,8},{1,9},{2,10},{3,11},{4,12},{5,13},{6,14},{7,15},{8,16},{9,17... | collective-permute-start | bytes 3538952 | tf_op jit(solution)/shard_map/ppermute | solution.py:169
  25.1 33.2 %collective-permute-start.4 = (bf16[192,3072]{1,0:T(8,128)(2,1)}, bf16[192,3072]{1,0:T(8,128)(2,1)}, u32[]{:S(2)}, u32[]{:S(2)}) collective-permute-start(bf16[192,3072]{1,0:T(8,128)(2,1)} %get-tuple-element.38.refs_0_), channel_id=1, source_target_pairs={{8,0},{9,1},{10,2},{11,3},{12,4},{13,5},{14,6},{15,7},{16,8},{17,9... | collective-permute-start | bytes 3538952 | tf_op jit(solution)/shard_map/ppermute | solution.py:169
  27.2 2.9 %collective-permute-start = (f32[192,384]{1,0:T(8,128)S(1)}, f32[192,384]{1,0:T(8,128)S(1)}, u32[]{:S(2)}, u32[]{:S(2)}) collective-permute-start(f32[192,384]{1,0:T(8,128)S(1)} %pad_maximum_fusion.4), channel_id=1, source_target_pairs={{0,1},{1,0},{2,3},{3,2},{4,5},{5,4},{6,7},{7,6},{8,9},{9,8},{10,11... | collective-permute-start | bytes 884744 | tf_op jit(solution)/shard_map/ppermute | solution.py:169
  41.7 48.4 %collective-permute-start.10 = (bf16[256,3072]{1,0:T(8,128)(2,1)}, bf16[256,3072]{1,0:T(8,128)(2,1)}, u32[]{:S(2)}, u32[]{:S(2)}) collective-permute-start(bf16[256,3072]{1,0:T(8,128)(2,1)} %pad_maximum_fusion.2.refs_8_), channel_id=1, source_target_pairs={{0,2},{1,3},{2,0},{3,1},{4,6},{5,7},{6,4},{7,5},{8,10},{9,11},{10,... | collective-permute-start | bytes 4718600 | tf_op jit(solution)/shard_map/ppermute | solution.py:169
  42.1 48.0 %collective-permute-start.9 = (bf16[256,3072]{1,0:T(8,128)(2,1)}, bf16[256,3072]{1,0:T(8,128)(2,1)}, u32[]{:S(2)}, u32[]{:S(2)}) collective-permute-start(bf16[256,3072]{1,0:T(8,128)(2,1)} %pad_maximum_fusion.2.refs_8_), channel_id=1, source_target_pairs={{0,4},{1,5},{2,6},{3,7},{4,0},{5,1},{6,2},{7,3},{8,12},{9,13},{10,... | collective-permute-start | bytes 4718600 | tf_op jit(solution)/shard_map/ppermute | solution.py:169
  58.3 9.0 %collective-permute-start.5 = (bf16[192,3072]{1,0:T(8,128)(2,1)}, bf16[192,3072]{1,0:T(8,128)(2,1)S(1)}, u32[]{:S(2)}, u32[]{:S(2)}) collective-permute-start(bf16[192,3072]{1,0:T(8,128)(2,1)} %collective-permute-done.3.refs_1_), channel_id=1, source_target_pairs={{8,16},{9,17},{10,18},{11,19},{12,20},{13,21},{14,22},{15,23},{16,... | collective-permute-start | bytes 3538952 | tf_op jit(solution)/shard_map/ppermute | solution.py:169
  59.1 29.7 %collective-permute-start.7 = (bf16[192,3072]{1,0:T(8,128)(2,1)}, bf16[192,3072]{1,0:T(8,128)(2,1)}, u32[]{:S(2)}, u32[]{:S(2)}) collective-permute-start(bf16[192,3072]{1,0:T(8,128)(2,1)} %collective-permute-done.4.refs_4_), channel_id=1, source_target_pairs={{8,0},{9,1},{10,2},{11,3},{12,4},{13,5},{14,6},{15,7},{16,8},{17,9... | collective-permute-start | bytes 3538952 | tf_op jit(solution)/shard_map/ppermute | solution.py:169
  62.9 34.6 %all-to-all-start = ((bf16[4,4,240,256]{3,1,2,0:T(4,128)(2,1)}), bf16[4,4,240,256]{3,1,2,0:T(4,128)(2,1)}, u32[]{:S(2)}, u32[]{:S(2)}) async-start(bf16[4,4,240,256]{3,1,2,0:T(4,128)(2,1)} %pad_maximum_fusion), calls=%async_computation | async-start | bytes 3932160 | tf_op jit(solution)/shard_map/all_to_all | solution.py:407
  67.4 34.8 %copy-start.4 = (bf16[192,3072]{1,0:T(8,128)(2,1)}, bf16[192,3072]{1,0:T(8,128)(2,1)S(1)}, u32[]{:S(2)}) copy-start(bf16[192,3072]{1,0:T(8,128)(2,1)S(1)} %collective-permute-done.5.refs_2_) | copy-start | bytes 3538948
  67.4 56.8 %collective-permute-start.6 = (bf16[192,3072]{1,0:T(8,128)(2,1)S(1)}, bf16[192,3072]{1,0:T(8,128)(2,1)}, u32[]{:S(2)}, u32[]{:S(2)}) collective-permute-start(bf16[192,3072]{1,0:T(8,128)(2,1)S(1)} %collective-permute-done.5.refs_2_), channel_id=1, source_target_pairs={{16,24},{17,25},{18,26},{19,27},{20,28},{21,29},{22,30},{23,31}} | collective-permute-start | bytes 3538952 | tf_op jit(solution)/shard_map/ppermute | solution.py:169
  88.8 35.4 %collective-permute-start.8 = (bf16[192,3072]{1,0:T(8,128)(2,1)}, bf16[192,3072]{1,0:T(8,128)(2,1)}, u32[]{:S(2)}, u32[]{:S(2)}) collective-permute-start(bf16[192,3072]{1,0:T(8,128)(2,1)} %collective-permute-done.7.refs_5_), channel_id=1, source_target_pairs={{8,0},{9,1},{10,2},{11,3},{12,4},{13,5},{14,6},{15,7}} | collective-permute-start | bytes 3538952 | tf_op jit(solution)/shard_map/ppermute | solution.py:169
  90.1 47.3 %collective-permute-start.11 = (bf16[256,3072]{1,0:T(8,128)(2,1)}, bf16[256,3072]{1,0:T(8,128)(2,1)}, u32[]{:S(2)}, u32[]{:S(2)}) collective-permute-start(bf16[256,3072]{1,0:T(8,128)(2,1)} %collective-permute-done.1.refs_9_), channel_id=1, source_target_pairs={{0,4},{1,5},{2,6},{3,7},{4,0},{5,1},{6,2},{7,3},{8,12},{9,13},{10,... | collective-permute-start | bytes 4718600 | tf_op jit(solution)/shard_map/ppermute | solution.py:169
  90.4 47.8 %collective-permute-start.12 = (bf16[256,3072]{1,0:T(8,128)(2,1)}, bf16[256,3072]{1,0:T(8,128)(2,1)}, u32[]{:S(2)}, u32[]{:S(2)}) collective-permute-start(bf16[256,3072]{1,0:T(8,128)(2,1)} %collective-permute-done.9.refs_12_), channel_id=1, source_target_pairs={{0,2},{1,3},{2,0},{3,1},{4,6},{5,7},{6,4},{7,5},{8,10},{9,11},{10,... | collective-permute-start | bytes 4718600 | tf_op jit(solution)/shard_map/ppermute | solution.py:169
  125.0 12.4 %all-to-all-start.2 = ((bf16[4,240,256]{2,1,0:T(8,128)(2,1)}), bf16[4,240,256]{2,1,0:T(8,128)(2,1)S(1)}, u32[]{:S(2)}, u32[]{:S(2)}) async-start(bf16[4,240,256]{2,1,0:T(8,128)(2,1)} %broadcast_in_dim.4), calls=%async_computation.2 | async-start | bytes 983040 | tf_op jit(solution)/shard_map/all_to_all | solution.py:412
  139.5 23.6 %copy-start.17 = (bf16[4,240,256]{2,1,0:T(8,128)(2,1)S(1)}, bf16[4,240,256]{2,1,0:T(8,128)(2,1)}, u32[]{:S(2)}) copy-start(bf16[4,240,256]{2,1,0:T(8,128)(2,1)} %copy-done.16) | copy-start | bytes 1474564
  157.2 11.7 %collective-permute-start.13 = (bf16[768,1024]{1,0:T(8,128)(2,1)}, bf16[768,1024]{1,0:T(8,128)(2,1)S(1)}, u32[]{:S(2)}, u32[]{:S(2)}) collective-permute-start(bf16[768,1024]{1,0:T(8,128)(2,1)} %get-tuple-element.46), channel_id=1, source_target_pairs={{0,1},{1,0},{2,3},{3,2},{4,5},{5,4},{6,7},{7,6},{8,9},{9,8},{10,11... | collective-permute-start | bytes 4718600 | tf_op jit(solution)/shard_map/ppermute | solution.py:169
  164.5 28.1 %all-to-all-start.3 = ((bf16[4,4,240,256]{3,2,1,0:T(8,128)(2,1)}), bf16[4,4,240,256]{3,2,1,0:T(8,128)(2,1)}, u32[]{:S(2)}, u32[]{:S(2)}) async-start(bf16[4,4,240,256]{3,2,1,0:T(8,128)(2,1)} %broadcast_in_dim.5), calls=%async_computation.3 | async-start | bytes 3932160 | tf_op jit(solution)/shard_map/all_to_all | solution.py:412
  170.8 29.1 %collective-permute-start.14 = (bf16[192,1024]{1,0:T(8,128)(2,1)}, bf16[192,1024]{1,0:T(8,128)(2,1)S(1)}, u32[]{:S(2)}, u32[]{:S(2)}) collective-permute-start(bf16[192,1024]{1,0:T(8,128)(2,1)} %get-tuple-element.53), channel_id=1, source_target_pairs={{0,0},{1,8},{2,2},{3,10},{4,4},{5,12},{6,6},{7,14},{8,16},{9,24},{... | collective-permute-start | bytes 1179656 | tf_op jit(solution)/shard_map/ppermute | solution.py:169
  175.4 38.9 %collective-permute-start.15 = (bf16[192,1024]{1,0:T(8,128)(2,1)}, bf16[192,1024]{1,0:T(8,128)(2,1)S(1)}, u32[]{:S(2)}, u32[]{:S(2)}) collective-permute-start(bf16[192,1024]{1,0:T(8,128)(2,1)} %get-tuple-element.52), channel_id=1, source_target_pairs={{0,8},{1,16},{2,10},{3,18},{4,12},{5,20},{6,14},{7,22},{8,24},{9,0... | collective-permute-start | bytes 1179656 | tf_op jit(solution)/shard_map/ppermute | solution.py:169
  179.9 34.4 %collective-permute-start.16 = (bf16[192,1024]{1,0:T(8,128)(2,1)}, bf16[192,1024]{1,0:T(8,128)(2,1)S(1)}, u32[]{:S(2)}, u32[]{:S(2)}) collective-permute-start(bf16[192,1024]{1,0:T(8,128)(2,1)} %get-tuple-element.51), channel_id=1, source_target_pairs={{0,16},{1,24},{2,18},{3,26},{4,20},{5,28},{6,22},{7,30},{8,0},{9,8... | collective-permute-start | bytes 1179656 | tf_op jit(solution)/shard_map/ppermute | solution.py:169
  179.9 34.3 %collective-permute-start.17 = (bf16[192,1024]{1,0:T(8,128)(2,1)}, bf16[192,1024]{1,0:T(8,128)(2,1)S(1)}, u32[]{:S(2)}, u32[]{:S(2)}) collective-permute-start(bf16[192,1024]{1,0:T(8,128)(2,1)} %get-tuple-element.50), channel_id=1, source_target_pairs={{0,24},{1,0},{2,26},{3,2},{4,28},{5,4},{6,30},{7,6},{8,8},{9,16},{... | collective-permute-start | bytes 1179656 | tf_op jit(solution)/shard_map/ppermute | solution.py:169
  (20 other events, 73.3 us)

commit v8 on v7

--- a/solution.py
+++ b/solution.py
@@ -395,11 +395,45 @@
     ).astype(jnp.bfloat16)
 
 
-def dp_results(every, rank, up_shape):
-    rows, width = every.shape[2:]
-    down = every[:, :, :rank].transpose(1, 0, 3, 2).reshape(16 * width, rank)
-    up = every[:, :, rank:].reshape(-1, 4, 16, width).transpose(1, 2, 0, 3).reshape(up_shape)
-    return down.astype(jnp.float32), up.astype(jnp.float32)
+def results_kernel(every_ref, down_ref, query_ref, key_value_ref):
+    rank = down_ref.shape[0]
+    width = every_ref.shape[3]
+    each = (every_ref.shape[2] - rank) // 16
+    for hi in range(4):
+        for lo in range(4):
+            piece = every_ref[lo, hi].astype(jnp.float32)
+            start = (hi * 4 + lo) * width
+            down_ref[:, start : start + width] = piece[:rank]
+            for n in range(each):
+                part = piece[rank + n * 16 : rank + (n + 1) * 16]
+                column, row = divmod((lo * 4 + hi) * each + n, 4)
+                rows = slice(row * 16, (row + 1) * 16)
+                column = column * width
+                if column < query_ref.shape[1]:
+                    query_ref[rows, column : column + width] = part
+                else:
+                    which, column = divmod(column - query_ref.shape[1], key_value_ref.shape[2])
+                    key_value_ref[which, rows, column : column + width] = part
+
+
+def dp_results(every, rank, q_width, k_width):
+    width = every.shape[3]
+    down_turned, query, key_value = pl.pallas_call(
+        results_kernel,
+        out_shape=(
+            jax.ShapeDtypeStruct((rank, 16 * width), jnp.float32),
+            jax.ShapeDtypeStruct((ADAPTER_RANK, q_width), jnp.float32),
+            jax.ShapeDtypeStruct((2, ADAPTER_RANK, k_width), jnp.float32),
+        ),
+        in_specs=[pl.BlockSpec(memory_space=pltpu.VMEM)],
+        out_specs=(pl.BlockSpec(memory_space=pltpu.VMEM),) * 3,
+        compiler_params=pltpu.CompilerParams(vmem_limit_bytes=24 << 20),
+        cost_estimate=pl.CostEstimate(
+            flops=every.size, bytes_accessed=6 * every.size, transcendentals=0
+        ),
+        name="results",
+    )(every)
+    return down_turned.T, query, key_value
 
 
 def scatter_sum(value, axis):
@@ -445,7 +479,7 @@
         x_a, y_a = swap_lo(own_a, 1), swap_lo(own_a, 2)
         next_b = after(own_b, (x_a, y_a))
         x_b, y_b = swap_lo(next_b, 1), swap_lo(next_b, 2)
-        stored_queries = after(stored_queries, own_a)
+        document_index = after(document_index, own_a)
 
         own, middle_part = attention(
             stored_queries,
@@ -481,6 +515,7 @@
             middle_gradient, normed, (((0,), (0,)), ((), ())), preferred_element_type=jnp.float32
         )
         ups = up_gradients(adapter_middle, query_gradient, key_gradient, value_gradient)
+        down_turned, ups = after((down_turned, ups), (right[0], left[0]))
         up_local = jnp.concatenate(ups, axis=1)
         column = scatter_sum(dp_pieces(down_turned, up_local), "lo")
         piece = scatter_sum(after(column, (right[1], left[1])), "hi")
@@ -499,11 +534,7 @@
             send(pick(summed, (source + step) % 4, 0), owner(step)) for step in range(4)
         ]
         every = after(gather(line, "lo"), received[0])
-        down_total, up_total = dp_results(every, rank, up_local.shape)
-        query_total = up_total[:, :q_width]
-        key_value_total = jnp.stack(
-            [up_total[:, q_width : q_width + k_width], up_total[:, q_width + k_width :]]
-        )
+        down_total, query_total, key_value_total = dp_results(every, rank, q_width, k_width)
 
         spots = [
             (((hi - step) % 4) // 2) * 16 + (lo ^ block) * 4 + part * 2 + (hi - step) % 2

time: 220 us -> 207 us (0.941)
  local copies, waits for them, and re-layouts: 37.8 us -> 23.6 us
  waiting for transfers between devices: 63.5 us -> 74.3 us
  blocking collectives: 20.9 us -> 14.1 us
  other arithmetic: 12.9 us -> 10.2 us
    convert_element_type x3 -> x0, local copies, waits for them, and re-layouts: 9.38 us -> none  [dp_results(): return (down.astype(jnp.float32), up.astype(jnp.float32))]
    ppermute x18, waiting for transfers between devices: 38.6 us -> 46 us  [send(): return lax.ppermute(value, AXES, pairs)]
    all_to_all x1, blocking collectives: 20.9 us -> 14.1 us  [scatter_sum(): lax.all_to_all(value, axis, 0, 0)]
    all_to_all x1, waiting for transfers between devices: 6.09 us -> 12.5 us  [scatter_sum(): lax.all_to_all(value, axis, 0, 0)]
    dot_general x3, matrix products: 3.71 us -> 0.72 us  [up_gradients(): lax.dot_general(adapter_middle[:, place * rank:(place + 1) * rank], gradi...]
    all_to_all x2, waiting for transfers between devices: 18.8 us -> 15.8 us  [gather(): lax.all_to_all(jnp.broadcast_to(value[None], (4, *value.shape)), axis, 0, 0)]
    unnamed x47 -> x44, local copies, waits for them, and re-layouts: 9.47 us -> 8.12 us
  transfers between devices with their start and end apart: 21 -> 21, of which waited for: 7 -> 11; matrix products, arithmetic and copies ran while one was open for 21% -> 14% of each run, Pallas kernels for 4% -> 4%
where the time goes in v8:
time: 207 us; the launch traced here: 206 us
  waiting for transfers between devices  74.3 us (36%)
  starting transfers between devices  46.7 us (23%)
  Pallas kernels  28.8 us (14%)
  local copies, waits for them, and re-layouts  23.6 us (11%)
  blocking collectives  14.1 us (7%)
  other arithmetic  10.2 us (5%)
  matrix products  6.85 us (3%)
    ppermute x18, waiting for transfers between devices, send(): return lax.ppermute(value, AXES, pairs)  46 us
    ppermute x18, starting transfers between devices, send(): return lax.ppermute(value, AXES, pairs)  34.3 us
    pallas_call x1, Pallas kernels, term_halves(): pl.pallas_call(term_kernel, out_shape=(out, out), grid_spec=pltpu.Prefetc...  17.4 us
    all_to_all x2, waiting for transfers between devices, gather(): lax.all_to_all(jnp.broadcast_to(value[None], (4, *value.shape)), axis, 0, 0)  15.8 us
    all_to_all x1, blocking collectives, scatter_sum(): lax.all_to_all(value, axis, 0, 0)  14.1 us
    all_to_all x1, waiting for transfers between devices, scatter_sum(): lax.all_to_all(value, axis, 0, 0)  12.5 us
    unnamed x44, local copies, waits for them, and re-layouts  8.12 us
    all_to_all x2, starting transfers between devices, gather(): lax.all_to_all(jnp.broadcast_to(value[None], (4, *value.shape)), axis, 0, 0)  8.03 us
  transfers between devices with their start and end apart: 21, of which 11 were waited for; matrix products, arithmetic and copies ran while one was open for 14% of the time, Pallas kernels for 4%

profile of v8, /device:TPU:1, one launch (start us, length us, event | category | flops | bytes accessed | tf_op | source)
XLA Modules:
  0.0 205.9 jit_solution(7811848832492542106)
XLA Ops:
  0.7 2.9 %fusion.10 = (bf16[256,2048]{1,0:T(8,128)(2,1)}, bf16[256,2048]{1,0:T(8,128)(2,1)S(1)}) fusion(bf16[512,2048]{1,0:T(8,128)(2,1)} %param.18), kind=kLoop, calls=%fused_computation.26 | loop fusion | bytes 4194304 | tf_op jit(solution)/shard_map/slice | solution.py:478
  13.0 7.0 %attention.1 = (bf16[192,3072]{1,0:T(8,128)(2,1)S(1)}, f32[192,192]{1,0:T(8,128)S(1)}) custom-call(bf16[192,2048]{1,0:T(8,128)(2,1)S(1)} %copy-done.8, bf16[192,512]{1,0:T(8,128)(2,1)S(1)} %copy-done.11, bf16[192,512]{1,0:T(8,128)(2,1)S(1)} %copy-done.12, bf16[192,2048]{1,0:T(8,128)(2,1)S(1)} %copy-done.9, s32[192,1]{1,0:T(8,128)S(1)} %copy.24.row_ids, ...), custom_call_target="tpu_custom_call" | custom-call | flops 754974720 | bytes 2359296 | tf_op jit(solution)/shard_map/attention/pallas_call | solution.py:257
  20.1 4.5 %collective-permute-start.3 = (bf16[192,3072]{1,0:T(8,128)(2,1)S(1)}, bf16[192,3072]{1,0:T(8,128)(2,1)}, u32[]{:S(2)}, u32[]{:S(2)}) collective-permute-start(bf16[192,3072]{1,0:T(8,128)(2,1)S(1)} %get-tuple-element.49.refs_0_), channel_id=1, source_target_pairs={{0,8},{1,9},{2,10},{3,11},{4,12},{5,13},{6,14},{7,15},{8,16},{9,17... | collective-permute-start | bytes 3538952 | tf_op jit(solution)/shard_map/ppermute | solution.py:169
  29.7 11.2 %collective-permute-done.1.refs_9_ = bf16[256,3072]{1,0:T(8,128)(2,1)} collective-permute-done((bf16[256,3072]{1,0:T(8,128)(2,1)S(1)}, bf16[256,3072]{1,0:T(8,128)(2,1)}, u32[]{:S(2)}, u32[]{:S(2)}) %collective-permute-start.1) | collective-permute-done | bytes 1572896 | tf_op jit(solution)/shard_map/ppermute | solution.py:169
  47.5 5.0 %collective-permute-done.4.refs_4_ = bf16[192,3072]{1,0:T(8,128)(2,1)} collective-permute-done((bf16[192,3072]{1,0:T(8,128)(2,1)S(1)}, bf16[192,3072]{1,0:T(8,128)(2,1)}, u32[]{:S(2)}, u32[]{:S(2)}) %collective-permute-start.4) | collective-permute-done | bytes 1179680 | tf_op jit(solution)/shard_map/ppermute | solution.py:169
  55.5 2.9 %reshape.25 = bf16[192,4,4,256]{3,2,1,0:T(4,128)(2,1)S(1)} reshape(bf16[192,4096]{1,0:T(8,128)(2,1)} %fusion.3) | data formatting | bytes 3145728 | tf_op jit(solution)/shard_map/reshape | solution.py:391
  62.6 2.5 %pad_maximum_fusion = bf16[4,4,240,256]{3,1,2,0:T(4,128)(2,1)} fusion(bf16[4,4,48,256]{3,1,2,0:T(4,128)(2,1)S(1)} %copy.27, bf16[4,4,192,256]{3,1,2,0:T(4,128)(2,1)S(1)} %bitcast.55), kind=kLoop, calls=%fused_computation.2 | loop fusion | flops 983040 | bytes 3932160 | tf_op jit(solution)/shard_map/concatenate | solution.py:389
  65.2 4.4 %all-to-all-start = ((bf16[4,4,240,256]{3,1,2,0:T(4,128)(2,1)}), bf16[4,4,240,256]{3,1,2,0:T(4,128)(2,1)}, u32[]{:S(2)}, u32[]{:S(2)}) async-start(bf16[4,4,240,256]{3,1,2,0:T(4,128)(2,1)} %pad_maximum_fusion), calls=%async_computation | async-start | bytes 3932160 | tf_op jit(solution)/shard_map/all_to_all | solution.py:441
  71.3 11.5 %collective-permute-done.7.refs_5_ = bf16[192,3072]{1,0:T(8,128)(2,1)} collective-permute-done((bf16[192,3072]{1,0:T(8,128)(2,1)}, bf16[192,3072]{1,0:T(8,128)(2,1)}, u32[]{:S(2)}, u32[]{:S(2)}) %collective-permute-start.7) | collective-permute-done | bytes 1179680 | tf_op jit(solution)/shard_map/ppermute | solution.py:169
  85.0 12.5 %all-to-all-done = bf16[4,4,240,256]{3,1,2,0:T(4,128)(2,1)} async-done(((bf16[4,4,240,256]{3,1,2,0:T(4,128)(2,1)}), bf16[4,4,240,256]{3,1,2,0:T(4,128)(2,1)}, u32[]{:S(2)}, u32[]{:S(2)}) %all-to-all-start) | async-done | bytes 1966112 | tf_op jit(solution)/shard_map/all_to_all | solution.py:441
  97.5 2.7 %reduce_sum.24 = bf16[4,240,256]{2,0,1:T(4,128)(2,1)S(1)} reduce(bf16[4,4,240,256]{3,1,2,0:T(4,128)(2,1)} %all-to-all-done, bf16[]{:T(256)} %constant.301.clone.1), dimensions={0}, to_apply=%region_0.0 | reduce | flops 737280 | bytes 2457602 | tf_op jit(solution)/shard_map/reduce_sum | solution.py:440
  100.3 14.1 %all_to_all.20 = bf16[4,240,256]{2,1,0:T(8,128)(2,1)} all-to-all(bf16[4,240,256]{2,1,0:T(8,128)(2,1)S(1)} %copy.29), channel_id=1, replica_groups=mesh['hi'=4,'lo'=4,'tensor'=2] {'hi'}, dimensions={0} | all-to-all | bytes 983040 | tf_op jit(solution)/shard_map/all_to_all | solution.py:441
  116.3 4.3 %all-to-all-start.2 = ((bf16[4,240,256]{2,1,0:T(8,128)(2,1)}), bf16[4,240,256]{2,1,0:T(8,128)(2,1)}, u32[]{:S(2)}, u32[]{:S(2)}) async-start(bf16[4,240,256]{2,1,0:T(8,128)(2,1)} %broadcast_in_dim.4), calls=%async_computation.2 | async-start | bytes 983040 | tf_op jit(solution)/shard_map/all_to_all | solution.py:446
  120.7 8.6 %all-to-all-done.2 = bf16[4,240,256]{2,1,0:T(8,128)(2,1)} async-done(((bf16[4,240,256]{2,1,0:T(8,128)(2,1)}), bf16[4,240,256]{2,1,0:T(8,128)(2,1)}, u32[]{:S(2)}, u32[]{:S(2)}) %all-to-all-start.2) | async-done | bytes 491552 | tf_op jit(solution)/shard_map/all_to_all | solution.py:446
  131.2 17.4 %term.1 = (bf16[768,1024]{1,0:T(8,128)(2,1)}, bf16[768,1024]{1,0:T(8,128)(2,1)S(1)}) custom-call(s32[2]{0:T(128)S(1)} %pad_add_fusion.place_ref, bf16[192,3072]{1,0:T(8,128)(2,1)S(1)} %copy-done.6, bf16[192,3072]{1,0:T(8,128)(2,1)} %collective-permute-done.3.refs_1_, bf16[192,3072]{1,0:T(8,128)(2,1)} %collective-permute-done.5.refs_2_, ...), custom_call_target="tpu_custom_call" | custom-call | flops 9663676416 | bytes 20447232 | tf_op jit(solution)/shard_map/term/pallas_call | solution.py:333
  149.8 6.2 %collective-permute-start.13 = (bf16[768,1024]{1,0:T(8,128)(2,1)}, bf16[768,1024]{1,0:T(8,128)(2,1)}, u32[]{:S(2)}, u32[]{:S(2)}) collective-permute-start(bf16[768,1024]{1,0:T(8,128)(2,1)} %get-tuple-element.57), channel_id=1, source_target_pairs={{0,1},{1,0},{2,3},{3,2},{4,5},{5,4},{6,7},{7,6},{8,9},{9,8},{10,11... | collective-permute-start | bytes 4718600 | tf_op jit(solution)/shard_map/ppermute | solution.py:169
  156.0 2.4 %broadcast_in_dim.5 = bf16[4,4,240,256]{3,2,1,0:T(8,128)(2,1)} broadcast(bf16[4,240,256]{2,1,0:T(8,128)(2,1)} %all-to-all-done.2), dimensions={1,2,3} | broadcast | bytes 2457600 | tf_op jit(solution)/shard_map/broadcast_in_dim | solution.py:446
  158.4 3.7 %all-to-all-start.3 = ((bf16[4,4,240,256]{3,2,1,0:T(8,128)(2,1)}), bf16[4,4,240,256]{3,2,1,0:T(8,128)(2,1)S(1)}, u32[]{:S(2)}, u32[]{:S(2)}) async-start(bf16[4,4,240,256]{3,2,1,0:T(8,128)(2,1)} %broadcast_in_dim.5), calls=%async_computation.3 | async-start | bytes 3932160 | tf_op jit(solution)/shard_map/all_to_all | solution.py:446
  167.4 4.5 %collective-permute-start.15 = (bf16[192,1024]{1,0:T(8,128)(2,1)}, bf16[192,1024]{1,0:T(8,128)(2,1)S(1)}, u32[]{:S(2)}, u32[]{:S(2)}) collective-permute-start(bf16[192,1024]{1,0:T(8,128)(2,1)} %get-tuple-element.66), channel_id=1, source_target_pairs={{0,8},{1,16},{2,10},{3,18},{4,12},{5,20},{6,14},{7,22},{8,24},{9,0... | collective-permute-start | bytes 1179656 | tf_op jit(solution)/shard_map/ppermute | solution.py:169
  172.0 2.4 %collective-permute-start.17 = (bf16[192,1024]{1,0:T(8,128)(2,1)}, bf16[192,1024]{1,0:T(8,128)(2,1)S(1)}, u32[]{:S(2)}, u32[]{:S(2)}) collective-permute-start(bf16[192,1024]{1,0:T(8,128)(2,1)} %get-tuple-element.64), channel_id=1, source_target_pairs={{0,24},{1,0},{2,26},{3,2},{4,28},{5,4},{6,30},{7,6},{8,8},{9,16},{... | collective-permute-start | bytes 1179656 | tf_op jit(solution)/shard_map/ppermute | solution.py:169
  174.8 3.7 %fusion.5.added_ref = f32[192,4096]{1,0:T(8,128)} fusion(bf16[4096,192]{0,1:T(8,128)(2,1)} %param.21, bf16[192,384]{1,0:T(8,128)(2,1)} %copy-done.17), kind=kOutput, calls=%fused_computation.20 | convolution fusion | flops 301989888 | bytes 4816896 | tf_op jit(solution)/shard_map/dot_general | solution.py:56
  178.5 7.2 %all-to-all-done.3.every_ref = bf16[4,4,240,256]{3,2,1,0:T(8,128)(2,1)S(1)} async-done(((bf16[4,4,240,256]{3,2,1,0:T(8,128)(2,1)}), bf16[4,4,240,256]{3,2,1,0:T(8,128)(2,1)S(1)}, u32[]{:S(2)}, u32[]{:S(2)}) %all-to-all-start.3) | async-done | bytes 1966112 | tf_op jit(solution)/shard_map/all_to_all | solution.py:446
  185.8 11.1 %collective-permute-done.14.refs_0_ = bf16[192,1024]{1,0:T(8,128)(2,1)S(1)} collective-permute-done((bf16[192,1024]{1,0:T(8,128)(2,1)}, bf16[192,1024]{1,0:T(8,128)(2,1)S(1)}, u32[]{:S(2)}, u32[]{:S(2)}) %collective-permute-start.14) | collective-permute-done | bytes 393248 | tf_op jit(solution)/shard_map/ppermute | solution.py:169
  198.9 2.7 %collective-permute-done.17.refs_3_ = bf16[192,1024]{1,0:T(8,128)(2,1)S(1)} collective-permute-done((bf16[192,1024]{1,0:T(8,128)(2,1)}, bf16[192,1024]{1,0:T(8,128)(2,1)S(1)}, u32[]{:S(2)}, u32[]{:S(2)}) %collective-permute-start.17) | collective-permute-done | bytes 393248 | tf_op jit(solution)/shard_map/ppermute | solution.py:169
  (96 shorter events, 49.0 us)
Async XLA Ops:
  0.6 25.3 %copy-start = (bf16[192,4096]{1,0:T(8,128)(2,1)S(1)}, bf16[192,4096]{1,0:T(8,128)(2,1)}, u32[]{:S(2)}) copy-start(bf16[192,4096]{1,0:T(8,128)(2,1)} %param.12) | copy-start | bytes 4718596
  4.5 36.3 %collective-permute-start.1 = (bf16[256,3072]{1,0:T(8,128)(2,1)S(1)}, bf16[256,3072]{1,0:T(8,128)(2,1)}, u32[]{:S(2)}, u32[]{:S(2)}) collective-permute-start(bf16[256,3072]{1,0:T(8,128)(2,1)S(1)} %pad_maximum_fusion.1.refs_7_), channel_id=1, source_target_pairs={{0,2},{1,3},{2,0},{3,1},{4,6},{5,7},{6,4},{7,5},{8,10},{9,11},{10,... | collective-permute-start | bytes 4718600 | tf_op jit(solution)/shard_map/ppermute | solution.py:169
  6.6 35.0 %collective-permute-start.2 = (bf16[256,3072]{1,0:T(8,128)(2,1)S(1)}, bf16[256,3072]{1,0:T(8,128)(2,1)}, u32[]{:S(2)}, u32[]{:S(2)}) collective-permute-start(bf16[256,3072]{1,0:T(8,128)(2,1)S(1)} %pad_maximum_fusion.1.refs_7_), channel_id=1, source_target_pairs={{0,4},{1,5},{2,6},{3,7},{4,0},{5,1},{6,2},{7,3},{8,12},{9,13},{10,... | collective-permute-start | bytes 4718600 | tf_op jit(solution)/shard_map/ppermute | solution.py:169
  20.0 23.7 %copy-start.5 = (bf16[192,3072]{1,0:T(8,128)(2,1)}, bf16[192,3072]{1,0:T(8,128)(2,1)S(1)}, u32[]{:S(2)}) copy-start(bf16[192,3072]{1,0:T(8,128)(2,1)S(1)} %get-tuple-element.49.refs_0_) | copy-start | bytes 3538948
  20.1 27.4 %collective-permute-start.3 = (bf16[192,3072]{1,0:T(8,128)(2,1)S(1)}, bf16[192,3072]{1,0:T(8,128)(2,1)}, u32[]{:S(2)}, u32[]{:S(2)}) collective-permute-start(bf16[192,3072]{1,0:T(8,128)(2,1)S(1)} %get-tuple-element.49.refs_0_), channel_id=1, source_target_pairs={{0,8},{1,9},{2,10},{3,11},{4,12},{5,13},{6,14},{7,15},{8,16},{9,17... | collective-permute-start | bytes 3538952 | tf_op jit(solution)/shard_map/ppermute | solution.py:169
  24.6 27.9 %collective-permute-start.4 = (bf16[192,3072]{1,0:T(8,128)(2,1)S(1)}, bf16[192,3072]{1,0:T(8,128)(2,1)}, u32[]{:S(2)}, u32[]{:S(2)}) collective-permute-start(bf16[192,3072]{1,0:T(8,128)(2,1)S(1)} %get-tuple-element.49.refs_0_), channel_id=1, source_target_pairs={{8,0},{9,1},{10,2},{11,3},{12,4},{13,5},{14,6},{15,7},{16,8},{17,9... | collective-permute-start | bytes 3538952 | tf_op jit(solution)/shard_map/ppermute | solution.py:169
  26.6 2.9 %collective-permute-start = (f32[192,384]{1,0:T(8,128)S(1)}, f32[192,384]{1,0:T(8,128)S(1)}, u32[]{:S(2)}, u32[]{:S(2)}) collective-permute-start(f32[192,384]{1,0:T(8,128)S(1)} %pad_maximum_fusion.4), channel_id=1, source_target_pairs={{0,1},{1,0},{2,3},{3,2},{4,5},{5,4},{6,7},{7,6},{8,9},{9,8},{10,11... | collective-permute-start | bytes 884744 | tf_op jit(solution)/shard_map/ppermute | solution.py:169
  41.7 42.4 %collective-permute-start.10 = (bf16[256,3072]{1,0:T(8,128)(2,1)}, bf16[256,3072]{1,0:T(8,128)(2,1)}, u32[]{:S(2)}, u32[]{:S(2)}) collective-permute-start(bf16[256,3072]{1,0:T(8,128)(2,1)} %pad_maximum_fusion.2.refs_8_), channel_id=1, source_target_pairs={{0,2},{1,3},{2,0},{3,1},{4,6},{5,7},{6,4},{7,5},{8,10},{9,11},{10,... | collective-permute-start | bytes 4718600 | tf_op jit(solution)/shard_map/ppermute | solution.py:169
  42.1 42.0 %collective-permute-start.9 = (bf16[256,3072]{1,0:T(8,128)(2,1)}, bf16[256,3072]{1,0:T(8,128)(2,1)}, u32[]{:S(2)}, u32[]{:S(2)}) collective-permute-start(bf16[256,3072]{1,0:T(8,128)(2,1)} %pad_maximum_fusion.2.refs_8_), channel_id=1, source_target_pairs={{0,4},{1,5},{2,6},{3,7},{4,0},{5,1},{6,2},{7,3},{8,12},{9,13},{10,... | collective-permute-start | bytes 4718600 | tf_op jit(solution)/shard_map/ppermute | solution.py:169
  52.5 17.1 %collective-permute-start.5 = (bf16[192,3072]{1,0:T(8,128)(2,1)}, bf16[192,3072]{1,0:T(8,128)(2,1)}, u32[]{:S(2)}, u32[]{:S(2)}) collective-permute-start(bf16[192,3072]{1,0:T(8,128)(2,1)} %collective-permute-done.3.refs_1_), channel_id=1, source_target_pairs={{8,16},{9,17},{10,18},{11,19},{12,20},{13,21},{14,22},{15,23},{16,... | collective-permute-start | bytes 3538952 | tf_op jit(solution)/shard_map/ppermute | solution.py:169
  54.2 28.6 %collective-permute-start.7 = (bf16[192,3072]{1,0:T(8,128)(2,1)}, bf16[192,3072]{1,0:T(8,128)(2,1)}, u32[]{:S(2)}, u32[]{:S(2)}) collective-permute-start(bf16[192,3072]{1,0:T(8,128)(2,1)} %collective-permute-done.4.refs_4_), channel_id=1, source_target_pairs={{8,0},{9,1},{10,2},{11,3},{12,4},{13,5},{14,6},{15,7},{16,8},{17,9... | collective-permute-start | bytes 3538952 | tf_op jit(solution)/shard_map/ppermute | solution.py:169
  65.2 32.4 %all-to-all-start = ((bf16[4,4,240,256]{3,1,2,0:T(4,128)(2,1)}), bf16[4,4,240,256]{3,1,2,0:T(4,128)(2,1)}, u32[]{:S(2)}, u32[]{:S(2)}) async-start(bf16[4,4,240,256]{3,1,2,0:T(4,128)(2,1)} %pad_maximum_fusion), calls=%async_computation | async-start | bytes 3932160 | tf_op jit(solution)/shard_map/all_to_all | solution.py:441
  69.6 45.9 %collective-permute-start.6 = (bf16[192,3072]{1,0:T(8,128)(2,1)}, bf16[192,3072]{1,0:T(8,128)(2,1)}, u32[]{:S(2)}, u32[]{:S(2)}) collective-permute-start(bf16[192,3072]{1,0:T(8,128)(2,1)} %collective-permute-done.5.refs_2_), channel_id=1, source_target_pairs={{16,24},{17,25},{18,26},{19,27},{20,28},{21,29},{22,30},{23,31}} | collective-permute-start | bytes 3538952 | tf_op jit(solution)/shard_map/ppermute | solution.py:169
  82.8 32.7 %collective-permute-start.8 = (bf16[192,3072]{1,0:T(8,128)(2,1)}, bf16[192,3072]{1,0:T(8,128)(2,1)}, u32[]{:S(2)}, u32[]{:S(2)}) collective-permute-start(bf16[192,3072]{1,0:T(8,128)(2,1)} %collective-permute-done.7.refs_5_), channel_id=1, source_target_pairs={{8,0},{9,1},{10,2},{11,3},{12,4},{13,5},{14,6},{15,7}} | collective-permute-start | bytes 3538952 | tf_op jit(solution)/shard_map/ppermute | solution.py:169
  84.1 47.1 %collective-permute-start.11 = (bf16[256,3072]{1,0:T(8,128)(2,1)}, bf16[256,3072]{1,0:T(8,128)(2,1)}, u32[]{:S(2)}, u32[]{:S(2)}) collective-permute-start(bf16[256,3072]{1,0:T(8,128)(2,1)} %collective-permute-done.1.refs_9_), channel_id=1, source_target_pairs={{0,4},{1,5},{2,6},{3,7},{4,0},{5,1},{6,2},{7,3},{8,12},{9,13},{10,... | collective-permute-start | bytes 4718600 | tf_op jit(solution)/shard_map/ppermute | solution.py:169
  84.4 46.9 %collective-permute-start.12 = (bf16[256,3072]{1,0:T(8,128)(2,1)}, bf16[256,3072]{1,0:T(8,128)(2,1)}, u32[]{:S(2)}, u32[]{:S(2)}) collective-permute-start(bf16[256,3072]{1,0:T(8,128)(2,1)} %collective-permute-done.9.refs_12_), channel_id=1, source_target_pairs={{0,2},{1,3},{2,0},{3,1},{4,6},{5,7},{6,4},{7,5},{8,10},{9,11},{10,... | collective-permute-start | bytes 4718600 | tf_op jit(solution)/shard_map/ppermute | solution.py:169
  100.3 30.9 %copy-start.6 = (bf16[192,3072]{1,0:T(8,128)(2,1)S(1)}, bf16[192,3072]{1,0:T(8,128)(2,1)}, u32[]{:S(2)}) copy-start(bf16[192,3072]{1,0:T(8,128)(2,1)} %copy-done.5) | copy-start | bytes 3538948
  116.3 13.0 %all-to-all-start.2 = ((bf16[4,240,256]{2,1,0:T(8,128)(2,1)}), bf16[4,240,256]{2,1,0:T(8,128)(2,1)}, u32[]{:S(2)}, u32[]{:S(2)}) async-start(bf16[4,240,256]{2,1,0:T(8,128)(2,1)} %broadcast_in_dim.4), calls=%async_computation.2 | async-start | bytes 983040 | tf_op jit(solution)/shard_map/all_to_all | solution.py:446
  149.8 12.4 %collective-permute-start.13 = (bf16[768,1024]{1,0:T(8,128)(2,1)}, bf16[768,1024]{1,0:T(8,128)(2,1)}, u32[]{:S(2)}, u32[]{:S(2)}) collective-permute-start(bf16[768,1024]{1,0:T(8,128)(2,1)} %get-tuple-element.57), channel_id=1, source_target_pairs={{0,1},{1,0},{2,3},{3,2},{4,5},{5,4},{6,7},{7,6},{8,9},{9,8},{10,11... | collective-permute-start | bytes 4718600 | tf_op jit(solution)/shard_map/ppermute | solution.py:169
  158.4 27.3 %all-to-all-start.3 = ((bf16[4,4,240,256]{3,2,1,0:T(8,128)(2,1)}), bf16[4,4,240,256]{3,2,1,0:T(8,128)(2,1)S(1)}, u32[]{:S(2)}, u32[]{:S(2)}) async-start(bf16[4,4,240,256]{3,2,1,0:T(8,128)(2,1)} %broadcast_in_dim.5), calls=%async_computation.3 | async-start | bytes 3932160 | tf_op jit(solution)/shard_map/all_to_all | solution.py:446
  165.5 31.3 %collective-permute-start.14 = (bf16[192,1024]{1,0:T(8,128)(2,1)}, bf16[192,1024]{1,0:T(8,128)(2,1)S(1)}, u32[]{:S(2)}, u32[]{:S(2)}) collective-permute-start(bf16[192,1024]{1,0:T(8,128)(2,1)} %get-tuple-element.67), channel_id=1, source_target_pairs={{0,0},{1,8},{2,2},{3,10},{4,4},{5,12},{6,6},{7,14},{8,16},{9,24},{... | collective-permute-start | bytes 1179656 | tf_op jit(solution)/shard_map/ppermute | solution.py:169
  167.4 31.5 %collective-permute-start.15 = (bf16[192,1024]{1,0:T(8,128)(2,1)}, bf16[192,1024]{1,0:T(8,128)(2,1)S(1)}, u32[]{:S(2)}, u32[]{:S(2)}) collective-permute-start(bf16[192,1024]{1,0:T(8,128)(2,1)} %get-tuple-element.66), channel_id=1, source_target_pairs={{0,8},{1,16},{2,10},{3,18},{4,12},{5,20},{6,14},{7,22},{8,24},{9,0... | collective-permute-start | bytes 1179656 | tf_op jit(solution)/shard_map/ppermute | solution.py:169
  172.0 26.9 %collective-permute-start.16 = (bf16[192,1024]{1,0:T(8,128)(2,1)}, bf16[192,1024]{1,0:T(8,128)(2,1)S(1)}, u32[]{:S(2)}, u32[]{:S(2)}) collective-permute-start(bf16[192,1024]{1,0:T(8,128)(2,1)} %get-tuple-element.65), channel_id=1, source_target_pairs={{0,16},{1,24},{2,18},{3,26},{4,20},{5,28},{6,22},{7,30},{8,0},{9,8... | collective-permute-start | bytes 1179656 | tf_op jit(solution)/shard_map/ppermute | solution.py:169
  172.0 29.6 %collective-permute-start.17 = (bf16[192,1024]{1,0:T(8,128)(2,1)}, bf16[192,1024]{1,0:T(8,128)(2,1)S(1)}, u32[]{:S(2)}, u32[]{:S(2)}) collective-permute-start(bf16[192,1024]{1,0:T(8,128)(2,1)} %get-tuple-element.64), channel_id=1, source_target_pairs={{0,24},{1,0},{2,26},{3,2},{4,28},{5,4},{6,30},{7,6},{8,8},{9,16},{... | collective-permute-start | bytes 1179656 | tf_op jit(solution)/shard_map/ppermute | solution.py:169
  (19 other events, 83.1 us)

commit v9 on v8

--- a/solution.py
+++ b/solution.py
@@ -275,7 +275,7 @@
             pl.BlockSpec((tokens, queries.shape[1] + 2 * key_width), lambda h: (0, 0)),
             pl.BlockSpec((tokens, 3 * rank), lambda h: (0, 0)),
         ),
-        compiler_params=pltpu.CompilerParams(vmem_limit_bytes=32 << 20),
+        compiler_params=pltpu.CompilerParams(vmem_limit_bytes=56 << 20),
         cost_estimate=pl.CostEstimate(
             flops=10 * tokens * tokens * queries.shape[1],
             bytes_accessed=6 * tokens * queries.shape[1],
@@ -295,34 +295,49 @@
 
 
 def term_kernel(place_ref, *refs):
-    blocks, weights, (sent_ref, kept_ref, left, arrived) = refs[:7], refs[7:-4], refs[-4:]
+    blocks, weights = refs[:7], refs[7:-6]
+    sent_ref, kept_ref, left, right, arrived, landed = refs[-6:]
     tokens = blocks[0].shape[0]
-    hi = place_ref[1]
-
-    @pl.when(pl.program_id(0) == 0)
-    def _():
-        for n in range(4):
-            there = left.at[pl.ds(n * tokens, tokens), :]
-            for step, block in zip((0, 1, 2, 3, -1, -2, -3), blocks):
-
-                @pl.when(hi == n + step)
-                def _(block=block, there=there, n=n):
-                    pltpu.make_async_copy(block, there, arrived.at[n]).start()
-
-        for n in range(4):
-            there = left.at[pl.ds(n * tokens, tokens), :]
-            pltpu.make_async_copy(blocks[0], there, arrived.at[n]).wait()
-
-    for turn, out_ref in enumerate((sent_ref, kept_ref)):
-
-        @pl.when(pl.program_id(0) == turn)
-        def _(out_ref=out_ref):
-            width = 2 * weights[0].shape[0]
-            for n in range(len(weights) // 2):
-                right = jnp.concatenate([weights[2 * n][...], weights[2 * n + 1][...]], axis=0)
-                out_ref[:, n * width : (n + 1) * width] = lax.dot_general(
-                    left[...], right, (((1,), (1,)), ((), ())), preferred_element_type=jnp.float32
-                ).astype(jnp.bfloat16)
+    core, hi = place_ref[0], place_ref[1]
+    rows = weights[0].shape[0] // 2
+    pairs = len(weights) // 2
+    steps = [(turn, n) for turn in range(2) for n in range(pairs)]
+
+    def fetch(step):
+        turn, n = steps[step]
+        start = pl.multiple_of(lax.rem(core + 1 - turn, 2) * rows, rows)
+        return [
+            pltpu.make_async_copy(
+                weights[2 * n + part].at[pl.ds(start, rows), :],
+                right.at[step, pl.ds(part * rows, rows), :],
+                landed.at[step, part],
+            )
+            for part in range(2)
+        ]
+
+    for n in range(4):
+        there = left.at[pl.ds(n * tokens, tokens), :]
+        for step, block in zip((0, 1, 2, 3, -1, -2, -3), blocks):
+
+            @pl.when(hi == n + step)
+            def _(block=block, there=there, n=n):
+                pltpu.make_async_copy(block, there, arrived.at[n]).start()
+
+    for copy in fetch(0):
+        copy.start()
+    for n in range(4):
+        there = left.at[pl.ds(n * tokens, tokens), :]
+        pltpu.make_async_copy(blocks[0], there, arrived.at[n]).wait()
+    for step in range(1, len(steps)):
+        for copy in fetch(step):
+            copy.start()
+    for step, (turn, n) in enumerate(steps):
+        for copy in fetch(step):
+            copy.wait()
+        out_ref = (sent_ref, kept_ref)[turn]
+        out_ref[:, n * 2 * rows : (n + 1) * 2 * rows] = lax.dot_general(
+            left[...], right[step], (((1,), (1,)), ((), ())), preferred_element_type=jnp.float32
+        ).astype(jnp.bfloat16)
 
 
 def term_halves(blocks, weights, core, hi):
@@ -333,18 +348,15 @@
     return pl.pallas_call(
         term_kernel,
         out_shape=(out, out),
-        grid_spec=pltpu.PrefetchScalarGridSpec(
-            num_scalar_prefetch=1,
-            grid=(2,),
-            in_specs=[pl.BlockSpec(memory_space=pl.ANY)] * 7
-            + [pl.BlockSpec((rows, depth), lambda i, place: (lax.rem(place[0] + 1 - i, 2), 0))]
-            * count,
-            out_specs=(pl.BlockSpec(out.shape, lambda i, place: (0, 0)),) * 2,
-            scratch_shapes=[
-                pltpu.VMEM((4 * tokens, depth), jnp.bfloat16),
-                pltpu.SemaphoreType.DMA((4,)),
-            ],
-        ),
+        in_specs=[pl.BlockSpec(memory_space=pltpu.SMEM)]
+        + [pl.BlockSpec(memory_space=pl.ANY)] * (7 + count),
+        out_specs=(pl.BlockSpec(memory_space=pltpu.VMEM),) * 2,
+        scratch_shapes=[
+            pltpu.VMEM((4 * tokens, depth), jnp.bfloat16),
+            pltpu.VMEM((count, 2 * rows, depth), jnp.bfloat16),
+            pltpu.SemaphoreType.DMA((4,)),
+            pltpu.SemaphoreType.DMA((count, 2)),
+        ],
         compiler_params=pltpu.CompilerParams(vmem_limit_bytes=40 << 20),
         cost_estimate=pl.CostEstimate(
             flops=16 * tokens * depth * rows * count,
@@ -383,16 +395,52 @@
     )(spots, added, *pieces)
 
 
-def dp_pieces(down_turned, up_local):
-    rank, rows = down_turned.shape
-    width = rows // 16
-    return jnp.concatenate(
-        [
-            down_turned.reshape(rank, 4, 4, width).transpose(2, 1, 0, 3),
-            up_local.reshape(4, 16, -1, width).transpose(2, 0, 1, 3).reshape(4, 4, -1, width),
-        ],
-        axis=2,
-    ).astype(jnp.bfloat16)
+def pieces_kernel(middle_ref, normed_ref, own_ref, out_ref):
+    rank = middle_ref.shape[1] // 2
+    width = out_ref.shape[3]
+    each = (out_ref.shape[2] - rank) // 16
+    heads = own_ref.shape[1] // 6
+
+    def product(left, right):
+        return lax.dot_general(
+            left, right, (((0,), (0,)), ((), ())), preferred_element_type=jnp.float32
+        )
+
+    turned = middle_ref[:, rank:]
+    for hi in range(4):
+        for lo in range(4):
+            start = (hi * 4 + lo) * width
+            down = product(turned, normed_ref[:, start : start + width])
+            out_ref[lo, hi, :rank, :] = down.astype(jnp.bfloat16)
+    for column in range(own_ref.shape[1] // width):
+        which = max(column * width // heads - 3, 0)
+        part = middle_ref[:, which * ADAPTER_RANK : (which + 1) * ADAPTER_RANK]
+        up = adapter_scale * product(part, own_ref[:, column * width : (column + 1) * width])
+        for row in range(4):
+            owner, n = divmod(column * 4 + row, each)
+            lo, hi = divmod(owner, 4)
+            out_ref[lo, hi, rank + n * 16 : rank + (n + 1) * 16, :] = up[
+                row * 16 : (row + 1) * 16
+            ].astype(jnp.bfloat16)
+
+
+def dp_pieces(middle, normed, own):
+    rank = middle.shape[1] // 2
+    width = normed.shape[1] // 16
+    rows = rank + ADAPTER_RANK * own.shape[1] // (16 * width)
+    return pl.pallas_call(
+        pieces_kernel,
+        out_shape=jax.ShapeDtypeStruct((4, 4, rows, width), jnp.bfloat16),
+        in_specs=[pl.BlockSpec(memory_space=pltpu.VMEM)] * 3,
+        out_specs=pl.BlockSpec(memory_space=pltpu.VMEM),
+        compiler_params=pltpu.CompilerParams(vmem_limit_bytes=24 << 20),
+        cost_estimate=pl.CostEstimate(
+            flops=2 * normed.size * rank + 2 * own.size * ADAPTER_RANK,
+            bytes_accessed=2 * (normed.size + own.size) + 32 * rows * width,
+            transcendentals=0,
+        ),
+        name="pieces",
+    )(middle, normed, own)
 
 
 def results_kernel(every_ref, down_ref, query_ref, key_value_ref):
@@ -511,13 +559,7 @@
         middle = after(middle, (x_a, y_a))
         rank = adapter_down_maps.shape[1]
         adapter_middle, middle_gradient = middle[:, :rank], middle[:, rank:]
-        down_turned = lax.dot_general(
-            middle_gradient, normed, (((0,), (0,)), ((), ())), preferred_element_type=jnp.float32
-        )
-        ups = up_gradients(adapter_middle, query_gradient, key_gradient, value_gradient)
-        down_turned, ups = after((down_turned, ups), (right[0], left[0]))
-        up_local = jnp.concatenate(ups, axis=1)
-        column = scatter_sum(dp_pieces(down_turned, up_local), "lo")
+        column = scatter_sum(dp_pieces(middle, normed, own), "lo")
         piece = scatter_sum(after(column, (right[1], left[1])), "hi")
         tokens = own.shape[0]
         source = (hi % 2) * 2 + core

time: 207 us -> 217 us (1.048)
  waiting for transfers between devices: 74.3 us -> 90.4 us
  Pallas kernels: 28.8 us -> 40.7 us
  local copies, waits for them, and re-layouts: 23.6 us -> 13.7 us
  starting transfers between devices: 46.7 us -> 43.5 us
  matrix products: 6.85 us -> 3.73 us
    ppermute x18, waiting for transfers between devices: 46 us -> 61 us  [send(): return lax.ppermute(value, AXES, pairs)]
    pallas_call x1 -> x2, Pallas kernels: 17.4 us -> 26.5 us  [the longest x1 24.4 us: term_halves(): pl.pallas_call(term_kernel, out_shape=(out, out), in_specs=[pl.BlockSpec(...]
    reshape x4 -> x0, local copies, waits for them, and re-layouts: 5.9 us -> none  [the longest x2 4.64 us: dp_pieces(): down_turned.reshape(rank, 4, 4, width).transpose(2, 1, 0, 3)]
    all_to_all x1, waiting for transfers between devices: 12.5 us -> 15.5 us  [scatter_sum(): lax.all_to_all(value, axis, 0, 0)]
    concatenate x2 -> x0, other arithmetic: 2.57 us -> none  [the longest x1 2.54 us: dp_pieces(): jnp.concatenate([down_turned.reshape(rank, 4, 4, width).transpose(2, 1, 0...]
    dot_general x4 -> x0, matrix products: 2.53 us -> none  [the longest x1 1.81 us: shards(): lax.dot_general(middle_gradient, normed, (((0,), (0,)), ((), ())), prefer...]
    unnamed x44 -> x32, local copies, waits for them, and re-layouts: 8.12 us -> 5.63 us
    ppermute x18, starting transfers between devices: 34.3 us -> 32 us  [send(): return lax.ppermute(value, AXES, pairs)]
  transfers between devices with their start and end apart: 21 -> 21, of which waited for: 11 -> 11; matrix products, arithmetic and copies ran while one was open for 14% -> 7% of each run, Pallas kernels for 4% -> 6%
where the time goes in v9:
time: 217 us; the launch traced here: 215 us
  waiting for transfers between devices  90.4 us (42%)
  starting transfers between devices  43.5 us (20%)
  Pallas kernels  40.7 us (19%)
  local copies, waits for them, and re-layouts  13.7 us (6%)
  blocking collectives  13.2 us (6%)
  other arithmetic  8.32 us (4%)
  matrix products  3.73 us (2%)
    ppermute x18, waiting for transfers between devices, send(): return lax.ppermute(value, AXES, pairs)  61 us
    ppermute x18, starting transfers between devices, send(): return lax.ppermute(value, AXES, pairs)  32 us
    pallas_call x1, Pallas kernels, term_halves(): pl.pallas_call(term_kernel, out_shape=(out, out), in_specs=[pl.BlockSpec(...  24.4 us
    all_to_all x1, waiting for transfers between devices, scatter_sum(): lax.all_to_all(value, axis, 0, 0)  15.5 us
    all_to_all x2, waiting for transfers between devices, gather(): lax.all_to_all(jnp.broadcast_to(value[None], (4, *value.shape)), axis, 0, 0)  14 us
    all_to_all x1, blocking collectives, scatter_sum(): lax.all_to_all(value, axis, 0, 0)  13.2 us
    pallas_call x1, Pallas kernels, attention(): pl.pallas_call(attention_kernel, out_shape=(jax.ShapeDtypeStruct((tokens,...  8.89 us
    all_to_all x2, starting transfers between devices, gather(): lax.all_to_all(jnp.broadcast_to(value[None], (4, *value.shape)), axis, 0, 0)  7.07 us
  transfers between devices with their start and end apart: 21, of which 11 were waited for; matrix products, arithmetic and copies ran while one was open for 7% of the time, Pallas kernels for 6%

profile of v9, /device:TPU:1, one launch (start us, length us, event | category | flops | bytes accessed | tf_op | source)
XLA Modules:
  0.0 214.8 jit_solution(14676280840011668645)
XLA Ops:
  0.7 2.9 %fusion.2 = (bf16[256,2048]{1,0:T(8,128)(2,1)}, bf16[256,2048]{1,0:T(8,128)(2,1)S(1)}) fusion(bf16[512,2048]{1,0:T(8,128)(2,1)} %param.18), kind=kLoop, calls=%fused_computation.12 | loop fusion | bytes 4194304 | tf_op jit(solution)/shard_map/slice | solution.py:526
  9.8 8.9 %attention.1 = (bf16[192,3072]{1,0:T(8,128)(2,1)}, f32[192,192]{1,0:T(8,128)}) custom-call(bf16[192,2048]{1,0:T(8,128)(2,1)} %query_ref.1, bf16[192,512]{1,0:T(8,128)(2,1)} %key_ref.1, bf16[192,512]{1,0:T(8,128)(2,1)} %value_ref.1, bf16[192,2048]{1,0:T(8,128)(2,1)} %grad_ref.1, s32[192,1]{1,0:T(8,128)} %copy.17.row_ids, s32[1,192]{1,0:T(1,128)} %column_ids, ...), custom_call_target="tpu_custom_call" | custom-call | flops 754974720 | bytes 2359296 | tf_op jit(solution)/shard_map/attention/pallas_call | solution.py:257
  18.7 4.4 %collective-permute-start.3 = (bf16[192,3072]{1,0:T(8,128)(2,1)}, bf16[192,3072]{1,0:T(8,128)(2,1)}, u32[]{:S(2)}, u32[]{:S(2)}) collective-permute-start(bf16[192,3072]{1,0:T(8,128)(2,1)} %get-tuple-element.41.own_ref.refs_0_), channel_id=1, source_target_pairs={{0,8},{1,9},{2,10},{3,11},{4,12},{5,13},{6,14},{7,15},{8,16},{9,17... | collective-permute-start | bytes 3538952 | tf_op jit(solution)/shard_map/ppermute | solution.py:169
  28.1 14.2 %collective-permute-done.1.refs_9_ = bf16[256,3072]{1,0:T(8,128)(2,1)} collective-permute-done((bf16[256,3072]{1,0:T(8,128)(2,1)}, bf16[256,3072]{1,0:T(8,128)(2,1)}, u32[]{:S(2)}, u32[]{:S(2)}) %collective-permute-start.1) | collective-permute-done | bytes 1572896 | tf_op jit(solution)/shard_map/ppermute | solution.py:169
  46.4 4.8 %collective-permute-done.4.refs_4_ = bf16[192,3072]{1,0:T(8,128)(2,1)} collective-permute-done((bf16[192,3072]{1,0:T(8,128)(2,1)}, bf16[192,3072]{1,0:T(8,128)(2,1)}, u32[]{:S(2)}, u32[]{:S(2)}) %collective-permute-start.4) | collective-permute-done | bytes 1179680 | tf_op jit(solution)/shard_map/ppermute | solution.py:169
  56.5 4.4 %all-to-all-start = ((bf16[4,4,240,256]{3,2,1,0:T(8,128)(2,1)}), bf16[4,4,240,256]{3,2,1,0:T(8,128)(2,1)}, u32[]{:S(2)}, u32[]{:S(2)}) async-start(bf16[4,4,240,256]{3,2,1,0:T(8,128)(2,1)} %pieces.1), calls=%async_computation | async-start | bytes 3932160 | tf_op jit(solution)/shard_map/all_to_all | solution.py:489
  61.7 19.8 %collective-permute-done.7.refs_5_ = bf16[192,3072]{1,0:T(8,128)(2,1)} collective-permute-done((bf16[192,3072]{1,0:T(8,128)(2,1)}, bf16[192,3072]{1,0:T(8,128)(2,1)}, u32[]{:S(2)}, u32[]{:S(2)}) %collective-permute-start.7) | collective-permute-done | bytes 1179680 | tf_op jit(solution)/shard_map/ppermute | solution.py:169
  83.4 15.5 %all-to-all-done = bf16[4,4,240,256]{3,2,1,0:T(8,128)(2,1)} async-done(((bf16[4,4,240,256]{3,2,1,0:T(8,128)(2,1)}), bf16[4,4,240,256]{3,2,1,0:T(8,128)(2,1)}, u32[]{:S(2)}, u32[]{:S(2)}) %all-to-all-start) | async-done | bytes 1966112 | tf_op jit(solution)/shard_map/all_to_all | solution.py:489
  98.9 2.7 %reduce_sum.24 = bf16[4,240,256]{2,1,0:T(8,128)(2,1)} reduce(bf16[4,4,240,256]{3,2,1,0:T(8,128)(2,1)} %all-to-all-done, bf16[]{:T(256)} %constant.298.clone.1), dimensions={0}, to_apply=%region_0.0 | reduce | flops 737280 | bytes 2457602 | tf_op jit(solution)/shard_map/reduce_sum | solution.py:488
  101.6 13.2 %all_to_all.20 = bf16[4,240,256]{2,1,0:T(8,128)(2,1)S(1)} all-to-all(bf16[4,240,256]{2,1,0:T(8,128)(2,1)} %reduce_sum.24), channel_id=1, replica_groups=mesh['hi'=4,'lo'=4,'tensor'=2] {'hi'}, dimensions={0} | all-to-all | bytes 983040 | tf_op jit(solution)/shard_map/all_to_all | solution.py:489
  115.8 3.5 %all-to-all-start.2 = ((bf16[4,240,256]{2,1,0:T(8,128)(2,1)}), bf16[4,240,256]{2,1,0:T(8,128)(2,1)S(1)}, u32[]{:S(2)}, u32[]{:S(2)}) async-start(bf16[4,240,256]{2,1,0:T(8,128)(2,1)} %broadcast_in_dim.4), calls=%async_computation.2 | async-start | bytes 983040 | tf_op jit(solution)/shard_map/all_to_all | solution.py:494
  119.3 8.7 %all-to-all-done.2 = bf16[4,240,256]{2,1,0:T(8,128)(2,1)S(1)} async-done(((bf16[4,240,256]{2,1,0:T(8,128)(2,1)}), bf16[4,240,256]{2,1,0:T(8,128)(2,1)S(1)}, u32[]{:S(2)}, u32[]{:S(2)}) %all-to-all-start.2) | async-done | bytes 491552 | tf_op jit(solution)/shard_map/all_to_all | solution.py:494
  128.0 4.6 %collective-permute-done.11.refs_13_ = bf16[256,3072]{1,0:T(8,128)(2,1)} collective-permute-done((bf16[256,3072]{1,0:T(8,128)(2,1)}, bf16[256,3072]{1,0:T(8,128)(2,1)}, u32[]{:S(2)}, u32[]{:S(2)}) %collective-permute-start.11) | collective-permute-done | bytes 1572896 | tf_op jit(solution)/shard_map/ppermute | solution.py:169
  135.1 24.4 %term.1 = (bf16[768,1024]{1,0:T(8,128)(2,1)}, bf16[768,1024]{1,0:T(8,128)(2,1)S(1)}) custom-call(s32[2]{0:T(128)S(1)} %pad_add_fusion.place_ref, bf16[192,3072]{1,0:T(8,128)(2,1)S(1)} %copy-done.5, bf16[192,3072]{1,0:T(8,128)(2,1)} %collective-permute-done.3.refs_1_, bf16[192,3072]{1,0:T(8,128)(2,1)} %collective-permute-done.5.refs_2_, ...), custom_call_target="tpu_custom_call" | custom-call | flops 9663676416 | bytes 20447232 | tf_op jit(solution)/shard_map/term/pallas_call | solution.py:348
  160.7 3.5 %collective-permute-start.13 = (bf16[768,1024]{1,0:T(8,128)(2,1)}, bf16[768,1024]{1,0:T(8,128)(2,1)}, u32[]{:S(2)}, u32[]{:S(2)}) collective-permute-start(bf16[768,1024]{1,0:T(8,128)(2,1)} %get-tuple-element.49), channel_id=1, source_target_pairs={{0,1},{1,0},{2,3},{3,2},{4,5},{5,4},{6,7},{7,6},{8,9},{9,8},{10,11... | collective-permute-start | bytes 4718600 | tf_op jit(solution)/shard_map/ppermute | solution.py:169
  165.6 3.6 %all-to-all-start.3 = ((bf16[4,4,240,256]{3,2,1,0:T(8,128)(2,1)}), bf16[4,4,240,256]{3,2,1,0:T(8,128)(2,1)S(1)}, u32[]{:S(2)}, u32[]{:S(2)}) async-start(bf16[4,4,240,256]{3,2,1,0:T(8,128)(2,1)} %broadcast_in_dim.5), calls=%async_computation.3 | async-start | bytes 3932160 | tf_op jit(solution)/shard_map/all_to_all | solution.py:494
  169.3 2.5 %add_convert_fusion = bf16[768,1024]{1,0:T(8,128)(2,1)S(1)} fusion(bf16[768,1024]{1,0:T(8,128)(2,1)} %collective-permute-done.13, bf16[768,1024]{1,0:T(8,128)(2,1)} %copy-done.3), kind=kLoop, calls=%fused_computation | loop fusion | flops 3145728 | bytes 4718592 | tf_op jit(solution)/shard_map/convert_element_type | solution.py:574
  175.1 4.4 %collective-permute-start.15 = (bf16[192,1024]{1,0:T(8,128)(2,1)}, bf16[192,1024]{1,0:T(8,128)(2,1)}, u32[]{:S(2)}, u32[]{:S(2)}) collective-permute-start(bf16[192,1024]{1,0:T(8,128)(2,1)} %get-tuple-element.58), channel_id=1, source_target_pairs={{0,8},{1,16},{2,10},{3,18},{4,12},{5,20},{6,14},{7,22},{8,24},{9,0... | collective-permute-start | bytes 1179656 | tf_op jit(solution)/shard_map/ppermute | solution.py:169
  179.5 2.5 %collective-permute-start.16 = (bf16[192,1024]{1,0:T(8,128)(2,1)}, bf16[192,1024]{1,0:T(8,128)(2,1)}, u32[]{:S(2)}, u32[]{:S(2)}) collective-permute-start(bf16[192,1024]{1,0:T(8,128)(2,1)} %get-tuple-element.57), channel_id=1, source_target_pairs={{0,16},{1,24},{2,18},{3,26},{4,20},{5,28},{6,22},{7,30},{8,0},{9,8... | collective-permute-start | bytes 1179656 | tf_op jit(solution)/shard_map/ppermute | solution.py:169
  184.3 3.1 %fusion.added_ref = f32[192,4096]{1,0:T(8,128)} fusion(bf16[4096,192]{0,1:T(8,128)(2,1)S(1)} %copy-done, bf16[192,384]{1,0:T(8,128)(2,1)} %copy-done.6), kind=kOutput, calls=%fused_computation.9 | convolution fusion | flops 301989888 | bytes 4816896 | tf_op jit(solution)/shard_map/dot_general | solution.py:56
  187.4 5.3 %all-to-all-done.3.every_ref = bf16[4,4,240,256]{3,2,1,0:T(8,128)(2,1)S(1)} async-done(((bf16[4,4,240,256]{3,2,1,0:T(8,128)(2,1)}), bf16[4,4,240,256]{3,2,1,0:T(8,128)(2,1)S(1)}, u32[]{:S(2)}, u32[]{:S(2)}) %all-to-all-start.3) | async-done | bytes 1966112 | tf_op jit(solution)/shard_map/all_to_all | solution.py:494
  192.7 11.7 %collective-permute-done.14.refs_0_ = bf16[192,1024]{1,0:T(8,128)(2,1)} collective-permute-done((bf16[192,1024]{1,0:T(8,128)(2,1)}, bf16[192,1024]{1,0:T(8,128)(2,1)}, u32[]{:S(2)}, u32[]{:S(2)}) %collective-permute-start.14) | collective-permute-done | bytes 393248 | tf_op jit(solution)/shard_map/ppermute | solution.py:169
  206.5 3.2 %collective-permute-done.17.refs_3_ = bf16[192,1024]{1,0:T(8,128)(2,1)} collective-permute-done((bf16[192,1024]{1,0:T(8,128)(2,1)}, bf16[192,1024]{1,0:T(8,128)(2,1)}, u32[]{:S(2)}, u32[]{:S(2)}) %collective-permute-start.17) | collective-permute-done | bytes 393248 | tf_op jit(solution)/shard_map/ppermute | solution.py:169
  211.6 3.2 %finish.1 = bf16[192,4096]{1,0:T(8,128)(2,1)} custom-call(s32[32]{0:T(128)S(1)} %stack.140.spot_ref, f32[192,4096]{1,0:T(8,128)S(1)} %copy-done.1, bf16[192,1024]{1,0:T(8,128)(2,1)} %collective-permute-done.14.refs_0_, bf16[192,1024]{1,0:T(8,128)(2,1)} %collective-permute-done.15.refs_1_, bf16[192,1024]{1,0:T(8,128)(2,1)} %collective-permute-done.16.refs_2_, ...), custom_call_target="tpu_custom_call" | custom-call | flops 786432 | bytes 6291456 | tf_op jit(solution)/shard_map/finish/pallas_call | solution.py:384
  (73 shorter events, 38.4 us)
Async XLA Ops:
  0.6 23.7 %copy-start = (bf16[4096,192]{0,1:T(8,128)(2,1)S(1)}, bf16[4096,192]{0,1:T(8,128)(2,1)}, u32[]{:S(2)}) copy-start(bf16[4096,192]{0,1:T(8,128)(2,1)} %param.21) | copy-start | bytes 4718596
  5.7 18.6 %copy-start.2 = (bf16[192,4096]{1,0:T(8,128)(2,1)S(1)}, bf16[192,4096]{1,0:T(8,128)(2,1)}, u32[]{:S(2)}) copy-start(bf16[192,4096]{1,0:T(8,128)(2,1)} %normed_ref.1) | copy-start | bytes 4718596
  5.7 36.5 %collective-permute-start.1 = (bf16[256,3072]{1,0:T(8,128)(2,1)}, bf16[256,3072]{1,0:T(8,128)(2,1)}, u32[]{:S(2)}, u32[]{:S(2)}) collective-permute-start(bf16[256,3072]{1,0:T(8,128)(2,1)} %pad_maximum_fusion.refs_7_), channel_id=1, source_target_pairs={{0,2},{1,3},{2,0},{3,1},{4,6},{5,7},{6,4},{7,5},{8,10},{9,11},{10,... | collective-permute-start | bytes 4718600 | tf_op jit(solution)/shard_map/ppermute | solution.py:169
  7.8 35.3 %collective-permute-start.2 = (bf16[256,3072]{1,0:T(8,128)(2,1)}, bf16[256,3072]{1,0:T(8,128)(2,1)}, u32[]{:S(2)}, u32[]{:S(2)}) collective-permute-start(bf16[256,3072]{1,0:T(8,128)(2,1)} %pad_maximum_fusion.refs_7_), channel_id=1, source_target_pairs={{0,4},{1,5},{2,6},{3,7},{4,0},{5,1},{6,2},{7,3},{8,12},{9,13},{10,... | collective-permute-start | bytes 4718600 | tf_op jit(solution)/shard_map/ppermute | solution.py:169
  18.7 27.7 %collective-permute-start.3 = (bf16[192,3072]{1,0:T(8,128)(2,1)}, bf16[192,3072]{1,0:T(8,128)(2,1)}, u32[]{:S(2)}, u32[]{:S(2)}) collective-permute-start(bf16[192,3072]{1,0:T(8,128)(2,1)} %get-tuple-element.41.own_ref.refs_0_), channel_id=1, source_target_pairs={{0,8},{1,9},{2,10},{3,11},{4,12},{5,13},{6,14},{7,15},{8,16},{9,17... | collective-permute-start | bytes 3538952 | tf_op jit(solution)/shard_map/ppermute | solution.py:169
  23.1 28.1 %collective-permute-start.4 = (bf16[192,3072]{1,0:T(8,128)(2,1)}, bf16[192,3072]{1,0:T(8,128)(2,1)}, u32[]{:S(2)}, u32[]{:S(2)}) collective-permute-start(bf16[192,3072]{1,0:T(8,128)(2,1)} %get-tuple-element.41.own_ref.refs_0_), channel_id=1, source_target_pairs={{8,0},{9,1},{10,2},{11,3},{12,4},{13,5},{14,6},{15,7},{16,8},{17,9... | collective-permute-start | bytes 3538952 | tf_op jit(solution)/shard_map/ppermute | solution.py:169
  25.1 29.1 %collective-permute-start = (f32[192,384]{1,0:T(8,128)S(1)}, f32[192,384]{1,0:T(8,128)S(1)}, u32[]{:S(2)}, u32[]{:S(2)}) collective-permute-start(f32[192,384]{1,0:T(8,128)S(1)} %pad_maximum_fusion.2), channel_id=1, source_target_pairs={{0,1},{1,0},{2,3},{3,2},{4,5},{5,4},{6,7},{7,6},{8,9},{9,8},{10,11... | collective-permute-start | bytes 884744 | tf_op jit(solution)/shard_map/ppermute | solution.py:169
  26.7 27.6 %copy-start.4 = (bf16[192,3072]{1,0:T(8,128)(2,1)S(1)}, bf16[192,3072]{1,0:T(8,128)(2,1)}, u32[]{:S(2)}) copy-start(bf16[192,3072]{1,0:T(8,128)(2,1)} %get-tuple-element.41.own_ref.refs_0_) | copy-start | bytes 3538948
  43.1 39.7 %collective-permute-start.10 = (bf16[256,3072]{1,0:T(8,128)(2,1)}, bf16[256,3072]{1,0:T(8,128)(2,1)}, u32[]{:S(2)}, u32[]{:S(2)}) collective-permute-start(bf16[256,3072]{1,0:T(8,128)(2,1)} %pad_maximum_fusion.1.refs_8_), channel_id=1, source_target_pairs={{0,2},{1,3},{2,0},{3,1},{4,6},{5,7},{6,4},{7,5},{8,10},{9,11},{10,... | collective-permute-start | bytes 4718600 | tf_op jit(solution)/shard_map/ppermute | solution.py:169
  43.4 39.4 %collective-permute-start.9 = (bf16[256,3072]{1,0:T(8,128)(2,1)}, bf16[256,3072]{1,0:T(8,128)(2,1)}, u32[]{:S(2)}, u32[]{:S(2)}) collective-permute-start(bf16[256,3072]{1,0:T(8,128)(2,1)} %pad_maximum_fusion.1.refs_8_), channel_id=1, source_target_pairs={{0,4},{1,5},{2,6},{3,7},{4,0},{5,1},{6,2},{7,3},{8,12},{9,13},{10,... | collective-permute-start | bytes 4718600 | tf_op jit(solution)/shard_map/ppermute | solution.py:169
  51.2 9.7 %collective-permute-start.5 = (bf16[192,3072]{1,0:T(8,128)(2,1)}, bf16[192,3072]{1,0:T(8,128)(2,1)}, u32[]{:S(2)}, u32[]{:S(2)}) collective-permute-start(bf16[192,3072]{1,0:T(8,128)(2,1)} %collective-permute-done.3.refs_1_), channel_id=1, source_target_pairs={{8,16},{9,17},{10,18},{11,19},{12,20},{13,21},{14,22},{15,23},{16,... | collective-permute-start | bytes 3538952 | tf_op jit(solution)/shard_map/ppermute | solution.py:169
  52.9 28.6 %collective-permute-start.7 = (bf16[192,3072]{1,0:T(8,128)(2,1)}, bf16[192,3072]{1,0:T(8,128)(2,1)}, u32[]{:S(2)}, u32[]{:S(2)}) collective-permute-start(bf16[192,3072]{1,0:T(8,128)(2,1)} %collective-permute-done.4.refs_4_), channel_id=1, source_target_pairs={{8,0},{9,1},{10,2},{11,3},{12,4},{13,5},{14,6},{15,7},{16,8},{17,9... | collective-permute-start | bytes 3538952 | tf_op jit(solution)/shard_map/ppermute | solution.py:169
  56.5 42.4 %all-to-all-start = ((bf16[4,4,240,256]{3,2,1,0:T(8,128)(2,1)}), bf16[4,4,240,256]{3,2,1,0:T(8,128)(2,1)}, u32[]{:S(2)}, u32[]{:S(2)}) async-start(bf16[4,4,240,256]{3,2,1,0:T(8,128)(2,1)} %pieces.1), calls=%async_computation | async-start | bytes 3932160 | tf_op jit(solution)/shard_map/all_to_all | solution.py:489
  60.9 53.9 %collective-permute-start.6 = (bf16[192,3072]{1,0:T(8,128)(2,1)}, bf16[192,3072]{1,0:T(8,128)(2,1)S(1)}, u32[]{:S(2)}, u32[]{:S(2)}) collective-permute-start(bf16[192,3072]{1,0:T(8,128)(2,1)} %collective-permute-done.5.refs_2_), channel_id=1, source_target_pairs={{16,24},{17,25},{18,26},{19,27},{20,28},{21,29},{22,30},{23,31}} | collective-permute-start | bytes 3538952 | tf_op jit(solution)/shard_map/ppermute | solution.py:169
  81.5 33.4 %collective-permute-start.8 = (bf16[192,3072]{1,0:T(8,128)(2,1)}, bf16[192,3072]{1,0:T(8,128)(2,1)}, u32[]{:S(2)}, u32[]{:S(2)}) collective-permute-start(bf16[192,3072]{1,0:T(8,128)(2,1)} %collective-permute-done.7.refs_5_), channel_id=1, source_target_pairs={{8,0},{9,1},{10,2},{11,3},{12,4},{13,5},{14,6},{15,7}} | collective-permute-start | bytes 3538952 | tf_op jit(solution)/shard_map/ppermute | solution.py:169
  82.8 49.8 %collective-permute-start.11 = (bf16[256,3072]{1,0:T(8,128)(2,1)}, bf16[256,3072]{1,0:T(8,128)(2,1)}, u32[]{:S(2)}, u32[]{:S(2)}) collective-permute-start(bf16[256,3072]{1,0:T(8,128)(2,1)} %collective-permute-done.1.refs_9_), channel_id=1, source_target_pairs={{0,4},{1,5},{2,6},{3,7},{4,0},{5,1},{6,2},{7,3},{8,12},{9,13},{10,... | collective-permute-start | bytes 4718600 | tf_op jit(solution)/shard_map/ppermute | solution.py:169
  83.1 49.5 %collective-permute-start.12 = (bf16[256,3072]{1,0:T(8,128)(2,1)}, bf16[256,3072]{1,0:T(8,128)(2,1)}, u32[]{:S(2)}, u32[]{:S(2)}) collective-permute-start(bf16[256,3072]{1,0:T(8,128)(2,1)} %collective-permute-done.9.refs_12_), channel_id=1, source_target_pairs={{0,2},{1,3},{2,0},{3,1},{4,6},{5,7},{6,4},{7,5},{8,10},{9,11},{10,... | collective-permute-start | bytes 4718600 | tf_op jit(solution)/shard_map/ppermute | solution.py:169
  115.8 12.2 %all-to-all-start.2 = ((bf16[4,240,256]{2,1,0:T(8,128)(2,1)}), bf16[4,240,256]{2,1,0:T(8,128)(2,1)S(1)}, u32[]{:S(2)}, u32[]{:S(2)}) async-start(bf16[4,240,256]{2,1,0:T(8,128)(2,1)} %broadcast_in_dim.4), calls=%async_computation.2 | async-start | bytes 983040 | tf_op jit(solution)/shard_map/all_to_all | solution.py:494
  160.7 8.6 %collective-permute-start.13 = (bf16[768,1024]{1,0:T(8,128)(2,1)}, bf16[768,1024]{1,0:T(8,128)(2,1)}, u32[]{:S(2)}, u32[]{:S(2)}) collective-permute-start(bf16[768,1024]{1,0:T(8,128)(2,1)} %get-tuple-element.49), channel_id=1, source_target_pairs={{0,1},{1,0},{2,3},{3,2},{4,5},{5,4},{6,7},{7,6},{8,9},{9,8},{10,11... | collective-permute-start | bytes 4718600 | tf_op jit(solution)/shard_map/ppermute | solution.py:169
  165.6 27.1 %all-to-all-start.3 = ((bf16[4,4,240,256]{3,2,1,0:T(8,128)(2,1)}), bf16[4,4,240,256]{3,2,1,0:T(8,128)(2,1)S(1)}, u32[]{:S(2)}, u32[]{:S(2)}) async-start(bf16[4,4,240,256]{3,2,1,0:T(8,128)(2,1)} %broadcast_in_dim.5), calls=%async_computation.3 | async-start | bytes 3932160 | tf_op jit(solution)/shard_map/all_to_all | solution.py:494
  173.0 31.4 %collective-permute-start.14 = (bf16[192,1024]{1,0:T(8,128)(2,1)}, bf16[192,1024]{1,0:T(8,128)(2,1)}, u32[]{:S(2)}, u32[]{:S(2)}) collective-permute-start(bf16[192,1024]{1,0:T(8,128)(2,1)} %get-tuple-element.59), channel_id=1, source_target_pairs={{0,0},{1,8},{2,2},{3,10},{4,4},{5,12},{6,6},{7,14},{8,16},{9,24},{... | collective-permute-start | bytes 1179656 | tf_op jit(solution)/shard_map/ppermute | solution.py:169
  175.1 31.5 %collective-permute-start.15 = (bf16[192,1024]{1,0:T(8,128)(2,1)}, bf16[192,1024]{1,0:T(8,128)(2,1)}, u32[]{:S(2)}, u32[]{:S(2)}) collective-permute-start(bf16[192,1024]{1,0:T(8,128)(2,1)} %get-tuple-element.58), channel_id=1, source_target_pairs={{0,8},{1,16},{2,10},{3,18},{4,12},{5,20},{6,14},{7,22},{8,24},{9,0... | collective-permute-start | bytes 1179656 | tf_op jit(solution)/shard_map/ppermute | solution.py:169
  179.5 27.0 %collective-permute-start.16 = (bf16[192,1024]{1,0:T(8,128)(2,1)}, bf16[192,1024]{1,0:T(8,128)(2,1)}, u32[]{:S(2)}, u32[]{:S(2)}) collective-permute-start(bf16[192,1024]{1,0:T(8,128)(2,1)} %get-tuple-element.57), channel_id=1, source_target_pairs={{0,16},{1,24},{2,18},{3,26},{4,20},{5,28},{6,22},{7,30},{8,0},{9,8... | collective-permute-start | bytes 1179656 | tf_op jit(solution)/shard_map/ppermute | solution.py:169
  182.0 27.7 %collective-permute-start.17 = (bf16[192,1024]{1,0:T(8,128)(2,1)}, bf16[192,1024]{1,0:T(8,128)(2,1)}, u32[]{:S(2)}, u32[]{:S(2)}) collective-permute-start(bf16[192,1024]{1,0:T(8,128)(2,1)} %get-tuple-element.56), channel_id=1, source_target_pairs={{0,24},{1,0},{2,26},{3,2},{4,28},{5,4},{6,30},{7,6},{8,8},{9,16},{... | collective-permute-start | bytes 1179656 | tf_op jit(solution)/shard_map/ppermute | solution.py:169
  (13 other events, 66.2 us)

commit v10 on v8

--- a/solution.py
+++ b/solution.py
@@ -275,7 +275,7 @@
             pl.BlockSpec((tokens, queries.shape[1] + 2 * key_width), lambda h: (0, 0)),
             pl.BlockSpec((tokens, 3 * rank), lambda h: (0, 0)),
         ),
-        compiler_params=pltpu.CompilerParams(vmem_limit_bytes=32 << 20),
+        compiler_params=pltpu.CompilerParams(vmem_limit_bytes=56 << 20),
         cost_estimate=pl.CostEstimate(
             flops=10 * tokens * tokens * queries.shape[1],
             bytes_accessed=6 * tokens * queries.shape[1],
@@ -383,16 +383,52 @@
     )(spots, added, *pieces)
 
 
-def dp_pieces(down_turned, up_local):
-    rank, rows = down_turned.shape
-    width = rows // 16
-    return jnp.concatenate(
-        [
-            down_turned.reshape(rank, 4, 4, width).transpose(2, 1, 0, 3),
-            up_local.reshape(4, 16, -1, width).transpose(2, 0, 1, 3).reshape(4, 4, -1, width),
-        ],
-        axis=2,
-    ).astype(jnp.bfloat16)
+def pieces_kernel(middle_ref, normed_ref, own_ref, out_ref):
+    rank = middle_ref.shape[1] // 2
+    width = out_ref.shape[3]
+    each = (out_ref.shape[2] - rank) // 16
+    heads = own_ref.shape[1] // 6
+
+    def product(left, right):
+        return lax.dot_general(
+            left, right, (((0,), (0,)), ((), ())), preferred_element_type=jnp.float32
+        )
+
+    turned = middle_ref[:, rank:]
+    for hi in range(4):
+        for lo in range(4):
+            start = (hi * 4 + lo) * width
+            down = product(turned, normed_ref[:, start : start + width])
+            out_ref[lo, hi, :rank, :] = down.astype(jnp.bfloat16)
+    for column in range(own_ref.shape[1] // width):
+        which = max(column * width // heads - 3, 0)
+        part = middle_ref[:, which * ADAPTER_RANK : (which + 1) * ADAPTER_RANK]
+        up = adapter_scale * product(part, own_ref[:, column * width : (column + 1) * width])
+        for row in range(4):
+            owner, n = divmod(column * 4 + row, each)
+            lo, hi = divmod(owner, 4)
+            out_ref[lo, hi, rank + n * 16 : rank + (n + 1) * 16, :] = up[
+                row * 16 : (row + 1) * 16
+            ].astype(jnp.bfloat16)
+
+
+def dp_pieces(middle, normed, own):
+    rank = middle.shape[1] // 2
+    width = normed.shape[1] // 16
+    rows = rank + ADAPTER_RANK * own.shape[1] // (16 * width)
+    return pl.pallas_call(
+        pieces_kernel,
+        out_shape=jax.ShapeDtypeStruct((4, 4, rows, width), jnp.bfloat16),
+        in_specs=[pl.BlockSpec(memory_space=pltpu.VMEM)] * 3,
+        out_specs=pl.BlockSpec(memory_space=pltpu.VMEM),
+        compiler_params=pltpu.CompilerParams(vmem_limit_bytes=24 << 20),
+        cost_estimate=pl.CostEstimate(
+            flops=2 * normed.size * rank + 2 * own.size * ADAPTER_RANK,
+            bytes_accessed=2 * (normed.size + own.size) + 32 * rows * width,
+            transcendentals=0,
+        ),
+        name="pieces",
+    )(middle, normed, own)
 
 
 def results_kernel(every_ref, down_ref, query_ref, key_value_ref):
@@ -495,11 +531,6 @@
         query_gradient = own[:, :q_width]
         key_gradient = own[:, q_width : q_width + k_width]
         value_gradient = own[:, q_width + k_width :]
-        right, left = chain_hi(own, (x_a, y_a))
-        blocks = (own, *right, *left)
-        from_a, from_b = after((x_a, y_b), (x_b, right[1], left[1]))
-        weights = (own_a, own_b, x_a, x_b, y_a, y_b, swap_lo(from_a, 2), swap_lo(from_b, 1))
-
         middle_local = jnp.concatenate(
             [
                 jnp.dot(normed, adapter_down_maps, preferred_element_type=jnp.float32),
@@ -508,16 +539,15 @@
             axis=1,
         )
         middle = (middle_local + swap_core(middle_local)).astype(jnp.bfloat16)
-        middle = after(middle, (x_a, y_a))
         rank = adapter_down_maps.shape[1]
         adapter_middle, middle_gradient = middle[:, :rank], middle[:, rank:]
-        down_turned = lax.dot_general(
-            middle_gradient, normed, (((0,), (0,)), ((), ())), preferred_element_type=jnp.float32
-        )
-        ups = up_gradients(adapter_middle, query_gradient, key_gradient, value_gradient)
-        down_turned, ups = after((down_turned, ups), (right[0], left[0]))
-        up_local = jnp.concatenate(ups, axis=1)
-        column = scatter_sum(dp_pieces(down_turned, up_local), "lo")
+        laid = dp_pieces(middle, normed, own)
+        right, left = chain_hi(own, (x_a, y_a, laid))
+        blocks = (own, *right, *left)
+        from_a, from_b = after((x_a, y_b), (x_b, right[1], left[1]))
+        weights = (own_a, own_b, x_a, x_b, y_a, y_b, swap_lo(from_a, 2), swap_lo(from_b, 1))
+
+        column = scatter_sum(laid, "lo")
         piece = scatter_sum(after(column, (right[1], left[1])), "hi")
         tokens = own.shape[0]
         source = (hi % 2) * 2 + core

time: 207 us -> 210 us (1.014)
  waiting for transfers between devices: 74.3 us -> 90.6 us
  local copies, waits for them, and re-layouts: 23.6 us -> 13.6 us
  Pallas kernels: 28.8 us -> 34.2 us
  matrix products: 6.85 us -> 3.75 us
  starting transfers between devices: 46.7 us -> 43.7 us
    ppermute x18, waiting for transfers between devices: 46 us -> 59.8 us  [send(): return lax.ppermute(value, AXES, pairs)]
    reshape x4 -> x0, local copies, waits for them, and re-layouts: 5.9 us -> none  [the longest x2 4.64 us: dp_pieces(): down_turned.reshape(rank, 4, 4, width).transpose(2, 1, 0, 3)]
    all_to_all x1, waiting for transfers between devices: 12.5 us -> 16.5 us  [scatter_sum(): lax.all_to_all(value, axis, 0, 0)]
    concatenate x2 -> x0, other arithmetic: 2.57 us -> none  [the longest x1 2.54 us: dp_pieces(): jnp.concatenate([down_turned.reshape(rank, 4, 4, width).transpose(2, 1, 0...]
    dot_general x4 -> x0, matrix products: 2.53 us -> none  [the longest x1 1.81 us: shards(): lax.dot_general(middle_gradient, normed, (((0,), (0,)), ((), ())), prefer...]
    unnamed x44 -> x36, local copies, waits for them, and re-layouts: 8.12 us -> 5.63 us
    ppermute x18, starting transfers between devices: 34.3 us -> 32 us  [send(): return lax.ppermute(value, AXES, pairs)]
    pallas_call x0 -> x1, Pallas kernels: none -> 2.13 us  [dp_pieces(): pl.pallas_call(pieces_kernel, out_shape=jax.ShapeDtypeStruct((4, 4, rows,...]
  transfers between devices with their start and end apart: 21 -> 21, of which waited for: 11 -> 10; matrix products, arithmetic and copies ran while one was open for 14% -> 7% of each run, Pallas kernels for 4% -> 6%
where the time goes in v10:
time: 210 us; the launch traced here: 209 us
  waiting for transfers between devices  90.6 us (43%)
  starting transfers between devices  43.7 us (21%)
  Pallas kernels  34.2 us (16%)
  local copies, waits for them, and re-layouts  13.6 us (6%)
  blocking collectives  13.1 us (6%)
  other arithmetic  8.31 us (4%)
  matrix products  3.75 us (2%)
    ppermute x18, waiting for transfers between devices, send(): return lax.ppermute(value, AXES, pairs)  59.8 us
    ppermute x18, starting transfers between devices, send(): return lax.ppermute(value, AXES, pairs)  32 us
    pallas_call x1, Pallas kernels, term_halves(): pl.pallas_call(term_kernel, out_shape=(out, out), grid_spec=pltpu.Prefetc...  17.9 us
    all_to_all x1, waiting for transfers between devices, scatter_sum(): lax.all_to_all(value, axis, 0, 0)  16.5 us
    all_to_all x2, waiting for transfers between devices, gather(): lax.all_to_all(jnp.broadcast_to(value[None], (4, *value.shape)), axis, 0, 0)  14.4 us
    all_to_all x1, blocking collectives, scatter_sum(): lax.all_to_all(value, axis, 0, 0)  13.1 us
    pallas_call x1, Pallas kernels, attention(): pl.pallas_call(attention_kernel, out_shape=(jax.ShapeDtypeStruct((tokens,...  8.9 us
    all_to_all x2, starting transfers between devices, gather(): lax.all_to_all(jnp.broadcast_to(value[None], (4, *value.shape)), axis, 0, 0)  7.25 us
  transfers between devices with their start and end apart: 21, of which 10 were waited for; matrix products, arithmetic and copies ran while one was open for 7% of the time, Pallas kernels for 6%

profile of v10, /device:TPU:1, one launch (start us, length us, event | category | flops | bytes accessed | tf_op | source)
XLA Modules:
  0.0 208.5 jit_solution(10768732464634514868)
XLA Ops:
  0.7 2.9 %fusion.2 = (bf16[256,2048]{1,0:T(8,128)(2,1)}, bf16[256,2048]{1,0:T(8,128)(2,1)S(1)}) fusion(bf16[512,2048]{1,0:T(8,128)(2,1)} %param.18), kind=kLoop, calls=%fused_computation.12 | loop fusion | bytes 4194304 | tf_op jit(solution)/shard_map/slice | solution.py:514
  9.8 8.9 %attention.1 = (bf16[192,3072]{1,0:T(8,128)(2,1)}, f32[192,192]{1,0:T(8,128)}) custom-call(bf16[192,2048]{1,0:T(8,128)(2,1)} %query_ref.1, bf16[192,512]{1,0:T(8,128)(2,1)} %key_ref.1, bf16[192,512]{1,0:T(8,128)(2,1)} %value_ref.1, bf16[192,2048]{1,0:T(8,128)(2,1)} %grad_ref.1, s32[192,1]{1,0:T(8,128)} %copy.17.row_ids, s32[1,192]{1,0:T(1,128)} %column_ids, ...), custom_call_target="tpu_custom_call" | custom-call | flops 754974720 | bytes 2359296 | tf_op jit(solution)/shard_map/attention/pallas_call | solution.py:257
  18.7 4.4 %collective-permute-start.1 = (bf16[192,3072]{1,0:T(8,128)(2,1)}, bf16[192,3072]{1,0:T(8,128)(2,1)}, u32[]{:S(2)}, u32[]{:S(2)}) collective-permute-start(bf16[192,3072]{1,0:T(8,128)(2,1)} %get-tuple-element.39.own_ref.refs_0_), channel_id=1, source_target_pairs={{0,8},{1,9},{2,10},{3,11},{4,12},{5,13},{6,14},{7,15},{8,16},{9,17... | collective-permute-start | bytes 3538952 | tf_op jit(solution)/shard_map/ppermute | solution.py:169
  28.0 14.2 %collective-permute-done.3.refs_9_ = bf16[256,3072]{1,0:T(8,128)(2,1)} collective-permute-done((bf16[256,3072]{1,0:T(8,128)(2,1)}, bf16[256,3072]{1,0:T(8,128)(2,1)}, u32[]{:S(2)}, u32[]{:S(2)}) %collective-permute-start.3) | collective-permute-done | bytes 1572896 | tf_op jit(solution)/shard_map/ppermute | solution.py:169
  44.8 2.1 %pieces.1 = bf16[4,4,240,256]{3,2,1,0:T(8,128)(2,1)} custom-call(bf16[192,384]{1,0:T(8,128)(2,1)S(1)} %add_convert_fusion.1.middle_ref, bf16[192,4096]{1,0:T(8,128)(2,1)S(1)} %copy-done.2, bf16[192,3072]{1,0:T(8,128)(2,1)S(1)} %copy-done.4), custom_call_target="tpu_custom_call" | custom-call | flops 377487360 | bytes 4718592 | tf_op jit(solution)/shard_map/pieces/pallas_call | solution.py:419
  46.9 4.3 %collective-permute-done.2.refs_4_ = bf16[192,3072]{1,0:T(8,128)(2,1)} collective-permute-done((bf16[192,3072]{1,0:T(8,128)(2,1)}, bf16[192,3072]{1,0:T(8,128)(2,1)}, u32[]{:S(2)}, u32[]{:S(2)}) %collective-permute-start.2) | collective-permute-done | bytes 1179680 | tf_op jit(solution)/shard_map/ppermute | solution.py:169
  53.3 4.4 %all-to-all-start = ((bf16[4,4,240,256]{3,2,1,0:T(8,128)(2,1)}), bf16[4,4,240,256]{3,2,1,0:T(8,128)(2,1)}, u32[]{:S(2)}, u32[]{:S(2)}) async-start(bf16[4,4,240,256]{3,2,1,0:T(8,128)(2,1)} %pieces.1), calls=%async_computation | async-start | bytes 3932160 | tf_op jit(solution)/shard_map/all_to_all | solution.py:477
  59.4 21.1 %collective-permute-done.7.refs_5_ = bf16[192,3072]{1,0:T(8,128)(2,1)} collective-permute-done((bf16[192,3072]{1,0:T(8,128)(2,1)}, bf16[192,3072]{1,0:T(8,128)(2,1)}, u32[]{:S(2)}, u32[]{:S(2)}) %collective-permute-start.7) | collective-permute-done | bytes 1179680 | tf_op jit(solution)/shard_map/ppermute | solution.py:169
  82.4 16.5 %all-to-all-done = bf16[4,4,240,256]{3,2,1,0:T(8,128)(2,1)} async-done(((bf16[4,4,240,256]{3,2,1,0:T(8,128)(2,1)}), bf16[4,4,240,256]{3,2,1,0:T(8,128)(2,1)}, u32[]{:S(2)}, u32[]{:S(2)}) %all-to-all-start) | async-done | bytes 1966112 | tf_op jit(solution)/shard_map/all_to_all | solution.py:477
  98.9 2.7 %reduce_sum.24 = bf16[4,240,256]{2,1,0:T(8,128)(2,1)} reduce(bf16[4,4,240,256]{3,2,1,0:T(8,128)(2,1)} %all-to-all-done, bf16[]{:T(256)} %constant.298.clone.1), dimensions={0}, to_apply=%region_0.0 | reduce | flops 737280 | bytes 2457602 | tf_op jit(solution)/shard_map/reduce_sum | solution.py:476
  101.6 13.1 %all_to_all.20 = bf16[4,240,256]{2,1,0:T(8,128)(2,1)S(1)} all-to-all(bf16[4,240,256]{2,1,0:T(8,128)(2,1)} %reduce_sum.24), channel_id=1, replica_groups=mesh['hi'=4,'lo'=4,'tensor'=2] {'hi'}, dimensions={0} | all-to-all | bytes 983040 | tf_op jit(solution)/shard_map/all_to_all | solution.py:477
  115.6 3.6 %all-to-all-start.2 = ((bf16[4,240,256]{2,1,0:T(8,128)(2,1)}), bf16[4,240,256]{2,1,0:T(8,128)(2,1)S(1)}, u32[]{:S(2)}, u32[]{:S(2)}) async-start(bf16[4,240,256]{2,1,0:T(8,128)(2,1)} %broadcast_in_dim.4), calls=%async_computation.2 | async-start | bytes 983040 | tf_op jit(solution)/shard_map/all_to_all | solution.py:482
  119.3 8.5 %all-to-all-done.2 = bf16[4,240,256]{2,1,0:T(8,128)(2,1)S(1)} async-done(((bf16[4,240,256]{2,1,0:T(8,128)(2,1)}), bf16[4,240,256]{2,1,0:T(8,128)(2,1)S(1)}, u32[]{:S(2)}, u32[]{:S(2)}) %all-to-all-start.2) | async-done | bytes 491552 | tf_op jit(solution)/shard_map/all_to_all | solution.py:482
  127.8 4.7 %collective-permute-done.11.refs_13_ = bf16[256,3072]{1,0:T(8,128)(2,1)} collective-permute-done((bf16[256,3072]{1,0:T(8,128)(2,1)}, bf16[256,3072]{1,0:T(8,128)(2,1)}, u32[]{:S(2)}, u32[]{:S(2)}) %collective-permute-start.11) | collective-permute-done | bytes 1572896 | tf_op jit(solution)/shard_map/ppermute | solution.py:169
  135.1 17.9 %term.1 = (bf16[768,1024]{1,0:T(8,128)(2,1)}, bf16[768,1024]{1,0:T(8,128)(2,1)S(1)}) custom-call(s32[2]{0:T(128)S(1)} %pad_add_fusion.place_ref, bf16[192,3072]{1,0:T(8,128)(2,1)S(1)} %copy-done.5, bf16[192,3072]{1,0:T(8,128)(2,1)} %collective-permute-done.1.refs_1_, bf16[192,3072]{1,0:T(8,128)(2,1)S(1)} %copy-done.8, ...), custom_call_target="tpu_custom_call" | custom-call | flops 9663676416 | bytes 20447232 | tf_op jit(solution)/shard_map/term/pallas_call | solution.py:333
  154.2 4.2 %collective-permute-start.13 = (bf16[768,1024]{1,0:T(8,128)(2,1)}, bf16[768,1024]{1,0:T(8,128)(2,1)}, u32[]{:S(2)}, u32[]{:S(2)}) collective-permute-start(bf16[768,1024]{1,0:T(8,128)(2,1)} %get-tuple-element.47), channel_id=1, source_target_pairs={{0,1},{1,0},{2,3},{3,2},{4,5},{5,4},{6,7},{7,6},{8,9},{9,8},{10,11... | collective-permute-start | bytes 4718600 | tf_op jit(solution)/shard_map/ppermute | solution.py:169
  159.8 3.6 %all-to-all-start.3 = ((bf16[4,4,240,256]{3,2,1,0:T(8,128)(2,1)}), bf16[4,4,240,256]{3,2,1,0:T(8,128)(2,1)S(1)}, u32[]{:S(2)}, u32[]{:S(2)}) async-start(bf16[4,4,240,256]{3,2,1,0:T(8,128)(2,1)} %broadcast_in_dim.5), calls=%async_computation.3 | async-start | bytes 3932160 | tf_op jit(solution)/shard_map/all_to_all | solution.py:482
  163.5 2.5 %add_convert_fusion = bf16[768,1024]{1,0:T(8,128)(2,1)S(1)} fusion(bf16[768,1024]{1,0:T(8,128)(2,1)} %collective-permute-done.13, bf16[768,1024]{1,0:T(8,128)(2,1)} %copy-done.3), kind=kLoop, calls=%fused_computation | loop fusion | flops 3145728 | bytes 4718592 | tf_op jit(solution)/shard_map/convert_element_type | solution.py:562
  169.1 4.5 %collective-permute-start.15 = (bf16[192,1024]{1,0:T(8,128)(2,1)}, bf16[192,1024]{1,0:T(8,128)(2,1)}, u32[]{:S(2)}, u32[]{:S(2)}) collective-permute-start(bf16[192,1024]{1,0:T(8,128)(2,1)} %get-tuple-element.56), channel_id=1, source_target_pairs={{0,8},{1,16},{2,10},{3,18},{4,12},{5,20},{6,14},{7,22},{8,24},{9,0... | collective-permute-start | bytes 1179656 | tf_op jit(solution)/shard_map/ppermute | solution.py:169
  177.8 3.2 %fusion.added_ref = f32[192,4096]{1,0:T(8,128)} fusion(bf16[4096,192]{0,1:T(8,128)(2,1)S(1)} %copy-done, bf16[192,384]{1,0:T(8,128)(2,1)} %copy-done.6), kind=kOutput, calls=%fused_computation.9 | convolution fusion | flops 301989888 | bytes 4816896 | tf_op jit(solution)/shard_map/dot_general | solution.py:56
  180.9 5.9 %all-to-all-done.3.every_ref = bf16[4,4,240,256]{3,2,1,0:T(8,128)(2,1)S(1)} async-done(((bf16[4,4,240,256]{3,2,1,0:T(8,128)(2,1)}), bf16[4,4,240,256]{3,2,1,0:T(8,128)(2,1)S(1)}, u32[]{:S(2)}, u32[]{:S(2)}) %all-to-all-start.3) | async-done | bytes 1966112 | tf_op jit(solution)/shard_map/all_to_all | solution.py:482
  186.8 11.8 %collective-permute-done.14.refs_0_ = bf16[192,1024]{1,0:T(8,128)(2,1)} collective-permute-done((bf16[192,1024]{1,0:T(8,128)(2,1)}, bf16[192,1024]{1,0:T(8,128)(2,1)}, u32[]{:S(2)}, u32[]{:S(2)}) %collective-permute-start.14) | collective-permute-done | bytes 393248 | tf_op jit(solution)/shard_map/ppermute | solution.py:169
  200.7 2.7 %collective-permute-done.17.refs_3_ = bf16[192,1024]{1,0:T(8,128)(2,1)} collective-permute-done((bf16[192,1024]{1,0:T(8,128)(2,1)}, bf16[192,1024]{1,0:T(8,128)(2,1)}, u32[]{:S(2)}, u32[]{:S(2)}) %collective-permute-start.17) | collective-permute-done | bytes 393248 | tf_op jit(solution)/shard_map/ppermute | solution.py:169
  205.3 3.2 %finish.1 = bf16[192,4096]{1,0:T(8,128)(2,1)} custom-call(s32[32]{0:T(128)S(1)} %stack.140.spot_ref, f32[192,4096]{1,0:T(8,128)S(1)} %copy-done.1, bf16[192,1024]{1,0:T(8,128)(2,1)} %collective-permute-done.14.refs_0_, bf16[192,1024]{1,0:T(8,128)(2,1)} %collective-permute-done.15.refs_1_, bf16[192,1024]{1,0:T(8,128)(2,1)} %collective-permute-done.16.refs_2_, ...), custom_call_target="tpu_custom_call" | custom-call | flops 786432 | bytes 6291456 | tf_op jit(solution)/shard_map/finish/pallas_call | solution.py:372
  (77 shorter events, 36.2 us)
Async XLA Ops:
  0.6 23.7 %copy-start = (bf16[4096,192]{0,1:T(8,128)(2,1)S(1)}, bf16[4096,192]{0,1:T(8,128)(2,1)}, u32[]{:S(2)}) copy-start(bf16[4096,192]{0,1:T(8,128)(2,1)} %param.21) | copy-start | bytes 4718596
  5.7 36.5 %collective-permute-start.3 = (bf16[256,3072]{1,0:T(8,128)(2,1)}, bf16[256,3072]{1,0:T(8,128)(2,1)}, u32[]{:S(2)}, u32[]{:S(2)}) collective-permute-start(bf16[256,3072]{1,0:T(8,128)(2,1)} %pad_maximum_fusion.refs_7_), channel_id=1, source_target_pairs={{0,2},{1,3},{2,0},{3,1},{4,6},{5,7},{6,4},{7,5},{8,10},{9,11},{10,... | collective-permute-start | bytes 4718600 | tf_op jit(solution)/shard_map/ppermute | solution.py:169
  7.8 35.3 %collective-permute-start.4 = (bf16[256,3072]{1,0:T(8,128)(2,1)}, bf16[256,3072]{1,0:T(8,128)(2,1)}, u32[]{:S(2)}, u32[]{:S(2)}) collective-permute-start(bf16[256,3072]{1,0:T(8,128)(2,1)} %pad_maximum_fusion.refs_7_), channel_id=1, source_target_pairs={{0,4},{1,5},{2,6},{3,7},{4,0},{5,1},{6,2},{7,3},{8,12},{9,13},{10,... | collective-permute-start | bytes 4718600 | tf_op jit(solution)/shard_map/ppermute | solution.py:169
  18.7 28.2 %collective-permute-start.1 = (bf16[192,3072]{1,0:T(8,128)(2,1)}, bf16[192,3072]{1,0:T(8,128)(2,1)}, u32[]{:S(2)}, u32[]{:S(2)}) collective-permute-start(bf16[192,3072]{1,0:T(8,128)(2,1)} %get-tuple-element.39.own_ref.refs_0_), channel_id=1, source_target_pairs={{0,8},{1,9},{2,10},{3,11},{4,12},{5,13},{6,14},{7,15},{8,16},{9,17... | collective-permute-start | bytes 3538952 | tf_op jit(solution)/shard_map/ppermute | solution.py:169
  23.1 28.2 %collective-permute-start.2 = (bf16[192,3072]{1,0:T(8,128)(2,1)}, bf16[192,3072]{1,0:T(8,128)(2,1)}, u32[]{:S(2)}, u32[]{:S(2)}) collective-permute-start(bf16[192,3072]{1,0:T(8,128)(2,1)} %get-tuple-element.39.own_ref.refs_0_), channel_id=1, source_target_pairs={{8,0},{9,1},{10,2},{11,3},{12,4},{13,5},{14,6},{15,7},{16,8},{17,9... | collective-permute-start | bytes 3538952 | tf_op jit(solution)/shard_map/ppermute | solution.py:169
  25.1 19.5 %collective-permute-start = (f32[192,384]{1,0:T(8,128)S(1)}, f32[192,384]{1,0:T(8,128)S(1)}, u32[]{:S(2)}, u32[]{:S(2)}) collective-permute-start(f32[192,384]{1,0:T(8,128)S(1)} %pad_maximum_fusion.2), channel_id=1, source_target_pairs={{0,1},{1,0},{2,3},{3,2},{4,5},{5,4},{6,7},{7,6},{8,9},{9,8},{10,11... | collective-permute-start | bytes 884744 | tf_op jit(solution)/shard_map/ppermute | solution.py:169
  43.1 38.8 %collective-permute-start.10 = (bf16[256,3072]{1,0:T(8,128)(2,1)}, bf16[256,3072]{1,0:T(8,128)(2,1)}, u32[]{:S(2)}, u32[]{:S(2)}) collective-permute-start(bf16[256,3072]{1,0:T(8,128)(2,1)} %pad_maximum_fusion.1.refs_8_), channel_id=1, source_target_pairs={{0,2},{1,3},{2,0},{3,1},{4,6},{5,7},{6,4},{7,5},{8,10},{9,11},{10,... | collective-permute-start | bytes 4718600 | tf_op jit(solution)/shard_map/ppermute | solution.py:169
  43.4 38.4 %collective-permute-start.9 = (bf16[256,3072]{1,0:T(8,128)(2,1)}, bf16[256,3072]{1,0:T(8,128)(2,1)}, u32[]{:S(2)}, u32[]{:S(2)}) collective-permute-start(bf16[256,3072]{1,0:T(8,128)(2,1)} %pad_maximum_fusion.1.refs_8_), channel_id=1, source_target_pairs={{0,4},{1,5},{2,6},{3,7},{4,0},{5,1},{6,2},{7,3},{8,12},{9,13},{10,... | collective-permute-start | bytes 4718600 | tf_op jit(solution)/shard_map/ppermute | solution.py:169
  51.2 6.5 %collective-permute-start.5 = (bf16[192,3072]{1,0:T(8,128)(2,1)}, bf16[192,3072]{1,0:T(8,128)(2,1)S(1)}, u32[]{:S(2)}, u32[]{:S(2)}) collective-permute-start(bf16[192,3072]{1,0:T(8,128)(2,1)} %collective-permute-done.1.refs_1_), channel_id=1, source_target_pairs={{8,16},{9,17},{10,18},{11,19},{12,20},{13,21},{14,22},{15,23},{16,... | collective-permute-start | bytes 3538952 | tf_op jit(solution)/shard_map/ppermute | solution.py:169
  52.0 28.6 %collective-permute-start.7 = (bf16[192,3072]{1,0:T(8,128)(2,1)}, bf16[192,3072]{1,0:T(8,128)(2,1)}, u32[]{:S(2)}, u32[]{:S(2)}) collective-permute-start(bf16[192,3072]{1,0:T(8,128)(2,1)} %collective-permute-done.2.refs_4_), channel_id=1, source_target_pairs={{8,0},{9,1},{10,2},{11,3},{12,4},{13,5},{14,6},{15,7},{16,8},{17,9... | collective-permute-start | bytes 3538952 | tf_op jit(solution)/shard_map/ppermute | solution.py:169
  53.3 45.6 %all-to-all-start = ((bf16[4,4,240,256]{3,2,1,0:T(8,128)(2,1)}), bf16[4,4,240,256]{3,2,1,0:T(8,128)(2,1)}, u32[]{:S(2)}, u32[]{:S(2)}) async-start(bf16[4,4,240,256]{3,2,1,0:T(8,128)(2,1)} %pieces.1), calls=%async_computation | async-start | bytes 3932160 | tf_op jit(solution)/shard_map/all_to_all | solution.py:477
  57.7 57.0 %copy-start.7 = (bf16[192,3072]{1,0:T(8,128)(2,1)}, bf16[192,3072]{1,0:T(8,128)(2,1)S(1)}, u32[]{:S(2)}) copy-start(bf16[192,3072]{1,0:T(8,128)(2,1)S(1)} %collective-permute-done.5.refs_2_) | copy-start | bytes 3538948
  57.7 57.0 %collective-permute-start.6 = (bf16[192,3072]{1,0:T(8,128)(2,1)S(1)}, bf16[192,3072]{1,0:T(8,128)(2,1)}, u32[]{:S(2)}, u32[]{:S(2)}) collective-permute-start(bf16[192,3072]{1,0:T(8,128)(2,1)S(1)} %collective-permute-done.5.refs_2_), channel_id=1, source_target_pairs={{16,24},{17,25},{18,26},{19,27},{20,28},{21,29},{22,30},{23,31}} | collective-permute-start | bytes 3538952 | tf_op jit(solution)/shard_map/ppermute | solution.py:169
  80.6 34.2 %collective-permute-start.8 = (bf16[192,3072]{1,0:T(8,128)(2,1)}, bf16[192,3072]{1,0:T(8,128)(2,1)}, u32[]{:S(2)}, u32[]{:S(2)}) collective-permute-start(bf16[192,3072]{1,0:T(8,128)(2,1)} %collective-permute-done.7.refs_5_), channel_id=1, source_target_pairs={{8,0},{9,1},{10,2},{11,3},{12,4},{13,5},{14,6},{15,7}} | collective-permute-start | bytes 3538952 | tf_op jit(solution)/shard_map/ppermute | solution.py:169
  81.9 50.7 %collective-permute-start.11 = (bf16[256,3072]{1,0:T(8,128)(2,1)}, bf16[256,3072]{1,0:T(8,128)(2,1)}, u32[]{:S(2)}, u32[]{:S(2)}) collective-permute-start(bf16[256,3072]{1,0:T(8,128)(2,1)} %collective-permute-done.3.refs_9_), channel_id=1, source_target_pairs={{0,4},{1,5},{2,6},{3,7},{4,0},{5,1},{6,2},{7,3},{8,12},{9,13},{10,... | collective-permute-start | bytes 4718600 | tf_op jit(solution)/shard_map/ppermute | solution.py:169
  82.2 50.4 %collective-permute-start.12 = (bf16[256,3072]{1,0:T(8,128)(2,1)}, bf16[256,3072]{1,0:T(8,128)(2,1)}, u32[]{:S(2)}, u32[]{:S(2)}) collective-permute-start(bf16[256,3072]{1,0:T(8,128)(2,1)} %collective-permute-done.9.refs_12_), channel_id=1, source_target_pairs={{0,2},{1,3},{2,0},{3,1},{4,6},{5,7},{6,4},{7,5},{8,10},{9,11},{10,... | collective-permute-start | bytes 4718600 | tf_op jit(solution)/shard_map/ppermute | solution.py:169
  115.6 12.2 %all-to-all-start.2 = ((bf16[4,240,256]{2,1,0:T(8,128)(2,1)}), bf16[4,240,256]{2,1,0:T(8,128)(2,1)S(1)}, u32[]{:S(2)}, u32[]{:S(2)}) async-start(bf16[4,240,256]{2,1,0:T(8,128)(2,1)} %broadcast_in_dim.4), calls=%async_computation.2 | async-start | bytes 983040 | tf_op jit(solution)/shard_map/all_to_all | solution.py:482
  135.1 23.3 %copy-start.11 = (bf16[4,240,256]{2,1,0:T(8,128)(2,1)S(1)}, bf16[4,240,256]{2,1,0:T(8,128)(2,1)}, u32[]{:S(2)}) copy-start(bf16[4,240,256]{2,1,0:T(8,128)(2,1)} %copy-done.10) | copy-start | bytes 1474564
  154.2 9.3 %collective-permute-start.13 = (bf16[768,1024]{1,0:T(8,128)(2,1)}, bf16[768,1024]{1,0:T(8,128)(2,1)}, u32[]{:S(2)}, u32[]{:S(2)}) collective-permute-start(bf16[768,1024]{1,0:T(8,128)(2,1)} %get-tuple-element.47), channel_id=1, source_target_pairs={{0,1},{1,0},{2,3},{3,2},{4,5},{5,4},{6,7},{7,6},{8,9},{9,8},{10,11... | collective-permute-start | bytes 4718600 | tf_op jit(solution)/shard_map/ppermute | solution.py:169
  159.8 27.0 %all-to-all-start.3 = ((bf16[4,4,240,256]{3,2,1,0:T(8,128)(2,1)}), bf16[4,4,240,256]{3,2,1,0:T(8,128)(2,1)S(1)}, u32[]{:S(2)}, u32[]{:S(2)}) async-start(bf16[4,4,240,256]{3,2,1,0:T(8,128)(2,1)} %broadcast_in_dim.5), calls=%async_computation.3 | async-start | bytes 3932160 | tf_op jit(solution)/shard_map/all_to_all | solution.py:482
  167.2 31.4 %collective-permute-start.14 = (bf16[192,1024]{1,0:T(8,128)(2,1)}, bf16[192,1024]{1,0:T(8,128)(2,1)}, u32[]{:S(2)}, u32[]{:S(2)}) collective-permute-start(bf16[192,1024]{1,0:T(8,128)(2,1)} %get-tuple-element.57), channel_id=1, source_target_pairs={{0,0},{1,8},{2,2},{3,10},{4,4},{5,12},{6,6},{7,14},{8,16},{9,24},{... | collective-permute-start | bytes 1179656 | tf_op jit(solution)/shard_map/ppermute | solution.py:169
  169.1 31.6 %collective-permute-start.15 = (bf16[192,1024]{1,0:T(8,128)(2,1)}, bf16[192,1024]{1,0:T(8,128)(2,1)}, u32[]{:S(2)}, u32[]{:S(2)}) collective-permute-start(bf16[192,1024]{1,0:T(8,128)(2,1)} %get-tuple-element.56), channel_id=1, source_target_pairs={{0,8},{1,16},{2,10},{3,18},{4,12},{5,20},{6,14},{7,22},{8,24},{9,0... | collective-permute-start | bytes 1179656 | tf_op jit(solution)/shard_map/ppermute | solution.py:169
  173.7 27.0 %collective-permute-start.16 = (bf16[192,1024]{1,0:T(8,128)(2,1)}, bf16[192,1024]{1,0:T(8,128)(2,1)}, u32[]{:S(2)}, u32[]{:S(2)}) collective-permute-start(bf16[192,1024]{1,0:T(8,128)(2,1)} %get-tuple-element.55), channel_id=1, source_target_pairs={{0,16},{1,24},{2,18},{3,26},{4,20},{5,28},{6,22},{7,30},{8,0},{9,8... | collective-permute-start | bytes 1179656 | tf_op jit(solution)/shard_map/ppermute | solution.py:169
  175.5 27.9 %collective-permute-start.17 = (bf16[192,1024]{1,0:T(8,128)(2,1)}, bf16[192,1024]{1,0:T(8,128)(2,1)}, u32[]{:S(2)}, u32[]{:S(2)}) collective-permute-start(bf16[192,1024]{1,0:T(8,128)(2,1)} %get-tuple-element.54), channel_id=1, source_target_pairs={{0,24},{1,0},{2,26},{3,2},{4,28},{5,4},{6,30},{7,6},{8,8},{9,16},{... | collective-permute-start | bytes 1179656 | tf_op jit(solution)/shard_map/ppermute | solution.py:169
  (15 other events, 89.9 us)

commit v11 on v10

--- a/solution.py
+++ b/solution.py
@@ -345,7 +345,7 @@
                 pltpu.SemaphoreType.DMA((4,)),
             ],
         ),
-        compiler_params=pltpu.CompilerParams(vmem_limit_bytes=40 << 20),
+        compiler_params=pltpu.CompilerParams(vmem_limit_bytes=56 << 20),
         cost_estimate=pl.CostEstimate(
             flops=16 * tokens * depth * rows * count,
             bytes_accessed=8 * tokens * depth + (4 * rows * depth + 16 * tokens * rows) * count,

time: 210 us -> 208 us (level)
  local copies, waits for them, and re-layouts: 13.6 us -> 9.96 us
    ppermute x18, waiting for transfers between devices: 59.8 us -> 64.4 us  [send(): return lax.ppermute(value, AXES, pairs)]
    unnamed x36 -> x24, local copies, waits for them, and re-layouts: 5.63 us -> 1.94 us
where the time goes in v11:
time: 208 us; the launch traced here: 207 us
  waiting for transfers between devices  92.3 us (44%)
  starting transfers between devices  44.2 us (21%)
  Pallas kernels  35.2 us (17%)
  blocking collectives  13.2 us (6%)
  local copies, waits for them, and re-layouts  9.96 us (5%)
  other arithmetic  7.24 us (3%)
  matrix products  3.74 us (2%)
    ppermute x18, waiting for transfers between devices, send(): return lax.ppermute(value, AXES, pairs)  64.4 us
    ppermute x18, starting transfers between devices, send(): return lax.ppermute(value, AXES, pairs)  33.4 us
    pallas_call x1, Pallas kernels, term_halves(): pl.pallas_call(term_kernel, out_shape=(out, out), grid_spec=pltpu.Prefetc...  18.9 us
    all_to_all x1, waiting for transfers between devices, scatter_sum(): lax.all_to_all(value, axis, 0, 0)  15.6 us
    all_to_all x1, blocking collectives, scatter_sum(): lax.all_to_all(value, axis, 0, 0)  13.2 us
    all_to_all x2, waiting for transfers between devices, gather(): lax.all_to_all(jnp.broadcast_to(value[None], (4, *value.shape)), axis, 0, 0)  12.3 us
    pallas_call x1, Pallas kernels, attention(): pl.pallas_call(attention_kernel, out_shape=(jax.ShapeDtypeStruct((tokens,...  8.89 us
    all_to_all x2, starting transfers between devices, gather(): lax.all_to_all(jnp.broadcast_to(value[None], (4, *value.shape)), axis, 0, 0)  7.25 us
  transfers between devices with their start and end apart: 21, of which 10 were waited for; matrix products, arithmetic and copies ran while one was open for 7% of the time, Pallas kernels for 6%

profile of v11, /device:TPU:1, one launch (start us, length us, event | category | flops | bytes accessed | tf_op | source)
XLA Modules:
  0.0 207.0 jit_solution(10698041406989974532)
XLA Ops:
  0.7 2.9 %fusion.2 = (bf16[256,2048]{1,0:T(8,128)(2,1)}, bf16[256,2048]{1,0:T(8,128)(2,1)S(1)}) fusion(bf16[512,2048]{1,0:T(8,128)(2,1)} %param.18), kind=kLoop, calls=%fused_computation.12 | loop fusion | bytes 4194304 | tf_op jit(solution)/shard_map/slice | solution.py:514
  9.8 8.9 %attention.1 = (bf16[192,3072]{1,0:T(8,128)(2,1)}, f32[192,192]{1,0:T(8,128)}) custom-call(bf16[192,2048]{1,0:T(8,128)(2,1)} %query_ref.1, bf16[192,512]{1,0:T(8,128)(2,1)} %key_ref.1, bf16[192,512]{1,0:T(8,128)(2,1)} %value_ref.1, bf16[192,2048]{1,0:T(8,128)(2,1)} %grad_ref.1, s32[192,1]{1,0:T(8,128)} %copy.17.row_ids, s32[1,192]{1,0:T(1,128)} %column_ids, ...), custom_call_target="tpu_custom_call" | custom-call | flops 754974720 | bytes 2359296 | tf_op jit(solution)/shard_map/attention/pallas_call | solution.py:257
  18.7 4.4 %collective-permute-start.1 = (bf16[192,3072]{1,0:T(8,128)(2,1)}, bf16[192,3072]{1,0:T(8,128)(2,1)}, u32[]{:S(2)}, u32[]{:S(2)}) collective-permute-start(bf16[192,3072]{1,0:T(8,128)(2,1)} %get-tuple-element.39.own_ref.refs_0_), channel_id=1, source_target_pairs={{0,8},{1,9},{2,10},{3,11},{4,12},{5,13},{6,14},{7,15},{8,16},{9,17... | collective-permute-start | bytes 3538952 | tf_op jit(solution)/shard_map/ppermute | solution.py:169
  28.0 14.2 %collective-permute-done.3.refs_9_ = bf16[256,3072]{1,0:T(8,128)(2,1)} collective-permute-done((bf16[256,3072]{1,0:T(8,128)(2,1)}, bf16[256,3072]{1,0:T(8,128)(2,1)}, u32[]{:S(2)}, u32[]{:S(2)}) %collective-permute-start.3) | collective-permute-done | bytes 1572896 | tf_op jit(solution)/shard_map/ppermute | solution.py:169
  46.9 4.3 %collective-permute-done.2.refs_4_ = bf16[192,3072]{1,0:T(8,128)(2,1)} collective-permute-done((bf16[192,3072]{1,0:T(8,128)(2,1)}, bf16[192,3072]{1,0:T(8,128)(2,1)}, u32[]{:S(2)}, u32[]{:S(2)}) %collective-permute-start.2) | collective-permute-done | bytes 1179680 | tf_op jit(solution)/shard_map/ppermute | solution.py:169
  54.2 3.6 %all-to-all-start = ((bf16[4,4,240,256]{3,2,1,0:T(8,128)(2,1)}), bf16[4,4,240,256]{3,2,1,0:T(8,128)(2,1)S(1)}, u32[]{:S(2)}, u32[]{:S(2)}) async-start(bf16[4,4,240,256]{3,2,1,0:T(8,128)(2,1)} %pieces.1), calls=%async_computation | async-start | bytes 3932160 | tf_op jit(solution)/shard_map/all_to_all | solution.py:477
  59.5 22.0 %collective-permute-done.7.refs_5_ = bf16[192,3072]{1,0:T(8,128)(2,1)} collective-permute-done((bf16[192,3072]{1,0:T(8,128)(2,1)}, bf16[192,3072]{1,0:T(8,128)(2,1)}, u32[]{:S(2)}, u32[]{:S(2)}) %collective-permute-start.7) | collective-permute-done | bytes 1179680 | tf_op jit(solution)/shard_map/ppermute | solution.py:169
  83.3 15.6 %all-to-all-done = bf16[4,4,240,256]{3,2,1,0:T(8,128)(2,1)S(1)} async-done(((bf16[4,4,240,256]{3,2,1,0:T(8,128)(2,1)}), bf16[4,4,240,256]{3,2,1,0:T(8,128)(2,1)S(1)}, u32[]{:S(2)}, u32[]{:S(2)}) %all-to-all-start) | async-done | bytes 1966112 | tf_op jit(solution)/shard_map/all_to_all | solution.py:477
  100.1 13.2 %all_to_all.20 = bf16[4,240,256]{2,1,0:T(8,128)(2,1)S(1)} all-to-all(bf16[4,240,256]{2,1,0:T(8,128)(2,1)} %reduce_sum.24), channel_id=1, replica_groups=mesh['hi'=4,'lo'=4,'tensor'=2] {'hi'}, dimensions={0} | all-to-all | bytes 983040 | tf_op jit(solution)/shard_map/all_to_all | solution.py:477
  114.1 3.6 %all-to-all-start.2 = ((bf16[4,240,256]{2,1,0:T(8,128)(2,1)}), bf16[4,240,256]{2,1,0:T(8,128)(2,1)S(1)}, u32[]{:S(2)}, u32[]{:S(2)}) async-start(bf16[4,240,256]{2,1,0:T(8,128)(2,1)} %broadcast_in_dim.4), calls=%async_computation.2 | async-start | bytes 983040 | tf_op jit(solution)/shard_map/all_to_all | solution.py:482
  118.4 8.0 %all-to-all-done.2 = bf16[4,240,256]{2,1,0:T(8,128)(2,1)S(1)} async-done(((bf16[4,240,256]{2,1,0:T(8,128)(2,1)}), bf16[4,240,256]{2,1,0:T(8,128)(2,1)S(1)}, u32[]{:S(2)}, u32[]{:S(2)}) %all-to-all-start.2) | async-done | bytes 491552 | tf_op jit(solution)/shard_map/all_to_all | solution.py:482
  126.4 6.2 %collective-permute-done.11.refs_13_ = bf16[256,3072]{1,0:T(8,128)(2,1)} collective-permute-done((bf16[256,3072]{1,0:T(8,128)(2,1)}, bf16[256,3072]{1,0:T(8,128)(2,1)}, u32[]{:S(2)}, u32[]{:S(2)}) %collective-permute-start.11) | collective-permute-done | bytes 1572896 | tf_op jit(solution)/shard_map/ppermute | solution.py:169
  132.6 18.9 %term.1 = (bf16[768,1024]{1,0:T(8,128)(2,1)}, bf16[768,1024]{1,0:T(8,128)(2,1)}) custom-call(s32[2]{0:T(128)} %pad_add_fusion.place_ref, bf16[192,3072]{1,0:T(8,128)(2,1)} %get-tuple-element.39.own_ref.refs_0_, bf16[192,3072]{1,0:T(8,128)(2,1)} %collective-permute-done.1.refs_1_, bf16[192,3072]{1,0:T(8,128)(2,1)} %collective-permute-done.5.refs_2_, ...), custom_call_target="tpu_custom_call" | custom-call | flops 9663676416 | bytes 20447232 | tf_op jit(solution)/shard_map/term/pallas_call | solution.py:333
  151.5 2.8 %collective-permute-start.13 = (bf16[768,1024]{1,0:T(8,128)(2,1)}, bf16[768,1024]{1,0:T(8,128)(2,1)}, u32[]{:S(2)}, u32[]{:S(2)}) collective-permute-start(bf16[768,1024]{1,0:T(8,128)(2,1)} %get-tuple-element.47), channel_id=1, source_target_pairs={{0,1},{1,0},{2,3},{3,2},{4,5},{5,4},{6,7},{7,6},{8,9},{9,8},{10,11... | collective-permute-start | bytes 4718600 | tf_op jit(solution)/shard_map/ppermute | solution.py:169
  155.7 3.6 %all-to-all-start.3 = ((bf16[4,4,240,256]{3,2,1,0:T(8,128)(2,1)}), bf16[4,4,240,256]{3,2,1,0:T(8,128)(2,1)S(1)}, u32[]{:S(2)}, u32[]{:S(2)}) async-start(bf16[4,4,240,256]{3,2,1,0:T(8,128)(2,1)} %broadcast_in_dim.5), calls=%async_computation.3 | async-start | bytes 3932160 | tf_op jit(solution)/shard_map/all_to_all | solution.py:482
  159.4 2.5 %add_convert_fusion = bf16[768,1024]{1,0:T(8,128)(2,1)S(1)} fusion(bf16[768,1024]{1,0:T(8,128)(2,1)} %collective-permute-done.13, bf16[768,1024]{1,0:T(8,128)(2,1)} %get-tuple-element.46), kind=kLoop, calls=%fused_computation | loop fusion | flops 3145728 | bytes 4718592 | tf_op jit(solution)/shard_map/convert_element_type | solution.py:562
  163.1 3.0 %collective-permute-start.14 = (bf16[192,1024]{1,0:T(8,128)(2,1)}, bf16[192,1024]{1,0:T(8,128)(2,1)}, u32[]{:S(2)}, u32[]{:S(2)}) collective-permute-start(bf16[192,1024]{1,0:T(8,128)(2,1)} %get-tuple-element.57), channel_id=1, source_target_pairs={{0,0},{1,8},{2,2},{3,10},{4,4},{5,12},{6,6},{7,14},{8,16},{9,24},{... | collective-permute-start | bytes 1179656 | tf_op jit(solution)/shard_map/ppermute | solution.py:169
  166.2 3.4 %collective-permute-start.15 = (bf16[192,1024]{1,0:T(8,128)(2,1)}, bf16[192,1024]{1,0:T(8,128)(2,1)}, u32[]{:S(2)}, u32[]{:S(2)}) collective-permute-start(bf16[192,1024]{1,0:T(8,128)(2,1)} %get-tuple-element.56), channel_id=1, source_target_pairs={{0,8},{1,16},{2,10},{3,18},{4,12},{5,20},{6,14},{7,22},{8,24},{9,0... | collective-permute-start | bytes 1179656 | tf_op jit(solution)/shard_map/ppermute | solution.py:169
  169.6 3.7 %collective-permute-start.16 = (bf16[192,1024]{1,0:T(8,128)(2,1)}, bf16[192,1024]{1,0:T(8,128)(2,1)}, u32[]{:S(2)}, u32[]{:S(2)}) collective-permute-start(bf16[192,1024]{1,0:T(8,128)(2,1)} %get-tuple-element.55), channel_id=1, source_target_pairs={{0,16},{1,24},{2,18},{3,26},{4,20},{5,28},{6,22},{7,30},{8,0},{9,8... | collective-permute-start | bytes 1179656 | tf_op jit(solution)/shard_map/ppermute | solution.py:169
  175.5 3.1 %fusion.added_ref = f32[192,4096]{1,0:T(8,128)} fusion(bf16[4096,192]{0,1:T(8,128)(2,1)S(1)} %copy-done, bf16[192,384]{1,0:T(8,128)(2,1)} %copy-done.4), kind=kOutput, calls=%fused_computation.9 | convolution fusion | flops 301989888 | bytes 4816896 | tf_op jit(solution)/shard_map/dot_general | solution.py:56
  178.7 4.3 %all-to-all-done.3.every_ref = bf16[4,4,240,256]{3,2,1,0:T(8,128)(2,1)S(1)} async-done(((bf16[4,4,240,256]{3,2,1,0:T(8,128)(2,1)}), bf16[4,4,240,256]{3,2,1,0:T(8,128)(2,1)S(1)}, u32[]{:S(2)}, u32[]{:S(2)}) %all-to-all-start.3) | async-done | bytes 1966112 | tf_op jit(solution)/shard_map/all_to_all | solution.py:482
  183.0 11.4 %collective-permute-done.14.refs_0_ = bf16[192,1024]{1,0:T(8,128)(2,1)} collective-permute-done((bf16[192,1024]{1,0:T(8,128)(2,1)}, bf16[192,1024]{1,0:T(8,128)(2,1)}, u32[]{:S(2)}, u32[]{:S(2)}) %collective-permute-start.14) | collective-permute-done | bytes 393248 | tf_op jit(solution)/shard_map/ppermute | solution.py:169
  196.5 5.4 %collective-permute-done.17.refs_3_ = bf16[192,1024]{1,0:T(8,128)(2,1)} collective-permute-done((bf16[192,1024]{1,0:T(8,128)(2,1)}, bf16[192,1024]{1,0:T(8,128)(2,1)}, u32[]{:S(2)}, u32[]{:S(2)}) %collective-permute-start.17) | collective-permute-done | bytes 393248 | tf_op jit(solution)/shard_map/ppermute | solution.py:169
  203.9 3.2 %finish.1 = bf16[192,4096]{1,0:T(8,128)(2,1)} custom-call(s32[32]{0:T(128)S(1)} %stack.140.spot_ref, f32[192,4096]{1,0:T(8,128)S(1)} %copy-done.1, bf16[192,1024]{1,0:T(8,128)(2,1)} %collective-permute-done.14.refs_0_, bf16[192,1024]{1,0:T(8,128)(2,1)} %collective-permute-done.15.refs_1_, bf16[192,1024]{1,0:T(8,128)(2,1)} %collective-permute-done.16.refs_2_, ...), custom_call_target="tpu_custom_call" | custom-call | flops 786432 | bytes 6291456 | tf_op jit(solution)/shard_map/finish/pallas_call | solution.py:372
  (65 shorter events, 33.5 us)
Async XLA Ops:
  0.6 23.7 %copy-start = (bf16[4096,192]{0,1:T(8,128)(2,1)S(1)}, bf16[4096,192]{0,1:T(8,128)(2,1)}, u32[]{:S(2)}) copy-start(bf16[4096,192]{0,1:T(8,128)(2,1)} %param.21) | copy-start | bytes 4718596
  5.7 18.6 %copy-start.2 = (bf16[192,4096]{1,0:T(8,128)(2,1)S(1)}, bf16[192,4096]{1,0:T(8,128)(2,1)}, u32[]{:S(2)}) copy-start(bf16[192,4096]{1,0:T(8,128)(2,1)} %normed_ref.1) | copy-start | bytes 4718596
  5.7 36.5 %collective-permute-start.3 = (bf16[256,3072]{1,0:T(8,128)(2,1)}, bf16[256,3072]{1,0:T(8,128)(2,1)}, u32[]{:S(2)}, u32[]{:S(2)}) collective-permute-start(bf16[256,3072]{1,0:T(8,128)(2,1)} %pad_maximum_fusion.refs_7_), channel_id=1, source_target_pairs={{0,2},{1,3},{2,0},{3,1},{4,6},{5,7},{6,4},{7,5},{8,10},{9,11},{10,... | collective-permute-start | bytes 4718600 | tf_op jit(solution)/shard_map/ppermute | solution.py:169
  7.8 35.3 %collective-permute-start.4 = (bf16[256,3072]{1,0:T(8,128)(2,1)}, bf16[256,3072]{1,0:T(8,128)(2,1)}, u32[]{:S(2)}, u32[]{:S(2)}) collective-permute-start(bf16[256,3072]{1,0:T(8,128)(2,1)} %pad_maximum_fusion.refs_7_), channel_id=1, source_target_pairs={{0,4},{1,5},{2,6},{3,7},{4,0},{5,1},{6,2},{7,3},{8,12},{9,13},{10,... | collective-permute-start | bytes 4718600 | tf_op jit(solution)/shard_map/ppermute | solution.py:169
  18.7 28.2 %collective-permute-start.1 = (bf16[192,3072]{1,0:T(8,128)(2,1)}, bf16[192,3072]{1,0:T(8,128)(2,1)}, u32[]{:S(2)}, u32[]{:S(2)}) collective-permute-start(bf16[192,3072]{1,0:T(8,128)(2,1)} %get-tuple-element.39.own_ref.refs_0_), channel_id=1, source_target_pairs={{0,8},{1,9},{2,10},{3,11},{4,12},{5,13},{6,14},{7,15},{8,16},{9,17... | collective-permute-start | bytes 3538952 | tf_op jit(solution)/shard_map/ppermute | solution.py:169
  23.1 28.1 %collective-permute-start.2 = (bf16[192,3072]{1,0:T(8,128)(2,1)}, bf16[192,3072]{1,0:T(8,128)(2,1)}, u32[]{:S(2)}, u32[]{:S(2)}) collective-permute-start(bf16[192,3072]{1,0:T(8,128)(2,1)} %get-tuple-element.39.own_ref.refs_0_), channel_id=1, source_target_pairs={{8,0},{9,1},{10,2},{11,3},{12,4},{13,5},{14,6},{15,7},{16,8},{17,9... | collective-permute-start | bytes 3538952 | tf_op jit(solution)/shard_map/ppermute | solution.py:169
  25.1 19.5 %collective-permute-start = (f32[192,384]{1,0:T(8,128)S(1)}, f32[192,384]{1,0:T(8,128)S(1)}, u32[]{:S(2)}, u32[]{:S(2)}) collective-permute-start(f32[192,384]{1,0:T(8,128)S(1)} %pad_maximum_fusion.2), channel_id=1, source_target_pairs={{0,1},{1,0},{2,3},{3,2},{4,5},{5,4},{6,7},{7,6},{8,9},{9,8},{10,11... | collective-permute-start | bytes 884744 | tf_op jit(solution)/shard_map/ppermute | solution.py:169
  26.7 18.0 %copy-start.3 = (bf16[192,3072]{1,0:T(8,128)(2,1)S(1)}, bf16[192,3072]{1,0:T(8,128)(2,1)}, u32[]{:S(2)}) copy-start(bf16[192,3072]{1,0:T(8,128)(2,1)} %get-tuple-element.39.own_ref.refs_0_) | copy-start | bytes 3538948
  43.1 39.7 %collective-permute-start.10 = (bf16[256,3072]{1,0:T(8,128)(2,1)}, bf16[256,3072]{1,0:T(8,128)(2,1)}, u32[]{:S(2)}, u32[]{:S(2)}) collective-permute-start(bf16[256,3072]{1,0:T(8,128)(2,1)} %pad_maximum_fusion.1.refs_8_), channel_id=1, source_target_pairs={{0,2},{1,3},{2,0},{3,1},{4,6},{5,7},{6,4},{7,5},{8,10},{9,11},{10,... | collective-permute-start | bytes 4718600 | tf_op jit(solution)/shard_map/ppermute | solution.py:169
  43.4 39.3 %collective-permute-start.9 = (bf16[256,3072]{1,0:T(8,128)(2,1)}, bf16[256,3072]{1,0:T(8,128)(2,1)}, u32[]{:S(2)}, u32[]{:S(2)}) collective-permute-start(bf16[256,3072]{1,0:T(8,128)(2,1)} %pad_maximum_fusion.1.refs_8_), channel_id=1, source_target_pairs={{0,4},{1,5},{2,6},{3,7},{4,0},{5,1},{6,2},{7,3},{8,12},{9,13},{10,... | collective-permute-start | bytes 4718600 | tf_op jit(solution)/shard_map/ppermute | solution.py:169
  51.2 6.6 %collective-permute-start.5 = (bf16[192,3072]{1,0:T(8,128)(2,1)}, bf16[192,3072]{1,0:T(8,128)(2,1)}, u32[]{:S(2)}, u32[]{:S(2)}) collective-permute-start(bf16[192,3072]{1,0:T(8,128)(2,1)} %collective-permute-done.1.refs_1_), channel_id=1, source_target_pairs={{8,16},{9,17},{10,18},{11,19},{12,20},{13,21},{14,22},{15,23},{16,... | collective-permute-start | bytes 3538952 | tf_op jit(solution)/shard_map/ppermute | solution.py:169
  52.9 28.6 %collective-permute-start.7 = (bf16[192,3072]{1,0:T(8,128)(2,1)}, bf16[192,3072]{1,0:T(8,128)(2,1)}, u32[]{:S(2)}, u32[]{:S(2)}) collective-permute-start(bf16[192,3072]{1,0:T(8,128)(2,1)} %collective-permute-done.2.refs_4_), channel_id=1, source_target_pairs={{8,0},{9,1},{10,2},{11,3},{12,4},{13,5},{14,6},{15,7},{16,8},{17,9... | collective-permute-start | bytes 3538952 | tf_op jit(solution)/shard_map/ppermute | solution.py:169
  54.2 44.7 %all-to-all-start = ((bf16[4,4,240,256]{3,2,1,0:T(8,128)(2,1)}), bf16[4,4,240,256]{3,2,1,0:T(8,128)(2,1)S(1)}, u32[]{:S(2)}, u32[]{:S(2)}) async-start(bf16[4,4,240,256]{3,2,1,0:T(8,128)(2,1)} %pieces.1), calls=%async_computation | async-start | bytes 3932160 | tf_op jit(solution)/shard_map/all_to_all | solution.py:477
  57.8 55.5 %collective-permute-start.6 = (bf16[192,3072]{1,0:T(8,128)(2,1)}, bf16[192,3072]{1,0:T(8,128)(2,1)}, u32[]{:S(2)}, u32[]{:S(2)}) collective-permute-start(bf16[192,3072]{1,0:T(8,128)(2,1)} %collective-permute-done.5.refs_2_), channel_id=1, source_target_pairs={{16,24},{17,25},{18,26},{19,27},{20,28},{21,29},{22,30},{23,31}} | collective-permute-start | bytes 3538952 | tf_op jit(solution)/shard_map/ppermute | solution.py:169
  81.5 31.9 %collective-permute-start.8 = (bf16[192,3072]{1,0:T(8,128)(2,1)}, bf16[192,3072]{1,0:T(8,128)(2,1)}, u32[]{:S(2)}, u32[]{:S(2)}) collective-permute-start(bf16[192,3072]{1,0:T(8,128)(2,1)} %collective-permute-done.7.refs_5_), channel_id=1, source_target_pairs={{8,0},{9,1},{10,2},{11,3},{12,4},{13,5},{14,6},{15,7}} | collective-permute-start | bytes 3538952 | tf_op jit(solution)/shard_map/ppermute | solution.py:169
  82.8 49.8 %collective-permute-start.11 = (bf16[256,3072]{1,0:T(8,128)(2,1)}, bf16[256,3072]{1,0:T(8,128)(2,1)}, u32[]{:S(2)}, u32[]{:S(2)}) collective-permute-start(bf16[256,3072]{1,0:T(8,128)(2,1)} %collective-permute-done.3.refs_9_), channel_id=1, source_target_pairs={{0,4},{1,5},{2,6},{3,7},{4,0},{5,1},{6,2},{7,3},{8,12},{9,13},{10,... | collective-permute-start | bytes 4718600 | tf_op jit(solution)/shard_map/ppermute | solution.py:169
  83.1 49.5 %collective-permute-start.12 = (bf16[256,3072]{1,0:T(8,128)(2,1)}, bf16[256,3072]{1,0:T(8,128)(2,1)}, u32[]{:S(2)}, u32[]{:S(2)}) collective-permute-start(bf16[256,3072]{1,0:T(8,128)(2,1)} %collective-permute-done.9.refs_12_), channel_id=1, source_target_pairs={{0,2},{1,3},{2,0},{3,1},{4,6},{5,7},{6,4},{7,5},{8,10},{9,11},{10,... | collective-permute-start | bytes 4718600 | tf_op jit(solution)/shard_map/ppermute | solution.py:169
  114.1 12.2 %all-to-all-start.2 = ((bf16[4,240,256]{2,1,0:T(8,128)(2,1)}), bf16[4,240,256]{2,1,0:T(8,128)(2,1)S(1)}, u32[]{:S(2)}, u32[]{:S(2)}) async-start(bf16[4,240,256]{2,1,0:T(8,128)(2,1)} %broadcast_in_dim.4), calls=%async_computation.2 | async-start | bytes 983040 | tf_op jit(solution)/shard_map/all_to_all | solution.py:482
  151.5 7.9 %collective-permute-start.13 = (bf16[768,1024]{1,0:T(8,128)(2,1)}, bf16[768,1024]{1,0:T(8,128)(2,1)}, u32[]{:S(2)}, u32[]{:S(2)}) collective-permute-start(bf16[768,1024]{1,0:T(8,128)(2,1)} %get-tuple-element.47), channel_id=1, source_target_pairs={{0,1},{1,0},{2,3},{3,2},{4,5},{5,4},{6,7},{7,6},{8,9},{9,8},{10,11... | collective-permute-start | bytes 4718600 | tf_op jit(solution)/shard_map/ppermute | solution.py:169
  155.7 27.3 %all-to-all-start.3 = ((bf16[4,4,240,256]{3,2,1,0:T(8,128)(2,1)}), bf16[4,4,240,256]{3,2,1,0:T(8,128)(2,1)S(1)}, u32[]{:S(2)}, u32[]{:S(2)}) async-start(bf16[4,4,240,256]{3,2,1,0:T(8,128)(2,1)} %broadcast_in_dim.5), calls=%async_computation.3 | async-start | bytes 3932160 | tf_op jit(solution)/shard_map/all_to_all | solution.py:482
  163.1 31.3 %collective-permute-start.14 = (bf16[192,1024]{1,0:T(8,128)(2,1)}, bf16[192,1024]{1,0:T(8,128)(2,1)}, u32[]{:S(2)}, u32[]{:S(2)}) collective-permute-start(bf16[192,1024]{1,0:T(8,128)(2,1)} %get-tuple-element.57), channel_id=1, source_target_pairs={{0,0},{1,8},{2,2},{3,10},{4,4},{5,12},{6,6},{7,14},{8,16},{9,24},{... | collective-permute-start | bytes 1179656 | tf_op jit(solution)/shard_map/ppermute | solution.py:169
  166.2 30.3 %collective-permute-start.15 = (bf16[192,1024]{1,0:T(8,128)(2,1)}, bf16[192,1024]{1,0:T(8,128)(2,1)}, u32[]{:S(2)}, u32[]{:S(2)}) collective-permute-start(bf16[192,1024]{1,0:T(8,128)(2,1)} %get-tuple-element.56), channel_id=1, source_target_pairs={{0,8},{1,16},{2,10},{3,18},{4,12},{5,20},{6,14},{7,22},{8,24},{9,0... | collective-permute-start | bytes 1179656 | tf_op jit(solution)/shard_map/ppermute | solution.py:169
  169.6 26.9 %collective-permute-start.16 = (bf16[192,1024]{1,0:T(8,128)(2,1)}, bf16[192,1024]{1,0:T(8,128)(2,1)}, u32[]{:S(2)}, u32[]{:S(2)}) collective-permute-start(bf16[192,1024]{1,0:T(8,128)(2,1)} %get-tuple-element.55), channel_id=1, source_target_pairs={{0,16},{1,24},{2,18},{3,26},{4,20},{5,28},{6,22},{7,30},{8,0},{9,8... | collective-permute-start | bytes 1179656 | tf_op jit(solution)/shard_map/ppermute | solution.py:169
  173.3 28.7 %collective-permute-start.17 = (bf16[192,1024]{1,0:T(8,128)(2,1)}, bf16[192,1024]{1,0:T(8,128)(2,1)}, u32[]{:S(2)}, u32[]{:S(2)}) collective-permute-start(bf16[192,1024]{1,0:T(8,128)(2,1)} %get-tuple-element.54), channel_id=1, source_target_pairs={{0,24},{1,0},{2,26},{3,2},{4,28},{5,4},{6,30},{7,6},{8,8},{9,16},{... | collective-permute-start | bytes 1179656 | tf_op jit(solution)/shard_map/ppermute | solution.py:169
  (9 other events, 44.8 us)

commit v12 on v11

--- a/solution.py
+++ b/solution.py
@@ -275,7 +275,7 @@
             pl.BlockSpec((tokens, queries.shape[1] + 2 * key_width), lambda h: (0, 0)),
             pl.BlockSpec((tokens, 3 * rank), lambda h: (0, 0)),
         ),
-        compiler_params=pltpu.CompilerParams(vmem_limit_bytes=56 << 20),
+        compiler_params=pltpu.CompilerParams(vmem_limit_bytes=32 << 20),
         cost_estimate=pl.CostEstimate(
             flops=10 * tokens * tokens * queries.shape[1],
             bytes_accessed=6 * tokens * queries.shape[1],

time: 208 us -> 208 us (level)
  waiting for transfers between devices: 92.3 us -> 84.1 us
  local copies, waits for them, and re-layouts: 9.96 us -> 15 us
  blocking collectives: 13.2 us -> 17.5 us
    ppermute x18, waiting for transfers between devices: 64.4 us -> 57.3 us  [send(): return lax.ppermute(value, AXES, pairs)]
    unnamed x24 -> x36, local copies, waits for them, and re-layouts: 1.94 us -> 6.96 us
    all_to_all x1, blocking collectives: 13.2 us -> 17.5 us  [scatter_sum(): lax.all_to_all(value, axis, 0, 0)]
    all_to_all x1, waiting for transfers between devices: 15.6 us -> 12.5 us  [scatter_sum(): lax.all_to_all(value, axis, 0, 0)]
  transfers between devices with their start and end apart: 21 -> 21, of which waited for: 10 -> 11; matrix products, arithmetic and copies ran while one was open for 7% -> 7% of each run, Pallas kernels for 6% -> 5%
where the time goes in v12:
time: 208 us; the launch traced here: 206 us
  waiting for transfers between devices  84.1 us (40%)
  starting transfers between devices  44.3 us (21%)
  Pallas kernels  33.3 us (16%)
  blocking collectives  17.5 us (8%)
  local copies, waits for them, and re-layouts  15 us (7%)
  other arithmetic  7.22 us (3%)
  matrix products  3.75 us (2%)
    ppermute x18, waiting for transfers between devices, send(): return lax.ppermute(value, AXES, pairs)  57.3 us
    ppermute x18, starting transfers between devices, send(): return lax.ppermute(value, AXES, pairs)  33.5 us
    pallas_call x1, Pallas kernels, term_halves(): pl.pallas_call(term_kernel, out_shape=(out, out), grid_spec=pltpu.Prefetc...  18.9 us
    all_to_all x1, blocking collectives, scatter_sum(): lax.all_to_all(value, axis, 0, 0)  17.5 us
    all_to_all x2, waiting for transfers between devices, gather(): lax.all_to_all(jnp.broadcast_to(value[None], (4, *value.shape)), axis, 0, 0)  14.4 us
    all_to_all x1, waiting for transfers between devices, scatter_sum(): lax.all_to_all(value, axis, 0, 0)  12.5 us
    all_to_all x2, starting transfers between devices, gather(): lax.all_to_all(jnp.broadcast_to(value[None], (4, *value.shape)), axis, 0, 0)  7.25 us
    pallas_call x1, Pallas kernels, attention(): pl.pallas_call(attention_kernel, out_shape=(jax.ShapeDtypeStruct((tokens,...  6.97 us
  transfers between devices with their start and end apart: 21, of which 11 were waited for; matrix products, arithmetic and copies ran while one was open for 7% of the time, Pallas kernels for 5%

profile of v12, /device:TPU:1, one launch (start us, length us, event | category | flops | bytes accessed | tf_op | source)
XLA Modules:
  0.0 206.4 jit_solution(4448477527921795294)
XLA Ops:
  0.7 2.9 %fusion.2 = (bf16[256,2048]{1,0:T(8,128)(2,1)}, bf16[256,2048]{1,0:T(8,128)(2,1)S(1)}) fusion(bf16[512,2048]{1,0:T(8,128)(2,1)} %param.18), kind=kLoop, calls=%fused_computation.12 | loop fusion | bytes 4194304 | tf_op jit(solution)/shard_map/slice | solution.py:514
  14.8 7.0 %attention.1 = (bf16[192,3072]{1,0:T(8,128)(2,1)S(1)}, f32[192,192]{1,0:T(8,128)S(1)}) custom-call(bf16[192,2048]{1,0:T(8,128)(2,1)S(1)} %copy-done.7, bf16[192,512]{1,0:T(8,128)(2,1)S(1)} %copy-done.10, bf16[192,512]{1,0:T(8,128)(2,1)S(1)} %copy-done.11, bf16[192,2048]{1,0:T(8,128)(2,1)S(1)} %copy-done.8, s32[192,1]{1,0:T(8,128)S(1)} %copy-done.5, ...), custom_call_target="tpu_custom_call" | custom-call | flops 754974720 | bytes 2359296 | tf_op jit(solution)/shard_map/attention/pallas_call | solution.py:257
  21.8 4.5 %collective-permute-start.1 = (bf16[192,3072]{1,0:T(8,128)(2,1)S(1)}, bf16[192,3072]{1,0:T(8,128)(2,1)}, u32[]{:S(2)}, u32[]{:S(2)}) collective-permute-start(bf16[192,3072]{1,0:T(8,128)(2,1)S(1)} %get-tuple-element.39.own_ref.refs_0_), channel_id=1, source_target_pairs={{0,8},{1,9},{2,10},{3,11},{4,12},{5,13},{6,14},{7,15},{8,16},{9,17... | collective-permute-start | bytes 3538952 | tf_op jit(solution)/shard_map/ppermute | solution.py:169
  31.2 11.0 %collective-permute-done.3.refs_9_ = bf16[256,3072]{1,0:T(8,128)(2,1)} collective-permute-done((bf16[256,3072]{1,0:T(8,128)(2,1)}, bf16[256,3072]{1,0:T(8,128)(2,1)}, u32[]{:S(2)}, u32[]{:S(2)}) %collective-permute-start.3) | collective-permute-done | bytes 1572896 | tf_op jit(solution)/shard_map/ppermute | solution.py:169
  44.8 2.1 %pieces.1 = bf16[4,4,240,256]{3,2,1,0:T(8,128)(2,1)} custom-call(bf16[192,384]{1,0:T(8,128)(2,1)S(1)} %add_convert_fusion.1.middle_ref, bf16[192,4096]{1,0:T(8,128)(2,1)S(1)} %copy-done.2, bf16[192,3072]{1,0:T(8,128)(2,1)S(1)} %get-tuple-element.39.own_ref.refs_0_), custom_call_target="tpu_custom_call" | custom-call | flops 377487360 | bytes 4718592 | tf_op jit(solution)/shard_map/pieces/pallas_call | solution.py:419
  46.9 2.4 %collective-permute-done.1.refs_1_ = bf16[192,3072]{1,0:T(8,128)(2,1)} collective-permute-done((bf16[192,3072]{1,0:T(8,128)(2,1)S(1)}, bf16[192,3072]{1,0:T(8,128)(2,1)}, u32[]{:S(2)}, u32[]{:S(2)}) %collective-permute-start.1) | collective-permute-done | bytes 1179680 | tf_op jit(solution)/shard_map/ppermute | solution.py:169
  49.3 4.9 %collective-permute-done.2.refs_4_ = bf16[192,3072]{1,0:T(8,128)(2,1)} collective-permute-done((bf16[192,3072]{1,0:T(8,128)(2,1)S(1)}, bf16[192,3072]{1,0:T(8,128)(2,1)}, u32[]{:S(2)}, u32[]{:S(2)}) %collective-permute-start.2) | collective-permute-done | bytes 1179680 | tf_op jit(solution)/shard_map/ppermute | solution.py:169
  57.3 3.6 %all-to-all-start = ((bf16[4,4,240,256]{3,2,1,0:T(8,128)(2,1)}), bf16[4,4,240,256]{3,2,1,0:T(8,128)(2,1)S(1)}, u32[]{:S(2)}, u32[]{:S(2)}) async-start(bf16[4,4,240,256]{3,2,1,0:T(8,128)(2,1)} %pieces.1), calls=%async_computation | async-start | bytes 3932160 | tf_op jit(solution)/shard_map/all_to_all | solution.py:477
  62.6 22.0 %collective-permute-done.7.refs_5_ = bf16[192,3072]{1,0:T(8,128)(2,1)} collective-permute-done((bf16[192,3072]{1,0:T(8,128)(2,1)}, bf16[192,3072]{1,0:T(8,128)(2,1)}, u32[]{:S(2)}, u32[]{:S(2)}) %collective-permute-start.7) | collective-permute-done | bytes 1179680 | tf_op jit(solution)/shard_map/ppermute | solution.py:169
  86.4 12.5 %all-to-all-done = bf16[4,4,240,256]{3,2,1,0:T(8,128)(2,1)S(1)} async-done(((bf16[4,4,240,256]{3,2,1,0:T(8,128)(2,1)}), bf16[4,4,240,256]{3,2,1,0:T(8,128)(2,1)S(1)}, u32[]{:S(2)}, u32[]{:S(2)}) %all-to-all-start) | async-done | bytes 1966112 | tf_op jit(solution)/shard_map/all_to_all | solution.py:477
  100.1 17.5 %all_to_all.20 = bf16[4,240,256]{2,1,0:T(8,128)(2,1)S(1)} all-to-all(bf16[4,240,256]{2,1,0:T(8,128)(2,1)} %reduce_sum.24), channel_id=1, replica_groups=mesh['hi'=4,'lo'=4,'tensor'=2] {'hi'}, dimensions={0} | all-to-all | bytes 983040 | tf_op jit(solution)/shard_map/all_to_all | solution.py:477
  118.5 3.6 %all-to-all-start.2 = ((bf16[4,240,256]{2,1,0:T(8,128)(2,1)}), bf16[4,240,256]{2,1,0:T(8,128)(2,1)S(1)}, u32[]{:S(2)}, u32[]{:S(2)}) async-start(bf16[4,240,256]{2,1,0:T(8,128)(2,1)} %broadcast_in_dim.4), calls=%async_computation.2 | async-start | bytes 983040 | tf_op jit(solution)/shard_map/all_to_all | solution.py:482
  122.7 8.1 %all-to-all-done.2 = bf16[4,240,256]{2,1,0:T(8,128)(2,1)S(1)} async-done(((bf16[4,240,256]{2,1,0:T(8,128)(2,1)}), bf16[4,240,256]{2,1,0:T(8,128)(2,1)S(1)}, u32[]{:S(2)}, u32[]{:S(2)}) %all-to-all-start.2) | async-done | bytes 491552 | tf_op jit(solution)/shard_map/all_to_all | solution.py:482
  132.6 18.9 %term.1 = (bf16[768,1024]{1,0:T(8,128)(2,1)}, bf16[768,1024]{1,0:T(8,128)(2,1)}) custom-call(s32[2]{0:T(128)} %pad_add_fusion.place_ref, bf16[192,3072]{1,0:T(8,128)(2,1)} %copy-done.3, bf16[192,3072]{1,0:T(8,128)(2,1)} %collective-permute-done.1.refs_1_, bf16[192,3072]{1,0:T(8,128)(2,1)} %collective-permute-done.5.refs_2_, ...), custom_call_target="tpu_custom_call" | custom-call | flops 9663676416 | bytes 20447232 | tf_op jit(solution)/shard_map/term/pallas_call | solution.py:333
  151.5 4.7 %collective-permute-start.13 = (bf16[768,1024]{1,0:T(8,128)(2,1)}, bf16[768,1024]{1,0:T(8,128)(2,1)}, u32[]{:S(2)}, u32[]{:S(2)}) collective-permute-start(bf16[768,1024]{1,0:T(8,128)(2,1)} %get-tuple-element.47), channel_id=1, source_target_pairs={{0,1},{1,0},{2,3},{3,2},{4,5},{5,4},{6,7},{7,6},{8,9},{9,8},{10,11... | collective-permute-start | bytes 4718600 | tf_op jit(solution)/shard_map/ppermute | solution.py:169
  157.6 3.6 %all-to-all-start.3 = ((bf16[4,4,240,256]{3,2,1,0:T(8,128)(2,1)}), bf16[4,4,240,256]{3,2,1,0:T(8,128)(2,1)S(1)}, u32[]{:S(2)}, u32[]{:S(2)}) async-start(bf16[4,4,240,256]{3,2,1,0:T(8,128)(2,1)} %broadcast_in_dim.5), calls=%async_computation.3 | async-start | bytes 3932160 | tf_op jit(solution)/shard_map/all_to_all | solution.py:482
  161.3 2.5 %add_convert_fusion = bf16[768,1024]{1,0:T(8,128)(2,1)S(1)} fusion(bf16[768,1024]{1,0:T(8,128)(2,1)} %collective-permute-done.13, bf16[768,1024]{1,0:T(8,128)(2,1)} %get-tuple-element.46), kind=kLoop, calls=%fused_computation | loop fusion | flops 3145728 | bytes 4718592 | tf_op jit(solution)/shard_map/convert_element_type | solution.py:562
  167.0 4.5 %collective-permute-start.15 = (bf16[192,1024]{1,0:T(8,128)(2,1)}, bf16[192,1024]{1,0:T(8,128)(2,1)}, u32[]{:S(2)}, u32[]{:S(2)}) collective-permute-start(bf16[192,1024]{1,0:T(8,128)(2,1)} %get-tuple-element.56), channel_id=1, source_target_pairs={{0,8},{1,16},{2,10},{3,18},{4,12},{5,20},{6,14},{7,22},{8,24},{9,0... | collective-permute-start | bytes 1179656 | tf_op jit(solution)/shard_map/ppermute | solution.py:169
  175.5 3.2 %fusion.added_ref = f32[192,4096]{1,0:T(8,128)} fusion(bf16[4096,192]{0,1:T(8,128)(2,1)S(1)} %copy-done, bf16[192,384]{1,0:T(8,128)(2,1)} %copy-done.4), kind=kOutput, calls=%fused_computation.9 | convolution fusion | flops 301989888 | bytes 4816896 | tf_op jit(solution)/shard_map/dot_general | solution.py:56
  178.6 6.3 %all-to-all-done.3.every_ref = bf16[4,4,240,256]{3,2,1,0:T(8,128)(2,1)S(1)} async-done(((bf16[4,4,240,256]{3,2,1,0:T(8,128)(2,1)}), bf16[4,4,240,256]{3,2,1,0:T(8,128)(2,1)S(1)}, u32[]{:S(2)}, u32[]{:S(2)}) %all-to-all-start.3) | async-done | bytes 1966112 | tf_op jit(solution)/shard_map/all_to_all | solution.py:482
  184.9 11.6 %collective-permute-done.14.refs_0_ = bf16[192,1024]{1,0:T(8,128)(2,1)} collective-permute-done((bf16[192,1024]{1,0:T(8,128)(2,1)}, bf16[192,1024]{1,0:T(8,128)(2,1)}, u32[]{:S(2)}, u32[]{:S(2)}) %collective-permute-start.14) | collective-permute-done | bytes 393248 | tf_op jit(solution)/shard_map/ppermute | solution.py:169
  196.5 2.1 %results.1 = (f32[192,4096]{1,0:T(8,128)}, f32[64,2048]{1,0:T(8,128)}, f32[2,64,512]{2,1,0:T(8,128)}) custom-call(bf16[4,4,240,256]{3,2,1,0:T(8,128)(2,1)S(1)} %all-to-all-done.3.every_ref), custom_call_target="tpu_custom_call" | custom-call | flops 983040 | bytes 5898240 | tf_op jit(solution)/shard_map/results/pallas_call | solution.py:457
  198.6 2.7 %collective-permute-done.17.refs_3_ = bf16[192,1024]{1,0:T(8,128)(2,1)} collective-permute-done((bf16[192,1024]{1,0:T(8,128)(2,1)}, bf16[192,1024]{1,0:T(8,128)(2,1)}, u32[]{:S(2)}, u32[]{:S(2)}) %collective-permute-start.17) | collective-permute-done | bytes 393248 | tf_op jit(solution)/shard_map/ppermute | solution.py:169
  203.2 3.2 %finish.1 = bf16[192,4096]{1,0:T(8,128)(2,1)} custom-call(s32[32]{0:T(128)S(1)} %stack.140.spot_ref, f32[192,4096]{1,0:T(8,128)S(1)} %copy-done.1, bf16[192,1024]{1,0:T(8,128)(2,1)} %collective-permute-done.14.refs_0_, bf16[192,1024]{1,0:T(8,128)(2,1)} %collective-permute-done.15.refs_1_, bf16[192,1024]{1,0:T(8,128)(2,1)} %collective-permute-done.16.refs_2_, ...), custom_call_target="tpu_custom_call" | custom-call | flops 786432 | bytes 6291456 | tf_op jit(solution)/shard_map/finish/pallas_call | solution.py:372
  (77 shorter events, 39.7 us)
Async XLA Ops:
  0.6 27.0 %copy-start = (bf16[4096,192]{0,1:T(8,128)(2,1)S(1)}, bf16[4096,192]{0,1:T(8,128)(2,1)}, u32[]{:S(2)}) copy-start(bf16[4096,192]{0,1:T(8,128)(2,1)} %param.21) | copy-start | bytes 4718596
  5.8 21.9 %copy-start.2 = (bf16[192,4096]{1,0:T(8,128)(2,1)S(1)}, bf16[192,4096]{1,0:T(8,128)(2,1)}, u32[]{:S(2)}) copy-start(bf16[192,4096]{1,0:T(8,128)(2,1)} %normed_ref.1) | copy-start | bytes 4718596
  5.8 36.5 %collective-permute-start.3 = (bf16[256,3072]{1,0:T(8,128)(2,1)}, bf16[256,3072]{1,0:T(8,128)(2,1)}, u32[]{:S(2)}, u32[]{:S(2)}) collective-permute-start(bf16[256,3072]{1,0:T(8,128)(2,1)} %pad_maximum_fusion.refs_7_), channel_id=1, source_target_pairs={{0,2},{1,3},{2,0},{3,1},{4,6},{5,7},{6,4},{7,5},{8,10},{9,11},{10,... | collective-permute-start | bytes 4718600 | tf_op jit(solution)/shard_map/ppermute | solution.py:169
  7.8 35.3 %collective-permute-start.4 = (bf16[256,3072]{1,0:T(8,128)(2,1)}, bf16[256,3072]{1,0:T(8,128)(2,1)}, u32[]{:S(2)}, u32[]{:S(2)}) collective-permute-start(bf16[256,3072]{1,0:T(8,128)(2,1)} %pad_maximum_fusion.refs_7_), channel_id=1, source_target_pairs={{0,4},{1,5},{2,6},{3,7},{4,0},{5,1},{6,2},{7,3},{8,12},{9,13},{10,... | collective-permute-start | bytes 4718600 | tf_op jit(solution)/shard_map/ppermute | solution.py:169
  21.8 22.9 %copy-start.3 = (bf16[192,3072]{1,0:T(8,128)(2,1)}, bf16[192,3072]{1,0:T(8,128)(2,1)S(1)}, u32[]{:S(2)}) copy-start(bf16[192,3072]{1,0:T(8,128)(2,1)S(1)} %get-tuple-element.39.own_ref.refs_0_) | copy-start | bytes 3538948
  21.8 27.5 %collective-permute-start.1 = (bf16[192,3072]{1,0:T(8,128)(2,1)S(1)}, bf16[192,3072]{1,0:T(8,128)(2,1)}, u32[]{:S(2)}, u32[]{:S(2)}) collective-permute-start(bf16[192,3072]{1,0:T(8,128)(2,1)S(1)} %get-tuple-element.39.own_ref.refs_0_), channel_id=1, source_target_pairs={{0,8},{1,9},{2,10},{3,11},{4,12},{5,13},{6,14},{7,15},{8,16},{9,17... | collective-permute-start | bytes 3538952 | tf_op jit(solution)/shard_map/ppermute | solution.py:169
  26.3 27.9 %collective-permute-start.2 = (bf16[192,3072]{1,0:T(8,128)(2,1)S(1)}, bf16[192,3072]{1,0:T(8,128)(2,1)}, u32[]{:S(2)}, u32[]{:S(2)}) collective-permute-start(bf16[192,3072]{1,0:T(8,128)(2,1)S(1)} %get-tuple-element.39.own_ref.refs_0_), channel_id=1, source_target_pairs={{8,0},{9,1},{10,2},{11,3},{12,4},{13,5},{14,6},{15,7},{16,8},{17,9... | collective-permute-start | bytes 3538952 | tf_op jit(solution)/shard_map/ppermute | solution.py:169
  28.3 16.3 %collective-permute-start = (f32[192,384]{1,0:T(8,128)S(1)}, f32[192,384]{1,0:T(8,128)S(1)}, u32[]{:S(2)}, u32[]{:S(2)}) collective-permute-start(f32[192,384]{1,0:T(8,128)S(1)} %pad_maximum_fusion.2), channel_id=1, source_target_pairs={{0,1},{1,0},{2,3},{3,2},{4,5},{5,4},{6,7},{7,6},{8,9},{9,8},{10,11... | collective-permute-start | bytes 884744 | tf_op jit(solution)/shard_map/ppermute | solution.py:169
  43.1 42.8 %collective-permute-start.10 = (bf16[256,3072]{1,0:T(8,128)(2,1)}, bf16[256,3072]{1,0:T(8,128)(2,1)}, u32[]{:S(2)}, u32[]{:S(2)}) collective-permute-start(bf16[256,3072]{1,0:T(8,128)(2,1)} %pad_maximum_fusion.1.refs_8_), channel_id=1, source_target_pairs={{0,2},{1,3},{2,0},{3,1},{4,6},{5,7},{6,4},{7,5},{8,10},{9,11},{10,... | collective-permute-start | bytes 4718600 | tf_op jit(solution)/shard_map/ppermute | solution.py:169
  43.4 42.5 %collective-permute-start.9 = (bf16[256,3072]{1,0:T(8,128)(2,1)}, bf16[256,3072]{1,0:T(8,128)(2,1)}, u32[]{:S(2)}, u32[]{:S(2)}) collective-permute-start(bf16[256,3072]{1,0:T(8,128)(2,1)} %pad_maximum_fusion.1.refs_8_), channel_id=1, source_target_pairs={{0,4},{1,5},{2,6},{3,7},{4,0},{5,1},{6,2},{7,3},{8,12},{9,13},{10,... | collective-permute-start | bytes 4718600 | tf_op jit(solution)/shard_map/ppermute | solution.py:169
  54.3 6.6 %collective-permute-start.5 = (bf16[192,3072]{1,0:T(8,128)(2,1)}, bf16[192,3072]{1,0:T(8,128)(2,1)}, u32[]{:S(2)}, u32[]{:S(2)}) collective-permute-start(bf16[192,3072]{1,0:T(8,128)(2,1)} %collective-permute-done.1.refs_1_), channel_id=1, source_target_pairs={{8,16},{9,17},{10,18},{11,19},{12,20},{13,21},{14,22},{15,23},{16,... | collective-permute-start | bytes 3538952 | tf_op jit(solution)/shard_map/ppermute | solution.py:169
  56.0 28.6 %collective-permute-start.7 = (bf16[192,3072]{1,0:T(8,128)(2,1)}, bf16[192,3072]{1,0:T(8,128)(2,1)}, u32[]{:S(2)}, u32[]{:S(2)}) collective-permute-start(bf16[192,3072]{1,0:T(8,128)(2,1)} %collective-permute-done.2.refs_4_), channel_id=1, source_target_pairs={{8,0},{9,1},{10,2},{11,3},{12,4},{13,5},{14,6},{15,7},{16,8},{17,9... | collective-permute-start | bytes 3538952 | tf_op jit(solution)/shard_map/ppermute | solution.py:169
  57.3 41.6 %all-to-all-start = ((bf16[4,4,240,256]{3,2,1,0:T(8,128)(2,1)}), bf16[4,4,240,256]{3,2,1,0:T(8,128)(2,1)S(1)}, u32[]{:S(2)}, u32[]{:S(2)}) async-start(bf16[4,4,240,256]{3,2,1,0:T(8,128)(2,1)} %pieces.1), calls=%async_computation | async-start | bytes 3932160 | tf_op jit(solution)/shard_map/all_to_all | solution.py:477
  60.9 56.8 %collective-permute-start.6 = (bf16[192,3072]{1,0:T(8,128)(2,1)}, bf16[192,3072]{1,0:T(8,128)(2,1)}, u32[]{:S(2)}, u32[]{:S(2)}) collective-permute-start(bf16[192,3072]{1,0:T(8,128)(2,1)} %collective-permute-done.5.refs_2_), channel_id=1, source_target_pairs={{16,24},{17,25},{18,26},{19,27},{20,28},{21,29},{22,30},{23,31}} | collective-permute-start | bytes 3538952 | tf_op jit(solution)/shard_map/ppermute | solution.py:169
  84.6 33.1 %collective-permute-start.8 = (bf16[192,3072]{1,0:T(8,128)(2,1)}, bf16[192,3072]{1,0:T(8,128)(2,1)}, u32[]{:S(2)}, u32[]{:S(2)}) collective-permute-start(bf16[192,3072]{1,0:T(8,128)(2,1)} %collective-permute-done.7.refs_5_), channel_id=1, source_target_pairs={{8,0},{9,1},{10,2},{11,3},{12,4},{13,5},{14,6},{15,7}} | collective-permute-start | bytes 3538952 | tf_op jit(solution)/shard_map/ppermute | solution.py:169
  85.9 46.7 %collective-permute-start.11 = (bf16[256,3072]{1,0:T(8,128)(2,1)}, bf16[256,3072]{1,0:T(8,128)(2,1)}, u32[]{:S(2)}, u32[]{:S(2)}) collective-permute-start(bf16[256,3072]{1,0:T(8,128)(2,1)} %collective-permute-done.3.refs_9_), channel_id=1, source_target_pairs={{0,4},{1,5},{2,6},{3,7},{4,0},{5,1},{6,2},{7,3},{8,12},{9,13},{10,... | collective-permute-start | bytes 4718600 | tf_op jit(solution)/shard_map/ppermute | solution.py:169
  86.1 46.5 %collective-permute-start.12 = (bf16[256,3072]{1,0:T(8,128)(2,1)}, bf16[256,3072]{1,0:T(8,128)(2,1)}, u32[]{:S(2)}, u32[]{:S(2)}) collective-permute-start(bf16[256,3072]{1,0:T(8,128)(2,1)} %collective-permute-done.9.refs_12_), channel_id=1, source_target_pairs={{0,2},{1,3},{2,0},{3,1},{4,6},{5,7},{6,4},{7,5},{8,10},{9,11},{10,... | collective-permute-start | bytes 4718600 | tf_op jit(solution)/shard_map/ppermute | solution.py:169
  118.5 12.3 %all-to-all-start.2 = ((bf16[4,240,256]{2,1,0:T(8,128)(2,1)}), bf16[4,240,256]{2,1,0:T(8,128)(2,1)S(1)}, u32[]{:S(2)}, u32[]{:S(2)}) async-start(bf16[4,240,256]{2,1,0:T(8,128)(2,1)} %broadcast_in_dim.4), calls=%async_computation.2 | async-start | bytes 983040 | tf_op jit(solution)/shard_map/all_to_all | solution.py:482
  151.5 9.8 %collective-permute-start.13 = (bf16[768,1024]{1,0:T(8,128)(2,1)}, bf16[768,1024]{1,0:T(8,128)(2,1)}, u32[]{:S(2)}, u32[]{:S(2)}) collective-permute-start(bf16[768,1024]{1,0:T(8,128)(2,1)} %get-tuple-element.47), channel_id=1, source_target_pairs={{0,1},{1,0},{2,3},{3,2},{4,5},{5,4},{6,7},{7,6},{8,9},{9,8},{10,11... | collective-permute-start | bytes 4718600 | tf_op jit(solution)/shard_map/ppermute | solution.py:169
  157.6 27.3 %all-to-all-start.3 = ((bf16[4,4,240,256]{3,2,1,0:T(8,128)(2,1)}), bf16[4,4,240,256]{3,2,1,0:T(8,128)(2,1)S(1)}, u32[]{:S(2)}, u32[]{:S(2)}) async-start(bf16[4,4,240,256]{3,2,1,0:T(8,128)(2,1)} %broadcast_in_dim.5), calls=%async_computation.3 | async-start | bytes 3932160 | tf_op jit(solution)/shard_map/all_to_all | solution.py:482
  165.1 31.4 %collective-permute-start.14 = (bf16[192,1024]{1,0:T(8,128)(2,1)}, bf16[192,1024]{1,0:T(8,128)(2,1)}, u32[]{:S(2)}, u32[]{:S(2)}) collective-permute-start(bf16[192,1024]{1,0:T(8,128)(2,1)} %get-tuple-element.57), channel_id=1, source_target_pairs={{0,0},{1,8},{2,2},{3,10},{4,4},{5,12},{6,6},{7,14},{8,16},{9,24},{... | collective-permute-start | bytes 1179656 | tf_op jit(solution)/shard_map/ppermute | solution.py:169
  167.0 31.6 %collective-permute-start.15 = (bf16[192,1024]{1,0:T(8,128)(2,1)}, bf16[192,1024]{1,0:T(8,128)(2,1)}, u32[]{:S(2)}, u32[]{:S(2)}) collective-permute-start(bf16[192,1024]{1,0:T(8,128)(2,1)} %get-tuple-element.56), channel_id=1, source_target_pairs={{0,8},{1,16},{2,10},{3,18},{4,12},{5,20},{6,14},{7,22},{8,24},{9,0... | collective-permute-start | bytes 1179656 | tf_op jit(solution)/shard_map/ppermute | solution.py:169
  171.5 27.0 %collective-permute-start.16 = (bf16[192,1024]{1,0:T(8,128)(2,1)}, bf16[192,1024]{1,0:T(8,128)(2,1)}, u32[]{:S(2)}, u32[]{:S(2)}) collective-permute-start(bf16[192,1024]{1,0:T(8,128)(2,1)} %get-tuple-element.55), channel_id=1, source_target_pairs={{0,16},{1,24},{2,18},{3,26},{4,20},{5,28},{6,22},{7,30},{8,0},{9,8... | collective-permute-start | bytes 1179656 | tf_op jit(solution)/shard_map/ppermute | solution.py:169
  173.2 28.1 %collective-permute-start.17 = (bf16[192,1024]{1,0:T(8,128)(2,1)}, bf16[192,1024]{1,0:T(8,128)(2,1)}, u32[]{:S(2)}, u32[]{:S(2)}) collective-permute-start(bf16[192,1024]{1,0:T(8,128)(2,1)} %get-tuple-element.54), channel_id=1, source_target_pairs={{0,24},{1,0},{2,26},{3,2},{4,28},{5,4},{6,30},{7,6},{8,8},{9,16},{... | collective-permute-start | bytes 1179656 | tf_op jit(solution)/shard_map/ppermute | solution.py:169
  (15 other events, 54.6 us)
